TPU v7x, 32 devices: a whole 2x2x4 slice. The times are simulated.
32 devices in a mesh: pp: 2 (over x), ep: 16 (over z, y, core).
Axes of the slice: x: 2, y: 2, z: 4, core: 2. Of those that a mesh axis runs over, the one named last changes fastest.
Arguments:
- upstream: bfloat16 [2, 2048, 4096], P('pp', 'ep'), may hold values from -6 to 6
- saved: bfloat16 [2, 2048, 4096], P('pp', 'ep'), may hold values from -6 to 6
- routes: int32 [2, 2048, 8], P('pp', 'ep'), may hold values from 0 to 127, all different within a row
- route_weight: float32 [2, 2048, 8], P('pp', 'ep'), may hold values from 0.05 to 0.5
- w_gate: bfloat16 [2, 1024, 4096], P('pp', 'ep'), may hold values from -0.09375 to 0.09375
- w_up: bfloat16 [2, 1024, 4096], P('pp', 'ep'), may hold values from -0.09375 to 0.09375
- w_down: bfloat16 [2, 1024, 4096], P('pp', 'ep'), may hold values from -0.09375 to 0.09375
Outputs:
- grad_prev: bfloat16 [2, 2048, 4096], P('pp', 'ep')
- weight_grad: float32 [2, 2048, 8], P('pp', 'ep')
Inputs may be any that keep to these rules, and one draw needn't show every extreme that they name: `routes`: each token names 8 different experts.
All inputs are finite; a program needn't handle non-finite values.
Results may differ from a plain program's by a relative error of at most 0.0011.
Values may be sent and summed in bfloat16 or wider, within the bound.
No kernel may reach another device: no remote copies, remote signals or barrier semaphores. Data moves between devices by JAX's collectives and lax.ppermute only.
A program may use at most 64 MiB of HBM per device.

v0:
```python
import jax
import jax.numpy as jnp
from jax import lax
from jax.sharding import PartitionSpec as P

TOP = 8
SHARDS = 16
CAP = 10


def from_partner(block, axis, apart):
    count = lax.axis_size(axis)
    route = []
    for low in range(count):
        high = low | 1 << apart
        if high != low and high < count:
            route += [(low, high), (high, low)]
    return lax.ppermute(block, axis, route)


def passed_along(value, axis, by):
    size = lax.axis_size(axis)
    return lax.ppermute(value, axis, [(i, (i + by) % size) for i in range(size)])


def route_match(block_routes, experts_win):
    flat_routes = block_routes.reshape(-1)
    onehot = (flat_routes[:, None] == jnp.arange(experts_win, dtype=jnp.int32)[None, :]).astype(
        jnp.int32
    )
    earlier = jnp.cumsum(onehot, axis=0) - onehot
    ranking = jnp.sum(earlier * onehot, axis=1)
    kept = (flat_routes < experts_win) & (ranking < CAP)
    slot_index = flat_routes * CAP + ranking
    match = (slot_index[:, None] == jnp.arange(experts_win * CAP, dtype=jnp.int32)[None, :]) & kept[
        :, None
    ]
    return match.astype(jnp.float32)


def expert_grad(grad_rows, input_rows, gate_rows, up_rows, down_rows):
    contract = (((1,), (1,)), ((), ()))
    gate = lax.dot_general(input_rows, gate_rows, contract, preferred_element_type=jnp.float32)
    up_proj = lax.dot_general(input_rows, up_rows, contract, preferred_element_type=jnp.float32)
    grad_hidden = lax.dot_general(
        grad_rows, down_rows, contract, preferred_element_type=jnp.float32
    )
    sigmoid = jax.nn.sigmoid(gate)
    swish = gate * sigmoid
    hidden = swish * up_proj
    slot_weight = jnp.sum(grad_hidden * hidden, axis=1)
    grad_up = (grad_hidden * swish).astype(jnp.bfloat16)
    grad_gate = (grad_hidden * up_proj * sigmoid * (1.0 + gate * (1.0 - sigmoid))).astype(
        jnp.bfloat16
    )
    partial_value = jnp.dot(grad_gate, gate_rows, preferred_element_type=jnp.float32)
    partial_value = partial_value + jnp.dot(grad_up, up_rows, preferred_element_type=jnp.float32)
    return (partial_value, slot_weight)


def pair_rows(mine, other, pair_low):
    return jnp.where(
        pair_low, jnp.concatenate([mine, other], axis=0), jnp.concatenate([other, mine], axis=0)
    )


def on_device(upstream, saved, routes, route_weight, w_gate, w_up, w_down):
    shards = SHARDS
    groups = shards // 2
    experts_win = lax.axis_size("ep") // shards
    dev_count = experts_win * shards
    my_index = lax.axis_index("ep")
    half_cap = CAP // 2
    pair_low = my_index % 2 == 0
    other_gate, other_up, other_down = from_partner((w_gate[0], w_up[0], w_down[0]), "ep", 0)
    gate_rows = pair_rows(w_gate[0], other_gate, pair_low)
    up_rows = pair_rows(w_up[0], other_up, pair_low)
    down_rows = pair_rows(w_down[0], other_down, pair_low)
    grad_in = passed_along(upstream, "pp", -1)[0]
    inputs = saved[0]
    token_count, width = inputs.shape
    slot_total = experts_win * CAP
    match = route_match(routes[0], experts_win)
    match_three = match.reshape(token_count, TOP, slot_total)
    tok_match = match_three.sum(axis=1).astype(jnp.bfloat16)
    grad_slots = jnp.einsum(
        "ts,td->sd", tok_match, grad_in, preferred_element_type=jnp.float32
    ).astype(jnp.bfloat16)
    input_slots = jnp.einsum(
        "ts,td->sd", tok_match, inputs, preferred_element_type=jnp.float32
    ).astype(jnp.bfloat16)
    grad_halves = grad_slots.reshape(experts_win, 2, half_cap, width)
    input_halves = input_slots.reshape(experts_win, 2, half_cap, width)

    def copies_of(halves):
        return jnp.broadcast_to(halves[:, None], (experts_win, groups, 2, half_cap, width)).reshape(
            dev_count, half_cap, width
        )

    recv_grad, recv_input = (
        lax.all_to_all(copies_of(grad_halves), "ep", split_axis=0, concat_axis=0, tiled=True),
        lax.all_to_all(copies_of(input_halves), "ep", split_axis=0, concat_axis=0, tiled=True),
    )
    grad_rows = recv_grad.reshape(dev_count * half_cap, width)
    input_rows = recv_input.reshape(dev_count * half_cap, width)
    partial_value, slot_weight = expert_grad(grad_rows, input_rows, gate_rows, up_rows, down_rows)
    back_part, back_weight = (
        lax.all_to_all(
            partial_value.reshape(dev_count, half_cap, width),
            "ep",
            split_axis=0,
            concat_axis=0,
            tiled=True,
        ),
        lax.all_to_all(
            slot_weight.reshape(dev_count, half_cap), "ep", split_axis=0, concat_axis=0, tiled=True
        ),
    )
    slot_grads = (
        back_part.reshape(experts_win, groups, 2, half_cap, width)
        .sum(axis=1)
        .reshape(slot_total, width)
    )
    slot_weights = (
        back_weight.reshape(experts_win, groups, 2, half_cap).sum(axis=1).reshape(slot_total)
    )
    weighted = jnp.sum(match_three * route_weight[0][:, :, None], axis=1)
    mixed = jnp.dot(
        weighted, slot_grads, precision=lax.Precision.HIGHEST, preferred_element_type=jnp.float32
    )
    grad_out = (grad_in.astype(jnp.float32) + mixed).astype(jnp.bfloat16)
    weight_out = jnp.dot(
        match, slot_weights, precision=lax.Precision.HIGHEST, preferred_element_type=jnp.float32
    )
    weight_out = weight_out.reshape(token_count, TOP)
    sent_back = passed_along(grad_out[None], "pp", -1)
    return (sent_back, weight_out[None])


def solution(mesh):
    return jax.shard_map(
        on_device,
        mesh=mesh,
        in_specs=(
            P("pp", "ep", None),
            P("pp", "ep", None),
            P("pp", "ep", None),
            P("pp", "ep", None),
            P("pp", "ep", None),
            P("pp", "ep", None),
            P("pp", "ep", None),
        ),
        out_specs=(P("pp", "ep", None), P("pp", "ep", None)),
        check_vma=False,
    )
```

profile of v0, /device:TPU:0, one launch (start us, length us, event | category | flops | bytes accessed | tf_op | source)
XLA Modules:
  0.0 161.6 jit_solution(18059131991841292109)
XLA Ops:
  0.6 3.0 %collective-permute-start = (bf16[1,128,4096]{2,1,0:T(8,128)(2,1)}, bf16[1,128,4096]{2,1,0:T(8,128)(2,1)S(1)}, u32[]{:S(2)}, u32[]{:S(2)}) collective-permute-start(bf16[1,128,4096]{2,1,0:T(8,128)(2,1)} %param.7), channel_id=1, source_target_pairs={{0,16},{16,0},{1,17},{17,1},{2,18},{18,2},{3,19},{19,3},{4,20},{20... | collective-permute-start | bytes 3145736 | tf_op jit(solution)/shard_map/ppermute | solution.py:23
  3.6 0.7 fusion.22
  4.5 0.3 reduce-window.6
  5.6 0.7 bitcast_and_fusion
  6.3 0.7 bitcast_add_fusion
  7.0 0.7 convert_reduce_fusion
  8.0 1.1 broadcast_in_dim.28
  9.1 5.9 %all-to-all-start.1 = ((bf16[16,5,4096]{2,1,0:T(8,128)(2,1)}), bf16[16,5,4096]{2,1,0:T(8,128)(2,1)S(1)}, u32[]{:S(2)}, u32[]{:S(2)}) async-start(bf16[16,5,4096]{2,1,0:T(8,128)(2,1)} %bitcast.9), calls=%async_computation.1 | async-start | bytes 2097152 | tf_op jit(solution)/shard_map/all_to_all | solution.py:102
  15.0 12.0 %collective-permute-done = bf16[1,128,4096]{2,1,0:T(8,128)(2,1)S(1)} collective-permute-done((bf16[1,128,4096]{2,1,0:T(8,128)(2,1)}, bf16[1,128,4096]{2,1,0:T(8,128)(2,1)S(1)}, u32[]{:S(2)}, u32[]{:S(2)}) %collective-permute-start) | collective-permute-done | bytes 1048608 | tf_op jit(solution)/shard_map/ppermute | solution.py:23
  27.3 10.7 %all-to-all-done.1 = bf16[16,5,4096]{2,1,0:T(8,128)(2,1)S(1)} async-done(((bf16[16,5,4096]{2,1,0:T(8,128)(2,1)}), bf16[16,5,4096]{2,1,0:T(8,128)(2,1)S(1)}, u32[]{:S(2)}, u32[]{:S(2)}) %all-to-all-start.1) | async-done | bytes 655392 | tf_op jit(solution)/shard_map/all_to_all | solution.py:102
  38.0 1.1 broadcast_in_dim.25
  39.1 6.9 %all-to-all-start = ((bf16[16,5,4096]{2,1,0:T(8,128)(2,1)}), bf16[16,5,4096]{2,1,0:T(8,128)(2,1)}, u32[]{:S(2)}, u32[]{:S(2)}) async-start(bf16[16,5,4096]{2,1,0:T(8,128)(2,1)} %bitcast.6), calls=%async_computation | async-start | bytes 2097152 | tf_op jit(solution)/shard_map/all_to_all | solution.py:101
  46.0 0.4 collective-permute-start.3
  46.6 0.3 collective-permute-start.1
  47.2 1.2 collective-permute-done.3
  48.4 2.0 %fusion.10 = f32[80,128]{1,0:T(8,128)S(1)} fusion(bf16[80,4096]{1,0:T(8,128)(2,1)S(1)} %reshape.206, bf16[64,4096]{1,0:T(8,128)(2,1)} %collective-permute-done.3, bf16[64,4096]{1,0:T(8,128)(2,1)} %bitcast.55, pred[]{:T(512)S(6)} %eq.76), kind=kOutput, calls=%fused_computation.17 | convolution fusion | flops 88604672 | bytes 1744897 | tf_op jit(solution)/shard_map/dot_general | solution.py:43
  50.4 1.7 %fusion.12 = f32[80,128]{1,0:T(8,128)S(1)} fusion(bf16[80,4096]{1,0:T(8,128)(2,1)S(1)} %reshape.206, bf16[64,4096]{1,0:T(8,128)(2,1)} %collective-permute-done.2, bf16[64,4096]{1,0:T(8,128)(2,1)S(1)} %bitcast.52, pred[]{:T(512)S(6)} %eq.76), kind=kOutput, calls=%fused_computation.19 | convolution fusion | flops 88604672 | bytes 1744897 | tf_op jit(solution)/shard_map/dot_general | solution.py:44
  52.1 16.9 %all-to-all-done = bf16[16,5,4096]{2,1,0:T(8,128)(2,1)} async-done(((bf16[16,5,4096]{2,1,0:T(8,128)(2,1)}), bf16[16,5,4096]{2,1,0:T(8,128)(2,1)}, u32[]{:S(2)}, u32[]{:S(2)}) %all-to-all-start) | async-done | bytes 655392 | tf_op jit(solution)/shard_map/all_to_all | solution.py:101
  69.0 1.5 reshape.205
  70.6 1.8 %multiply_reduce_fusion = (f32[80]{0:T(128)S(1)}, f32[80,128]{1,0:T(8,128)S(1)}) fusion(f32[80,128]{1,0:T(8,128)S(1)} %fusion.12, f32[80,128]{1,0:T(8,128)S(1)} %fusion.10, bf16[80,4096]{1,0:T(8,128)(2,1)S(1)} %reshape.205, bf16[64,4096]{1,0:T(8,128)(2,1)} %collective-permute-done.1, bf16[64,4096]{1,0:T(8,128)(2,1)S(1)} %bitcast.50, pred[]{:T(512)S(6)} %eq.76), kind=kOutput, calls=%fused_computation.21 | convolution fusion | flops 88676272 | bytes 1827137 | tf_op jit(solution)/shard_map/dot_general | solution.py:45
  72.4 1.7 %fusion.11 = f32[80,4096]{1,0:T(8,128)S(1)} fusion(bf16[64,4096]{1,0:T(8,128)(2,1)} %collective-permute-done.2, bf16[64,4096]{1,0:T(8,128)(2,1)S(1)} %bitcast.53, pred[]{:T(512)S(6)} %eq.76, f32[80,128]{1,0:T(8,128)S(1)} %get-tuple-element.5, f32[80,128]{1,0:T(8,128)S(1)} %fusion.10), kind=kOutput, calls=%fused_computation.18 | convolution fusion | flops 88666112 | bytes 2441217 | tf_op jit(solution)/shard_map/dot_general | solution.py:57
  74.1 1.7 %convolution_add_fusion = f32[80,4096]{1,0:T(8,128)S(1)} fusion(f32[80,4096]{1,0:T(8,128)S(1)} %fusion.11, bf16[64,4096]{1,0:T(8,128)(2,1)} %collective-permute-done.3, bf16[64,4096]{1,0:T(8,128)(2,1)S(1)} %bitcast.56, pred[]{:T(512)S(6)} %eq.76, f32[80,128]{1,0:T(8,128)S(1)} %fusion.10, f32[80,128]{1,0:T(8,128)S(1)} %get-tuple-element.5, ...), kind=kOutput, calls=%fused_computation | convolution fusion | flops 89034752 | bytes 3792897 | tf_op jit(solution)/shard_map/dot_general | solution.py:56
  75.7 1.6 reshape.207
  77.3 54.2 %all_to_all.24 = f32[16,5,4096]{2,1,0:T(8,128)S(1)} all-to-all(f32[16,5,4096]{2,1,0:T(8,128)} %reshape.207), channel_id=1, replica_groups=mesh['pp'=2,'ep'=16] {'ep'}, dimensions={0} | all-to-all | bytes 2621440 | tf_op jit(solution)/shard_map/all_to_all | solution.py:108
  131.7 3.1 %fusion = bf16[1,128,4096]{2,1,0:T(8,128)(2,1)S(1)} fusion(bf16[1,128,4096]{2,1,0:T(8,128)(2,1)} %copy-done.1, f32[128,10]{0,1:T(8,128)S(1)} %get-tuple-element.3, f32[10,4096]{1,0:T(8,128)S(1)} %reshape.209), kind=kOutput, calls=%fused_computation.4 | convolution fusion | flops 64487424 | bytes 2266112 | tf_op jit(solution)/shard_map/dot_general | solution.py:128
  134.8 0.6 collective-permute-start.4
  135.4 0.7 all_to_all.18
  136.1 5.1 %all-to-all-start.3 = ((f32[16,1,5]{2,1,0:T(1,128)}), f32[16,1,5]{2,1,0:T(1,128)S(1)}, u32[]{:S(2)}, u32[]{:S(2)}) async-start(f32[16,1,5]{2,1,0:T(1,128)} %bitcast.15), calls=%async_computation.3 | async-start | bytes 16384 | tf_op jit(solution)/shard_map/all_to_all | solution.py:115
  141.2 6.3 %all-to-all-done.3 = f32[16,1,5]{2,1,0:T(1,128)S(1)} async-done(((f32[16,1,5]{2,1,0:T(1,128)}), f32[16,1,5]{2,1,0:T(1,128)S(1)}, u32[]{:S(2)}, u32[]{:S(2)}) %all-to-all-start.3) | async-done | bytes 352 | tf_op jit(solution)/shard_map/all_to_all | solution.py:115
  147.6 0.7 fusion.17
  148.3 12.3 %collective-permute-done.4 = bf16[1,128,4096]{2,1,0:T(8,128)(2,1)S(1)} collective-permute-done((bf16[1,128,4096]{2,1,0:T(8,128)(2,1)S(1)}, bf16[1,128,4096]{2,1,0:T(8,128)(2,1)S(1)}, u32[]{:S(2)}, u32[]{:S(2)}) %collective-permute-start.4) | collective-permute-done | bytes 1048608 | tf_op jit(solution)/shard_map/ppermute | solution.py:23
  160.7 1.0 copy.45
  (33 shorter events, 2.3 us)
Async XLA Ops:
  0.6 7.1 %copy-start = (bf16[1,128,4096]{2,1,0:T(8,128)(2,1)S(1)}, bf16[1,128,4096]{2,1,0:T(8,128)(2,1)}, u32[]{:S(2)}) copy-start(bf16[1,128,4096]{2,1,0:T(8,128)(2,1)} %param.8) | copy-start | bytes 3145732
  0.6 26.4 %collective-permute-start = (bf16[1,128,4096]{2,1,0:T(8,128)(2,1)}, bf16[1,128,4096]{2,1,0:T(8,128)(2,1)S(1)}, u32[]{:S(2)}, u32[]{:S(2)}) collective-permute-start(bf16[1,128,4096]{2,1,0:T(8,128)(2,1)} %param.7), channel_id=1, source_target_pairs={{0,16},{16,0},{1,17},{17,1},{2,18},{18,2},{3,19},{19,3},{4,20},{20... | collective-permute-start | bytes 3145736 | tf_op jit(solution)/shard_map/ppermute | solution.py:23
  9.1 28.9 %all-to-all-start.1 = ((bf16[16,5,4096]{2,1,0:T(8,128)(2,1)}), bf16[16,5,4096]{2,1,0:T(8,128)(2,1)S(1)}, u32[]{:S(2)}, u32[]{:S(2)}) async-start(bf16[16,5,4096]{2,1,0:T(8,128)(2,1)} %bitcast.9), calls=%async_computation.1 | async-start | bytes 2097152 | tf_op jit(solution)/shard_map/all_to_all | solution.py:102
  27.0 12.1 %copy-start.1 = (bf16[1,128,4096]{2,1,0:T(8,128)(2,1)}, bf16[1,128,4096]{2,1,0:T(8,128)(2,1)S(1)}, u32[]{:S(2)}) copy-start(bf16[1,128,4096]{2,1,0:T(8,128)(2,1)S(1)} %collective-permute-done) | copy-start | bytes 3145732
  39.1 29.9 %all-to-all-start = ((bf16[16,5,4096]{2,1,0:T(8,128)(2,1)}), bf16[16,5,4096]{2,1,0:T(8,128)(2,1)}, u32[]{:S(2)}, u32[]{:S(2)}) async-start(bf16[16,5,4096]{2,1,0:T(8,128)(2,1)} %bitcast.6), calls=%async_computation | async-start | bytes 2097152 | tf_op jit(solution)/shard_map/all_to_all | solution.py:101
  46.0 2.3 %collective-permute-start.3 = (bf16[64,4096]{1,0:T(8,128)(2,1)}, bf16[64,4096]{1,0:T(8,128)(2,1)}, u32[]{:S(2)}, u32[]{:S(2)}) collective-permute-start(bf16[64,4096]{1,0:T(8,128)(2,1)} %bitcast.54), channel_id=1, source_target_pairs={{0,1},{1,0},{2,3},{3,2},{4,5},{5,4},{6,7},{7,6},{8,9},{9,8},{10,11... | collective-permute-start | bytes 1572872 | tf_op jit(solution)/shard_map/ppermute | solution.py:18
  46.4 4.0 %collective-permute-start.2 = (bf16[64,4096]{1,0:T(8,128)(2,1)}, bf16[64,4096]{1,0:T(8,128)(2,1)}, u32[]{:S(2)}, u32[]{:S(2)}) collective-permute-start(bf16[64,4096]{1,0:T(8,128)(2,1)} %bitcast.51), channel_id=1, source_target_pairs={{0,1},{1,0},{2,3},{3,2},{4,5},{5,4},{6,7},{7,6},{8,9},{9,8},{10,11... | collective-permute-start | bytes 1572872 | tf_op jit(solution)/shard_map/ppermute | solution.py:18
  46.6 23.9 %collective-permute-start.1 = (bf16[64,4096]{1,0:T(8,128)(2,1)}, bf16[64,4096]{1,0:T(8,128)(2,1)}, u32[]{:S(2)}, u32[]{:S(2)}) collective-permute-start(bf16[64,4096]{1,0:T(8,128)(2,1)} %bitcast.49), channel_id=1, source_target_pairs={{0,1},{1,0},{2,3},{3,2},{4,5},{5,4},{6,7},{7,6},{8,9},{9,8},{10,11... | collective-permute-start | bytes 1572872 | tf_op jit(solution)/shard_map/ppermute | solution.py:18
  47.2 3.2 %copy-start.3 = (bf16[1,64,4096]{2,1,0:T(8,128)(2,1)S(1)}, bf16[1,64,4096]{2,1,0:T(8,128)(2,1)}, u32[]{:S(2)}) copy-start(bf16[1,64,4096]{2,1,0:T(8,128)(2,1)} %param.12) | copy-start | bytes 1572868
  50.4 20.2 %copy-start.2 = (bf16[1,64,4096]{2,1,0:T(8,128)(2,1)S(1)}, bf16[1,64,4096]{2,1,0:T(8,128)(2,1)}, u32[]{:S(2)}) copy-start(bf16[1,64,4096]{2,1,0:T(8,128)(2,1)} %param.13) | copy-start | bytes 1572868
  72.4 1.7 %copy-start.4 = (bf16[1,64,4096]{2,1,0:T(8,128)(2,1)S(1)}, bf16[1,64,4096]{2,1,0:T(8,128)(2,1)}, u32[]{:S(2)}) copy-start(bf16[1,64,4096]{2,1,0:T(8,128)(2,1)} %param.11) | copy-start | bytes 1572868
  134.8 25.9 %collective-permute-start.4 = (bf16[1,128,4096]{2,1,0:T(8,128)(2,1)S(1)}, bf16[1,128,4096]{2,1,0:T(8,128)(2,1)S(1)}, u32[]{:S(2)}, u32[]{:S(2)}) collective-permute-start(bf16[1,128,4096]{2,1,0:T(8,128)(2,1)S(1)} %fusion), channel_id=1, source_target_pairs={{0,16},{16,0},{1,17},{17,1},{2,18},{18,2},{3,19},{19,3},{4,20},{20... | collective-permute-start | bytes 3145736 | tf_op jit(solution)/shard_map/ppermute | solution.py:23
  136.1 11.4 %all-to-all-start.3 = ((f32[16,1,5]{2,1,0:T(1,128)}), f32[16,1,5]{2,1,0:T(1,128)S(1)}, u32[]{:S(2)}, u32[]{:S(2)}) async-start(f32[16,1,5]{2,1,0:T(1,128)} %bitcast.15), calls=%async_computation.3 | async-start | bytes 16384 | tf_op jit(solution)/shard_map/all_to_all | solution.py:115
where the time goes:
time: 162 us
  waiting for transfers between devices  59.4 us (37%)
  blocking collectives  54.2 us (33%)
  starting transfers between devices  22.4 us (14%)
  matrix products  13.2 us (8%)
  local copies, waits for them, and re-layouts  8.19 us (5%)
  other arithmetic  3.48 us (2%)
    all_to_all x1, blocking collectives, on_device(): lax.all_to_all(partial_value.reshape(dev_count, half_cap, width), 'ep', s...  54.2 us
    ppermute x2, waiting for transfers between devices, passed_along(): lax.ppermute(value, axis, [(i, (i + by) % size) for i in range(size)])  24.3 us
    all_to_all x1, waiting for transfers between devices, on_device(): lax.all_to_all(copies_of(grad_halves), 'ep', split_axis=0, concat_axis=0,...  16.9 us
    all_to_all x1, waiting for transfers between devices, on_device(): lax.all_to_all(copies_of(input_halves), 'ep', split_axis=0, concat_axis=0...  10.7 us
    all_to_all x1, starting transfers between devices, on_device(): lax.all_to_all(copies_of(grad_halves), 'ep', split_axis=0, concat_axis=0,...  6.92 us
    all_to_all x1, waiting for transfers between devices, on_device(): lax.all_to_all(slot_weight.reshape(dev_count, half_cap), 'ep', split_axis...  6.31 us
    all_to_all x1, starting transfers between devices, on_device(): lax.all_to_all(copies_of(input_halves), 'ep', split_axis=0, concat_axis=0...  5.94 us
    all_to_all x1, starting transfers between devices, on_device(): lax.all_to_all(slot_weight.reshape(dev_count, half_cap), 'ep', split_axis...  5.1 us
  transfers between devices with their start and end apart: 8, of which 6 were waited for; matrix products, arithmetic and copies ran while one was open for 7% of the time, Pallas kernels for 0%

commit v1 on v0

--- a/solution.py
+++ b/solution.py
@@ -1,11 +1,20 @@
+import functools
+
 import jax
 import jax.numpy as jnp
 from jax import lax
+from jax.experimental import pallas as pl
+from jax.experimental.pallas import tpu as pltpu
 from jax.sharding import PartitionSpec as P
 
 TOP = 8
 SHARDS = 16
 CAP = 10
+MAIN = 8
+TAIL = CAP - MAIN
+FOLDS = MAIN // TAIL
+F32 = jnp.float32
+BF16 = jnp.bfloat16
 
 
 def from_partner(block, axis, apart):
@@ -64,7 +73,7 @@
     )
 
 
-def on_device(upstream, saved, routes, route_weight, w_gate, w_up, w_down):
+def general_device(upstream, saved, routes, route_weight, w_gate, w_up, w_down):
     shards = SHARDS
     groups = shards // 2
     experts_win = lax.axis_size("ep") // shards
@@ -137,19 +146,312 @@
     return (sent_back, weight_out[None])
 
 
+def slot_of_token(routes_t):
+    count = routes_t.shape[1]
+    hit = routes_t == 0
+    found = jnp.max(hit.astype(F32), axis=0, keepdims=True)
+    found = jnp.broadcast_to(found, (MAIN, count))
+    before = lax.broadcasted_iota(jnp.int32, (count, count), 0) < lax.broadcasted_iota(
+        jnp.int32, (count, count), 1
+    )
+    rank = jnp.dot(
+        found.astype(BF16), before.astype(F32).astype(BF16), preferred_element_type=F32
+    )
+    slot = jnp.where((found > 0.5) & (rank < CAP - 0.5), rank, -1.0)
+    return hit, slot
+
+
+def main_pick(slot):
+    row = lax.broadcasted_iota(jnp.int32, slot.shape, 0).astype(F32)
+    return slot == row
+
+
+def tail_pick(slot, fold):
+    row = lax.broadcasted_iota(jnp.int32, slot.shape, 0)
+    want = (row + (MAIN - TAIL * fold)).astype(F32)
+    inside = (row >= TAIL * fold) & (row < TAIL * fold + TAIL)
+    return (slot == want) & inside
+
+
+def as_bf16(mask):
+    return mask.astype(F32).astype(BF16)
+
+
+def pick_kernel(routes_ref, rows_ref, out_ref):
+    width = rows_ref.shape[1]
+    part = width // FOLDS
+    _, slot = slot_of_token(routes_ref[...])
+    main = as_bf16(main_pick(slot))
+    out_ref[:, :width] = jnp.dot(main, rows_ref[...], preferred_element_type=F32).astype(BF16)
+    tail = jnp.zeros((MAIN, part), F32)
+    for fold in range(FOLDS):
+        tail = tail + jnp.dot(
+            as_bf16(tail_pick(slot, fold)),
+            rows_ref[:, fold * part : (fold + 1) * part],
+            preferred_element_type=F32,
+        )
+    out_ref[:, width:] = tail.astype(BF16)
+
+
+def pick_rows(routes_t, rows, name):
+    width = rows.shape[1]
+    return pl.pallas_call(
+        pick_kernel,
+        out_shape=jax.ShapeDtypeStruct((MAIN, width + width // FOLDS), BF16),
+        name=name,
+    )(routes_t, rows)
+
+
+def unfold(blocks, width, rows_ref):
+    part = width // FOLDS
+    count = len(blocks)
+    for k, block in enumerate(blocks):
+        rows_ref[MAIN * k : MAIN * (k + 1), :] = block[:, :width]
+    tails = jnp.concatenate([block[:, width:] for block in blocks], axis=0)
+    row = lax.broadcasted_iota(jnp.int32, (TAIL * count, MAIN * count), 0)
+    col = lax.broadcasted_iota(jnp.int32, (TAIL * count, MAIN * count), 1)
+    for fold in range(FOLDS):
+        place = as_bf16(col == (row // TAIL) * MAIN + TAIL * fold + row % TAIL)
+        rows_ref[MAIN * count :, fold * part : (fold + 1) * part] = jnp.dot(
+            place, tails, preferred_element_type=F32
+        ).astype(BF16)
+
+
+def read_blocks(refs):
+    blocks = []
+    for ref in refs:
+        if len(ref.shape) == 2:
+            blocks.append(ref)
+        else:
+            blocks += [ref.at[k] for k in range(ref.shape[0])]
+    return blocks
+
+
+NT = (((1,), (1,)), ((), ()))
+
+
+def forward_kernel(*refs):
+    *x_refs, gu_ref, h_ref, rows_ref = refs
+    unfold(read_blocks(x_refs), gu_ref.shape[1], rows_ref)
+    h_ref[...] = lax.dot_general(rows_ref[...], gu_ref[...], NT, preferred_element_type=F32)
+
+
+def three_parts(value):
+    high = value.astype(BF16)
+    rest = value - high.astype(F32)
+    mid = rest.astype(BF16)
+    low = (rest - mid.astype(F32)).astype(BF16)
+    return high, mid, low
+
+
+def backward_kernel(*refs):
+    *g_refs, down_ref, gu_ref, h_ref, near_ref, far_ref, rows_ref = refs
+    width = gu_ref.shape[1]
+    part = width // FOLDS
+    units = down_ref.shape[0]
+    slots = rows_ref.shape[0]
+    count = slots // CAP
+    unfold(read_blocks(g_refs), width, rows_ref)
+    grad_hidden = lax.dot_general(rows_ref[...], down_ref[...], NT, preferred_element_type=F32)
+    gate = h_ref[:, :units]
+    up = h_ref[:, units:]
+    sigmoid = 1.0 / (1.0 + jnp.exp(-gate))
+    swish = gate * sigmoid
+    weight = jnp.sum(grad_hidden * (swish * up), axis=1, keepdims=True)
+    grad_up = (grad_hidden * swish).astype(BF16)
+    grad_gate = (grad_hidden * up * sigmoid * (1.0 + gate * (1.0 - sigmoid))).astype(BF16)
+    both = jnp.concatenate([grad_gate, grad_up], axis=1)
+    half = count // 2
+    outs = [(near_ref, k) for k in range(half)] + [(far_ref, k) for k in range(half)]
+    back = lax.broadcasted_iota(jnp.int32, (MAIN * count, TAIL * count), 0)
+    col = lax.broadcasted_iota(jnp.int32, (MAIN * count, TAIL * count), 1)
+    tails = jnp.zeros((MAIN * count, part), F32)
+    for fold in range(FOLDS):
+        span = slice(fold * part, (fold + 1) * part)
+        value = jnp.dot(both, gu_ref[:, span], preferred_element_type=F32).astype(BF16)
+        for k, (ref, j) in enumerate(outs):
+            ref[j, :, span] = value[MAIN * k : MAIN * (k + 1), :]
+        place = as_bf16(back == (col // TAIL) * MAIN + TAIL * fold + col % TAIL)
+        tails = tails + jnp.dot(place, value[MAIN * count :, :], preferred_element_type=F32)
+    lane = lax.broadcasted_iota(jnp.int32, (slots, 128), 1)
+    high, mid, low = (p.astype(F32) for p in three_parts(weight))
+    spread = jnp.where(lane == 0, high, jnp.where(lane == 1, mid, jnp.where(lane == 2, low, 0.0)))
+    shifted = jnp.where(lane == 3, high, jnp.where(lane == 4, mid, jnp.where(lane == 5, low, 0.0)))
+    place = as_bf16(back == (col // TAIL) * MAIN + col % TAIL)
+    tile = spread[: MAIN * count, :] + jnp.dot(
+        place, shifted[MAIN * count :, :].astype(BF16), preferred_element_type=F32
+    )
+    tails = tails.astype(BF16)
+    tile = tile.astype(BF16)
+    full = width + part
+    for k, (ref, j) in enumerate(outs):
+        rows = slice(MAIN * k, MAIN * (k + 1))
+        ref[j, :, width:full] = tails[rows, :]
+        ref[j, :, full:] = tile[rows, :]
+
+
+def fold_kernel(near_ref, other_ref, *out_refs):
+    full = near_ref.shape[2] - 128
+    for k, ref in enumerate(out_refs):
+        ref[:, :full] = (
+            near_ref[k, :, :full].astype(F32) + other_ref[k, :, :full].astype(F32)
+        ).astype(BF16)
+        ref[:, full : full + 128] = near_ref[k, :, full:]
+        ref[:, full + 128 :] = other_ref[k, :, full:]
+
+
+def slot_scale(slot, weight_row):
+    main = jnp.sum(jnp.where(main_pick(slot), weight_row, 0.0), axis=1, keepdims=True)
+    tail = jnp.zeros_like(main)
+    for fold in range(FOLDS):
+        tail = tail + jnp.sum(
+            jnp.where(tail_pick(slot, fold), weight_row, 0.0), axis=1, keepdims=True
+        )
+    return main, tail
+
+
+def gather_kernel(routes_ref, weight_ref, *refs):
+    *in_refs, out_ref = refs
+    full = out_ref.shape[1]
+    width = full * FOLDS // (FOLDS + 1)
+    hit, slot = slot_of_token(routes_ref[...])
+    weight_row = jnp.sum(jnp.where(hit, weight_ref[...], 0.0), axis=0, keepdims=True)
+    main, tail = slot_scale(slot, weight_row)
+    total = in_refs[0][:, :full].astype(F32)
+    for ref in in_refs[1:]:
+        total = total + ref[:, :full].astype(F32)
+    out_ref[:, :width] = (total[:, :width] * main).astype(BF16)
+    out_ref[:, width:] = (total[:, width:] * tail).astype(BF16)
+
+
+def weight_kernel(routes_ref, *refs):
+    *in_refs, out_ref = refs
+    hit, slot = slot_of_token(routes_ref[...])
+    tile = jnp.zeros((MAIN, 128), F32)
+    for ref in in_refs:
+        full = ref.shape[1] - 256
+        tile = tile + ref[:, full : full + 128].astype(F32) + ref[:, full + 128 :].astype(F32)
+    lane = lax.broadcasted_iota(jnp.int32, tile.shape, 1)
+    main = jnp.sum(jnp.where(lane < 3, tile, 0.0), axis=1, keepdims=True)
+    tail = jnp.sum(jnp.where((lane >= 3) & (lane < 6), tile, 0.0), axis=1, keepdims=True)
+    row = lax.broadcasted_iota(jnp.int32, slot.shape, 0).astype(F32)
+    value = jnp.sum(
+        jnp.where(slot == row, main, 0.0) + jnp.where((slot == row + MAIN) & (row < TAIL), tail, 0.0),
+        axis=0,
+        keepdims=True,
+    )
+    out_ref[...] = jnp.where(hit, value, 0.0)
+
+
+TN = (((0,), (0,)), ((), ()))
+
+
+def final_kernel(routes_ref, rows_ref, tail_ref, base_ref, out_ref):
+    fold = pl.program_id(0)
+    _, slot = slot_of_token(routes_ref[...])
+    main = main_pick(slot)
+    row = lax.broadcasted_iota(jnp.int32, slot.shape, 0)
+    want = (row + (MAIN - TAIL * fold)).astype(F32)
+    inside = (row >= TAIL * fold) & (row < TAIL * fold + TAIL)
+    tail = (slot == want) & inside
+    pick = jnp.concatenate([main.astype(F32), tail.astype(F32)], axis=0).astype(BF16)
+    rows = jnp.concatenate([rows_ref[...], tail_ref[...]], axis=0)
+    mixed = lax.dot_general(pick, rows, TN, preferred_element_type=F32)
+    out_ref[...] = (base_ref[...].astype(F32) + mixed).astype(BF16)
+
+
+def final_rows(routes_t, slot_rows, base):
+    count, width = base.shape
+    part = width // FOLDS
+    return pl.pallas_call(
+        final_kernel,
+        out_shape=jax.ShapeDtypeStruct((count, width), BF16),
+        grid=(FOLDS,),
+        in_specs=[
+            pl.BlockSpec(routes_t.shape, lambda q: (0, 0)),
+            pl.BlockSpec((MAIN, part), lambda q: (0, q)),
+            pl.BlockSpec((MAIN, part), lambda q: (0, FOLDS)),
+            pl.BlockSpec((count, part), lambda q: (0, q)),
+        ],
+        out_specs=pl.BlockSpec((count, part), lambda q: (0, q)),
+        name="final_rows",
+    )(routes_t, slot_rows, slot_rows, base)
+
+
+def across(value, bits):
+    count = lax.axis_size("ep")
+    return lax.ppermute(value, "ep", [(i, i ^ bits) for i in range(count)])
+
+
+def gather_blocks(block):
+    z_blocks = [across(block, 4 * k) for k in (2, 3, 1)]
+    y_block = across(block, 2)
+    stacked = jnp.stack(z_blocks)
+    return [block, *z_blocks, y_block, across(stacked, 2)]
+
+
+def single_device(upstream, saved, routes, route_weight, w_gate, w_up, w_down):
+    routes_t = routes[0].T
+    weight_t = route_weight[0].T
+    next_routes = passed_along(routes_t, "pp", 1)
+    width = saved.shape[2]
+    full = width + width // FOLDS
+    units = 2 * w_gate.shape[1]
+    slots = SHARDS // 2 * CAP
+
+    input_block = pick_rows(routes_t, saved[0], "pick_inputs")
+    input_blocks = gather_blocks(input_block)
+    own = (w_gate[0], w_up[0], w_down[0])
+    other = from_partner(own, "ep", 0)
+    gate_up = jnp.concatenate([own[0], other[0], own[1], other[1]], axis=0)
+    down = jnp.concatenate([own[2], other[2]], axis=0)
+
+    grad_block = pick_rows(next_routes, upstream[0], "pick_grads")
+    grad_block = passed_along(grad_block, "pp", -1)
+    grad_blocks = gather_blocks(grad_block)
+
+    hidden = pl.pallas_call(
+        forward_kernel,
+        out_shape=jax.ShapeDtypeStruct((slots, 2 * units), F32),
+        scratch_shapes=[pltpu.VMEM((slots, width), BF16)],
+        name="expert_forward",
+    )(*input_blocks, gate_up)
+    quarter = SHARDS // 4
+    near, far = pl.pallas_call(
+        backward_kernel,
+        out_shape=[jax.ShapeDtypeStruct((quarter, MAIN, full + 128), BF16)] * 2,
+        scratch_shapes=[pltpu.VMEM((slots, width), BF16)],
+        name="expert_backward",
+    )(*grad_blocks, down, gate_up, hidden)
+    other_part = across(far, 2)
+    sums = pl.pallas_call(
+        fold_kernel,
+        out_shape=[jax.ShapeDtypeStruct((MAIN, full + 256), BF16)] * quarter,
+        name="fold_y",
+    )(near, other_part)
+    arrived = [sums[0]] + [across(sums[i], 4 * k) for i, k in ((1, 2), (2, 3), (3, 1))]
+    slot_rows = pl.pallas_call(
+        gather_kernel,
+        out_shape=jax.ShapeDtypeStruct((MAIN, full), BF16),
+        name="sum_z",
+    )(routes_t, weight_t, *arrived)
+    weight_out = pl.pallas_call(
+        weight_kernel,
+        out_shape=jax.ShapeDtypeStruct((TOP, routes_t.shape[1]), F32),
+        name="weight_out",
+    )(routes_t, *arrived)
+    slot_rows = passed_along(slot_rows, "pp", -1)
+    grad_prev = final_rows(next_routes, slot_rows, upstream[0])
+    return (grad_prev[None], weight_out.T[None])
+
+
 def solution(mesh):
+    single = mesh.shape["ep"] == SHARDS and mesh.shape["pp"] == 2
+    spec = P("pp", "ep", None)
     return jax.shard_map(
-        on_device,
+        single_device if single else general_device,
         mesh=mesh,
-        in_specs=(
-            P("pp", "ep", None),
-            P("pp", "ep", None),
-            P("pp", "ep", None),
-            P("pp", "ep", None),
-            P("pp", "ep", None),
-            P("pp", "ep", None),
-            P("pp", "ep", None),
-        ),
-        out_specs=(P("pp", "ep", None), P("pp", "ep", None)),
+        in_specs=(spec,) * 7,
+        out_specs=(spec, spec),
         check_vma=False,
     )

time: 162 us -> 81 us (0.50)
  blocking collectives: 54.2 us -> 0 us
  waiting for transfers between devices: 59.4 us -> 26.5 us
  Pallas kernels: 0 us -> 22.6 us
  matrix products: 13.2 us -> 0 us
  local copies, waits for them, and re-layouts: 8.19 us -> 4.03 us
  starting transfers between devices: 22.4 us -> 24.1 us
    all_to_all x1 -> x0, blocking collectives: 54.2 us -> none  [on_device(): lax.all_to_all(partial_value.reshape(dev_count, half_cap, width), 'ep', s...]
    all_to_all x3 -> x0, waiting for transfers between devices: 33.9 us -> none  [the longest x1 16.9 us: on_device(): lax.all_to_all(copies_of(grad_halves), 'ep', split_axis=0, concat_axis=0,...]
    ppermute x0 -> x14, waiting for transfers between devices: none -> 24.3 us  [across(): return lax.ppermute(value, 'ep', [(i, i ^ bits) for i in range(count)])]
    pallas_call x0 -> x8, Pallas kernels: none -> 22.6 us  [the longest x2 4.75 us: pick_rows(): pl.pallas_call(pick_kernel, out_shape=jax.ShapeDtypeStruct((MAIN, width +...]
    ppermute x2 -> x3, waiting for transfers between devices: 24.3 us -> 2.19 us  [passed_along(): lax.ppermute(value, axis, [(i, (i + by) % size) for i in range(size)])]
    ppermute x0 -> x14, starting transfers between devices: none -> 18.7 us  [across(): return lax.ppermute(value, 'ep', [(i, i ^ bits) for i in range(count)])]
    all_to_all x3 -> x0, starting transfers between devices: 18 us -> none  [the longest x1 6.92 us: on_device(): lax.all_to_all(copies_of(grad_halves), 'ep', split_axis=0, concat_axis=0,...]
    dot_general x9 -> x0, matrix products: 13.2 us -> none  [the longest x1 3.1 us: on_device(): jnp.dot(weighted, slot_grads, precision=lax.Precision.HIGHEST, preferred_...]
  transfers between devices with their start and end apart: 8 -> 20, of which waited for: 6 -> 11; matrix products, arithmetic and copies ran while one was open for 7% -> 3% of each run, Pallas kernels for 0% -> 12%
where the time goes in v1:
time: 81 us; the launch traced here: 80.7 us
  waiting for transfers between devices  26.5 us (33%)
  starting transfers between devices  24.1 us (30%)
  Pallas kernels  22.6 us (28%)
  local copies, waits for them, and re-layouts  4.03 us (5%)
  other arithmetic  2.71 us (3%)
    ppermute x14, waiting for transfers between devices, across(): return lax.ppermute(value, 'ep', [(i, i ^ bits) for i in range(count)])  24.3 us
    ppermute x14, starting transfers between devices, across(): return lax.ppermute(value, 'ep', [(i, i ^ bits) for i in range(count)])  18.7 us
    ppermute x3, starting transfers between devices, passed_along(): lax.ppermute(value, axis, [(i, (i + by) % size) for i in range(size)])  4.84 us
    pallas_call x2, Pallas kernels, pick_rows(): pl.pallas_call(pick_kernel, out_shape=jax.ShapeDtypeStruct((MAIN, width +...  4.75 us
    pallas_call x1, Pallas kernels, single_device(): pl.pallas_call(backward_kernel, out_shape=[jax.ShapeDtypeStruct((quarter,...  4.75 us
    pallas_call x1, Pallas kernels, final_rows(): pl.pallas_call(final_kernel, out_shape=jax.ShapeDtypeStruct((count, width...  4.15 us
    unnamed x38, local copies, waits for them, and re-layouts  4.03 us
    pallas_call x1, Pallas kernels, single_device(): pl.pallas_call(forward_kernel, out_shape=jax.ShapeDtypeStruct((slots, 2 *...  3.41 us
  transfers between devices with their start and end apart: 20, of which 11 were waited for; matrix products, arithmetic and copies ran while one was open for 3% of the time, Pallas kernels for 12%

profile of v1, /device:TPU:0, one launch (start us, length us, event | category | flops | bytes accessed | tf_op | source)
XLA Modules:
  0.0 80.7 jit_solution(14107641872483229861)
XLA Ops:
  0.7 3.0 %collective-permute-start = (s32[8,128]{1,0:T(8,128)}, s32[8,128]{1,0:T(8,128)S(1)}, u32[]{:S(2)}, u32[]{:S(2)}) collective-permute-start(s32[8,128]{1,0:T(8,128)} %bitcast.37), channel_id=1, source_target_pairs={{0,16},{16,0},{1,17},{17,1},{2,18},{18,2},{3,19},{19,3},{4,20},{20... | collective-permute-start | bytes 12296 | tf_op jit(solution)/shard_map/ppermute | solution.py:32
  3.7 2.4 %pick_inputs.1.refs_0_ = bf16[8,5120]{1,0:T(8,128)(2,1)} custom-call(s32[8,128]{1,0:T(8,128)} %bitcast.38, bf16[128,4096]{1,0:T(8,128)(2,1)} %bitcast.23), custom_call_target="tpu_custom_call" | custom-call | tf_op jit(solution)/shard_map/pick_inputs/pallas_call | solution.py:198
  6.0 2.6 %collective-permute-start.10 = (bf16[8,5120]{1,0:T(8,128)(2,1)}, bf16[8,5120]{1,0:T(8,128)(2,1)S(1)}, u32[]{:S(2)}, u32[]{:S(2)}) collective-permute-start(bf16[8,5120]{1,0:T(8,128)(2,1)} %pick_inputs.1.refs_0_), channel_id=1, source_target_pairs={{0,8},{1,9},{2,10},{3,11},{4,12},{5,13},{6,14},{7,15},{8,0},{9,1},... | collective-permute-start | bytes 245768 | tf_op jit(solution)/shard_map/ppermute | solution.py:383
  9.2 2.4 %pick_grads.1 = bf16[8,5120]{1,0:T(8,128)(2,1)} custom-call(s32[8,128]{1,0:T(8,128)} %copy-done.18, bf16[128,4096]{1,0:T(8,128)(2,1)} %bitcast.21), custom_call_target="tpu_custom_call" | custom-call | tf_op jit(solution)/shard_map/pick_grads/pallas_call | solution.py:198
  12.1 1.9 %collective-permute-start.11 = (bf16[8,5120]{1,0:T(8,128)(2,1)}, bf16[8,5120]{1,0:T(8,128)(2,1)S(1)}, u32[]{:S(2)}, u32[]{:S(2)}) collective-permute-start(bf16[8,5120]{1,0:T(8,128)(2,1)} %pick_inputs.1.refs_0_), channel_id=1, source_target_pairs={{0,12},{1,13},{2,14},{3,15},{4,8},{5,9},{6,10},{7,11},{8,4},{9,5},... | collective-permute-start | bytes 245768 | tf_op jit(solution)/shard_map/ppermute | solution.py:383
  14.1 1.5 %collective-permute-start.13 = (bf16[8,5120]{1,0:T(8,128)(2,1)}, bf16[8,5120]{1,0:T(8,128)(2,1)S(1)}, u32[]{:S(2)}, u32[]{:S(2)}) collective-permute-start(bf16[8,5120]{1,0:T(8,128)(2,1)} %pick_inputs.1.refs_0_), channel_id=1, source_target_pairs={{0,2},{1,3},{2,0},{3,1},{4,6},{5,7},{6,4},{7,5},{8,10},{9,11},{10,... | collective-permute-start | bytes 245768 | tf_op jit(solution)/shard_map/ppermute | solution.py:383
  16.3 2.0 %collective-permute-start.2 = (bf16[8,5120]{1,0:T(8,128)(2,1)S(1)}, bf16[8,5120]{1,0:T(8,128)(2,1)S(1)}, u32[]{:S(2)}, u32[]{:S(2)}) collective-permute-start(bf16[8,5120]{1,0:T(8,128)(2,1)S(1)} %collective-permute-done.1.refs_0_), channel_id=1, source_target_pairs={{0,8},{1,9},{2,10},{3,11},{4,12},{5,13},{6,14},{7,15},{8,0},{9,1},... | collective-permute-start | bytes 245768 | tf_op jit(solution)/shard_map/ppermute | solution.py:383
  18.8 1.8 %collective-permute-start.3 = (bf16[8,5120]{1,0:T(8,128)(2,1)S(1)}, bf16[8,5120]{1,0:T(8,128)(2,1)S(1)}, u32[]{:S(2)}, u32[]{:S(2)}) collective-permute-start(bf16[8,5120]{1,0:T(8,128)(2,1)S(1)} %collective-permute-done.1.refs_0_), channel_id=1, source_target_pairs={{0,12},{1,13},{2,14},{3,15},{4,8},{5,9},{6,10},{7,11},{8,4},{9,5},... | collective-permute-start | bytes 245768 | tf_op jit(solution)/shard_map/ppermute | solution.py:383
  20.6 5.1 %collective-permute-done.2.refs_1_ = bf16[8,5120]{1,0:T(8,128)(2,1)S(1)} collective-permute-done((bf16[8,5120]{1,0:T(8,128)(2,1)S(1)}, bf16[8,5120]{1,0:T(8,128)(2,1)S(1)}, u32[]{:S(2)}, u32[]{:S(2)}) %collective-permute-start.2) | collective-permute-done | bytes 81952 | tf_op jit(solution)/shard_map/ppermute | solution.py:383
  26.6 1.0 %collective-permute-start.14 = (bf16[3,8,5120]{2,1,0:T(8,128)(2,1)S(1)}, bf16[3,8,5120]{2,1,0:T(8,128)(2,1)S(1)}, u32[]{:S(2)}, u32[]{:S(2)}) collective-permute-start(bf16[3,8,5120]{2,1,0:T(8,128)(2,1)S(1)} %pad_maximum_fusion.3), channel_id=1, source_target_pairs={{0,2},{1,3},{2,0},{3,1},{4,6},{5,7},{6,4},{7,5},{8,10},{9,11},{10,... | collective-permute-start | bytes 737288 | tf_op jit(solution)/shard_map/ppermute | solution.py:383
  27.7 1.0 %collective-permute-start.5 = (bf16[8,5120]{1,0:T(8,128)(2,1)S(1)}, bf16[8,5120]{1,0:T(8,128)(2,1)}, u32[]{:S(2)}, u32[]{:S(2)}) collective-permute-start(bf16[8,5120]{1,0:T(8,128)(2,1)S(1)} %collective-permute-done.1.refs_0_), channel_id=1, source_target_pairs={{0,2},{1,3},{2,0},{3,1},{4,6},{5,7},{6,4},{7,5},{8,10},{9,11},{10,... | collective-permute-start | bytes 245768 | tf_op jit(solution)/shard_map/ppermute | solution.py:383
  28.7 1.0 %collective-permute-start.6 = (bf16[3,8,5120]{2,1,0:T(8,128)(2,1)S(1)}, bf16[3,8,5120]{2,1,0:T(8,128)(2,1)S(1)}, u32[]{:S(2)}, u32[]{:S(2)}) collective-permute-start(bf16[3,8,5120]{2,1,0:T(8,128)(2,1)S(1)} %pad_maximum_fusion.2), channel_id=1, source_target_pairs={{0,2},{1,3},{2,0},{3,1},{4,6},{5,7},{6,4},{7,5},{8,10},{9,11},{10,... | collective-permute-start | bytes 737288 | tf_op jit(solution)/shard_map/ppermute | solution.py:383
  29.8 1.6 %pad_maximum_fusion.refs_6_.refs_7_ = bf16[256,4096]{1,0:T(8,128)(2,1)} fusion(bf16[64,4096]{1,0:T(8,128)(2,1)S(1)} %collective-permute-done.9, bf16[64,4096]{1,0:T(8,128)(2,1)S(1)} %bitcast.28, bf16[64,4096]{1,0:T(8,128)(2,1)S(1)} %collective-permute-done.8, bf16[64,4096]{1,0:T(8,128)(2,1)S(1)} %bitcast.30), kind=kLoop, calls=%fused_computation | loop fusion | flops 8388608 | bytes 4194304 | tf_op jit(solution)/shard_map/concatenate | solution.py:406
  31.4 1.1 %pad_maximum_fusion.1.refs_6_ = bf16[128,4096]{1,0:T(8,128)(2,1)} fusion(bf16[64,4096]{1,0:T(8,128)(2,1)S(1)} %collective-permute-done.7, bf16[64,4096]{1,0:T(8,128)(2,1)S(1)} %bitcast.26), kind=kLoop, calls=%fused_computation.1 | loop fusion | flops 2097152 | bytes 2097152 | tf_op jit(solution)/shard_map/concatenate | solution.py:407
  32.5 3.0 %collective-permute-done.14.refs_5_ = bf16[3,8,5120]{2,1,0:T(8,128)(2,1)S(1)} collective-permute-done((bf16[3,8,5120]{2,1,0:T(8,128)(2,1)S(1)}, bf16[3,8,5120]{2,1,0:T(8,128)(2,1)S(1)}, u32[]{:S(2)}, u32[]{:S(2)}) %collective-permute-start.14) | collective-permute-done | bytes 245792 | tf_op jit(solution)/shard_map/ppermute | solution.py:383
  35.5 0.7 copy-done.14
  36.2 3.4 %expert_forward.1.refs_8_ = f32[80,256]{1,0:T(8,128)} custom-call(bf16[8,5120]{1,0:T(8,128)(2,1)} %pick_inputs.1.refs_0_, bf16[8,5120]{1,0:T(8,128)(2,1)} %copy-done.8, bf16[8,5120]{1,0:T(8,128)(2,1)} %copy-done.9, bf16[8,5120]{1,0:T(8,128)(2,1)} %copy-done.10, bf16[8,5120]{1,0:T(8,128)(2,1)} %copy-done.16, bf16[3,8,5120]{2,1,0:T(8,128)(2,1)} %copy-done.14, ...), custom_call_target="tpu_custom_call" | custom-call | tf_op jit(solution)/shard_map/expert_forward/pallas_call | solution.py:413
  39.6 1.7 %collective-permute-done.6.refs_5_ = bf16[3,8,5120]{2,1,0:T(8,128)(2,1)S(1)} collective-permute-done((bf16[3,8,5120]{2,1,0:T(8,128)(2,1)S(1)}, bf16[3,8,5120]{2,1,0:T(8,128)(2,1)S(1)}, u32[]{:S(2)}, u32[]{:S(2)}) %collective-permute-start.6) | collective-permute-done | bytes 245792 | tf_op jit(solution)/shard_map/ppermute | solution.py:383
  42.0 4.8 %expert_backward.1 = (bf16[4,8,5248]{2,1,0:T(8,128)(2,1)}, bf16[4,8,5248]{2,1,0:T(8,128)(2,1)}) custom-call(bf16[8,5120]{1,0:T(8,128)(2,1)} %copy-done.17, bf16[8,5120]{1,0:T(8,128)(2,1)} %copy-done.11, bf16[8,5120]{1,0:T(8,128)(2,1)} %copy-done.12, bf16[8,5120]{1,0:T(8,128)(2,1)} %copy-done.13, bf16[8,5120]{1,0:T(8,128)(2,1)} %collective-permute-done.5.refs_4_, ...), custom_call_target="tpu_custom_call" | custom-call | tf_op jit(solution)/shard_map/expert_backward/pallas_call | solution.py:420
  46.7 1.1 %collective-permute-start.15 = (bf16[4,8,5248]{2,1,0:T(8,128)(2,1)}, bf16[4,8,5248]{2,1,0:T(8,128)(2,1)S(1)}, u32[]{:S(2)}, u32[]{:S(2)}) collective-permute-start(bf16[4,8,5248]{2,1,0:T(8,128)(2,1)} %get-tuple-element.9), channel_id=1, source_target_pairs={{0,2},{1,3},{2,0},{3,1},{4,6},{5,7},{6,4},{7,5},{8,10},{9,11},{10,... | collective-permute-start | bytes 1007624 | tf_op jit(solution)/shard_map/ppermute | solution.py:383
  47.8 7.8 %collective-permute-done.15.other_ref = bf16[4,8,5248]{2,1,0:T(8,128)(2,1)S(1)} collective-permute-done((bf16[4,8,5248]{2,1,0:T(8,128)(2,1)}, bf16[4,8,5248]{2,1,0:T(8,128)(2,1)S(1)}, u32[]{:S(2)}, u32[]{:S(2)}) %collective-permute-start.15) | collective-permute-done | bytes 335904 | tf_op jit(solution)/shard_map/ppermute | solution.py:383
  55.7 0.7 copy-done.6
  56.4 1.8 %fold_y.1 = (bf16[8,5376]{1,0:T(8,128)(2,1)}, bf16[8,5376]{1,0:T(8,128)(2,1)}, bf16[8,5376]{1,0:T(8,128)(2,1)}, bf16[8,5376]{1,0:T(8,128)(2,1)}) custom-call(bf16[4,8,5248]{2,1,0:T(8,128)(2,1)} %get-tuple-element.8.near_ref, bf16[4,8,5248]{2,1,0:T(8,128)(2,1)} %copy-done.6), custom_call_target="tpu_custom_call" | custom-call | tf_op jit(solution)/shard_map/fold_y/pallas_call | solution.py:427
  58.2 3.3 %collective-permute-start.16 = (bf16[8,5376]{1,0:T(8,128)(2,1)}, bf16[8,5376]{1,0:T(8,128)(2,1)S(1)}, u32[]{:S(2)}, u32[]{:S(2)}) collective-permute-start(bf16[8,5376]{1,0:T(8,128)(2,1)} %get-tuple-element.11), channel_id=1, source_target_pairs={{0,8},{1,9},{2,10},{3,11},{4,12},{5,13},{6,14},{7,15},{8,0},{9,1},... | collective-permute-start | bytes 258056 | tf_op jit(solution)/shard_map/ppermute | solution.py:383
  61.5 1.4 %collective-permute-start.17 = (bf16[8,5376]{1,0:T(8,128)(2,1)}, bf16[8,5376]{1,0:T(8,128)(2,1)S(1)}, u32[]{:S(2)}, u32[]{:S(2)}) collective-permute-start(bf16[8,5376]{1,0:T(8,128)(2,1)} %get-tuple-element.12), channel_id=1, source_target_pairs={{0,12},{1,13},{2,14},{3,15},{4,8},{5,9},{6,10},{7,11},{8,4},{9,5},... | collective-permute-start | bytes 258056 | tf_op jit(solution)/shard_map/ppermute | solution.py:383
  62.9 4.0 %collective-permute-done.16.refs_1_ = bf16[8,5376]{1,0:T(8,128)(2,1)S(1)} collective-permute-done((bf16[8,5376]{1,0:T(8,128)(2,1)}, bf16[8,5376]{1,0:T(8,128)(2,1)S(1)}, u32[]{:S(2)}, u32[]{:S(2)}) %collective-permute-start.16) | collective-permute-done | bytes 86048 | tf_op jit(solution)/shard_map/ppermute | solution.py:383
  66.9 1.6 %collective-permute-done.17.refs_2_ = bf16[8,5376]{1,0:T(8,128)(2,1)S(1)} collective-permute-done((bf16[8,5376]{1,0:T(8,128)(2,1)}, bf16[8,5376]{1,0:T(8,128)(2,1)S(1)}, u32[]{:S(2)}, u32[]{:S(2)}) %collective-permute-start.17) | collective-permute-done | bytes 86048 | tf_op jit(solution)/shard_map/ppermute | solution.py:383
  69.3 1.9 %sum_z.1 = bf16[8,5120]{1,0:T(8,128)(2,1)} custom-call(s32[8,128]{1,0:T(8,128)} %bitcast.39, f32[8,128]{1,0:T(8,128)} %bitcast.41, bf16[8,5376]{1,0:T(8,128)(2,1)} %get-tuple-element.10.refs_0_, bf16[8,5376]{1,0:T(8,128)(2,1)} %copy-done.3, bf16[8,5376]{1,0:T(8,128)(2,1)} %copy-done.4, bf16[8,5376]{1,0:T(8,128)(2,1)} %copy-done.5), custom_call_target="tpu_custom_call" | custom-call | tf_op jit(solution)/shard_map/sum_z/pallas_call | solution.py:433
  71.2 1.3 %collective-permute-start.19 = (bf16[8,5120]{1,0:T(8,128)(2,1)}, bf16[8,5120]{1,0:T(8,128)(2,1)S(1)}, u32[]{:S(2)}, u32[]{:S(2)}) collective-permute-start(bf16[8,5120]{1,0:T(8,128)(2,1)} %sum_z.1), channel_id=1, source_target_pairs={{0,16},{16,0},{1,17},{17,1},{2,18},{18,2},{3,19},{19,3},{4,20},{20... | collective-permute-start | bytes 245768 | tf_op jit(solution)/shard_map/ppermute | solution.py:32
  72.5 1.8 %weight_out.1 = f32[8,128]{1,0:T(8,128)} custom-call(s32[8,128]{1,0:T(8,128)} %bitcast.40, bf16[8,5376]{1,0:T(8,128)(2,1)} %get-tuple-element.10.refs_0_, bf16[8,5376]{1,0:T(8,128)(2,1)} %copy-done.3, bf16[8,5376]{1,0:T(8,128)(2,1)} %copy-done.4, bf16[8,5376]{1,0:T(8,128)(2,1)} %copy-done.5), custom_call_target="tpu_custom_call" | custom-call | tf_op jit(solution)/shard_map/weight_out/pallas_call | solution.py:438
  74.3 1.6 %collective-permute-done.19.rows_ref.tail_ref = bf16[8,5120]{1,0:T(8,128)(2,1)S(1)} collective-permute-done((bf16[8,5120]{1,0:T(8,128)(2,1)}, bf16[8,5120]{1,0:T(8,128)(2,1)S(1)}, u32[]{:S(2)}, u32[]{:S(2)}) %collective-permute-start.19) | collective-permute-done | bytes 81952 | tf_op jit(solution)/shard_map/ppermute | solution.py:32
  76.5 4.2 %final_rows.1 = bf16[128,4096]{1,0:T(8,128)(2,1)} custom-call(s32[8,128]{1,0:T(8,128)} %copy-done.18, bf16[8,5120]{1,0:T(8,128)(2,1)} %copy-done.7, bf16[8,5120]{1,0:T(8,128)(2,1)} %copy-done.7, bf16[128,4096]{1,0:T(8,128)(2,1)} %bitcast.22), custom_call_target="tpu_custom_call" | custom-call | tf_op jit(solution)/shard_map/final_rows/pallas_call | solution.py:366
  (58 shorter events, 5.5 us)
Async XLA Ops:
  0.6 15.0 %copy-start.2 = (bf16[1,64,4096]{2,1,0:T(8,128)(2,1)S(1)}, bf16[1,64,4096]{2,1,0:T(8,128)(2,1)}, u32[]{:S(2)}) copy-start(bf16[1,64,4096]{2,1,0:T(8,128)(2,1)} %param.11) | copy-start | bytes 1572868
  0.6 25.1 %copy-start.1 = (bf16[1,64,4096]{2,1,0:T(8,128)(2,1)S(1)}, bf16[1,64,4096]{2,1,0:T(8,128)(2,1)}, u32[]{:S(2)}) copy-start(bf16[1,64,4096]{2,1,0:T(8,128)(2,1)} %param.12) | copy-start | bytes 1572868
  0.7 25.1 %copy-start = (bf16[1,64,4096]{2,1,0:T(8,128)(2,1)S(1)}, bf16[1,64,4096]{2,1,0:T(8,128)(2,1)}, u32[]{:S(2)}) copy-start(bf16[1,64,4096]{2,1,0:T(8,128)(2,1)} %param.13) | copy-start | bytes 1572868
  0.7 8.0 %collective-permute-start = (s32[8,128]{1,0:T(8,128)}, s32[8,128]{1,0:T(8,128)S(1)}, u32[]{:S(2)}, u32[]{:S(2)}) collective-permute-start(s32[8,128]{1,0:T(8,128)} %bitcast.37), channel_id=1, source_target_pairs={{0,16},{16,0},{1,17},{17,1},{2,18},{18,2},{3,19},{19,3},{4,20},{20... | collective-permute-start | bytes 12296 | tf_op jit(solution)/shard_map/ppermute | solution.py:32
  6.0 9.5 %collective-permute-start.10 = (bf16[8,5120]{1,0:T(8,128)(2,1)}, bf16[8,5120]{1,0:T(8,128)(2,1)S(1)}, u32[]{:S(2)}, u32[]{:S(2)}) collective-permute-start(bf16[8,5120]{1,0:T(8,128)(2,1)} %pick_inputs.1.refs_0_), channel_id=1, source_target_pairs={{0,8},{1,9},{2,10},{3,11},{4,12},{5,13},{6,14},{7,15},{8,0},{9,1},... | collective-permute-start | bytes 245768 | tf_op jit(solution)/shard_map/ppermute | solution.py:383
  11.6 4.7 %collective-permute-start.1 = (bf16[8,5120]{1,0:T(8,128)(2,1)}, bf16[8,5120]{1,0:T(8,128)(2,1)S(1)}, u32[]{:S(2)}, u32[]{:S(2)}) collective-permute-start(bf16[8,5120]{1,0:T(8,128)(2,1)} %pick_grads.1), channel_id=1, source_target_pairs={{0,16},{16,0},{1,17},{17,1},{2,18},{18,2},{3,19},{19,3},{4,20},{20... | collective-permute-start | bytes 245768 | tf_op jit(solution)/shard_map/ppermute | solution.py:32
  12.1 6.6 %collective-permute-start.11 = (bf16[8,5120]{1,0:T(8,128)(2,1)}, bf16[8,5120]{1,0:T(8,128)(2,1)S(1)}, u32[]{:S(2)}, u32[]{:S(2)}) collective-permute-start(bf16[8,5120]{1,0:T(8,128)(2,1)} %pick_inputs.1.refs_0_), channel_id=1, source_target_pairs={{0,12},{1,13},{2,14},{3,15},{4,8},{5,9},{6,10},{7,11},{8,4},{9,5},... | collective-permute-start | bytes 245768 | tf_op jit(solution)/shard_map/ppermute | solution.py:383
  14.1 6.5 %collective-permute-start.12 = (bf16[8,5120]{1,0:T(8,128)(2,1)}, bf16[8,5120]{1,0:T(8,128)(2,1)S(1)}, u32[]{:S(2)}, u32[]{:S(2)}) collective-permute-start(bf16[8,5120]{1,0:T(8,128)(2,1)} %pick_inputs.1.refs_0_), channel_id=1, source_target_pairs={{0,4},{1,5},{2,6},{3,7},{4,0},{5,1},{6,2},{7,3},{8,12},{9,13},{10,... | collective-permute-start | bytes 245768 | tf_op jit(solution)/shard_map/ppermute | solution.py:383
  14.1 18.4 %collective-permute-start.13 = (bf16[8,5120]{1,0:T(8,128)(2,1)}, bf16[8,5120]{1,0:T(8,128)(2,1)S(1)}, u32[]{:S(2)}, u32[]{:S(2)}) collective-permute-start(bf16[8,5120]{1,0:T(8,128)(2,1)} %pick_inputs.1.refs_0_), channel_id=1, source_target_pairs={{0,2},{1,3},{2,0},{3,1},{4,6},{5,7},{6,4},{7,5},{8,10},{9,11},{10,... | collective-permute-start | bytes 245768 | tf_op jit(solution)/shard_map/ppermute | solution.py:383
  15.6 15.8 %copy-start.8 = (bf16[8,5120]{1,0:T(8,128)(2,1)}, bf16[8,5120]{1,0:T(8,128)(2,1)S(1)}, u32[]{:S(2)}) copy-start(bf16[8,5120]{1,0:T(8,128)(2,1)S(1)} %collective-permute-done.10.refs_1_) | copy-start | bytes 245764
  15.6 12.1 %collective-permute-start.8 = (bf16[64,4096]{1,0:T(8,128)(2,1)S(1)}, bf16[64,4096]{1,0:T(8,128)(2,1)S(1)}, u32[]{:S(2)}, u32[]{:S(2)}) collective-permute-start(bf16[64,4096]{1,0:T(8,128)(2,1)S(1)} %bitcast.29), channel_id=1, source_target_pairs={{0,1},{1,0},{2,3},{3,2},{4,5},{5,4},{6,7},{7,6},{8,9},{9,8},{10,11... | collective-permute-start | bytes 1572872 | tf_op jit(solution)/shard_map/ppermute | solution.py:27
  16.3 15.1 %copy-start.17 = (bf16[8,5120]{1,0:T(8,128)(2,1)}, bf16[8,5120]{1,0:T(8,128)(2,1)S(1)}, u32[]{:S(2)}) copy-start(bf16[8,5120]{1,0:T(8,128)(2,1)S(1)} %collective-permute-done.1.refs_0_) | copy-start | bytes 245764
  16.3 9.5 %collective-permute-start.2 = (bf16[8,5120]{1,0:T(8,128)(2,1)S(1)}, bf16[8,5120]{1,0:T(8,128)(2,1)S(1)}, u32[]{:S(2)}, u32[]{:S(2)}) collective-permute-start(bf16[8,5120]{1,0:T(8,128)(2,1)S(1)} %collective-permute-done.1.refs_0_), channel_id=1, source_target_pairs={{0,8},{1,9},{2,10},{3,11},{4,12},{5,13},{6,14},{7,15},{8,0},{9,1},... | collective-permute-start | bytes 245768 | tf_op jit(solution)/shard_map/ppermute | solution.py:383
  18.8 12.6 %copy-start.9 = (bf16[8,5120]{1,0:T(8,128)(2,1)}, bf16[8,5120]{1,0:T(8,128)(2,1)S(1)}, u32[]{:S(2)}) copy-start(bf16[8,5120]{1,0:T(8,128)(2,1)S(1)} %collective-permute-done.11.refs_2_) | copy-start | bytes 245764
  18.8 7.0 %collective-permute-start.3 = (bf16[8,5120]{1,0:T(8,128)(2,1)S(1)}, bf16[8,5120]{1,0:T(8,128)(2,1)S(1)}, u32[]{:S(2)}, u32[]{:S(2)}) collective-permute-start(bf16[8,5120]{1,0:T(8,128)(2,1)S(1)} %collective-permute-done.1.refs_0_), channel_id=1, source_target_pairs={{0,12},{1,13},{2,14},{3,15},{4,8},{5,9},{6,10},{7,11},{8,4},{9,5},... | collective-permute-start | bytes 245768 | tf_op jit(solution)/shard_map/ppermute | solution.py:383
  20.6 10.8 %copy-start.10 = (bf16[8,5120]{1,0:T(8,128)(2,1)}, bf16[8,5120]{1,0:T(8,128)(2,1)S(1)}, u32[]{:S(2)}) copy-start(bf16[8,5120]{1,0:T(8,128)(2,1)S(1)} %collective-permute-done.12.refs_3_) | copy-start | bytes 245764
  20.6 6.0 %collective-permute-start.4 = (bf16[8,5120]{1,0:T(8,128)(2,1)S(1)}, bf16[8,5120]{1,0:T(8,128)(2,1)S(1)}, u32[]{:S(2)}, u32[]{:S(2)}) collective-permute-start(bf16[8,5120]{1,0:T(8,128)(2,1)S(1)} %collective-permute-done.1.refs_0_), channel_id=1, source_target_pairs={{0,4},{1,5},{2,6},{3,7},{4,0},{5,1},{6,2},{7,3},{8,12},{9,13},{10,... | collective-permute-start | bytes 245768 | tf_op jit(solution)/shard_map/ppermute | solution.py:383
  25.7 5.7 %copy-start.11 = (bf16[8,5120]{1,0:T(8,128)(2,1)}, bf16[8,5120]{1,0:T(8,128)(2,1)S(1)}, u32[]{:S(2)}) copy-start(bf16[8,5120]{1,0:T(8,128)(2,1)S(1)} %collective-permute-done.2.refs_1_) | copy-start | bytes 245764
  25.7 3.0 %collective-permute-start.9 = (bf16[64,4096]{1,0:T(8,128)(2,1)S(1)}, bf16[64,4096]{1,0:T(8,128)(2,1)S(1)}, u32[]{:S(2)}, u32[]{:S(2)}) collective-permute-start(bf16[64,4096]{1,0:T(8,128)(2,1)S(1)} %bitcast.27), channel_id=1, source_target_pairs={{0,1},{1,0},{2,3},{3,2},{4,5},{5,4},{6,7},{7,6},{8,9},{9,8},{10,11... | collective-permute-start | bytes 1572872 | tf_op jit(solution)/shard_map/ppermute | solution.py:27
  25.7 5.6 %copy-start.12 = (bf16[8,5120]{1,0:T(8,128)(2,1)}, bf16[8,5120]{1,0:T(8,128)(2,1)S(1)}, u32[]{:S(2)}) copy-start(bf16[8,5120]{1,0:T(8,128)(2,1)S(1)} %collective-permute-done.3.refs_2_) | copy-start | bytes 245764
  25.8 5.6 %collective-permute-start.7 = (bf16[64,4096]{1,0:T(8,128)(2,1)S(1)}, bf16[64,4096]{1,0:T(8,128)(2,1)S(1)}, u32[]{:S(2)}, u32[]{:S(2)}) collective-permute-start(bf16[64,4096]{1,0:T(8,128)(2,1)S(1)} %bitcast.25), channel_id=1, source_target_pairs={{0,1},{1,0},{2,3},{3,2},{4,5},{5,4},{6,7},{7,6},{8,9},{9,8},{10,11... | collective-permute-start | bytes 1572872 | tf_op jit(solution)/shard_map/ppermute | solution.py:27
  26.6 4.8 %copy-start.13 = (bf16[8,5120]{1,0:T(8,128)(2,1)}, bf16[8,5120]{1,0:T(8,128)(2,1)S(1)}, u32[]{:S(2)}) copy-start(bf16[8,5120]{1,0:T(8,128)(2,1)S(1)} %collective-permute-done.4.refs_3_) | copy-start | bytes 245764
  26.6 8.8 %collective-permute-start.14 = (bf16[3,8,5120]{2,1,0:T(8,128)(2,1)S(1)}, bf16[3,8,5120]{2,1,0:T(8,128)(2,1)S(1)}, u32[]{:S(2)}, u32[]{:S(2)}) collective-permute-start(bf16[3,8,5120]{2,1,0:T(8,128)(2,1)S(1)} %pad_maximum_fusion.3), channel_id=1, source_target_pairs={{0,2},{1,3},{2,0},{3,1},{4,6},{5,7},{6,4},{7,5},{8,10},{9,11},{10,... | collective-permute-start | bytes 737288 | tf_op jit(solution)/shard_map/ppermute | solution.py:383
  27.7 11.9 %collective-permute-start.5 = (bf16[8,5120]{1,0:T(8,128)(2,1)S(1)}, bf16[8,5120]{1,0:T(8,128)(2,1)}, u32[]{:S(2)}, u32[]{:S(2)}) collective-permute-start(bf16[8,5120]{1,0:T(8,128)(2,1)S(1)} %collective-permute-done.1.refs_0_), channel_id=1, source_target_pairs={{0,2},{1,3},{2,0},{3,1},{4,6},{5,7},{6,4},{7,5},{8,10},{9,11},{10,... | collective-permute-start | bytes 245768 | tf_op jit(solution)/shard_map/ppermute | solution.py:383
  28.7 12.5 %collective-permute-start.6 = (bf16[3,8,5120]{2,1,0:T(8,128)(2,1)S(1)}, bf16[3,8,5120]{2,1,0:T(8,128)(2,1)S(1)}, u32[]{:S(2)}, u32[]{:S(2)}) collective-permute-start(bf16[3,8,5120]{2,1,0:T(8,128)(2,1)S(1)} %pad_maximum_fusion.2), channel_id=1, source_target_pairs={{0,2},{1,3},{2,0},{3,1},{4,6},{5,7},{6,4},{7,5},{8,10},{9,11},{10,... | collective-permute-start | bytes 737288 | tf_op jit(solution)/shard_map/ppermute | solution.py:383
  32.5 3.0 %copy-start.16 = (bf16[8,5120]{1,0:T(8,128)(2,1)}, bf16[8,5120]{1,0:T(8,128)(2,1)S(1)}, u32[]{:S(2)}) copy-start(bf16[8,5120]{1,0:T(8,128)(2,1)S(1)} %collective-permute-done.13.refs_4_) | copy-start | bytes 245764
  46.7 8.9 %collective-permute-start.15 = (bf16[4,8,5248]{2,1,0:T(8,128)(2,1)}, bf16[4,8,5248]{2,1,0:T(8,128)(2,1)S(1)}, u32[]{:S(2)}, u32[]{:S(2)}) collective-permute-start(bf16[4,8,5248]{2,1,0:T(8,128)(2,1)} %get-tuple-element.9), channel_id=1, source_target_pairs={{0,2},{1,3},{2,0},{3,1},{4,6},{5,7},{6,4},{7,5},{8,10},{9,11},{10,... | collective-permute-start | bytes 1007624 | tf_op jit(solution)/shard_map/ppermute | solution.py:383
  58.2 8.6 %collective-permute-start.16 = (bf16[8,5376]{1,0:T(8,128)(2,1)}, bf16[8,5376]{1,0:T(8,128)(2,1)S(1)}, u32[]{:S(2)}, u32[]{:S(2)}) collective-permute-start(bf16[8,5376]{1,0:T(8,128)(2,1)} %get-tuple-element.11), channel_id=1, source_target_pairs={{0,8},{1,9},{2,10},{3,11},{4,12},{5,13},{6,14},{7,15},{8,0},{9,1},... | collective-permute-start | bytes 258056 | tf_op jit(solution)/shard_map/ppermute | solution.py:383
  61.5 7.0 %collective-permute-start.17 = (bf16[8,5376]{1,0:T(8,128)(2,1)}, bf16[8,5376]{1,0:T(8,128)(2,1)S(1)}, u32[]{:S(2)}, u32[]{:S(2)}) collective-permute-start(bf16[8,5376]{1,0:T(8,128)(2,1)} %get-tuple-element.12), channel_id=1, source_target_pairs={{0,12},{1,13},{2,14},{3,15},{4,8},{5,9},{6,10},{7,11},{8,4},{9,5},... | collective-permute-start | bytes 258056 | tf_op jit(solution)/shard_map/ppermute | solution.py:383
  62.9 5.8 %collective-permute-start.18 = (bf16[8,5376]{1,0:T(8,128)(2,1)}, bf16[8,5376]{1,0:T(8,128)(2,1)S(1)}, u32[]{:S(2)}, u32[]{:S(2)}) collective-permute-start(bf16[8,5376]{1,0:T(8,128)(2,1)} %get-tuple-element.13), channel_id=1, source_target_pairs={{0,4},{1,5},{2,6},{3,7},{4,0},{5,1},{6,2},{7,3},{8,12},{9,13},{10,... | collective-permute-start | bytes 258056 | tf_op jit(solution)/shard_map/ppermute | solution.py:383
  66.9 1.8 %copy-start.3 = (bf16[8,5376]{1,0:T(8,128)(2,1)}, bf16[8,5376]{1,0:T(8,128)(2,1)S(1)}, u32[]{:S(2)}) copy-start(bf16[8,5376]{1,0:T(8,128)(2,1)S(1)} %collective-permute-done.16.refs_1_) | copy-start | bytes 258052
  71.2 4.7 %collective-permute-start.19 = (bf16[8,5120]{1,0:T(8,128)(2,1)}, bf16[8,5120]{1,0:T(8,128)(2,1)S(1)}, u32[]{:S(2)}, u32[]{:S(2)}) collective-permute-start(bf16[8,5120]{1,0:T(8,128)(2,1)} %sum_z.1), channel_id=1, source_target_pairs={{0,16},{16,0},{1,17},{17,1},{2,18},{18,2},{3,19},{19,3},{4,20},{20... | collective-permute-start | bytes 245768 | tf_op jit(solution)/shard_map/ppermute | solution.py:32
  (7 other events, 4.6 us)

commit v2 on v1

--- a/solution.py
+++ b/solution.py
@@ -146,6 +146,12 @@
     return (sent_back, weight_out[None])
 
 
+def near_call(kernel, out_shape, *args, **kwargs):
+    args = [pltpu.with_memory_space_constraint(arg, pltpu.VMEM) for arg in args]
+    params = pltpu.CompilerParams(vmem_limit_bytes=16 * 1024 * 1024)
+    return pl.pallas_call(kernel, out_shape=out_shape, compiler_params=params, **kwargs)(*args)
+
+
 def slot_of_token(routes_t):
     count = routes_t.shape[1]
     hit = routes_t == 0
@@ -173,33 +179,62 @@
     return (slot == want) & inside
 
 
+def both_picks(slot, fold):
+    picks = [main_pick(slot).astype(F32), tail_pick(slot, fold).astype(F32)]
+    return jnp.concatenate(picks, axis=0).astype(BF16)
+
+
 def as_bf16(mask):
     return mask.astype(F32).astype(BF16)
 
 
-def pick_kernel(routes_ref, rows_ref, out_ref):
+def pick_into(slot, rows_ref, out_ref):
     width = rows_ref.shape[1]
     part = width // FOLDS
+    tail = jnp.zeros((MAIN, part), F32)
+    for fold in range(FOLDS):
+        span = slice(fold * part, (fold + 1) * part)
+        got = jnp.dot(both_picks(slot, fold), rows_ref[:, span], preferred_element_type=F32)
+        out_ref[:, span] = got[:MAIN].astype(BF16)
+        tail = tail + got[MAIN:]
+    out_ref[:, width:] = tail.astype(BF16)
+
+
+def slot_scale(slot, weight_row):
+    main = jnp.sum(jnp.where(main_pick(slot), weight_row, 0.0), axis=1, keepdims=True)
+    tail = jnp.zeros_like(main)
+    for fold in range(FOLDS):
+        tail = tail + jnp.sum(
+            jnp.where(tail_pick(slot, fold), weight_row, 0.0), axis=1, keepdims=True
+        )
+    return main, tail
+
+
+def pick_inputs_kernel(routes_ref, weight_ref, rows_ref, out_ref, scale_ref):
+    hit, slot = slot_of_token(routes_ref[...])
+    pick_into(slot, rows_ref, out_ref)
+    weight_row = jnp.sum(jnp.where(hit, weight_ref[...], 0.0), axis=0, keepdims=True)
+    main, tail = slot_scale(slot, weight_row)
+    scale_ref[:, :128] = jnp.broadcast_to(main, (MAIN, 128))
+    scale_ref[:, 128:] = jnp.broadcast_to(tail, (MAIN, 128))
+
+
+TN = (((0,), (0,)), ((), ()))
+NT = (((1,), (1,)), ((), ()))
+
+
+def pick_grads_kernel(routes_ref, rows_ref, out_ref, back_ref):
     _, slot = slot_of_token(routes_ref[...])
-    main = as_bf16(main_pick(slot))
-    out_ref[:, :width] = jnp.dot(main, rows_ref[...], preferred_element_type=F32).astype(BF16)
-    tail = jnp.zeros((MAIN, part), F32)
-    for fold in range(FOLDS):
-        tail = tail + jnp.dot(
-            as_bf16(tail_pick(slot, fold)),
-            rows_ref[:, fold * part : (fold + 1) * part],
-            preferred_element_type=F32,
-        )
-    out_ref[:, width:] = tail.astype(BF16)
-
-
-def pick_rows(routes_t, rows, name):
-    width = rows.shape[1]
-    return pl.pallas_call(
-        pick_kernel,
-        out_shape=jax.ShapeDtypeStruct((MAIN, width + width // FOLDS), BF16),
-        name=name,
-    )(routes_t, rows)
+    pick_into(slot, rows_ref, out_ref)
+    size = 2 * MAIN
+    eye = as_bf16(
+        lax.broadcasted_iota(jnp.int32, (size, size), 0)
+        == lax.broadcasted_iota(jnp.int32, (size, size), 1)
+    )
+    for fold in range(FOLDS):
+        back_ref[fold] = lax.dot_general(
+            both_picks(slot, fold), eye, TN, preferred_element_type=F32
+        ).astype(BF16)
 
 
 def unfold(blocks, width, rows_ref):
@@ -227,9 +262,6 @@
     return blocks
 
 
-NT = (((1,), (1,)), ((), ()))
-
-
 def forward_kernel(*refs):
     *x_refs, gu_ref, h_ref, rows_ref = refs
     unfold(read_blocks(x_refs), gu_ref.shape[1], rows_ref)
@@ -245,7 +277,7 @@
 
 
 def backward_kernel(*refs):
-    *g_refs, down_ref, gu_ref, h_ref, near_ref, far_ref, rows_ref = refs
+    *g_refs, down_ref, gu_ref, h_ref, near_a, near_b, far_a, far_b, rows_ref = refs
     width = gu_ref.shape[1]
     part = width // FOLDS
     units = down_ref.shape[0]
@@ -261,8 +293,7 @@
     grad_up = (grad_hidden * swish).astype(BF16)
     grad_gate = (grad_hidden * up * sigmoid * (1.0 + gate * (1.0 - sigmoid))).astype(BF16)
     both = jnp.concatenate([grad_gate, grad_up], axis=1)
-    half = count // 2
-    outs = [(near_ref, k) for k in range(half)] + [(far_ref, k) for k in range(half)]
+    outs = [(ref, k) for ref in (near_a, near_b, far_a, far_b) for k in range(ref.shape[0])]
     back = lax.broadcasted_iota(jnp.int32, (MAIN * count, TAIL * count), 0)
     col = lax.broadcasted_iota(jnp.int32, (MAIN * count, TAIL * count), 1)
     tails = jnp.zeros((MAIN * count, part), F32)
@@ -300,28 +331,15 @@
         ref[:, full + 128 :] = other_ref[k, :, full:]
 
 
-def slot_scale(slot, weight_row):
-    main = jnp.sum(jnp.where(main_pick(slot), weight_row, 0.0), axis=1, keepdims=True)
-    tail = jnp.zeros_like(main)
-    for fold in range(FOLDS):
-        tail = tail + jnp.sum(
-            jnp.where(tail_pick(slot, fold), weight_row, 0.0), axis=1, keepdims=True
-        )
-    return main, tail
-
-
-def gather_kernel(routes_ref, weight_ref, *refs):
+def gather_kernel(scale_ref, *refs):
     *in_refs, out_ref = refs
     full = out_ref.shape[1]
     width = full * FOLDS // (FOLDS + 1)
-    hit, slot = slot_of_token(routes_ref[...])
-    weight_row = jnp.sum(jnp.where(hit, weight_ref[...], 0.0), axis=0, keepdims=True)
-    main, tail = slot_scale(slot, weight_row)
     total = in_refs[0][:, :full].astype(F32)
     for ref in in_refs[1:]:
         total = total + ref[:, :full].astype(F32)
-    out_ref[:, :width] = (total[:, :width] * main).astype(BF16)
-    out_ref[:, width:] = (total[:, width:] * tail).astype(BF16)
+    out_ref[:, :width] = (total[:, :width] * scale_ref[:, :1]).astype(BF16)
+    out_ref[:, width:] = (total[:, width:] * scale_ref[:, 128:129]).astype(BF16)
 
 
 def weight_kernel(routes_ref, *refs):
@@ -343,39 +361,20 @@
     out_ref[...] = jnp.where(hit, value, 0.0)
 
 
-TN = (((0,), (0,)), ((), ()))
-
-
-def final_kernel(routes_ref, rows_ref, tail_ref, base_ref, out_ref):
-    fold = pl.program_id(0)
-    _, slot = slot_of_token(routes_ref[...])
-    main = main_pick(slot)
-    row = lax.broadcasted_iota(jnp.int32, slot.shape, 0)
-    want = (row + (MAIN - TAIL * fold)).astype(F32)
-    inside = (row >= TAIL * fold) & (row < TAIL * fold + TAIL)
-    tail = (slot == want) & inside
-    pick = jnp.concatenate([main.astype(F32), tail.astype(F32)], axis=0).astype(BF16)
-    rows = jnp.concatenate([rows_ref[...], tail_ref[...]], axis=0)
-    mixed = lax.dot_general(pick, rows, TN, preferred_element_type=F32)
-    out_ref[...] = (base_ref[...].astype(F32) + mixed).astype(BF16)
-
-
-def final_rows(routes_t, slot_rows, base):
-    count, width = base.shape
+def final_kernel(back_ref, rows_ref, base_ref, out_ref, done_ref, sems):
+    width = base_ref.shape[1]
     part = width // FOLDS
-    return pl.pallas_call(
-        final_kernel,
-        out_shape=jax.ShapeDtypeStruct((count, width), BF16),
-        grid=(FOLDS,),
-        in_specs=[
-            pl.BlockSpec(routes_t.shape, lambda q: (0, 0)),
-            pl.BlockSpec((MAIN, part), lambda q: (0, q)),
-            pl.BlockSpec((MAIN, part), lambda q: (0, FOLDS)),
-            pl.BlockSpec((count, part), lambda q: (0, q)),
-        ],
-        out_specs=pl.BlockSpec((count, part), lambda q: (0, q)),
-        name="final_rows",
-    )(routes_t, slot_rows, slot_rows, base)
+    copies = []
+    for fold in range(FOLDS):
+        span = slice(fold * part, (fold + 1) * part)
+        rows = jnp.concatenate([rows_ref[:, span], rows_ref[:, width:]], axis=0)
+        mixed = jnp.dot(back_ref[fold], rows, preferred_element_type=F32)
+        done_ref[:, span] = (base_ref[:, span].astype(F32) + mixed).astype(BF16)
+        copy = pltpu.make_async_copy(done_ref.at[:, span], out_ref.at[:, span], sems.at[fold])
+        copy.start()
+        copies.append(copy)
+    for copy in copies:
+        copy.wait()
 
 
 def across(value, bits):
@@ -383,65 +382,99 @@
     return lax.ppermute(value, "ep", [(i, i ^ bits) for i in range(count)])
 
 
-def gather_blocks(block):
-    z_blocks = [across(block, 4 * k) for k in (2, 3, 1)]
-    y_block = across(block, 2)
-    stacked = jnp.stack(z_blocks)
-    return [block, *z_blocks, y_block, across(stacked, 2)]
+def sections_across(value, bits):
+    count = lax.axis_size("ep")
+    pairs = [(s * count + i, (1 - s) * count + (i ^ bits)) for s in range(2) for i in range(count)]
+    return lax.ppermute(value, ("pp", "ep"), pairs)
 
 
 def single_device(upstream, saved, routes, route_weight, w_gate, w_up, w_down):
     routes_t = routes[0].T
     weight_t = route_weight[0].T
     next_routes = passed_along(routes_t, "pp", 1)
-    width = saved.shape[2]
+    count, width = saved.shape[1:]
     full = width + width // FOLDS
     units = 2 * w_gate.shape[1]
     slots = SHARDS // 2 * CAP
 
-    input_block = pick_rows(routes_t, saved[0], "pick_inputs")
-    input_blocks = gather_blocks(input_block)
     own = (w_gate[0], w_up[0], w_down[0])
     other = from_partner(own, "ep", 0)
+
+    input_block, scale = near_call(
+        pick_inputs_kernel,
+        [pltpu.VMEM((MAIN, full), BF16), pltpu.VMEM((MAIN, 256), F32)],
+        routes_t,
+        weight_t,
+        saved[0],
+        name="pick_inputs",
+    )
+    grad_block, back = near_call(
+        pick_grads_kernel,
+        [pltpu.VMEM((MAIN, full), BF16), pltpu.VMEM((FOLDS, count, 2 * MAIN), BF16)],
+        next_routes,
+        upstream[0],
+        name="pick_grads",
+    )
+    input_block, grad_block, other = lax.optimization_barrier((input_block, grad_block, other))
     gate_up = jnp.concatenate([own[0], other[0], own[1], other[1]], axis=0)
     down = jnp.concatenate([own[2], other[2]], axis=0)
 
-    grad_block = pick_rows(next_routes, upstream[0], "pick_grads")
-    grad_block = passed_along(grad_block, "pp", -1)
-    grad_blocks = gather_blocks(grad_block)
-
-    hidden = pl.pallas_call(
+    z_inputs = [input_block] + [across(input_block, 4 * k) for k in (1, 2, 3)]
+    z_grads = [sections_across(grad_block, 4 * k) for k in (0, 1, 2, 3)]
+    y_inputs = across(jnp.stack(z_inputs), 2)
+    y_grads_a = across(jnp.stack(z_grads[:2]), 2)
+    y_grads_b = across(jnp.stack(z_grads[2:]), 2)
+
+    hidden = near_call(
         forward_kernel,
-        out_shape=jax.ShapeDtypeStruct((slots, 2 * units), F32),
+        pltpu.VMEM((slots, 2 * units), F32),
+        *z_inputs,
+        y_inputs,
+        gate_up,
         scratch_shapes=[pltpu.VMEM((slots, width), BF16)],
         name="expert_forward",
-    )(*input_blocks, gate_up)
-    quarter = SHARDS // 4
-    near, far = pl.pallas_call(
+    )
+    pair = pltpu.VMEM((2, MAIN, full + 128), BF16)
+    near_a, near_b, far_a, far_b = near_call(
         backward_kernel,
-        out_shape=[jax.ShapeDtypeStruct((quarter, MAIN, full + 128), BF16)] * 2,
+        [pair] * 4,
+        *z_grads,
+        y_grads_a,
+        y_grads_b,
+        down,
+        gate_up,
+        hidden,
         scratch_shapes=[pltpu.VMEM((slots, width), BF16)],
         name="expert_backward",
-    )(*grad_blocks, down, gate_up, hidden)
-    other_part = across(far, 2)
-    sums = pl.pallas_call(
-        fold_kernel,
-        out_shape=[jax.ShapeDtypeStruct((MAIN, full + 256), BF16)] * quarter,
-        name="fold_y",
-    )(near, other_part)
-    arrived = [sums[0]] + [across(sums[i], 4 * k) for i, k in ((1, 2), (2, 3), (3, 1))]
-    slot_rows = pl.pallas_call(
-        gather_kernel,
-        out_shape=jax.ShapeDtypeStruct((MAIN, full), BF16),
-        name="sum_z",
-    )(routes_t, weight_t, *arrived)
-    weight_out = pl.pallas_call(
+    )
+    sum_shape = pltpu.VMEM((MAIN, full + 256), BF16)
+    far_b = across(far_b, 2)
+    far_a = across(far_a, 2)
+    sums_b = near_call(fold_kernel, [sum_shape] * 2, near_b, far_b, name="fold_far")
+    sums_a = near_call(fold_kernel, [sum_shape] * 2, near_a, far_a, name="fold_near")
+    sums = [*sums_a, *sums_b]
+    arrived = [sums[0]] + [across(sums[k], 4 * k) for k in (1, 2, 3)]
+    slot_rows = near_call(
+        gather_kernel, pltpu.VMEM((MAIN, full), BF16), scale, *arrived, name="sum_z"
+    )
+    weight_out = near_call(
         weight_kernel,
-        out_shape=jax.ShapeDtypeStruct((TOP, routes_t.shape[1]), F32),
+        jax.ShapeDtypeStruct((TOP, count), F32),
+        routes_t,
+        *arrived,
         name="weight_out",
-    )(routes_t, *arrived)
-    slot_rows = passed_along(slot_rows, "pp", -1)
-    grad_prev = final_rows(next_routes, slot_rows, upstream[0])
+    )
+    slot_rows = sections_across(slot_rows, 0)
+    grad_prev = near_call(
+        final_kernel,
+        jax.ShapeDtypeStruct((count, width), BF16),
+        back,
+        slot_rows,
+        upstream[0],
+        out_specs=pl.BlockSpec(memory_space=pl.ANY),
+        scratch_shapes=[pltpu.VMEM((count, width), BF16), pltpu.SemaphoreType.DMA((FOLDS,))],
+        name="final_rows",
+    )
     return (grad_prev[None], weight_out.T[None])
 
 

time: 81 us -> 62.3 us (0.77)
  Pallas kernels: 22.6 us -> 5.51 us
  starting transfers between devices: 24.1 us -> 27.1 us
  other arithmetic: 2.71 us -> 0.28 us
  waiting for transfers between devices: 26.5 us -> 24.5 us
    pallas_call x8 -> x9, Pallas kernels: 22.6 us -> 5.51 us  [near_call(): pl.pallas_call(kernel, out_shape=out_shape, compiler_params=params, **kwa...]
    ppermute x0 -> x5, starting transfers between devices: none -> 6.01 us  [sections_across(): return lax.ppermute(value, ('pp', 'ep'), pairs)]
    ppermute x0 -> x5, waiting for transfers between devices: none -> 4.98 us  [sections_across(): return lax.ppermute(value, ('pp', 'ep'), pairs)]
    ppermute x14 -> x11, waiting for transfers between devices: 24.3 us -> 19.5 us  [across(): return lax.ppermute(value, 'ep', [(i, i ^ bits) for i in range(count)])]
    ppermute x3 -> x1, starting transfers between devices: 4.84 us -> 2.56 us  [passed_along(): lax.ppermute(value, axis, [(i, (i + by) % size) for i in range(size)])]
    ppermute x3 -> x1, waiting for transfers between devices: 2.19 us -> 0.01 us  [passed_along(): lax.ppermute(value, axis, [(i, (i + by) % size) for i in range(size)])]
    concatenate x1, other arithmetic: 1.58 us -> 0.14 us  [single_device(): gate_up = jnp.concatenate([own[0], other[0], own[1], other[1]], axis=0)]
    ppermute x14 -> x11, starting transfers between devices: 18.7 us -> 17.5 us  [across(): return lax.ppermute(value, 'ep', [(i, i ^ bits) for i in range(count)])]
  transfers between devices with their start and end apart: 20 -> 20, of which waited for: 11 -> 11; matrix products, arithmetic and copies ran while one was open for 3% -> 0% of each run, Pallas kernels for 12% -> 4%
where the time goes in v2:
time: 62.3 us; the launch traced here: 62 us
  starting transfers between devices  27.1 us (43%)
  waiting for transfers between devices  24.5 us (39%)
  Pallas kernels  5.51 us (9%)
  local copies, waits for them, and re-layouts  3.84 us (6%)
  between operations  0.79 us (1%)
    ppermute x11, waiting for transfers between devices, across(): return lax.ppermute(value, 'ep', [(i, i ^ bits) for i in range(count)])  19.5 us
    ppermute x11, starting transfers between devices, across(): return lax.ppermute(value, 'ep', [(i, i ^ bits) for i in range(count)])  17.5 us
    ppermute x5, starting transfers between devices, sections_across(): return lax.ppermute(value, ('pp', 'ep'), pairs)  6.01 us
    pallas_call x9, Pallas kernels, near_call(): pl.pallas_call(kernel, out_shape=out_shape, compiler_params=params, **kwa...  5.51 us
    ppermute x5, waiting for transfers between devices, sections_across(): return lax.ppermute(value, ('pp', 'ep'), pairs)  4.98 us
    unnamed x18, local copies, waits for them, and re-layouts  3.84 us
    ppermute x1, starting transfers between devices, passed_along(): lax.ppermute(value, axis, [(i, (i + by) % size) for i in range(size)])  2.56 us
  transfers between devices with their start and end apart: 20, of which 11 were waited for; matrix products, arithmetic and copies ran while one was open for 0% of the time, Pallas kernels for 4%

profile of v2, /device:TPU:0, one launch (start us, length us, event | category | flops | bytes accessed | tf_op | source)
XLA Modules:
  0.0 62.0 jit_solution(9412428437073990889)
XLA Ops:
  0.6 0.5 collective-permute-start.1
  1.7 2.6 %collective-permute-start = (s32[8,128]{1,0:T(8,128)}, s32[8,128]{1,0:T(8,128)S(1)}, u32[]{:S(2)}, u32[]{:S(2)}) collective-permute-start(s32[8,128]{1,0:T(8,128)} %bitcast.34), channel_id=1, source_target_pairs={{0,16},{16,0},{1,17},{17,1},{2,18},{18,2},{3,19},{19,3},{4,20},{20... | collective-permute-start | bytes 12296 | tf_op jit(solution)/shard_map/ppermute | solution.py:32
  4.2 1.2 %copy-done.2 = bf16[1,128,4096]{2,1,0:T(8,128)(2,1)S(1)} copy-done((bf16[1,128,4096]{2,1,0:T(8,128)(2,1)S(1)}, bf16[1,128,4096]{2,1,0:T(8,128)(2,1)}, u32[]{:S(2)}) %copy-start.2) | copy-done | bytes 1048600
  5.5 0.7 %copy-done.3 = s32[1,128,8]{1,2,0:T(8,128)S(1)} copy-done((s32[1,128,8]{1,2,0:T(8,128)S(1)}, s32[1,128,8]{1,2,0:T(8,128)}, u32[]{:S(2)}) %copy-start.3) | copy-done | bytes 4120
  6.1 0.7 %copy-done.5 = f32[1,128,8]{1,2,0:T(8,128)S(1)} copy-done((f32[1,128,8]{1,2,0:T(8,128)S(1)}, f32[1,128,8]{1,2,0:T(8,128)}, u32[]{:S(2)}) %copy-start.5) | copy-done | bytes 4120
  7.2 1.2 %copy-done = bf16[1,128,4096]{2,1,0:T(8,128)(2,1)S(1)} copy-done((bf16[1,128,4096]{2,1,0:T(8,128)(2,1)S(1)}, bf16[1,128,4096]{2,1,0:T(8,128)(2,1)}, u32[]{:S(2)}) %copy-start) | copy-done | bytes 1048600
  8.9 1.6 %collective-permute-start.10 = (bf16[8,5120]{1,0:T(8,128)(2,1)S(1)}, bf16[8,5120]{1,0:T(8,128)(2,1)S(1)}, u32[]{:S(2)}, u32[]{:S(2)}) collective-permute-start(bf16[8,5120]{1,0:T(8,128)(2,1)S(1)} %get-tuple-element.27.refs_0_), channel_id=1, source_target_pairs={{0,4},{1,5},{2,6},{3,7},{4,0},{5,1},{6,2},{7,3},{8,12},{9,13},{10,... | collective-permute-start | bytes 245768 | tf_op jit(solution)/shard_map/ppermute | solution.py:382
  10.5 2.6 %collective-permute-start.11 = (bf16[8,5120]{1,0:T(8,128)(2,1)S(1)}, bf16[8,5120]{1,0:T(8,128)(2,1)S(1)}, u32[]{:S(2)}, u32[]{:S(2)}) collective-permute-start(bf16[8,5120]{1,0:T(8,128)(2,1)S(1)} %get-tuple-element.27.refs_0_), channel_id=1, source_target_pairs={{0,8},{1,9},{2,10},{3,11},{4,12},{5,13},{6,14},{7,15},{8,0},{9,1},... | collective-permute-start | bytes 245768 | tf_op jit(solution)/shard_map/ppermute | solution.py:382
  13.4 2.0 %collective-permute-start.6 = (bf16[8,5120]{1,0:T(8,128)(2,1)S(1)}, bf16[8,5120]{1,0:T(8,128)(2,1)S(1)}, u32[]{:S(2)}, u32[]{:S(2)}) collective-permute-start(bf16[8,5120]{1,0:T(8,128)(2,1)S(1)} %get-tuple-element.23), channel_id=1, source_target_pairs={{0,24},{1,25},{2,26},{3,27},{4,28},{5,29},{6,30},{7,31},{8,16},{9,... | collective-permute-start | bytes 245768 | tf_op jit(solution)/shard_map/ppermute | solution.py:388
  15.3 2.0 %collective-permute-start.7 = (bf16[8,5120]{1,0:T(8,128)(2,1)S(1)}, bf16[8,5120]{1,0:T(8,128)(2,1)S(1)}, u32[]{:S(2)}, u32[]{:S(2)}) collective-permute-start(bf16[8,5120]{1,0:T(8,128)(2,1)S(1)} %get-tuple-element.23), channel_id=1, source_target_pairs={{0,28},{1,29},{2,30},{3,31},{4,24},{5,25},{6,26},{7,27},{8,20},{9,... | collective-permute-start | bytes 245768 | tf_op jit(solution)/shard_map/ppermute | solution.py:388
  17.5 1.2 %collective-permute-start.4 = (bf16[8,5120]{1,0:T(8,128)(2,1)S(1)}, bf16[8,5120]{1,0:T(8,128)(2,1)S(1)}, u32[]{:S(2)}, u32[]{:S(2)}) collective-permute-start(bf16[8,5120]{1,0:T(8,128)(2,1)S(1)} %get-tuple-element.23), channel_id=1, source_target_pairs={{0,16},{1,17},{2,18},{3,19},{4,20},{5,21},{6,22},{7,23},{8,24},{9,... | collective-permute-start | bytes 245768 | tf_op jit(solution)/shard_map/ppermute | solution.py:388
  18.7 4.9 %collective-permute-done.11.refs_2_ = bf16[8,5120]{1,0:T(8,128)(2,1)S(1)} collective-permute-done((bf16[8,5120]{1,0:T(8,128)(2,1)S(1)}, bf16[8,5120]{1,0:T(8,128)(2,1)S(1)}, u32[]{:S(2)}, u32[]{:S(2)}) %collective-permute-start.11) | collective-permute-done | bytes 81952 | tf_op jit(solution)/shard_map/ppermute | solution.py:382
  23.6 1.6 %collective-permute-start.13 = (bf16[4,8,5120]{2,1,0:T(8,128)(2,1)S(1)}, bf16[4,8,5120]{2,1,0:T(8,128)(2,1)S(1)}, u32[]{:S(2)}, u32[]{:S(2)}) collective-permute-start(bf16[4,8,5120]{2,1,0:T(8,128)(2,1)S(1)} %pad_maximum_fusion.2), channel_id=1, source_target_pairs={{0,2},{1,3},{2,0},{3,1},{4,6},{5,7},{6,4},{7,5},{8,10},{9,11},{10,... | collective-permute-start | bytes 983048 | tf_op jit(solution)/shard_map/ppermute | solution.py:382
  25.2 1.9 %collective-permute-done.6.refs_2_ = bf16[8,5120]{1,0:T(8,128)(2,1)S(1)} collective-permute-done((bf16[8,5120]{1,0:T(8,128)(2,1)S(1)}, bf16[8,5120]{1,0:T(8,128)(2,1)S(1)}, u32[]{:S(2)}, u32[]{:S(2)}) %collective-permute-start.6) | collective-permute-done | bytes 81952 | tf_op jit(solution)/shard_map/ppermute | solution.py:388
  27.1 1.6 %collective-permute-start.9 = (bf16[2,8,5120]{2,1,0:T(8,128)(2,1)S(1)}, bf16[2,8,5120]{2,1,0:T(8,128)(2,1)S(1)}, u32[]{:S(2)}, u32[]{:S(2)}) collective-permute-start(bf16[2,8,5120]{2,1,0:T(8,128)(2,1)S(1)} %pad_maximum_fusion.4), channel_id=1, source_target_pairs={{0,2},{1,3},{2,0},{3,1},{4,6},{5,7},{6,4},{7,5},{8,10},{9,11},{10,... | collective-permute-start | bytes 491528 | tf_op jit(solution)/shard_map/ppermute | solution.py:382
  28.9 1.6 %collective-permute-start.8 = (bf16[2,8,5120]{2,1,0:T(8,128)(2,1)S(1)}, bf16[2,8,5120]{2,1,0:T(8,128)(2,1)S(1)}, u32[]{:S(2)}, u32[]{:S(2)}) collective-permute-start(bf16[2,8,5120]{2,1,0:T(8,128)(2,1)S(1)} %pad_maximum_fusion.3), channel_id=1, source_target_pairs={{0,2},{1,3},{2,0},{3,1},{4,6},{5,7},{6,4},{7,5},{8,10},{9,11},{10,... | collective-permute-start | bytes 491528 | tf_op jit(solution)/shard_map/ppermute | solution.py:382
  30.6 3.2 %collective-permute-done.13.refs_4_ = bf16[4,8,5120]{2,1,0:T(8,128)(2,1)S(1)} collective-permute-done((bf16[4,8,5120]{2,1,0:T(8,128)(2,1)S(1)}, bf16[4,8,5120]{2,1,0:T(8,128)(2,1)S(1)}, u32[]{:S(2)}, u32[]{:S(2)}) %collective-permute-start.13) | collective-permute-done | bytes 327712 | tf_op jit(solution)/shard_map/ppermute | solution.py:382
  33.8 0.8 %expert_forward.1.refs_8_ = f32[80,256]{1,0:T(8,128)S(1)} custom-call(bf16[8,5120]{1,0:T(8,128)(2,1)S(1)} %get-tuple-element.27.refs_0_, bf16[8,5120]{1,0:T(8,128)(2,1)S(1)} %collective-permute-done.10.refs_1_, bf16[8,5120]{1,0:T(8,128)(2,1)S(1)} %collective-permute-done.11.refs_2_, bf16[8,5120]{1,0:T(8,128)(2,1)S(1)} %collective-permute-done.12.refs_3_, ...), custom_call_target="tpu_custom_call" | custom-call | tf_op jit(solution)/shard_map/expert_forward/pallas_call | solution.py:152
  34.6 1.4 %collective-permute-done.9.refs_5_ = bf16[2,8,5120]{2,1,0:T(8,128)(2,1)S(1)} collective-permute-done((bf16[2,8,5120]{2,1,0:T(8,128)(2,1)S(1)}, bf16[2,8,5120]{2,1,0:T(8,128)(2,1)S(1)}, u32[]{:S(2)}, u32[]{:S(2)}) %collective-permute-start.9) | collective-permute-done | bytes 163872 | tf_op jit(solution)/shard_map/ppermute | solution.py:382
  36.0 1.8 %collective-permute-done.8.refs_4_ = bf16[2,8,5120]{2,1,0:T(8,128)(2,1)S(1)} collective-permute-done((bf16[2,8,5120]{2,1,0:T(8,128)(2,1)S(1)}, bf16[2,8,5120]{2,1,0:T(8,128)(2,1)S(1)}, u32[]{:S(2)}, u32[]{:S(2)}) %collective-permute-start.8) | collective-permute-done | bytes 163872 | tf_op jit(solution)/shard_map/ppermute | solution.py:382
  37.8 1.8 %expert_backward.1 = (bf16[2,8,5248]{2,1,0:T(8,128)(2,1)S(1)}, bf16[2,8,5248]{2,1,0:T(8,128)(2,1)S(1)}, bf16[2,8,5248]{2,1,0:T(8,128)(2,1)S(1)}, bf16[2,8,5248]{2,1,0:T(8,128)(2,1)S(1)}) custom-call(bf16[8,5120]{1,0:T(8,128)(2,1)S(1)} %collective-permute-done.4.refs_0_, bf16[8,5120]{1,0:T(8,128)(2,1)S(1)} %collective-permute-done.5.refs_1_, ...), custom_call_target="tpu_custom_call" | custom-call | tf_op jit(solution)/shard_map/expert_backward/pallas_call | solution.py:152
  39.5 1.6 %collective-permute-start.16 = (bf16[2,8,5248]{2,1,0:T(8,128)(2,1)S(1)}, bf16[2,8,5248]{2,1,0:T(8,128)(2,1)S(1)}, u32[]{:S(2)}, u32[]{:S(2)}) collective-permute-start(bf16[2,8,5248]{2,1,0:T(8,128)(2,1)S(1)} %get-tuple-element.33), channel_id=1, source_target_pairs={{0,2},{1,3},{2,0},{3,1},{4,6},{5,7},{6,4},{7,5},{8,10},{9,11},{10,... | collective-permute-start | bytes 503816 | tf_op jit(solution)/shard_map/ppermute | solution.py:382
  41.1 0.5 collective-permute-start.14
  41.6 3.3 %collective-permute-done.16.other_ref = bf16[2,8,5248]{2,1,0:T(8,128)(2,1)S(1)} collective-permute-done((bf16[2,8,5248]{2,1,0:T(8,128)(2,1)S(1)}, bf16[2,8,5248]{2,1,0:T(8,128)(2,1)S(1)}, u32[]{:S(2)}, u32[]{:S(2)}) %collective-permute-start.16) | collective-permute-done | bytes 167968 | tf_op jit(solution)/shard_map/ppermute | solution.py:382
  45.0 4.0 %collective-permute-start.17 = (bf16[8,5376]{1,0:T(8,128)(2,1)S(1)}, bf16[8,5376]{1,0:T(8,128)(2,1)S(1)}, u32[]{:S(2)}, u32[]{:S(2)}) collective-permute-start(bf16[8,5376]{1,0:T(8,128)(2,1)S(1)} %get-tuple-element.34), channel_id=1, source_target_pairs={{0,8},{1,9},{2,10},{3,11},{4,12},{5,13},{6,14},{7,15},{8,0},{9,1},... | collective-permute-start | bytes 258056 | tf_op jit(solution)/shard_map/ppermute | solution.py:382
  49.0 2.1 %collective-permute-start.18 = (bf16[8,5376]{1,0:T(8,128)(2,1)S(1)}, bf16[8,5376]{1,0:T(8,128)(2,1)S(1)}, u32[]{:S(2)}, u32[]{:S(2)}) collective-permute-start(bf16[8,5376]{1,0:T(8,128)(2,1)S(1)} %get-tuple-element.35), channel_id=1, source_target_pairs={{0,12},{1,13},{2,14},{3,15},{4,8},{5,9},{6,10},{7,11},{8,4},{9,5},... | collective-permute-start | bytes 258056 | tf_op jit(solution)/shard_map/ppermute | solution.py:382
  51.6 3.8 %collective-permute-done.18.refs_3_ = bf16[8,5376]{1,0:T(8,128)(2,1)S(1)} collective-permute-done((bf16[8,5376]{1,0:T(8,128)(2,1)S(1)}, bf16[8,5376]{1,0:T(8,128)(2,1)S(1)}, u32[]{:S(2)}, u32[]{:S(2)}) %collective-permute-start.18) | collective-permute-done | bytes 86048 | tf_op jit(solution)/shard_map/ppermute | solution.py:382
  55.3 0.9 %collective-permute-done.15.refs_1_ = bf16[8,5376]{1,0:T(8,128)(2,1)S(1)} collective-permute-done((bf16[8,5376]{1,0:T(8,128)(2,1)S(1)}, bf16[8,5376]{1,0:T(8,128)(2,1)S(1)}, u32[]{:S(2)}, u32[]{:S(2)}) %collective-permute-start.15) | collective-permute-done | bytes 86048 | tf_op jit(solution)/shard_map/ppermute | solution.py:382
  56.3 0.9 %collective-permute-start.19 = (bf16[8,5120]{1,0:T(8,128)(2,1)S(1)}, bf16[8,5120]{1,0:T(8,128)(2,1)S(1)}, u32[]{:S(2)}, u32[]{:S(2)}) collective-permute-start(bf16[8,5120]{1,0:T(8,128)(2,1)S(1)} %sum_z.1), channel_id=1, source_target_pairs={{0,16},{1,17},{2,18},{3,19},{4,20},{5,21},{6,22},{7,23},{8,24},{9,... | collective-permute-start | bytes 245768 | tf_op jit(solution)/shard_map/ppermute | solution.py:388
  57.2 0.7 %weight_out.1 = f32[8,128]{1,0:T(8,128)} custom-call(s32[8,128]{1,0:T(8,128)S(1)} %bitcast.36, bf16[8,5376]{1,0:T(8,128)(2,1)S(1)} %get-tuple-element.30.refs_0_, bf16[8,5376]{1,0:T(8,128)(2,1)S(1)} %collective-permute-done.15.refs_1_, bf16[8,5376]{1,0:T(8,128)(2,1)S(1)} %collective-permute-done.17.refs_2_, bf16[8,5376]{1,0:T(8,128)(2,1)S(1)} %collective-permute-done.18.refs_3_), custom_call_target="tpu_custom_call" | custom-call | tf_op jit(solution)/shard_map/weight_out/pallas_call | solution.py:152
  57.9 2.9 %collective-permute-done.19.rows_ref = bf16[8,5120]{1,0:T(8,128)(2,1)S(1)} collective-permute-done((bf16[8,5120]{1,0:T(8,128)(2,1)S(1)}, bf16[8,5120]{1,0:T(8,128)(2,1)S(1)}, u32[]{:S(2)}, u32[]{:S(2)}) %collective-permute-start.19) | collective-permute-done | bytes 81952 | tf_op jit(solution)/shard_map/ppermute | solution.py:388
  60.8 1.2 %final_rows.1 = bf16[128,4096]{1,0:T(8,128)(2,1)} custom-call(bf16[4,128,16]{2,1,0:T(8,128)(2,1)S(1)} %get-tuple-element.19.back_ref, bf16[8,5120]{1,0:T(8,128)(2,1)S(1)} %collective-permute-done.19.rows_ref, bf16[128,4096]{1,0:T(8,128)(2,1)S(1)} %bitcast.24), custom_call_target="tpu_custom_call" | custom-call | tf_op jit(solution)/shard_map/final_rows/pallas_call | solution.py:152
  (40 shorter events, 2.6 us)
Async XLA Ops:
  0.6 8.2 %collective-permute-start.1 = (bf16[64,4096]{1,0:T(8,128)(2,1)}, bf16[64,4096]{1,0:T(8,128)(2,1)S(1)}, u32[]{:S(2)}, u32[]{:S(2)}) collective-permute-start(bf16[64,4096]{1,0:T(8,128)(2,1)} %bitcast.43), channel_id=1, source_target_pairs={{0,1},{1,0},{2,3},{3,2},{4,5},{5,4},{6,7},{7,6},{8,9},{9,8},{10,11... | collective-permute-start | bytes 1572872 | tf_op jit(solution)/shard_map/ppermute | solution.py:27
  1.1 7.7 %collective-permute-start.2 = (bf16[64,4096]{1,0:T(8,128)(2,1)}, bf16[64,4096]{1,0:T(8,128)(2,1)S(1)}, u32[]{:S(2)}, u32[]{:S(2)}) collective-permute-start(bf16[64,4096]{1,0:T(8,128)(2,1)} %bitcast.41), channel_id=1, source_target_pairs={{0,1},{1,0},{2,3},{3,2},{4,5},{5,4},{6,7},{7,6},{8,9},{9,8},{10,11... | collective-permute-start | bytes 1572872 | tf_op jit(solution)/shard_map/ppermute | solution.py:27
  1.2 7.7 %collective-permute-start.3 = (bf16[64,4096]{1,0:T(8,128)(2,1)}, bf16[64,4096]{1,0:T(8,128)(2,1)S(1)}, u32[]{:S(2)}, u32[]{:S(2)}) collective-permute-start(bf16[64,4096]{1,0:T(8,128)(2,1)} %bitcast.39), channel_id=1, source_target_pairs={{0,1},{1,0},{2,3},{3,2},{4,5},{5,4},{6,7},{7,6},{8,9},{9,8},{10,11... | collective-permute-start | bytes 1572872 | tf_op jit(solution)/shard_map/ppermute | solution.py:27
  1.7 5.5 %collective-permute-start = (s32[8,128]{1,0:T(8,128)}, s32[8,128]{1,0:T(8,128)S(1)}, u32[]{:S(2)}, u32[]{:S(2)}) collective-permute-start(s32[8,128]{1,0:T(8,128)} %bitcast.34), channel_id=1, source_target_pairs={{0,16},{16,0},{1,17},{17,1},{2,18},{18,2},{3,19},{19,3},{4,20},{20... | collective-permute-start | bytes 12296 | tf_op jit(solution)/shard_map/ppermute | solution.py:32
  4.2 1.2 %copy-start.2 = (bf16[1,128,4096]{2,1,0:T(8,128)(2,1)S(1)}, bf16[1,128,4096]{2,1,0:T(8,128)(2,1)}, u32[]{:S(2)}) copy-start(bf16[1,128,4096]{2,1,0:T(8,128)(2,1)} %param.8) | copy-start | bytes 3145732
  5.4 0.7 %copy-start.3 = (s32[1,128,8]{1,2,0:T(8,128)S(1)}, s32[1,128,8]{1,2,0:T(8,128)}, u32[]{:S(2)}) copy-start(s32[1,128,8]{1,2,0:T(8,128)} %param.9) | copy-start | bytes 12292
  6.1 0.7 %copy-start.5 = (f32[1,128,8]{1,2,0:T(8,128)S(1)}, f32[1,128,8]{1,2,0:T(8,128)}, u32[]{:S(2)}) copy-start(f32[1,128,8]{1,2,0:T(8,128)} %param.10) | copy-start | bytes 12292
  6.8 10.5 %copy-start.7 = (bf16[1,64,4096]{2,1,0:T(8,128)(2,1)S(1)}, bf16[1,64,4096]{2,1,0:T(8,128)(2,1)}, u32[]{:S(2)}) copy-start(bf16[1,64,4096]{2,1,0:T(8,128)(2,1)} %param.12) | copy-start | bytes 1572868
  6.8 10.5 %copy-start.8 = (bf16[1,64,4096]{2,1,0:T(8,128)(2,1)S(1)}, bf16[1,64,4096]{2,1,0:T(8,128)(2,1)}, u32[]{:S(2)}) copy-start(bf16[1,64,4096]{2,1,0:T(8,128)(2,1)} %param.11) | copy-start | bytes 1572868
  7.2 1.2 %copy-start = (bf16[1,128,4096]{2,1,0:T(8,128)(2,1)S(1)}, bf16[1,128,4096]{2,1,0:T(8,128)(2,1)}, u32[]{:S(2)}) copy-start(bf16[1,128,4096]{2,1,0:T(8,128)(2,1)} %param.7) | copy-start | bytes 3145732
  8.9 21.6 %copy-start.6 = (bf16[1,64,4096]{2,1,0:T(8,128)(2,1)S(1)}, bf16[1,64,4096]{2,1,0:T(8,128)(2,1)}, u32[]{:S(2)}) copy-start(bf16[1,64,4096]{2,1,0:T(8,128)(2,1)} %param.13) | copy-start | bytes 1572868
  8.9 8.5 %collective-permute-start.10 = (bf16[8,5120]{1,0:T(8,128)(2,1)S(1)}, bf16[8,5120]{1,0:T(8,128)(2,1)S(1)}, u32[]{:S(2)}, u32[]{:S(2)}) collective-permute-start(bf16[8,5120]{1,0:T(8,128)(2,1)S(1)} %get-tuple-element.27.refs_0_), channel_id=1, source_target_pairs={{0,4},{1,5},{2,6},{3,7},{4,0},{5,1},{6,2},{7,3},{8,12},{9,13},{10,... | collective-permute-start | bytes 245768 | tf_op jit(solution)/shard_map/ppermute | solution.py:382
  10.5 13.0 %collective-permute-start.11 = (bf16[8,5120]{1,0:T(8,128)(2,1)S(1)}, bf16[8,5120]{1,0:T(8,128)(2,1)S(1)}, u32[]{:S(2)}, u32[]{:S(2)}) collective-permute-start(bf16[8,5120]{1,0:T(8,128)(2,1)S(1)} %get-tuple-element.27.refs_0_), channel_id=1, source_target_pairs={{0,8},{1,9},{2,10},{3,11},{4,12},{5,13},{6,14},{7,15},{8,0},{9,1},... | collective-permute-start | bytes 245768 | tf_op jit(solution)/shard_map/ppermute | solution.py:382
  13.1 10.4 %collective-permute-start.12 = (bf16[8,5120]{1,0:T(8,128)(2,1)S(1)}, bf16[8,5120]{1,0:T(8,128)(2,1)S(1)}, u32[]{:S(2)}, u32[]{:S(2)}) collective-permute-start(bf16[8,5120]{1,0:T(8,128)(2,1)S(1)} %get-tuple-element.27.refs_0_), channel_id=1, source_target_pairs={{0,12},{1,13},{2,14},{3,15},{4,8},{5,9},{6,10},{7,11},{8,4},{9,5},... | collective-permute-start | bytes 245768 | tf_op jit(solution)/shard_map/ppermute | solution.py:382
  13.4 13.7 %collective-permute-start.6 = (bf16[8,5120]{1,0:T(8,128)(2,1)S(1)}, bf16[8,5120]{1,0:T(8,128)(2,1)S(1)}, u32[]{:S(2)}, u32[]{:S(2)}) collective-permute-start(bf16[8,5120]{1,0:T(8,128)(2,1)S(1)} %get-tuple-element.23), channel_id=1, source_target_pairs={{0,24},{1,25},{2,26},{3,27},{4,28},{5,29},{6,30},{7,31},{8,16},{9,... | collective-permute-start | bytes 245768 | tf_op jit(solution)/shard_map/ppermute | solution.py:388
  15.3 11.8 %collective-permute-start.7 = (bf16[8,5120]{1,0:T(8,128)(2,1)S(1)}, bf16[8,5120]{1,0:T(8,128)(2,1)S(1)}, u32[]{:S(2)}, u32[]{:S(2)}) collective-permute-start(bf16[8,5120]{1,0:T(8,128)(2,1)S(1)} %get-tuple-element.23), channel_id=1, source_target_pairs={{0,28},{1,29},{2,30},{3,31},{4,24},{5,25},{6,26},{7,27},{8,20},{9,... | collective-permute-start | bytes 245768 | tf_op jit(solution)/shard_map/ppermute | solution.py:388
  17.5 11.2 %collective-permute-start.4 = (bf16[8,5120]{1,0:T(8,128)(2,1)S(1)}, bf16[8,5120]{1,0:T(8,128)(2,1)S(1)}, u32[]{:S(2)}, u32[]{:S(2)}) collective-permute-start(bf16[8,5120]{1,0:T(8,128)(2,1)S(1)} %get-tuple-element.23), channel_id=1, source_target_pairs={{0,16},{1,17},{2,18},{3,19},{4,20},{5,21},{6,22},{7,23},{8,24},{9,... | collective-permute-start | bytes 245768 | tf_op jit(solution)/shard_map/ppermute | solution.py:388
  23.5 5.3 %collective-permute-start.5 = (bf16[8,5120]{1,0:T(8,128)(2,1)S(1)}, bf16[8,5120]{1,0:T(8,128)(2,1)S(1)}, u32[]{:S(2)}, u32[]{:S(2)}) collective-permute-start(bf16[8,5120]{1,0:T(8,128)(2,1)S(1)} %get-tuple-element.23), channel_id=1, source_target_pairs={{0,20},{1,21},{2,22},{3,23},{4,16},{5,17},{6,18},{7,19},{8,28},{9,... | collective-permute-start | bytes 245768 | tf_op jit(solution)/shard_map/ppermute | solution.py:388
  23.6 10.2 %collective-permute-start.13 = (bf16[4,8,5120]{2,1,0:T(8,128)(2,1)S(1)}, bf16[4,8,5120]{2,1,0:T(8,128)(2,1)S(1)}, u32[]{:S(2)}, u32[]{:S(2)}) collective-permute-start(bf16[4,8,5120]{2,1,0:T(8,128)(2,1)S(1)} %pad_maximum_fusion.2), channel_id=1, source_target_pairs={{0,2},{1,3},{2,0},{3,1},{4,6},{5,7},{6,4},{7,5},{8,10},{9,11},{10,... | collective-permute-start | bytes 983048 | tf_op jit(solution)/shard_map/ppermute | solution.py:382
  27.1 8.9 %collective-permute-start.9 = (bf16[2,8,5120]{2,1,0:T(8,128)(2,1)S(1)}, bf16[2,8,5120]{2,1,0:T(8,128)(2,1)S(1)}, u32[]{:S(2)}, u32[]{:S(2)}) collective-permute-start(bf16[2,8,5120]{2,1,0:T(8,128)(2,1)S(1)} %pad_maximum_fusion.4), channel_id=1, source_target_pairs={{0,2},{1,3},{2,0},{3,1},{4,6},{5,7},{6,4},{7,5},{8,10},{9,11},{10,... | collective-permute-start | bytes 491528 | tf_op jit(solution)/shard_map/ppermute | solution.py:382
  28.9 8.9 %collective-permute-start.8 = (bf16[2,8,5120]{2,1,0:T(8,128)(2,1)S(1)}, bf16[2,8,5120]{2,1,0:T(8,128)(2,1)S(1)}, u32[]{:S(2)}, u32[]{:S(2)}) collective-permute-start(bf16[2,8,5120]{2,1,0:T(8,128)(2,1)S(1)} %pad_maximum_fusion.3), channel_id=1, source_target_pairs={{0,2},{1,3},{2,0},{3,1},{4,6},{5,7},{6,4},{7,5},{8,10},{9,11},{10,... | collective-permute-start | bytes 491528 | tf_op jit(solution)/shard_map/ppermute | solution.py:382
  34.6 22.6 %copy-start.4 = (s32[1,128,8]{1,2,0:T(8,128)S(1)}, s32[1,128,8]{1,2,0:T(8,128)}, u32[]{:S(2)}) copy-start(s32[1,128,8]{1,2,0:T(8,128)} %param.9) | copy-start | bytes 12292
  34.6 26.2 %copy-start.1 = (bf16[1,128,4096]{2,1,0:T(8,128)(2,1)S(1)}, bf16[1,128,4096]{2,1,0:T(8,128)(2,1)}, u32[]{:S(2)}) copy-start(bf16[1,128,4096]{2,1,0:T(8,128)(2,1)} %param.7) | copy-start | bytes 3145732
  39.5 5.4 %collective-permute-start.16 = (bf16[2,8,5248]{2,1,0:T(8,128)(2,1)S(1)}, bf16[2,8,5248]{2,1,0:T(8,128)(2,1)S(1)}, u32[]{:S(2)}, u32[]{:S(2)}) collective-permute-start(bf16[2,8,5248]{2,1,0:T(8,128)(2,1)S(1)} %get-tuple-element.33), channel_id=1, source_target_pairs={{0,2},{1,3},{2,0},{3,1},{4,6},{5,7},{6,4},{7,5},{8,10},{9,11},{10,... | collective-permute-start | bytes 503816 | tf_op jit(solution)/shard_map/ppermute | solution.py:382
  41.1 10.0 %collective-permute-start.14 = (bf16[2,8,5248]{2,1,0:T(8,128)(2,1)S(1)}, bf16[2,8,5248]{2,1,0:T(8,128)(2,1)S(1)}, u32[]{:S(2)}, u32[]{:S(2)}) collective-permute-start(bf16[2,8,5248]{2,1,0:T(8,128)(2,1)S(1)} %get-tuple-element.29), channel_id=1, source_target_pairs={{0,2},{1,3},{2,0},{3,1},{4,6},{5,7},{6,4},{7,5},{8,10},{9,11},{10,... | collective-permute-start | bytes 503816 | tf_op jit(solution)/shard_map/ppermute | solution.py:382
  45.0 6.6 %collective-permute-start.17 = (bf16[8,5376]{1,0:T(8,128)(2,1)S(1)}, bf16[8,5376]{1,0:T(8,128)(2,1)S(1)}, u32[]{:S(2)}, u32[]{:S(2)}) collective-permute-start(bf16[8,5376]{1,0:T(8,128)(2,1)S(1)} %get-tuple-element.34), channel_id=1, source_target_pairs={{0,8},{1,9},{2,10},{3,11},{4,12},{5,13},{6,14},{7,15},{8,0},{9,1},... | collective-permute-start | bytes 258056 | tf_op jit(solution)/shard_map/ppermute | solution.py:382
  49.0 6.3 %collective-permute-start.18 = (bf16[8,5376]{1,0:T(8,128)(2,1)S(1)}, bf16[8,5376]{1,0:T(8,128)(2,1)S(1)}, u32[]{:S(2)}, u32[]{:S(2)}) collective-permute-start(bf16[8,5376]{1,0:T(8,128)(2,1)S(1)} %get-tuple-element.35), channel_id=1, source_target_pairs={{0,12},{1,13},{2,14},{3,15},{4,8},{5,9},{6,10},{7,11},{8,4},{9,5},... | collective-permute-start | bytes 258056 | tf_op jit(solution)/shard_map/ppermute | solution.py:382
  51.2 5.0 %collective-permute-start.15 = (bf16[8,5376]{1,0:T(8,128)(2,1)S(1)}, bf16[8,5376]{1,0:T(8,128)(2,1)S(1)}, u32[]{:S(2)}, u32[]{:S(2)}) collective-permute-start(bf16[8,5376]{1,0:T(8,128)(2,1)S(1)} %get-tuple-element.31), channel_id=1, source_target_pairs={{0,4},{1,5},{2,6},{3,7},{4,0},{5,1},{6,2},{7,3},{8,12},{9,13},{10,... | collective-permute-start | bytes 258056 | tf_op jit(solution)/shard_map/ppermute | solution.py:382
  56.3 4.5 %collective-permute-start.19 = (bf16[8,5120]{1,0:T(8,128)(2,1)S(1)}, bf16[8,5120]{1,0:T(8,128)(2,1)S(1)}, u32[]{:S(2)}, u32[]{:S(2)}) collective-permute-start(bf16[8,5120]{1,0:T(8,128)(2,1)S(1)} %sum_z.1), channel_id=1, source_target_pairs={{0,16},{1,17},{2,18},{3,19},{4,20},{5,21},{6,22},{7,23},{8,24},{9,... | collective-permute-start | bytes 245768 | tf_op jit(solution)/shard_map/ppermute | solution.py:388

commit v3 on v2

--- a/solution.py
+++ b/solution.py
@@ -147,9 +147,14 @@
 
 
 def near_call(kernel, out_shape, *args, **kwargs):
-    args = [pltpu.with_memory_space_constraint(arg, pltpu.VMEM) for arg in args]
+    if "in_specs" not in kwargs:
+        args = [pltpu.with_memory_space_constraint(arg, pltpu.VMEM) for arg in args]
     params = pltpu.CompilerParams(vmem_limit_bytes=16 * 1024 * 1024)
     return pl.pallas_call(kernel, out_shape=out_shape, compiler_params=params, **kwargs)(*args)
+
+
+def as_bf16(mask):
+    return mask.astype(F32).astype(BF16)
 
 
 def slot_of_token(routes_t):
@@ -160,9 +165,7 @@
     before = lax.broadcasted_iota(jnp.int32, (count, count), 0) < lax.broadcasted_iota(
         jnp.int32, (count, count), 1
     )
-    rank = jnp.dot(
-        found.astype(BF16), before.astype(F32).astype(BF16), preferred_element_type=F32
-    )
+    rank = jnp.dot(found.astype(BF16), as_bf16(before), preferred_element_type=F32)
     slot = jnp.where((found > 0.5) & (rank < CAP - 0.5), rank, -1.0)
     return hit, slot
 
@@ -184,15 +187,12 @@
     return jnp.concatenate(picks, axis=0).astype(BF16)
 
 
-def as_bf16(mask):
-    return mask.astype(F32).astype(BF16)
-
-
-def pick_into(slot, rows_ref, out_ref):
+def pick_into(slot, rows_ref, out_ref, before=lambda fold: None):
     width = rows_ref.shape[1]
     part = width // FOLDS
     tail = jnp.zeros((MAIN, part), F32)
     for fold in range(FOLDS):
+        before(fold)
         span = slice(fold * part, (fold + 1) * part)
         got = jnp.dot(both_picks(slot, fold), rows_ref[:, span], preferred_element_type=F32)
         out_ref[:, span] = got[:MAIN].astype(BF16)
@@ -200,41 +200,54 @@
     out_ref[:, width:] = tail.astype(BF16)
 
 
-def slot_scale(slot, weight_row):
+def pick_inputs_kernel(routes_in, rows_in, base_in, out_ref, routes_ref, base_ref, rows_ref, sems):
+    part = rows_ref.shape[1] // FOLDS
+    routes_copy = pltpu.make_async_copy(routes_in, routes_ref, sems.at[FOLDS])
+    routes_copy.start()
+    copies = []
+    for fold in range(FOLDS):
+        span = slice(fold * part, (fold + 1) * part)
+        copies.append(
+            pltpu.make_async_copy(rows_in.at[:, span], rows_ref.at[:, span], sems.at[fold])
+        )
+        copies[-1].start()
+    base_copy = pltpu.make_async_copy(base_in, base_ref, sems.at[FOLDS + 1])
+    base_copy.start()
+    routes_copy.wait()
+    _, slot = slot_of_token(routes_ref[...])
+    pick_into(slot, rows_ref, out_ref, lambda fold: copies[fold].wait())
+    base_copy.wait()
+
+
+def pick_grads_kernel(routes_ref, rows_ref, out_ref):
+    _, slot = slot_of_token(routes_ref[...])
+    pick_into(slot, rows_ref, out_ref)
+
+
+TN = (((0,), (0,)), ((), ()))
+NT = (((1,), (1,)), ((), ()))
+
+
+def back_kernel(routes_ref, weight_ref, back_ref, scale_ref):
+    hit, slot = slot_of_token(routes_ref[...])
+    size = 2 * MAIN
+    eye = as_bf16(
+        lax.broadcasted_iota(jnp.int32, (size, 2 * size), 0)
+        == lax.broadcasted_iota(jnp.int32, (size, 2 * size), 1) % size
+    )
+    for fold in range(FOLDS):
+        back_ref[fold] = lax.dot_general(
+            both_picks(slot, fold), eye, TN, preferred_element_type=F32
+        ).astype(BF16)
+    weight_row = jnp.sum(jnp.where(hit, weight_ref[...], 0.0), axis=0, keepdims=True)
     main = jnp.sum(jnp.where(main_pick(slot), weight_row, 0.0), axis=1, keepdims=True)
     tail = jnp.zeros_like(main)
     for fold in range(FOLDS):
         tail = tail + jnp.sum(
             jnp.where(tail_pick(slot, fold), weight_row, 0.0), axis=1, keepdims=True
         )
-    return main, tail
-
-
-def pick_inputs_kernel(routes_ref, weight_ref, rows_ref, out_ref, scale_ref):
-    hit, slot = slot_of_token(routes_ref[...])
-    pick_into(slot, rows_ref, out_ref)
-    weight_row = jnp.sum(jnp.where(hit, weight_ref[...], 0.0), axis=0, keepdims=True)
-    main, tail = slot_scale(slot, weight_row)
     scale_ref[:, :128] = jnp.broadcast_to(main, (MAIN, 128))
     scale_ref[:, 128:] = jnp.broadcast_to(tail, (MAIN, 128))
-
-
-TN = (((0,), (0,)), ((), ()))
-NT = (((1,), (1,)), ((), ()))
-
-
-def pick_grads_kernel(routes_ref, rows_ref, out_ref, back_ref):
-    _, slot = slot_of_token(routes_ref[...])
-    pick_into(slot, rows_ref, out_ref)
-    size = 2 * MAIN
-    eye = as_bf16(
-        lax.broadcasted_iota(jnp.int32, (size, size), 0)
-        == lax.broadcasted_iota(jnp.int32, (size, size), 1)
-    )
-    for fold in range(FOLDS):
-        back_ref[fold] = lax.dot_general(
-            both_picks(slot, fold), eye, TN, preferred_element_type=F32
-        ).astype(BF16)
 
 
 def unfold(blocks, width, rows_ref):
@@ -252,19 +265,9 @@
         ).astype(BF16)
 
 
-def read_blocks(refs):
-    blocks = []
-    for ref in refs:
-        if len(ref.shape) == 2:
-            blocks.append(ref)
-        else:
-            blocks += [ref.at[k] for k in range(ref.shape[0])]
-    return blocks
-
-
-def forward_kernel(*refs):
-    *x_refs, gu_ref, h_ref, rows_ref = refs
-    unfold(read_blocks(x_refs), gu_ref.shape[1], rows_ref)
+def forward_kernel(own, z2, y0, y2, low, high, gu_ref, h_ref, rows_ref):
+    blocks = [own, low.at[0], z2, high.at[0], y0, low.at[1], y2, high.at[1]]
+    unfold(blocks, gu_ref.shape[1], rows_ref)
     h_ref[...] = lax.dot_general(rows_ref[...], gu_ref[...], NT, preferred_element_type=F32)
 
 
@@ -277,13 +280,17 @@
 
 
 def backward_kernel(*refs):
-    *g_refs, down_ref, gu_ref, h_ref, near_a, near_b, far_a, far_b, rows_ref = refs
+    g0, g2, z_refs, y_refs, yz_refs, down_ref, gu_ref, h_ref, *outs, rows_ref = refs
+    near_a, far_a, near_b, far_b = outs
     width = gu_ref.shape[1]
-    part = width // FOLDS
+    half = width // 2
+    part = half // FOLDS
     units = down_ref.shape[0]
     slots = rows_ref.shape[0]
     count = slots // CAP
-    unfold(read_blocks(g_refs), width, rows_ref)
+    blocks = [g0, z_refs.at[0], g2, z_refs.at[1]]
+    blocks += [y_refs.at[0], yz_refs.at[0], y_refs.at[1], yz_refs.at[1]]
+    unfold(blocks, width, rows_ref)
     grad_hidden = lax.dot_general(rows_ref[...], down_ref[...], NT, preferred_element_type=F32)
     gate = h_ref[:, :units]
     up = h_ref[:, units:]
@@ -293,17 +300,25 @@
     grad_up = (grad_hidden * swish).astype(BF16)
     grad_gate = (grad_hidden * up * sigmoid * (1.0 + gate * (1.0 - sigmoid))).astype(BF16)
     both = jnp.concatenate([grad_gate, grad_up], axis=1)
-    outs = [(ref, k) for ref in (near_a, near_b, far_a, far_b) for k in range(ref.shape[0])]
+    place_a = [(near_a, 0), (near_a, 1), (near_a, 2), (near_a, 3)]
+    place_a += [(far_a, 0), (far_a, 1), (far_a, 2), (far_a, 3)]
+    place_b = [(near_b, 0), (far_b, 0), (near_b, 1), (far_b, 1)]
+    place_b += [(near_b, 2), (far_b, 2), (near_b, 3), (far_b, 3)]
     back = lax.broadcasted_iota(jnp.int32, (MAIN * count, TAIL * count), 0)
     col = lax.broadcasted_iota(jnp.int32, (MAIN * count, TAIL * count), 1)
-    tails = jnp.zeros((MAIN * count, part), F32)
-    for fold in range(FOLDS):
-        span = slice(fold * part, (fold + 1) * part)
-        value = jnp.dot(both, gu_ref[:, span], preferred_element_type=F32).astype(BF16)
-        for k, (ref, j) in enumerate(outs):
-            ref[j, :, span] = value[MAIN * k : MAIN * (k + 1), :]
-        place = as_bf16(back == (col // TAIL) * MAIN + TAIL * fold + col % TAIL)
-        tails = tails + jnp.dot(place, value[MAIN * count :, :], preferred_element_type=F32)
+    for side, places in enumerate((place_a, place_b)):
+        tails = jnp.zeros((MAIN * count, part), F32)
+        for fold in range(FOLDS):
+            start = side * half + fold * part
+            value = jnp.dot(both, gu_ref[:, start : start + part], preferred_element_type=F32)
+            value = value.astype(BF16)
+            for k, (ref, j) in enumerate(places):
+                ref[j, :, fold * part : (fold + 1) * part] = value[MAIN * k : MAIN * (k + 1), :]
+            place = as_bf16(back == (col // TAIL) * MAIN + TAIL * fold + col % TAIL)
+            tails = tails + jnp.dot(place, value[MAIN * count :, :], preferred_element_type=F32)
+        tails = tails.astype(BF16)
+        for k, (ref, j) in enumerate(places):
+            ref[j, :, half : half + part] = tails[MAIN * k : MAIN * (k + 1), :]
     lane = lax.broadcasted_iota(jnp.int32, (slots, 128), 1)
     high, mid, low = (p.astype(F32) for p in three_parts(weight))
     spread = jnp.where(lane == 0, high, jnp.where(lane == 1, mid, jnp.where(lane == 2, low, 0.0)))
@@ -312,43 +327,45 @@
     tile = spread[: MAIN * count, :] + jnp.dot(
         place, shifted[MAIN * count :, :].astype(BF16), preferred_element_type=F32
     )
-    tails = tails.astype(BF16)
     tile = tile.astype(BF16)
-    full = width + part
-    for k, (ref, j) in enumerate(outs):
-        rows = slice(MAIN * k, MAIN * (k + 1))
-        ref[j, :, width:full] = tails[rows, :]
-        ref[j, :, full:] = tile[rows, :]
-
-
-def fold_kernel(near_ref, other_ref, *out_refs):
+    for k, (ref, j) in enumerate(place_a):
+        ref[j, :, half + part :] = tile[MAIN * k : MAIN * (k + 1), :]
+
+
+def added(one, two):
+    return (one.astype(F32) + two.astype(F32)).astype(BF16)
+
+
+def fold_a_kernel(near_ref, got_ref, send_ref, keep_ref):
     full = near_ref.shape[2] - 128
-    for k, ref in enumerate(out_refs):
-        ref[:, :full] = (
-            near_ref[k, :, :full].astype(F32) + other_ref[k, :, :full].astype(F32)
-        ).astype(BF16)
-        ref[:, full : full + 128] = near_ref[k, :, full:]
-        ref[:, full + 128 :] = other_ref[k, :, full:]
-
-
-def gather_kernel(scale_ref, *refs):
-    *in_refs, out_ref = refs
-    full = out_ref.shape[1]
-    width = full * FOLDS // (FOLDS + 1)
-    total = in_refs[0][:, :full].astype(F32)
-    for ref in in_refs[1:]:
-        total = total + ref[:, :full].astype(F32)
-    out_ref[:, :width] = (total[:, :width] * scale_ref[:, :1]).astype(BF16)
-    out_ref[:, width:] = (total[:, width:] * scale_ref[:, 128:129]).astype(BF16)
-
-
-def weight_kernel(routes_ref, *refs):
-    *in_refs, out_ref = refs
+    for k in range(near_ref.shape[0]):
+        ref = (keep_ref, send_ref)[k % 2]
+        ref[k // 2, :, :full] = added(near_ref[k, :, :full], got_ref[k, :, :full])
+        ref[k // 2, :, full : full + 128] = near_ref[k, :, full:]
+        ref[k // 2, :, full + 128 :] = got_ref[k, :, full:]
+
+
+def fold_b_kernel(near_ref, got_ref, send_ref, keep_ref):
+    for k in range(near_ref.shape[0]):
+        ref = (keep_ref, send_ref)[k // 2]
+        ref[k % 2] = added(near_ref[k], got_ref[k])
+
+
+def fold_both_kernel(keep_a, got_a, keep_b, got_b, own_ref, send_ref, own_tile, send_tile):
+    full = keep_b.shape[2]
+    for k, (ref, tile_ref) in enumerate(((own_ref, own_tile), (send_ref, send_tile))):
+        ref[:, :full] = added(keep_a[k, :, :full], got_a[k, :, :full])
+        ref[:, full:] = added(keep_b[k], got_b[k])
+        tile = jnp.zeros((MAIN, 128), F32)
+        for source in (keep_a, got_a):
+            for start in (full, full + 128):
+                tile = tile + source[k, :, start : start + 128].astype(F32)
+        tile_ref[...] = tile
+
+
+def weight_kernel(routes_ref, own_tile, got_tile, out_ref):
     hit, slot = slot_of_token(routes_ref[...])
-    tile = jnp.zeros((MAIN, 128), F32)
-    for ref in in_refs:
-        full = ref.shape[1] - 256
-        tile = tile + ref[:, full : full + 128].astype(F32) + ref[:, full + 128 :].astype(F32)
+    tile = own_tile[...] + got_tile[...]
     lane = lax.broadcasted_iota(jnp.int32, tile.shape, 1)
     main = jnp.sum(jnp.where(lane < 3, tile, 0.0), axis=1, keepdims=True)
     tail = jnp.sum(jnp.where((lane >= 3) & (lane < 6), tile, 0.0), axis=1, keepdims=True)
@@ -361,18 +378,34 @@
     out_ref[...] = jnp.where(hit, value, 0.0)
 
 
-def final_kernel(back_ref, rows_ref, base_ref, out_ref, done_ref, sems):
+def final_kernel(back_ref, scale_ref, one_ref, two_ref, base_ref, out_ref, done_ref, sems):
     width = base_ref.shape[1]
-    part = width // FOLDS
+    half = width // 2
+    part = half // FOLDS
     copies = []
-    for fold in range(FOLDS):
-        span = slice(fold * part, (fold + 1) * part)
-        rows = jnp.concatenate([rows_ref[:, span], rows_ref[:, width:]], axis=0)
-        mixed = jnp.dot(back_ref[fold], rows, preferred_element_type=F32)
-        done_ref[:, span] = (base_ref[:, span].astype(F32) + mixed).astype(BF16)
-        copy = pltpu.make_async_copy(done_ref.at[:, span], out_ref.at[:, span], sems.at[fold])
-        copy.start()
-        copies.append(copy)
+    for side in range(2):
+        first = side * (half + part)
+        for fold in range(FOLDS):
+            rows = []
+            for lane, start in ((0, first + fold * part), (128, first + half)):
+                total = one_ref[:, start : start + part].astype(F32)
+                total = total + two_ref[:, start : start + part].astype(F32)
+                rows.append(total * scale_ref[:, lane : lane + 1])
+            rows = jnp.concatenate(rows, axis=0)
+            high = rows.astype(BF16)
+            low = (rows - high.astype(F32)).astype(BF16)
+            rows = jnp.concatenate([high, low], axis=0)
+            mixed = jnp.dot(back_ref[fold], rows, preferred_element_type=F32)
+            start = side * half + fold * part
+            span = slice(start, start + part)
+            done_ref[:, span] = (base_ref[:, span].astype(F32) + mixed).astype(BF16)
+            if fold % 2:
+                span = slice(start - part, start + part)
+                copy = pltpu.make_async_copy(
+                    done_ref.at[:, span], out_ref.at[:, span], sems.at[len(copies)]
+                )
+                copy.start()
+                copies.append(copy)
     for copy in copies:
         copy.wait()
 
@@ -388,90 +421,128 @@
     return lax.ppermute(value, ("pp", "ep"), pairs)
 
 
+Y1, Z1, Z2 = 2, 4, 8
+
+
 def single_device(upstream, saved, routes, route_weight, w_gate, w_up, w_down):
     routes_t = routes[0].T
     weight_t = route_weight[0].T
     next_routes = passed_along(routes_t, "pp", 1)
+    next_weight = passed_along(weight_t, "pp", 1)
     count, width = saved.shape[1:]
     full = width + width // FOLDS
+    half = full // 2
     units = 2 * w_gate.shape[1]
     slots = SHARDS // 2 * CAP
-
+    hbm = pl.BlockSpec(memory_space=pltpu.HBM)
+
+    next_routes, next_weight = lax.optimization_barrier((next_routes, next_weight))
+    input_block, near_routes, base = near_call(
+        pick_inputs_kernel,
+        [
+            pltpu.VMEM((MAIN, full), BF16),
+            pltpu.VMEM(routes_t.shape, jnp.int32),
+            pltpu.VMEM((count, width), BF16),
+        ],
+        *(pltpu.with_memory_space_constraint(v, pltpu.HBM) for v in (routes_t, saved[0], upstream[0])),
+        in_specs=[hbm] * 3,
+        scratch_shapes=[pltpu.VMEM((count, width), BF16), pltpu.SemaphoreType.DMA((FOLDS + 2,))],
+        name="pick_inputs",
+    )
+    grad_block = near_call(
+        pick_grads_kernel, pltpu.VMEM((MAIN, full), BF16), next_routes, base, name="pick_grads"
+    )
     own = (w_gate[0], w_up[0], w_down[0])
     other = from_partner(own, "ep", 0)
-
-    input_block, scale = near_call(
-        pick_inputs_kernel,
-        [pltpu.VMEM((MAIN, full), BF16), pltpu.VMEM((MAIN, 256), F32)],
-        routes_t,
-        weight_t,
-        saved[0],
-        name="pick_inputs",
-    )
-    grad_block, back = near_call(
-        pick_grads_kernel,
-        [pltpu.VMEM((MAIN, full), BF16), pltpu.VMEM((FOLDS, count, 2 * MAIN), BF16)],
-        next_routes,
-        upstream[0],
-        name="pick_grads",
-    )
     input_block, grad_block, other = lax.optimization_barrier((input_block, grad_block, other))
     gate_up = jnp.concatenate([own[0], other[0], own[1], other[1]], axis=0)
     down = jnp.concatenate([own[2], other[2]], axis=0)
-
-    z_inputs = [input_block] + [across(input_block, 4 * k) for k in (1, 2, 3)]
-    z_grads = [sections_across(grad_block, 4 * k) for k in (0, 1, 2, 3)]
-    y_inputs = across(jnp.stack(z_inputs), 2)
-    y_grads_a = across(jnp.stack(z_grads[:2]), 2)
-    y_grads_b = across(jnp.stack(z_grads[2:]), 2)
+    back, scale = near_call(
+        back_kernel,
+        [pltpu.VMEM((FOLDS, count, 4 * MAIN), BF16), pltpu.VMEM((MAIN, 256), F32)],
+        next_routes,
+        next_weight,
+        name="back_rows",
+    )
+
+    grad_z2 = sections_across(grad_block, Z2)
+    grad_z0 = sections_across(grad_block, 0)
+    input_z2 = across(input_block, Z2)
+    input_y0 = across(input_block, Y1)
+    grad_z = jnp.stack([grad_z0, grad_z2])
+    grad_z1 = across(grad_z, Z1)
+    grad_y = across(grad_z, Y1)
+    input_y2 = across(input_z2, Y1)
+    input_low = across(jnp.stack([input_block, input_y0]), Z1)
+    input_high = across(jnp.stack([input_z2, input_y2]), Z1)
+    grad_yz1 = across(grad_z1, Y1)
+    input_high, back, scale = lax.optimization_barrier((input_high, back, scale))
 
     hidden = near_call(
         forward_kernel,
         pltpu.VMEM((slots, 2 * units), F32),
-        *z_inputs,
-        y_inputs,
+        input_block,
+        input_z2,
+        input_y0,
+        input_y2,
+        input_low,
+        input_high,
         gate_up,
         scratch_shapes=[pltpu.VMEM((slots, width), BF16)],
         name="expert_forward",
     )
-    pair = pltpu.VMEM((2, MAIN, full + 128), BF16)
-    near_a, near_b, far_a, far_b = near_call(
+    side_a = pltpu.VMEM((4, MAIN, half + 128), BF16)
+    side_b = pltpu.VMEM((4, MAIN, half), BF16)
+    near_a, far_a, near_b, far_b = near_call(
         backward_kernel,
-        [pair] * 4,
-        *z_grads,
-        y_grads_a,
-        y_grads_b,
+        [side_a, side_a, side_b, side_b],
+        grad_z0,
+        grad_z2,
+        grad_z1,
+        grad_y,
+        grad_yz1,
         down,
         gate_up,
         hidden,
         scratch_shapes=[pltpu.VMEM((slots, width), BF16)],
         name="expert_backward",
     )
-    sum_shape = pltpu.VMEM((MAIN, full + 256), BF16)
-    far_b = across(far_b, 2)
-    far_a = across(far_a, 2)
-    sums_b = near_call(fold_kernel, [sum_shape] * 2, near_b, far_b, name="fold_far")
-    sums_a = near_call(fold_kernel, [sum_shape] * 2, near_a, far_a, name="fold_near")
-    sums = [*sums_a, *sums_b]
-    arrived = [sums[0]] + [across(sums[k], 4 * k) for k in (1, 2, 3)]
-    slot_rows = near_call(
-        gather_kernel, pltpu.VMEM((MAIN, full), BF16), scale, *arrived, name="sum_z"
-    )
+    got_a = across(far_a, Y1)
+    got_b = across(far_b, Z1)
+    send_a, keep_a = near_call(
+        fold_a_kernel, [pltpu.VMEM((2, MAIN, half + 256), BF16)] * 2, near_a, got_a, name="fold_a"
+    )
+    send_b, keep_b = near_call(
+        fold_b_kernel, [pltpu.VMEM((2, MAIN, half), BF16)] * 2, near_b, got_b, name="fold_b"
+    )
+    rows_0, rows_2, tile_0, tile_2 = near_call(
+        fold_both_kernel,
+        [pltpu.VMEM((MAIN, full), BF16)] * 2 + [pltpu.VMEM((MAIN, 128), F32)] * 2,
+        keep_a,
+        across(send_a, Z1),
+        keep_b,
+        across(send_b, Y1),
+        name="fold_both",
+    )
+    got_2 = sections_across(rows_2, Z2)
+    got_0 = sections_across(rows_0, 0)
     weight_out = near_call(
         weight_kernel,
         jax.ShapeDtypeStruct((TOP, count), F32),
-        routes_t,
-        *arrived,
+        near_routes,
+        tile_0,
+        across(tile_2, Z2),
         name="weight_out",
     )
-    slot_rows = sections_across(slot_rows, 0)
     grad_prev = near_call(
         final_kernel,
         jax.ShapeDtypeStruct((count, width), BF16),
         back,
-        slot_rows,
-        upstream[0],
-        out_specs=pl.BlockSpec(memory_space=pl.ANY),
+        scale,
+        got_0,
+        got_2,
+        base,
+        out_specs=hbm,
         scratch_shapes=[pltpu.VMEM((count, width), BF16), pltpu.SemaphoreType.DMA((FOLDS,))],
         name="final_rows",
     )

time: 62.3 us -> 59.8 us (0.960)
  starting transfers between devices: 27.1 us -> 21.8 us
  waiting for transfers between devices: 24.5 us -> 29.1 us
  local copies, waits for them, and re-layouts: 3.84 us -> 0.01 us
  Pallas kernels: 5.51 us -> 7.57 us
    unnamed x18 -> x6, local copies, waits for them, and re-layouts: 3.84 us -> 0.01 us
    ppermute x11 -> x13, starting transfers between devices: 17.5 us -> 14 us  [across(): return lax.ppermute(value, 'ep', [(i, i ^ bits) for i in range(count)])]
    ppermute x1 -> x2, waiting for transfers between devices: 0.01 us -> 2.15 us  [passed_along(): lax.ppermute(value, axis, [(i, (i + by) % size) for i in range(size)])]
    pallas_call x9 -> x10, Pallas kernels: 5.51 us -> 7.57 us  [near_call(): pl.pallas_call(kernel, out_shape=out_shape, compiler_params=params, **kwa...]
    ppermute x11 -> x13, waiting for transfers between devices: 19.5 us -> 21.5 us  [across(): return lax.ppermute(value, 'ep', [(i, i ^ bits) for i in range(count)])]
    ppermute x5 -> x4, starting transfers between devices: 6.01 us -> 4.14 us  [sections_across(): return lax.ppermute(value, ('pp', 'ep'), pairs)]
    ppermute x5 -> x4, waiting for transfers between devices: 4.98 us -> 5.43 us  [sections_across(): return lax.ppermute(value, ('pp', 'ep'), pairs)]
    ppermute x1 -> x2, starting transfers between devices: 2.56 us -> 2.6 us  [passed_along(): lax.ppermute(value, axis, [(i, (i + by) % size) for i in range(size)])]
  transfers between devices with their start and end apart: 20 -> 22, of which waited for: 11 -> 10; matrix products, arithmetic and copies ran while one was open for 0% -> 0% of each run, Pallas kernels for 4% -> 7%
where the time goes in v3:
time: 59.8 us; the launch traced here: 59.6 us
  waiting for transfers between devices  29.1 us (49%)
  starting transfers between devices  21.8 us (36%)
  Pallas kernels  7.57 us (13%)
  between operations  0.81 us (1%)
    ppermute x13, waiting for transfers between devices, across(): return lax.ppermute(value, 'ep', [(i, i ^ bits) for i in range(count)])  21.5 us
    ppermute x13, starting transfers between devices, across(): return lax.ppermute(value, 'ep', [(i, i ^ bits) for i in range(count)])  14 us
    pallas_call x10, Pallas kernels, near_call(): pl.pallas_call(kernel, out_shape=out_shape, compiler_params=params, **kwa...  7.57 us
    ppermute x4, waiting for transfers between devices, sections_across(): return lax.ppermute(value, ('pp', 'ep'), pairs)  5.43 us
    ppermute x4, starting transfers between devices, sections_across(): return lax.ppermute(value, ('pp', 'ep'), pairs)  4.14 us
    ppermute x2, starting transfers between devices, passed_along(): lax.ppermute(value, axis, [(i, (i + by) % size) for i in range(size)])  2.6 us
    ppermute x2, waiting for transfers between devices, passed_along(): lax.ppermute(value, axis, [(i, (i + by) % size) for i in range(size)])  2.15 us
  transfers between devices with their start and end apart: 22, of which 10 were waited for; matrix products, arithmetic and copies ran while one was open for 0% of the time, Pallas kernels for 7%

profile of v3, /device:TPU:0, one launch (start us, length us, event | category | flops | bytes accessed | tf_op | source)
XLA Modules:
  0.0 59.6 jit_solution(3783677272520965712)
XLA Ops:
  0.7 0.5 collective-permute-start.2
  1.2 0.4 collective-permute-start.4
  1.7 2.6 %collective-permute-start = (s32[8,128]{1,0:T(8,128)}, s32[8,128]{1,0:T(8,128)S(1)}, u32[]{:S(2)}, u32[]{:S(2)}) collective-permute-start(s32[8,128]{1,0:T(8,128)} %bitcast.36), channel_id=1, source_target_pairs={{0,16},{16,0},{1,17},{17,1},{2,18},{18,2},{3,19},{19,3},{4,20},{20... | collective-permute-start | bytes 12296 | tf_op jit(solution)/shard_map/ppermute | solution.py:32
  4.3 1.6 %pick_inputs.1 = (bf16[8,5120]{1,0:T(8,128)(2,1)S(1)}, s32[8,128]{1,0:T(8,128)S(1)}, bf16[128,4096]{1,0:T(8,128)(2,1)S(1)}) custom-call(s32[8,128]{1,0:T(8,128)} %bitcast.37, bf16[128,4096]{1,0:T(8,128)(2,1)} %bitcast.28, bf16[128,4096]{1,0:T(8,128)(2,1)} %bitcast.29), custom_call_target="tpu_custom_call" | custom-call | tf_op jit(solution)/shard_map/pick_inputs/pallas_call | solution.py:153
  6.0 2.0 %collective-permute-done.1.weight_ref = f32[8,128]{1,0:T(8,128)S(1)} collective-permute-done((f32[8,128]{1,0:T(8,128)}, f32[8,128]{1,0:T(8,128)S(1)}, u32[]{:S(2)}, u32[]{:S(2)}) %collective-permute-start.1) | collective-permute-done | bytes 4128 | tf_op jit(solution)/shard_map/ppermute | solution.py:32
  8.1 0.4 pick_grads.1
  8.4 0.4 back_rows.1
  8.9 2.7 %collective-permute-start.5 = (bf16[8,5120]{1,0:T(8,128)(2,1)S(1)}, bf16[8,5120]{1,0:T(8,128)(2,1)S(1)}, u32[]{:S(2)}, u32[]{:S(2)}) collective-permute-start(bf16[8,5120]{1,0:T(8,128)(2,1)S(1)} %get-tuple-element.32.own), channel_id=1, source_target_pairs={{0,8},{1,9},{2,10},{3,11},{4,12},{5,13},{6,14},{7,15},{8,0},{9,1},... | collective-permute-start | bytes 245768 | tf_op jit(solution)/shard_map/ppermute | solution.py:415
  11.5 1.5 %collective-permute-start.13 = (bf16[8,5120]{1,0:T(8,128)(2,1)S(1)}, bf16[8,5120]{1,0:T(8,128)(2,1)S(1)}, u32[]{:S(2)}, u32[]{:S(2)}) collective-permute-start(bf16[8,5120]{1,0:T(8,128)(2,1)S(1)} %get-tuple-element.32.own), channel_id=1, source_target_pairs={{0,2},{1,3},{2,0},{3,1},{4,6},{5,7},{6,4},{7,5},{8,10},{9,11},{10,... | collective-permute-start | bytes 245768 | tf_op jit(solution)/shard_map/ppermute | solution.py:415
  13.0 0.5 collective-permute-start.8
  13.6 1.3 %collective-permute-start.9 = (bf16[8,5120]{1,0:T(8,128)(2,1)S(1)}, bf16[8,5120]{1,0:T(8,128)(2,1)S(1)}, u32[]{:S(2)}, u32[]{:S(2)}) collective-permute-start(bf16[8,5120]{1,0:T(8,128)(2,1)S(1)} %pick_grads.1), channel_id=1, source_target_pairs={{0,24},{1,25},{2,26},{3,27},{4,28},{5,29},{6,30},{7,31},{8,16},{9,... | collective-permute-start | bytes 245768 | tf_op jit(solution)/shard_map/ppermute | solution.py:421
  15.0 3.1 %collective-permute-done.8.refs_0_ = bf16[8,5120]{1,0:T(8,128)(2,1)S(1)} collective-permute-done((bf16[8,5120]{1,0:T(8,128)(2,1)S(1)}, bf16[8,5120]{1,0:T(8,128)(2,1)S(1)}, u32[]{:S(2)}, u32[]{:S(2)}) %collective-permute-start.8) | collective-permute-done | bytes 81952 | tf_op jit(solution)/shard_map/ppermute | solution.py:421
  18.1 1.7 %collective-permute-done.9.refs_1_ = bf16[8,5120]{1,0:T(8,128)(2,1)S(1)} collective-permute-done((bf16[8,5120]{1,0:T(8,128)(2,1)S(1)}, bf16[8,5120]{1,0:T(8,128)(2,1)S(1)}, u32[]{:S(2)}, u32[]{:S(2)}) %collective-permute-start.9) | collective-permute-done | bytes 81952 | tf_op jit(solution)/shard_map/ppermute | solution.py:421
  19.8 1.6 %collective-permute-start.10 = (bf16[2,8,5120]{2,1,0:T(8,128)(2,1)S(1)}, bf16[2,8,5120]{2,1,0:T(8,128)(2,1)S(1)}, u32[]{:S(2)}, u32[]{:S(2)}) collective-permute-start(bf16[2,8,5120]{2,1,0:T(8,128)(2,1)S(1)} %pad_maximum_fusion.3), channel_id=1, source_target_pairs={{0,4},{1,5},{2,6},{3,7},{4,0},{5,1},{6,2},{7,3},{8,12},{9,13},{10,... | collective-permute-start | bytes 491528 | tf_op jit(solution)/shard_map/ppermute | solution.py:415
  21.5 0.5 collective-permute-start.11
  22.0 1.5 %collective-permute-start.6 = (bf16[8,5120]{1,0:T(8,128)(2,1)S(1)}, bf16[8,5120]{1,0:T(8,128)(2,1)S(1)}, u32[]{:S(2)}, u32[]{:S(2)}) collective-permute-start(bf16[8,5120]{1,0:T(8,128)(2,1)S(1)} %collective-permute-done.5.z2), channel_id=1, source_target_pairs={{0,2},{1,3},{2,0},{3,1},{4,6},{5,7},{6,4},{7,5},{8,10},{9,11},{10,... | collective-permute-start | bytes 245768 | tf_op jit(solution)/shard_map/ppermute | solution.py:415
  23.5 0.5 collective-permute-start.14
  24.0 4.6 %collective-permute-done.6.y2 = bf16[8,5120]{1,0:T(8,128)(2,1)S(1)} collective-permute-done((bf16[8,5120]{1,0:T(8,128)(2,1)S(1)}, bf16[8,5120]{1,0:T(8,128)(2,1)S(1)}, u32[]{:S(2)}, u32[]{:S(2)}) %collective-permute-start.6) | collective-permute-done | bytes 81952 | tf_op jit(solution)/shard_map/ppermute | solution.py:415
  29.0 5.1 %collective-permute-done.7.high = bf16[2,8,5120]{2,1,0:T(8,128)(2,1)S(1)} collective-permute-done((bf16[2,8,5120]{2,1,0:T(8,128)(2,1)S(1)}, bf16[2,8,5120]{2,1,0:T(8,128)(2,1)S(1)}, u32[]{:S(2)}, u32[]{:S(2)}) %collective-permute-start.7) | collective-permute-done | bytes 163872 | tf_op jit(solution)/shard_map/ppermute | solution.py:415
  34.1 0.8 %expert_forward.1.refs_7_ = f32[80,256]{1,0:T(8,128)S(1)} custom-call(bf16[8,5120]{1,0:T(8,128)(2,1)S(1)} %get-tuple-element.32.own, bf16[8,5120]{1,0:T(8,128)(2,1)S(1)} %collective-permute-done.5.z2, bf16[8,5120]{1,0:T(8,128)(2,1)S(1)} %collective-permute-done.13.y0, bf16[8,5120]{1,0:T(8,128)(2,1)S(1)} %collective-permute-done.6.y2, ...), custom_call_target="tpu_custom_call" | custom-call | tf_op jit(solution)/shard_map/expert_forward/pallas_call | solution.py:153
  34.9 2.2 %expert_backward.1 = (bf16[4,8,2688]{2,1,0:T(8,128)(2,1)S(1)}, bf16[4,8,2688]{2,1,0:T(8,128)(2,1)S(1)}, bf16[4,8,2560]{2,1,0:T(8,128)(2,1)S(1)}, bf16[4,8,2560]{2,1,0:T(8,128)(2,1)S(1)}) custom-call(bf16[8,5120]{1,0:T(8,128)(2,1)S(1)} %collective-permute-done.8.refs_0_, bf16[8,5120]{1,0:T(8,128)(2,1)S(1)} %collective-permute-done.9.refs_1_, ...), custom_call_target="tpu_custom_call" | custom-call | tf_op jit(solution)/shard_map/expert_backward/pallas_call | solution.py:153
  37.2 1.5 %collective-permute-start.17 = (bf16[4,8,2560]{2,1,0:T(8,128)(2,1)S(1)}, bf16[4,8,2560]{2,1,0:T(8,128)(2,1)S(1)}, u32[]{:S(2)}, u32[]{:S(2)}) collective-permute-start(bf16[4,8,2560]{2,1,0:T(8,128)(2,1)S(1)} %get-tuple-element.48), channel_id=1, source_target_pairs={{0,4},{1,5},{2,6},{3,7},{4,0},{5,1},{6,2},{7,3},{8,12},{9,13},{10,... | collective-permute-start | bytes 491528 | tf_op jit(solution)/shard_map/ppermute | solution.py:415
  38.8 4.7 %collective-permute-done.15.got_ref = bf16[4,8,2688]{2,1,0:T(8,128)(2,1)S(1)} collective-permute-done((bf16[4,8,2688]{2,1,0:T(8,128)(2,1)S(1)}, bf16[4,8,2688]{2,1,0:T(8,128)(2,1)S(1)}, u32[]{:S(2)}, u32[]{:S(2)}) %collective-permute-start.15) | collective-permute-done | bytes 172064 | tf_op jit(solution)/shard_map/ppermute | solution.py:415
  43.6 0.8 %collective-permute-start.16 = (bf16[2,8,2816]{2,1,0:T(8,128)(2,1)S(1)}, bf16[2,8,2816]{2,1,0:T(8,128)(2,1)S(1)}, u32[]{:S(2)}, u32[]{:S(2)}) collective-permute-start(bf16[2,8,2816]{2,1,0:T(8,128)(2,1)S(1)} %get-tuple-element.46), channel_id=1, source_target_pairs={{0,4},{1,5},{2,6},{3,7},{4,0},{5,1},{6,2},{7,3},{8,12},{9,13},{10,... | collective-permute-start | bytes 270344 | tf_op jit(solution)/shard_map/ppermute | solution.py:415
  44.4 0.8 %collective-permute-start.18 = (bf16[2,8,2560]{2,1,0:T(8,128)(2,1)S(1)}, bf16[2,8,2560]{2,1,0:T(8,128)(2,1)S(1)}, u32[]{:S(2)}, u32[]{:S(2)}) collective-permute-start(bf16[2,8,2560]{2,1,0:T(8,128)(2,1)S(1)} %get-tuple-element.50), channel_id=1, source_target_pairs={{0,2},{1,3},{2,0},{3,1},{4,6},{5,7},{6,4},{7,5},{8,10},{9,11},{10,... | collective-permute-start | bytes 245768 | tf_op jit(solution)/shard_map/ppermute | solution.py:415
  45.2 3.7 %collective-permute-done.18.got_b = bf16[2,8,2560]{2,1,0:T(8,128)(2,1)S(1)} collective-permute-done((bf16[2,8,2560]{2,1,0:T(8,128)(2,1)S(1)}, bf16[2,8,2560]{2,1,0:T(8,128)(2,1)S(1)}, u32[]{:S(2)}, u32[]{:S(2)}) %collective-permute-start.18) | collective-permute-done | bytes 81952 | tf_op jit(solution)/shard_map/ppermute | solution.py:415
  48.9 2.2 %collective-permute-start.19 = (bf16[8,5120]{1,0:T(8,128)(2,1)S(1)}, bf16[8,5120]{1,0:T(8,128)(2,1)S(1)}, u32[]{:S(2)}, u32[]{:S(2)}) collective-permute-start(bf16[8,5120]{1,0:T(8,128)(2,1)S(1)} %get-tuple-element.51), channel_id=1, source_target_pairs={{0,16},{1,17},{2,18},{3,19},{4,20},{5,21},{6,22},{7,23},{8,24},{9,... | collective-permute-start | bytes 245768 | tf_op jit(solution)/shard_map/ppermute | solution.py:421
  51.3 2.3 %collective-permute-start.21 = (f32[8,128]{1,0:T(8,128)S(1)}, f32[8,128]{1,0:T(8,128)S(1)}, u32[]{:S(2)}, u32[]{:S(2)}) collective-permute-start(f32[8,128]{1,0:T(8,128)S(1)} %get-tuple-element.55), channel_id=1, source_target_pairs={{0,8},{1,9},{2,10},{3,11},{4,12},{5,13},{6,14},{7,15},{8,0},{9,1},... | collective-permute-start | bytes 12296 | tf_op jit(solution)/shard_map/ppermute | solution.py:415
  53.6 3.4 %collective-permute-done.21.got_tile = f32[8,128]{1,0:T(8,128)S(1)} collective-permute-done((f32[8,128]{1,0:T(8,128)S(1)}, f32[8,128]{1,0:T(8,128)S(1)}, u32[]{:S(2)}, u32[]{:S(2)}) %collective-permute-start.21) | collective-permute-done | bytes 4128 | tf_op jit(solution)/shard_map/ppermute | solution.py:415
  57.0 0.7 %weight_out.1 = f32[8,128]{1,0:T(8,128)} custom-call(s32[8,128]{1,0:T(8,128)S(1)} %get-tuple-element.53.routes_ref, f32[8,128]{1,0:T(8,128)S(1)} %get-tuple-element.54.own_tile, f32[8,128]{1,0:T(8,128)S(1)} %collective-permute-done.21.got_tile), custom_call_target="tpu_custom_call" | custom-call | tf_op jit(solution)/shard_map/weight_out/pallas_call | solution.py:153
  57.7 0.6 %collective-permute-done.20.two_ref = bf16[8,5120]{1,0:T(8,128)(2,1)S(1)} collective-permute-done((bf16[8,5120]{1,0:T(8,128)(2,1)S(1)}, bf16[8,5120]{1,0:T(8,128)(2,1)S(1)}, u32[]{:S(2)}, u32[]{:S(2)}) %collective-permute-start.20) | collective-permute-done | bytes 81952 | tf_op jit(solution)/shard_map/ppermute | solution.py:421
  58.3 1.3 %final_rows.1 = bf16[128,4096]{1,0:T(8,128)(2,1)} custom-call(bf16[4,128,32]{2,1,0:T(8,128)(2,1)S(1)} %get-tuple-element.36.back_ref, f32[8,256]{1,0:T(8,128)S(1)} %get-tuple-element.37.scale_ref, bf16[8,5120]{1,0:T(8,128)(2,1)S(1)} %collective-permute-done.19.one_ref, bf16[8,5120]{1,0:T(8,128)(2,1)S(1)} %collective-permute-done.20.two_ref, ...), custom_call_target="tpu_custom_call" | custom-call | tf_op jit(solution)/shard_map/final_rows/pallas_call | solution.py:153
  (33 shorter events, 1.0 us)
Async XLA Ops:
  0.6 14.2 %copy-start.2 = (bf16[1,64,4096]{2,1,0:T(8,128)(2,1)S(1)}, bf16[1,64,4096]{2,1,0:T(8,128)(2,1)}, u32[]{:S(2)}) copy-start(bf16[1,64,4096]{2,1,0:T(8,128)(2,1)} %param.11) | copy-start | bytes 1572868
  0.6 14.2 %copy-start.1 = (bf16[1,64,4096]{2,1,0:T(8,128)(2,1)S(1)}, bf16[1,64,4096]{2,1,0:T(8,128)(2,1)}, u32[]{:S(2)}) copy-start(bf16[1,64,4096]{2,1,0:T(8,128)(2,1)} %param.12) | copy-start | bytes 1572868
  0.7 8.2 %collective-permute-start.2 = (bf16[64,4096]{1,0:T(8,128)(2,1)}, bf16[64,4096]{1,0:T(8,128)(2,1)S(1)}, u32[]{:S(2)}, u32[]{:S(2)}) collective-permute-start(bf16[64,4096]{1,0:T(8,128)(2,1)} %bitcast.34), channel_id=1, source_target_pairs={{0,1},{1,0},{2,3},{3,2},{4,5},{5,4},{6,7},{7,6},{8,9},{9,8},{10,11... | collective-permute-start | bytes 1572872 | tf_op jit(solution)/shard_map/ppermute | solution.py:27
  1.2 7.7 %collective-permute-start.3 = (bf16[64,4096]{1,0:T(8,128)(2,1)}, bf16[64,4096]{1,0:T(8,128)(2,1)S(1)}, u32[]{:S(2)}, u32[]{:S(2)}) collective-permute-start(bf16[64,4096]{1,0:T(8,128)(2,1)} %bitcast.32), channel_id=1, source_target_pairs={{0,1},{1,0},{2,3},{3,2},{4,5},{5,4},{6,7},{7,6},{8,9},{9,8},{10,11... | collective-permute-start | bytes 1572872 | tf_op jit(solution)/shard_map/ppermute | solution.py:27
  1.2 7.6 %collective-permute-start.4 = (bf16[64,4096]{1,0:T(8,128)(2,1)}, bf16[64,4096]{1,0:T(8,128)(2,1)S(1)}, u32[]{:S(2)}, u32[]{:S(2)}) collective-permute-start(bf16[64,4096]{1,0:T(8,128)(2,1)} %bitcast.30), channel_id=1, source_target_pairs={{0,1},{1,0},{2,3},{3,2},{4,5},{5,4},{6,7},{7,6},{8,9},{9,8},{10,11... | collective-permute-start | bytes 1572872 | tf_op jit(solution)/shard_map/ppermute | solution.py:27
  1.7 4.4 %collective-permute-start = (s32[8,128]{1,0:T(8,128)}, s32[8,128]{1,0:T(8,128)S(1)}, u32[]{:S(2)}, u32[]{:S(2)}) collective-permute-start(s32[8,128]{1,0:T(8,128)} %bitcast.36), channel_id=1, source_target_pairs={{0,16},{16,0},{1,17},{17,1},{2,18},{18,2},{3,19},{19,3},{4,20},{20... | collective-permute-start | bytes 12296 | tf_op jit(solution)/shard_map/ppermute | solution.py:32
  4.2 3.8 %collective-permute-start.1 = (f32[8,128]{1,0:T(8,128)}, f32[8,128]{1,0:T(8,128)S(1)}, u32[]{:S(2)}, u32[]{:S(2)}) collective-permute-start(f32[8,128]{1,0:T(8,128)} %bitcast.39), channel_id=1, source_target_pairs={{0,16},{16,0},{1,17},{17,1},{2,18},{18,2},{3,19},{19,3},{4,20},{20... | collective-permute-start | bytes 12296 | tf_op jit(solution)/shard_map/ppermute | solution.py:32
  8.8 20.0 %copy-start = (bf16[1,64,4096]{2,1,0:T(8,128)(2,1)S(1)}, bf16[1,64,4096]{2,1,0:T(8,128)(2,1)}, u32[]{:S(2)}) copy-start(bf16[1,64,4096]{2,1,0:T(8,128)(2,1)} %param.13) | copy-start | bytes 1572868
  8.9 13.1 %collective-permute-start.5 = (bf16[8,5120]{1,0:T(8,128)(2,1)S(1)}, bf16[8,5120]{1,0:T(8,128)(2,1)S(1)}, u32[]{:S(2)}, u32[]{:S(2)}) collective-permute-start(bf16[8,5120]{1,0:T(8,128)(2,1)S(1)} %get-tuple-element.32.own), channel_id=1, source_target_pairs={{0,8},{1,9},{2,10},{3,11},{4,12},{5,13},{6,14},{7,15},{8,0},{9,1},... | collective-permute-start | bytes 245768 | tf_op jit(solution)/shard_map/ppermute | solution.py:415
  11.5 12.0 %collective-permute-start.13 = (bf16[8,5120]{1,0:T(8,128)(2,1)S(1)}, bf16[8,5120]{1,0:T(8,128)(2,1)S(1)}, u32[]{:S(2)}, u32[]{:S(2)}) collective-permute-start(bf16[8,5120]{1,0:T(8,128)(2,1)S(1)} %get-tuple-element.32.own), channel_id=1, source_target_pairs={{0,2},{1,3},{2,0},{3,1},{4,6},{5,7},{6,4},{7,5},{8,10},{9,11},{10,... | collective-permute-start | bytes 245768 | tf_op jit(solution)/shard_map/ppermute | solution.py:415
  13.0 5.1 %collective-permute-start.8 = (bf16[8,5120]{1,0:T(8,128)(2,1)S(1)}, bf16[8,5120]{1,0:T(8,128)(2,1)S(1)}, u32[]{:S(2)}, u32[]{:S(2)}) collective-permute-start(bf16[8,5120]{1,0:T(8,128)(2,1)S(1)} %pick_grads.1), channel_id=1, source_target_pairs={{0,16},{1,17},{2,18},{3,19},{4,20},{5,21},{6,22},{7,23},{8,24},{9,... | collective-permute-start | bytes 245768 | tf_op jit(solution)/shard_map/ppermute | solution.py:421
  13.6 6.2 %collective-permute-start.9 = (bf16[8,5120]{1,0:T(8,128)(2,1)S(1)}, bf16[8,5120]{1,0:T(8,128)(2,1)S(1)}, u32[]{:S(2)}, u32[]{:S(2)}) collective-permute-start(bf16[8,5120]{1,0:T(8,128)(2,1)S(1)} %pick_grads.1), channel_id=1, source_target_pairs={{0,24},{1,25},{2,26},{3,27},{4,28},{5,29},{6,30},{7,31},{8,16},{9,... | collective-permute-start | bytes 245768 | tf_op jit(solution)/shard_map/ppermute | solution.py:421
  19.8 8.9 %collective-permute-start.10 = (bf16[2,8,5120]{2,1,0:T(8,128)(2,1)S(1)}, bf16[2,8,5120]{2,1,0:T(8,128)(2,1)S(1)}, u32[]{:S(2)}, u32[]{:S(2)}) collective-permute-start(bf16[2,8,5120]{2,1,0:T(8,128)(2,1)S(1)} %pad_maximum_fusion.3), channel_id=1, source_target_pairs={{0,4},{1,5},{2,6},{3,7},{4,0},{5,1},{6,2},{7,3},{8,12},{9,13},{10,... | collective-permute-start | bytes 491528 | tf_op jit(solution)/shard_map/ppermute | solution.py:415
  21.5 13.5 %collective-permute-start.11 = (bf16[2,8,5120]{2,1,0:T(8,128)(2,1)S(1)}, bf16[2,8,5120]{2,1,0:T(8,128)(2,1)S(1)}, u32[]{:S(2)}, u32[]{:S(2)}) collective-permute-start(bf16[2,8,5120]{2,1,0:T(8,128)(2,1)S(1)} %pad_maximum_fusion.3), channel_id=1, source_target_pairs={{0,2},{1,3},{2,0},{3,1},{4,6},{5,7},{6,4},{7,5},{8,10},{9,11},{10,... | collective-permute-start | bytes 491528 | tf_op jit(solution)/shard_map/ppermute | solution.py:415
  22.0 6.7 %collective-permute-start.6 = (bf16[8,5120]{1,0:T(8,128)(2,1)S(1)}, bf16[8,5120]{1,0:T(8,128)(2,1)S(1)}, u32[]{:S(2)}, u32[]{:S(2)}) collective-permute-start(bf16[8,5120]{1,0:T(8,128)(2,1)S(1)} %collective-permute-done.5.z2), channel_id=1, source_target_pairs={{0,2},{1,3},{2,0},{3,1},{4,6},{5,7},{6,4},{7,5},{8,10},{9,11},{10,... | collective-permute-start | bytes 245768 | tf_op jit(solution)/shard_map/ppermute | solution.py:415
  23.5 10.6 %collective-permute-start.14 = (bf16[2,8,5120]{2,1,0:T(8,128)(2,1)S(1)}, bf16[2,8,5120]{2,1,0:T(8,128)(2,1)S(1)}, u32[]{:S(2)}, u32[]{:S(2)}) collective-permute-start(bf16[2,8,5120]{2,1,0:T(8,128)(2,1)S(1)} %pad_maximum_fusion.4), channel_id=1, source_target_pairs={{0,4},{1,5},{2,6},{3,7},{4,0},{5,1},{6,2},{7,3},{8,12},{9,13},{10,... | collective-permute-start | bytes 491528 | tf_op jit(solution)/shard_map/ppermute | solution.py:415
  28.7 5.4 %collective-permute-start.7 = (bf16[2,8,5120]{2,1,0:T(8,128)(2,1)S(1)}, bf16[2,8,5120]{2,1,0:T(8,128)(2,1)S(1)}, u32[]{:S(2)}, u32[]{:S(2)}) collective-permute-start(bf16[2,8,5120]{2,1,0:T(8,128)(2,1)S(1)} %pad_maximum_fusion.2), channel_id=1, source_target_pairs={{0,4},{1,5},{2,6},{3,7},{4,0},{5,1},{6,2},{7,3},{8,12},{9,13},{10,... | collective-permute-start | bytes 491528 | tf_op jit(solution)/shard_map/ppermute | solution.py:415
  28.8 6.2 %collective-permute-start.12 = (bf16[2,8,5120]{2,1,0:T(8,128)(2,1)S(1)}, bf16[2,8,5120]{2,1,0:T(8,128)(2,1)S(1)}, u32[]{:S(2)}, u32[]{:S(2)}) collective-permute-start(bf16[2,8,5120]{2,1,0:T(8,128)(2,1)S(1)} %collective-permute-done.10.refs_2_), channel_id=1, source_target_pairs={{0,2},{1,3},{2,0},{3,1},{4,6},{5,7},{6,4},{7,5},{8,10},{9,11},{10,... | collective-permute-start | bytes 491528 | tf_op jit(solution)/shard_map/ppermute | solution.py:415
  37.2 6.3 %collective-permute-start.15 = (bf16[4,8,2688]{2,1,0:T(8,128)(2,1)S(1)}, bf16[4,8,2688]{2,1,0:T(8,128)(2,1)S(1)}, u32[]{:S(2)}, u32[]{:S(2)}) collective-permute-start(bf16[4,8,2688]{2,1,0:T(8,128)(2,1)S(1)} %get-tuple-element.44), channel_id=1, source_target_pairs={{0,2},{1,3},{2,0},{3,1},{4,6},{5,7},{6,4},{7,5},{8,10},{9,11},{10,... | collective-permute-start | bytes 516104 | tf_op jit(solution)/shard_map/ppermute | solution.py:415
  37.2 7.1 %collective-permute-start.17 = (bf16[4,8,2560]{2,1,0:T(8,128)(2,1)S(1)}, bf16[4,8,2560]{2,1,0:T(8,128)(2,1)S(1)}, u32[]{:S(2)}, u32[]{:S(2)}) collective-permute-start(bf16[4,8,2560]{2,1,0:T(8,128)(2,1)S(1)} %get-tuple-element.48), channel_id=1, source_target_pairs={{0,4},{1,5},{2,6},{3,7},{4,0},{5,1},{6,2},{7,3},{8,12},{9,13},{10,... | collective-permute-start | bytes 491528 | tf_op jit(solution)/shard_map/ppermute | solution.py:415
  43.6 5.3 %collective-permute-start.16 = (bf16[2,8,2816]{2,1,0:T(8,128)(2,1)S(1)}, bf16[2,8,2816]{2,1,0:T(8,128)(2,1)S(1)}, u32[]{:S(2)}, u32[]{:S(2)}) collective-permute-start(bf16[2,8,2816]{2,1,0:T(8,128)(2,1)S(1)} %get-tuple-element.46), channel_id=1, source_target_pairs={{0,4},{1,5},{2,6},{3,7},{4,0},{5,1},{6,2},{7,3},{8,12},{9,13},{10,... | collective-permute-start | bytes 270344 | tf_op jit(solution)/shard_map/ppermute | solution.py:415
  44.4 4.5 %collective-permute-start.18 = (bf16[2,8,2560]{2,1,0:T(8,128)(2,1)S(1)}, bf16[2,8,2560]{2,1,0:T(8,128)(2,1)S(1)}, u32[]{:S(2)}, u32[]{:S(2)}) collective-permute-start(bf16[2,8,2560]{2,1,0:T(8,128)(2,1)S(1)} %get-tuple-element.50), channel_id=1, source_target_pairs={{0,2},{1,3},{2,0},{3,1},{4,6},{5,7},{6,4},{7,5},{8,10},{9,11},{10,... | collective-permute-start | bytes 245768 | tf_op jit(solution)/shard_map/ppermute | solution.py:415
  48.9 8.8 %collective-permute-start.19 = (bf16[8,5120]{1,0:T(8,128)(2,1)S(1)}, bf16[8,5120]{1,0:T(8,128)(2,1)S(1)}, u32[]{:S(2)}, u32[]{:S(2)}) collective-permute-start(bf16[8,5120]{1,0:T(8,128)(2,1)S(1)} %get-tuple-element.51), channel_id=1, source_target_pairs={{0,16},{1,17},{2,18},{3,19},{4,20},{5,21},{6,22},{7,23},{8,24},{9,... | collective-permute-start | bytes 245768 | tf_op jit(solution)/shard_map/ppermute | solution.py:421
  51.2 7.2 %collective-permute-start.20 = (bf16[8,5120]{1,0:T(8,128)(2,1)S(1)}, bf16[8,5120]{1,0:T(8,128)(2,1)S(1)}, u32[]{:S(2)}, u32[]{:S(2)}) collective-permute-start(bf16[8,5120]{1,0:T(8,128)(2,1)S(1)} %get-tuple-element.52), channel_id=1, source_target_pairs={{0,24},{1,25},{2,26},{3,27},{4,28},{5,29},{6,30},{7,31},{8,16},{9,... | collective-permute-start | bytes 245768 | tf_op jit(solution)/shard_map/ppermute | solution.py:421
  51.3 5.7 %collective-permute-start.21 = (f32[8,128]{1,0:T(8,128)S(1)}, f32[8,128]{1,0:T(8,128)S(1)}, u32[]{:S(2)}, u32[]{:S(2)}) collective-permute-start(f32[8,128]{1,0:T(8,128)S(1)} %get-tuple-element.55), channel_id=1, source_target_pairs={{0,8},{1,9},{2,10},{3,11},{4,12},{5,13},{6,14},{7,15},{8,0},{9,1},... | collective-permute-start | bytes 12296 | tf_op jit(solution)/shard_map/ppermute | solution.py:415

commit v4 on v3

--- a/solution.py
+++ b/solution.py
@@ -211,12 +211,20 @@
             pltpu.make_async_copy(rows_in.at[:, span], rows_ref.at[:, span], sems.at[fold])
         )
         copies[-1].start()
-    base_copy = pltpu.make_async_copy(base_in, base_ref, sems.at[FOLDS + 1])
-    base_copy.start()
+    base_copies = []
+    for fold in range(FOLDS):
+        span = slice(fold * part, (fold + 1) * part)
+        base_copies.append(
+            pltpu.make_async_copy(
+                base_in.at[:, span], base_ref.at[:, span], sems.at[FOLDS + 1 + fold]
+            )
+        )
+        base_copies[-1].start()
     routes_copy.wait()
     _, slot = slot_of_token(routes_ref[...])
     pick_into(slot, rows_ref, out_ref, lambda fold: copies[fold].wait())
-    base_copy.wait()
+    for copy in base_copies:
+        copy.wait()
 
 
 def pick_grads_kernel(routes_ref, rows_ref, out_ref):
@@ -250,25 +258,34 @@
     scale_ref[:, 128:] = jnp.broadcast_to(tail, (MAIN, 128))
 
 
-def unfold(blocks, width, rows_ref):
+def against(blocks, weights_ref, rows_ref):
+    width = weights_ref.shape[1]
     part = width // FOLDS
-    count = len(blocks)
+    count = MAIN * len(blocks)
     for k, block in enumerate(blocks):
         rows_ref[MAIN * k : MAIN * (k + 1), :] = block[:, :width]
-    tails = jnp.concatenate([block[:, width:] for block in blocks], axis=0)
-    row = lax.broadcasted_iota(jnp.int32, (TAIL * count, MAIN * count), 0)
-    col = lax.broadcasted_iota(jnp.int32, (TAIL * count, MAIN * count), 1)
+        rows_ref[count + MAIN * k : count + MAIN * (k + 1), :part] = block[:, width:]
+    tails = rows_ref[count:, :part]
+    quarter = lax.broadcasted_iota(jnp.int32, (count, weights_ref.shape[0]), 0) % MAIN // TAIL
+    main = tail = None
     for fold in range(FOLDS):
-        place = as_bf16(col == (row // TAIL) * MAIN + TAIL * fold + row % TAIL)
-        rows_ref[MAIN * count :, fold * part : (fold + 1) * part] = jnp.dot(
-            place, tails, preferred_element_type=F32
-        ).astype(BF16)
+        span = slice(fold * part, (fold + 1) * part)
+        rows = jnp.concatenate([rows_ref[:count, span], tails], axis=0)
+        got = lax.dot_general(rows, weights_ref[:, span], NT, preferred_element_type=F32)
+        here = jnp.where(quarter == fold, got[count:], 0.0)
+        main = got[:count] if fold == 0 else main + got[:count]
+        tail = here if fold == 0 else tail + here
+    tail = tail.reshape(len(blocks), MAIN, -1)
+    turn = TAIL
+    while turn < MAIN:
+        tail = tail + pltpu.roll(tail, turn, 1)
+        turn *= 2
+    return jnp.concatenate([main, tail.reshape(count, -1)], axis=0)
 
 
 def forward_kernel(own, z2, y0, y2, low, high, gu_ref, h_ref, rows_ref):
     blocks = [own, low.at[0], z2, high.at[0], y0, low.at[1], y2, high.at[1]]
-    unfold(blocks, gu_ref.shape[1], rows_ref)
-    h_ref[...] = lax.dot_general(rows_ref[...], gu_ref[...], NT, preferred_element_type=F32)
+    h_ref[...] = against(blocks, gu_ref, rows_ref)
 
 
 def three_parts(value):
@@ -276,57 +293,49 @@
     rest = value - high.astype(F32)
     mid = rest.astype(BF16)
     low = (rest - mid.astype(F32)).astype(BF16)
-    return high, mid, low
+    return [part.astype(F32) for part in (high, mid, low)]
 
 
 def backward_kernel(*refs):
     g0, g2, z_refs, y_refs, yz_refs, down_ref, gu_ref, h_ref, *outs, rows_ref = refs
     near_a, far_a, near_b, far_b = outs
-    width = gu_ref.shape[1]
-    half = width // 2
+    half = gu_ref.shape[1] // 2
     part = half // FOLDS
     units = down_ref.shape[0]
-    slots = rows_ref.shape[0]
-    count = slots // CAP
     blocks = [g0, z_refs.at[0], g2, z_refs.at[1]]
     blocks += [y_refs.at[0], yz_refs.at[0], y_refs.at[1], yz_refs.at[1]]
-    unfold(blocks, width, rows_ref)
-    grad_hidden = lax.dot_general(rows_ref[...], down_ref[...], NT, preferred_element_type=F32)
+    count = MAIN * len(blocks)
+    grad_hidden = against(blocks, down_ref, rows_ref)
     gate = h_ref[:, :units]
     up = h_ref[:, units:]
     sigmoid = 1.0 / (1.0 + jnp.exp(-gate))
     swish = gate * sigmoid
-    weight = jnp.sum(grad_hidden * (swish * up), axis=1, keepdims=True)
     grad_up = (grad_hidden * swish).astype(BF16)
     grad_gate = (grad_hidden * up * sigmoid * (1.0 + gate * (1.0 - sigmoid))).astype(BF16)
     both = jnp.concatenate([grad_gate, grad_up], axis=1)
-    place_a = [(near_a, 0), (near_a, 1), (near_a, 2), (near_a, 3)]
-    place_a += [(far_a, 0), (far_a, 1), (far_a, 2), (far_a, 3)]
-    place_b = [(near_b, 0), (far_b, 0), (near_b, 1), (far_b, 1)]
-    place_b += [(near_b, 2), (far_b, 2), (near_b, 3), (far_b, 3)]
-    back = lax.broadcasted_iota(jnp.int32, (MAIN * count, TAIL * count), 0)
-    col = lax.broadcasted_iota(jnp.int32, (MAIN * count, TAIL * count), 1)
+    place_a = [(ref, k) for ref in (near_a, far_a) for k in range(4)]
+    place_b = [((near_b, far_b)[k % 2], k // 2) for k in range(8)]
+    quarter = lax.broadcasted_iota(jnp.int32, (count, part), 0) % MAIN // TAIL
     for side, places in enumerate((place_a, place_b)):
-        tails = jnp.zeros((MAIN * count, part), F32)
+        tails = None
         for fold in range(FOLDS):
             start = side * half + fold * part
             value = jnp.dot(both, gu_ref[:, start : start + part], preferred_element_type=F32)
-            value = value.astype(BF16)
+            here = jnp.where(quarter == fold, value[count:], 0.0)
+            tails = here if fold == 0 else tails + here
+            value = value[:count].astype(BF16)
             for k, (ref, j) in enumerate(places):
                 ref[j, :, fold * part : (fold + 1) * part] = value[MAIN * k : MAIN * (k + 1), :]
-            place = as_bf16(back == (col // TAIL) * MAIN + TAIL * fold + col % TAIL)
-            tails = tails + jnp.dot(place, value[MAIN * count :, :], preferred_element_type=F32)
         tails = tails.astype(BF16)
         for k, (ref, j) in enumerate(places):
             ref[j, :, half : half + part] = tails[MAIN * k : MAIN * (k + 1), :]
-    lane = lax.broadcasted_iota(jnp.int32, (slots, 128), 1)
-    high, mid, low = (p.astype(F32) for p in three_parts(weight))
-    spread = jnp.where(lane == 0, high, jnp.where(lane == 1, mid, jnp.where(lane == 2, low, 0.0)))
-    shifted = jnp.where(lane == 3, high, jnp.where(lane == 4, mid, jnp.where(lane == 5, low, 0.0)))
-    place = as_bf16(back == (col // TAIL) * MAIN + col % TAIL)
-    tile = spread[: MAIN * count, :] + jnp.dot(
-        place, shifted[MAIN * count :, :].astype(BF16), preferred_element_type=F32
-    )
+    weight = jnp.sum(grad_hidden * (swish * up), axis=1, keepdims=True)
+    lane = lax.broadcasted_iota(jnp.int32, (count, 128), 1)
+    first = lax.broadcasted_iota(jnp.int32, (count, 128), 0) % MAIN < TAIL
+    tile = jnp.zeros((count, 128), F32)
+    for k, piece in enumerate(three_parts(weight)):
+        tile = jnp.where(lane == k, piece[:count], tile)
+        tile = jnp.where((lane == k + 3) & first, piece[count:], tile)
     tile = tile.astype(BF16)
     for k, (ref, j) in enumerate(place_a):
         ref[j, :, half + part :] = tile[MAIN * k : MAIN * (k + 1), :]
@@ -363,9 +372,9 @@
         tile_ref[...] = tile
 
 
-def weight_kernel(routes_ref, own_tile, got_tile, out_ref):
+def weight_kernel(routes_ref, own_tile, got_tile, after_ref, out_ref):
     hit, slot = slot_of_token(routes_ref[...])
-    tile = own_tile[...] + got_tile[...]
+    tile = own_tile[...] + got_tile[...] + after_ref[...]
     lane = lax.broadcasted_iota(jnp.int32, tile.shape, 1)
     main = jnp.sum(jnp.where(lane < 3, tile, 0.0), axis=1, keepdims=True)
     tail = jnp.sum(jnp.where((lane >= 3) & (lane < 6), tile, 0.0), axis=1, keepdims=True)
@@ -378,7 +387,8 @@
     out_ref[...] = jnp.where(hit, value, 0.0)
 
 
-def final_kernel(back_ref, scale_ref, one_ref, two_ref, base_ref, out_ref, done_ref, sems):
+def final_kernel(back_ref, scale_ref, one_ref, two_ref, base_ref, out_ref, end_ref, done_ref, sems):
+    end_ref[...] = jnp.zeros_like(end_ref)
     width = base_ref.shape[1]
     half = width // 2
     part = half // FOLDS
@@ -428,15 +438,14 @@
     routes_t = routes[0].T
     weight_t = route_weight[0].T
     next_routes = passed_along(routes_t, "pp", 1)
-    next_weight = passed_along(weight_t, "pp", 1)
     count, width = saved.shape[1:]
     full = width + width // FOLDS
     half = full // 2
     units = 2 * w_gate.shape[1]
-    slots = SHARDS // 2 * CAP
+    slots = SHARDS // 2 * 2 * MAIN
     hbm = pl.BlockSpec(memory_space=pltpu.HBM)
-
-    next_routes, next_weight = lax.optimization_barrier((next_routes, next_weight))
+    tile = pltpu.VMEM((MAIN, 128), F32)
+
     input_block, near_routes, base = near_call(
         pick_inputs_kernel,
         [
@@ -446,29 +455,27 @@
         ],
         *(pltpu.with_memory_space_constraint(v, pltpu.HBM) for v in (routes_t, saved[0], upstream[0])),
         in_specs=[hbm] * 3,
-        scratch_shapes=[pltpu.VMEM((count, width), BF16), pltpu.SemaphoreType.DMA((FOLDS + 2,))],
+        scratch_shapes=[
+            pltpu.VMEM((count, width), BF16),
+            pltpu.SemaphoreType.DMA((2 * FOLDS + 1,)),
+        ],
         name="pick_inputs",
     )
     grad_block = near_call(
         pick_grads_kernel, pltpu.VMEM((MAIN, full), BF16), next_routes, base, name="pick_grads"
     )
+
     own = (w_gate[0], w_up[0], w_down[0])
     other = from_partner(own, "ep", 0)
     input_block, grad_block, other = lax.optimization_barrier((input_block, grad_block, other))
-    gate_up = jnp.concatenate([own[0], other[0], own[1], other[1]], axis=0)
-    down = jnp.concatenate([own[2], other[2]], axis=0)
-    back, scale = near_call(
-        back_kernel,
-        [pltpu.VMEM((FOLDS, count, 4 * MAIN), BF16), pltpu.VMEM((MAIN, 256), F32)],
-        next_routes,
-        next_weight,
-        name="back_rows",
-    )
 
     grad_z2 = sections_across(grad_block, Z2)
     grad_z0 = sections_across(grad_block, 0)
     input_z2 = across(input_block, Z2)
     input_y0 = across(input_block, Y1)
+    gate_up = jnp.concatenate([own[0], other[0], own[1], other[1]], axis=0)
+    down = jnp.concatenate([own[2], other[2]], axis=0)
+
     grad_z = jnp.stack([grad_z0, grad_z2])
     grad_z1 = across(grad_z, Z1)
     grad_y = across(grad_z, Y1)
@@ -476,8 +483,16 @@
     input_low = across(jnp.stack([input_block, input_y0]), Z1)
     input_high = across(jnp.stack([input_z2, input_y2]), Z1)
     grad_yz1 = across(grad_z1, Y1)
+
+    late_routes, weight_t, _ = lax.optimization_barrier((next_routes, weight_t, grad_z1))
+    back, scale = near_call(
+        back_kernel,
+        [pltpu.VMEM((FOLDS, count, 4 * MAIN), BF16), pltpu.VMEM((MAIN, 256), F32)],
+        late_routes,
+        passed_along(weight_t, "pp", 1),
+        name="back_rows",
+    )
     input_high, back, scale = lax.optimization_barrier((input_high, back, scale))
-
     hidden = near_call(
         forward_kernel,
         pltpu.VMEM((slots, 2 * units), F32),
@@ -517,7 +532,7 @@
     )
     rows_0, rows_2, tile_0, tile_2 = near_call(
         fold_both_kernel,
-        [pltpu.VMEM((MAIN, full), BF16)] * 2 + [pltpu.VMEM((MAIN, 128), F32)] * 2,
+        [pltpu.VMEM((MAIN, full), BF16)] * 2 + [tile] * 2,
         keep_a,
         across(send_a, Z1),
         keep_b,
@@ -526,25 +541,26 @@
     )
     got_2 = sections_across(rows_2, Z2)
     got_0 = sections_across(rows_0, 0)
+    grad_prev, end = near_call(
+        final_kernel,
+        [jax.ShapeDtypeStruct((count, width), BF16), tile],
+        back,
+        scale,
+        got_0,
+        got_2,
+        base,
+        out_specs=[hbm, pl.BlockSpec(memory_space=pltpu.VMEM)],
+        scratch_shapes=[pltpu.VMEM((count, width), BF16), pltpu.SemaphoreType.DMA((FOLDS,))],
+        name="final_rows",
+    )
     weight_out = near_call(
         weight_kernel,
         jax.ShapeDtypeStruct((TOP, count), F32),
         near_routes,
         tile_0,
         across(tile_2, Z2),
+        end,
         name="weight_out",
-    )
-    grad_prev = near_call(
-        final_kernel,
-        jax.ShapeDtypeStruct((count, width), BF16),
-        back,
-        scale,
-        got_0,
-        got_2,
-        base,
-        out_specs=hbm,
-        scratch_shapes=[pltpu.VMEM((count, width), BF16), pltpu.SemaphoreType.DMA((FOLDS,))],
-        name="final_rows",
     )
     return (grad_prev[None], weight_out.T[None])
 

time: 59.8 us -> 55.7 us (0.931)
  waiting for transfers between devices: 29.1 us -> 18 us
  starting transfers between devices: 21.8 us -> 29.8 us
  Pallas kernels: 7.57 us -> 6.69 us
    ppermute x13, waiting for transfers between devices: 21.5 us -> 10.3 us  [across(): return lax.ppermute(value, 'ep', [(i, i ^ bits) for i in range(count)])]
    ppermute x4, starting transfers between devices: 4.14 us -> 9.62 us  [sections_across(): return lax.ppermute(value, ('pp', 'ep'), pairs)]
    ppermute x13, starting transfers between devices: 14 us -> 15.7 us  [across(): return lax.ppermute(value, 'ep', [(i, i ^ bits) for i in range(count)])]
    ppermute x4, waiting for transfers between devices: 5.43 us -> 6.46 us  [sections_across(): return lax.ppermute(value, ('pp', 'ep'), pairs)]
    ppermute x2, waiting for transfers between devices: 2.15 us -> 1.21 us  [passed_along(): lax.ppermute(value, axis, [(i, (i + by) % size) for i in range(size)])]
    ppermute x2, starting transfers between devices: 2.6 us -> 3.49 us  [passed_along(): lax.ppermute(value, axis, [(i, (i + by) % size) for i in range(size)])]
    pallas_call x10, Pallas kernels: 7.57 us -> 6.69 us  [near_call(): pl.pallas_call(kernel, out_shape=out_shape, compiler_params=params, **kwa...]
  transfers between devices with their start and end apart: 22 -> 22, of which waited for: 10 -> 10; matrix products, arithmetic and copies ran while one was open for 0% -> 0% of each run, Pallas kernels for 7% -> 8%
where the time goes in v4:
time: 55.7 us; the launch traced here: 55.6 us
  starting transfers between devices  29.8 us (54%)
  waiting for transfers between devices  18 us (32%)
  Pallas kernels  6.69 us (12%)
  between operations  0.79 us (1%)
    ppermute x13, starting transfers between devices, across(): return lax.ppermute(value, 'ep', [(i, i ^ bits) for i in range(count)])  15.7 us
    ppermute x13, waiting for transfers between devices, across(): return lax.ppermute(value, 'ep', [(i, i ^ bits) for i in range(count)])  10.3 us
    ppermute x4, starting transfers between devices, sections_across(): return lax.ppermute(value, ('pp', 'ep'), pairs)  9.62 us
    pallas_call x10, Pallas kernels, near_call(): pl.pallas_call(kernel, out_shape=out_shape, compiler_params=params, **kwa...  6.69 us
    ppermute x4, waiting for transfers between devices, sections_across(): return lax.ppermute(value, ('pp', 'ep'), pairs)  6.46 us
    ppermute x2, starting transfers between devices, passed_along(): lax.ppermute(value, axis, [(i, (i + by) % size) for i in range(size)])  3.49 us
    ppermute x2, waiting for transfers between devices, passed_along(): lax.ppermute(value, axis, [(i, (i + by) % size) for i in range(size)])  1.21 us
  transfers between devices with their start and end apart: 22, of which 10 were waited for; matrix products, arithmetic and copies ran while one was open for 0% of the time, Pallas kernels for 8%

profile of v4, /device:TPU:0, one launch (start us, length us, event | category | flops | bytes accessed | tf_op | source)
XLA Modules:
  0.0 55.6 jit_solution(2479993527666049675)
XLA Ops:
  0.7 0.5 collective-permute-start.1
  1.2 0.4 collective-permute-start.3
  1.7 2.6 %collective-permute-start = (s32[8,128]{1,0:T(8,128)}, s32[8,128]{1,0:T(8,128)S(1)}, u32[]{:S(2)}, u32[]{:S(2)}) collective-permute-start(s32[8,128]{1,0:T(8,128)} %bitcast.35), channel_id=1, source_target_pairs={{0,16},{16,0},{1,17},{17,1},{2,18},{18,2},{3,19},{19,3},{4,20},{20... | collective-permute-start | bytes 12296 | tf_op jit(solution)/shard_map/ppermute | solution.py:32
  4.2 1.7 %pick_inputs.1 = (bf16[8,5120]{1,0:T(8,128)(2,1)S(1)}, s32[8,128]{1,0:T(8,128)S(1)}, bf16[128,4096]{1,0:T(8,128)(2,1)S(1)}) custom-call(s32[8,128]{1,0:T(8,128)} %bitcast.36, bf16[128,4096]{1,0:T(8,128)(2,1)} %bitcast.27, bf16[128,4096]{1,0:T(8,128)(2,1)} %bitcast.28), custom_call_target="tpu_custom_call" | custom-call | tf_op jit(solution)/shard_map/pick_inputs/pallas_call | solution.py:153
  6.5 2.1 %collective-permute-start.7 = (bf16[8,5120]{1,0:T(8,128)(2,1)S(1)}, bf16[8,5120]{1,0:T(8,128)(2,1)S(1)}, u32[]{:S(2)}, u32[]{:S(2)}) collective-permute-start(bf16[8,5120]{1,0:T(8,128)(2,1)S(1)} %pick_grads.1), channel_id=1, source_target_pairs={{0,16},{1,17},{2,18},{3,19},{4,20},{5,21},{6,22},{7,23},{8,24},{9,... | collective-permute-start | bytes 245768 | tf_op jit(solution)/shard_map/ppermute | solution.py:431
  8.5 2.6 %collective-permute-start.8 = (bf16[8,5120]{1,0:T(8,128)(2,1)S(1)}, bf16[8,5120]{1,0:T(8,128)(2,1)S(1)}, u32[]{:S(2)}, u32[]{:S(2)}) collective-permute-start(bf16[8,5120]{1,0:T(8,128)(2,1)S(1)} %pick_grads.1), channel_id=1, source_target_pairs={{0,24},{1,25},{2,26},{3,27},{4,28},{5,29},{6,30},{7,31},{8,16},{9,... | collective-permute-start | bytes 245768 | tf_op jit(solution)/shard_map/ppermute | solution.py:431
  11.1 1.8 %collective-permute-start.13 = (bf16[8,5120]{1,0:T(8,128)(2,1)S(1)}, bf16[8,5120]{1,0:T(8,128)(2,1)S(1)}, u32[]{:S(2)}, u32[]{:S(2)}) collective-permute-start(bf16[8,5120]{1,0:T(8,128)(2,1)S(1)} %get-tuple-element.33.own), channel_id=1, source_target_pairs={{0,2},{1,3},{2,0},{3,1},{4,6},{5,7},{6,4},{7,5},{8,10},{9,11},{10,... | collective-permute-start | bytes 245768 | tf_op jit(solution)/shard_map/ppermute | solution.py:425
  13.1 4.0 %collective-permute-done.8.refs_1_ = bf16[8,5120]{1,0:T(8,128)(2,1)S(1)} collective-permute-done((bf16[8,5120]{1,0:T(8,128)(2,1)S(1)}, bf16[8,5120]{1,0:T(8,128)(2,1)S(1)}, u32[]{:S(2)}, u32[]{:S(2)}) %collective-permute-start.8) | collective-permute-done | bytes 81952 | tf_op jit(solution)/shard_map/ppermute | solution.py:431
  17.4 1.5 %collective-permute-start.11 = (bf16[2,8,5120]{2,1,0:T(8,128)(2,1)S(1)}, bf16[2,8,5120]{2,1,0:T(8,128)(2,1)S(1)}, u32[]{:S(2)}, u32[]{:S(2)}) collective-permute-start(bf16[2,8,5120]{2,1,0:T(8,128)(2,1)S(1)} %pad_maximum_fusion.3), channel_id=1, source_target_pairs={{0,2},{1,3},{2,0},{3,1},{4,6},{5,7},{6,4},{7,5},{8,10},{9,11},{10,... | collective-permute-start | bytes 491528 | tf_op jit(solution)/shard_map/ppermute | solution.py:425
  18.9 1.1 %collective-permute-start.5 = (bf16[8,5120]{1,0:T(8,128)(2,1)S(1)}, bf16[8,5120]{1,0:T(8,128)(2,1)S(1)}, u32[]{:S(2)}, u32[]{:S(2)}) collective-permute-start(bf16[8,5120]{1,0:T(8,128)(2,1)S(1)} %collective-permute-done.4.z2), channel_id=1, source_target_pairs={{0,2},{1,3},{2,0},{3,1},{4,6},{5,7},{6,4},{7,5},{8,10},{9,11},{10,... | collective-permute-start | bytes 245768 | tf_op jit(solution)/shard_map/ppermute | solution.py:425
  20.0 1.4 %collective-permute-start.14 = (bf16[2,8,5120]{2,1,0:T(8,128)(2,1)S(1)}, bf16[2,8,5120]{2,1,0:T(8,128)(2,1)S(1)}, u32[]{:S(2)}, u32[]{:S(2)}) collective-permute-start(bf16[2,8,5120]{2,1,0:T(8,128)(2,1)S(1)} %pad_maximum_fusion.4), channel_id=1, source_target_pairs={{0,4},{1,5},{2,6},{3,7},{4,0},{5,1},{6,2},{7,3},{8,12},{9,13},{10,... | collective-permute-start | bytes 491528 | tf_op jit(solution)/shard_map/ppermute | solution.py:425
  21.4 3.5 %collective-permute-done.5.y2 = bf16[8,5120]{1,0:T(8,128)(2,1)S(1)} collective-permute-done((bf16[8,5120]{1,0:T(8,128)(2,1)S(1)}, bf16[8,5120]{1,0:T(8,128)(2,1)S(1)}, u32[]{:S(2)}, u32[]{:S(2)}) %collective-permute-start.5) | collective-permute-done | bytes 81952 | tf_op jit(solution)/shard_map/ppermute | solution.py:425
  24.9 0.7 %collective-permute-start.6 = (bf16[2,8,5120]{2,1,0:T(8,128)(2,1)S(1)}, bf16[2,8,5120]{2,1,0:T(8,128)(2,1)S(1)}, u32[]{:S(2)}, u32[]{:S(2)}) collective-permute-start(bf16[2,8,5120]{2,1,0:T(8,128)(2,1)S(1)} %pad_maximum_fusion.2), channel_id=1, source_target_pairs={{0,4},{1,5},{2,6},{3,7},{4,0},{5,1},{6,2},{7,3},{8,12},{9,13},{10,... | collective-permute-start | bytes 491528 | tf_op jit(solution)/shard_map/ppermute | solution.py:425
  25.6 0.9 %collective-permute-start.10 = (f32[8,128]{1,0:T(8,128)S(1)}, f32[8,128]{1,0:T(8,128)S(1)}, u32[]{:S(2)}, u32[]{:S(2)}) collective-permute-start(f32[8,128]{1,0:T(8,128)S(1)} %bitcast.39), channel_id=1, source_target_pairs={{0,16},{16,0},{1,17},{17,1},{2,18},{18,2},{3,19},{19,3},{4,20},{20... | collective-permute-start | bytes 12296 | tf_op jit(solution)/shard_map/ppermute | solution.py:32
  26.5 1.5 %collective-permute-start.12 = (bf16[2,8,5120]{2,1,0:T(8,128)(2,1)S(1)}, bf16[2,8,5120]{2,1,0:T(8,128)(2,1)S(1)}, u32[]{:S(2)}, u32[]{:S(2)}) collective-permute-start(bf16[2,8,5120]{2,1,0:T(8,128)(2,1)S(1)} %collective-permute-done.9.refs_2_), channel_id=1, source_target_pairs={{0,2},{1,3},{2,0},{3,1},{4,6},{5,7},{6,4},{7,5},{8,10},{9,11},{10,... | collective-permute-start | bytes 491528 | tf_op jit(solution)/shard_map/ppermute | solution.py:425
  28.1 1.1 %collective-permute-done.10.weight_ref = f32[8,128]{1,0:T(8,128)S(1)} collective-permute-done((f32[8,128]{1,0:T(8,128)S(1)}, f32[8,128]{1,0:T(8,128)S(1)}, u32[]{:S(2)}, u32[]{:S(2)}) %collective-permute-start.10) | collective-permute-done | bytes 4128 | tf_op jit(solution)/shard_map/ppermute | solution.py:32
  29.5 0.7 %collective-permute-done.6.high = bf16[2,8,5120]{2,1,0:T(8,128)(2,1)S(1)} collective-permute-done((bf16[2,8,5120]{2,1,0:T(8,128)(2,1)S(1)}, bf16[2,8,5120]{2,1,0:T(8,128)(2,1)S(1)}, u32[]{:S(2)}, u32[]{:S(2)}) %collective-permute-start.6) | collective-permute-done | bytes 163872 | tf_op jit(solution)/shard_map/ppermute | solution.py:425
  30.3 0.8 %expert_forward.1.refs_7_ = f32[128,256]{1,0:T(8,128)S(1)} custom-call(bf16[8,5120]{1,0:T(8,128)(2,1)S(1)} %get-tuple-element.33.own, bf16[8,5120]{1,0:T(8,128)(2,1)S(1)} %collective-permute-done.4.z2, bf16[8,5120]{1,0:T(8,128)(2,1)S(1)} %collective-permute-done.13.y0, bf16[8,5120]{1,0:T(8,128)(2,1)S(1)} %collective-permute-done.5.y2, ...), custom_call_target="tpu_custom_call" | custom-call | tf_op jit(solution)/shard_map/expert_forward/pallas_call | solution.py:153
  31.1 0.7 %collective-permute-done.12.refs_4_ = bf16[2,8,5120]{2,1,0:T(8,128)(2,1)S(1)} collective-permute-done((bf16[2,8,5120]{2,1,0:T(8,128)(2,1)S(1)}, bf16[2,8,5120]{2,1,0:T(8,128)(2,1)S(1)}, u32[]{:S(2)}, u32[]{:S(2)}) %collective-permute-start.12) | collective-permute-done | bytes 163872 | tf_op jit(solution)/shard_map/ppermute | solution.py:425
  31.8 1.3 %expert_backward.1 = (bf16[4,8,2688]{2,1,0:T(8,128)(2,1)S(1)}, bf16[4,8,2688]{2,1,0:T(8,128)(2,1)S(1)}, bf16[4,8,2560]{2,1,0:T(8,128)(2,1)S(1)}, bf16[4,8,2560]{2,1,0:T(8,128)(2,1)S(1)}) custom-call(bf16[8,5120]{1,0:T(8,128)(2,1)S(1)} %collective-permute-done.7.refs_0_, bf16[8,5120]{1,0:T(8,128)(2,1)S(1)} %collective-permute-done.8.refs_1_, ...), custom_call_target="tpu_custom_call" | custom-call | tf_op jit(solution)/shard_map/expert_backward/pallas_call | solution.py:153
  33.1 1.6 %collective-permute-start.15 = (bf16[4,8,2688]{2,1,0:T(8,128)(2,1)S(1)}, bf16[4,8,2688]{2,1,0:T(8,128)(2,1)S(1)}, u32[]{:S(2)}, u32[]{:S(2)}) collective-permute-start(bf16[4,8,2688]{2,1,0:T(8,128)(2,1)S(1)} %get-tuple-element.46), channel_id=1, source_target_pairs={{0,2},{1,3},{2,0},{3,1},{4,6},{5,7},{6,4},{7,5},{8,10},{9,11},{10,... | collective-permute-start | bytes 516104 | tf_op jit(solution)/shard_map/ppermute | solution.py:425
  34.7 1.7 %collective-permute-start.17 = (bf16[4,8,2560]{2,1,0:T(8,128)(2,1)S(1)}, bf16[4,8,2560]{2,1,0:T(8,128)(2,1)S(1)}, u32[]{:S(2)}, u32[]{:S(2)}) collective-permute-start(bf16[4,8,2560]{2,1,0:T(8,128)(2,1)S(1)} %get-tuple-element.50), channel_id=1, source_target_pairs={{0,4},{1,5},{2,6},{3,7},{4,0},{5,1},{6,2},{7,3},{8,12},{9,13},{10,... | collective-permute-start | bytes 491528 | tf_op jit(solution)/shard_map/ppermute | solution.py:425
  36.4 2.2 %collective-permute-done.15.got_ref = bf16[4,8,2688]{2,1,0:T(8,128)(2,1)S(1)} collective-permute-done((bf16[4,8,2688]{2,1,0:T(8,128)(2,1)S(1)}, bf16[4,8,2688]{2,1,0:T(8,128)(2,1)S(1)}, u32[]{:S(2)}, u32[]{:S(2)}) %collective-permute-start.15) | collective-permute-done | bytes 172064 | tf_op jit(solution)/shard_map/ppermute | solution.py:425
  38.7 1.9 %collective-permute-start.16 = (bf16[2,8,2816]{2,1,0:T(8,128)(2,1)S(1)}, bf16[2,8,2816]{2,1,0:T(8,128)(2,1)S(1)}, u32[]{:S(2)}, u32[]{:S(2)}) collective-permute-start(bf16[2,8,2816]{2,1,0:T(8,128)(2,1)S(1)} %get-tuple-element.48), channel_id=1, source_target_pairs={{0,4},{1,5},{2,6},{3,7},{4,0},{5,1},{6,2},{7,3},{8,12},{9,13},{10,... | collective-permute-start | bytes 270344 | tf_op jit(solution)/shard_map/ppermute | solution.py:425
  40.6 2.3 %collective-permute-start.18 = (bf16[2,8,2560]{2,1,0:T(8,128)(2,1)S(1)}, bf16[2,8,2560]{2,1,0:T(8,128)(2,1)S(1)}, u32[]{:S(2)}, u32[]{:S(2)}) collective-permute-start(bf16[2,8,2560]{2,1,0:T(8,128)(2,1)S(1)} %get-tuple-element.52), channel_id=1, source_target_pairs={{0,2},{1,3},{2,0},{3,1},{4,6},{5,7},{6,4},{7,5},{8,10},{9,11},{10,... | collective-permute-start | bytes 245768 | tf_op jit(solution)/shard_map/ppermute | solution.py:425
  42.9 2.4 %collective-permute-done.18.got_b = bf16[2,8,2560]{2,1,0:T(8,128)(2,1)S(1)} collective-permute-done((bf16[2,8,2560]{2,1,0:T(8,128)(2,1)S(1)}, bf16[2,8,2560]{2,1,0:T(8,128)(2,1)S(1)}, u32[]{:S(2)}, u32[]{:S(2)}) %collective-permute-start.18) | collective-permute-done | bytes 81952 | tf_op jit(solution)/shard_map/ppermute | solution.py:425
  45.4 0.9 %collective-permute-start.19 = (bf16[8,5120]{1,0:T(8,128)(2,1)S(1)}, bf16[8,5120]{1,0:T(8,128)(2,1)S(1)}, u32[]{:S(2)}, u32[]{:S(2)}) collective-permute-start(bf16[8,5120]{1,0:T(8,128)(2,1)S(1)} %get-tuple-element.53), channel_id=1, source_target_pairs={{0,16},{1,17},{2,18},{3,19},{4,20},{5,21},{6,22},{7,23},{8,24},{9,... | collective-permute-start | bytes 245768 | tf_op jit(solution)/shard_map/ppermute | solution.py:431
  46.3 4.0 %collective-permute-start.20 = (bf16[8,5120]{1,0:T(8,128)(2,1)S(1)}, bf16[8,5120]{1,0:T(8,128)(2,1)S(1)}, u32[]{:S(2)}, u32[]{:S(2)}) collective-permute-start(bf16[8,5120]{1,0:T(8,128)(2,1)S(1)} %get-tuple-element.54), channel_id=1, source_target_pairs={{0,24},{1,25},{2,26},{3,27},{4,28},{5,29},{6,30},{7,31},{8,16},{9,... | collective-permute-start | bytes 245768 | tf_op jit(solution)/shard_map/ppermute | solution.py:431
  50.4 2.4 %collective-permute-done.20.two_ref = bf16[8,5120]{1,0:T(8,128)(2,1)S(1)} collective-permute-done((bf16[8,5120]{1,0:T(8,128)(2,1)S(1)}, bf16[8,5120]{1,0:T(8,128)(2,1)S(1)}, u32[]{:S(2)}, u32[]{:S(2)}) %collective-permute-start.20) | collective-permute-done | bytes 81952 | tf_op jit(solution)/shard_map/ppermute | solution.py:431
  52.8 1.3 %final_rows.1 = (bf16[128,4096]{1,0:T(8,128)(2,1)}, f32[8,128]{1,0:T(8,128)S(1)}) custom-call(bf16[4,128,32]{2,1,0:T(8,128)(2,1)S(1)} %get-tuple-element.39.back_ref, f32[8,256]{1,0:T(8,128)S(1)} %get-tuple-element.40.scale_ref, bf16[8,5120]{1,0:T(8,128)(2,1)S(1)} %collective-permute-done.19.one_ref, bf16[8,5120]{1,0:T(8,128)(2,1)S(1)} %collective-permute-done.20.two_ref, ...), custom_call_target="tpu_custom_call" | custom-call | tf_op jit(solution)/shard_map/final_rows/pallas_call | solution.py:153
  54.1 0.8 %collective-permute-done.21.got_tile = f32[8,128]{1,0:T(8,128)S(1)} collective-permute-done((f32[8,128]{1,0:T(8,128)S(1)}, f32[8,128]{1,0:T(8,128)S(1)}, u32[]{:S(2)}, u32[]{:S(2)}) %collective-permute-start.21) | collective-permute-done | bytes 4128 | tf_op jit(solution)/shard_map/ppermute | solution.py:425
  54.9 0.7 %weight_out.1 = f32[8,128]{1,0:T(8,128)} custom-call(s32[8,128]{1,0:T(8,128)S(1)} %get-tuple-element.56.routes_ref, f32[8,128]{1,0:T(8,128)S(1)} %get-tuple-element.57.own_tile, f32[8,128]{1,0:T(8,128)S(1)} %collective-permute-done.21.got_tile, f32[8,128]{1,0:T(8,128)S(1)} %get-tuple-element.59.after_ref), custom_call_target="tpu_custom_call" | custom-call | tf_op jit(solution)/shard_map/weight_out/pallas_call | solution.py:153
  (35 shorter events, 1.6 us)
Async XLA Ops:
  0.6 12.3 %copy-start.2 = (bf16[1,64,4096]{2,1,0:T(8,128)(2,1)S(1)}, bf16[1,64,4096]{2,1,0:T(8,128)(2,1)}, u32[]{:S(2)}) copy-start(bf16[1,64,4096]{2,1,0:T(8,128)(2,1)} %param.11) | copy-start | bytes 1572868
  0.6 12.3 %copy-start.1 = (bf16[1,64,4096]{2,1,0:T(8,128)(2,1)S(1)}, bf16[1,64,4096]{2,1,0:T(8,128)(2,1)}, u32[]{:S(2)}) copy-start(bf16[1,64,4096]{2,1,0:T(8,128)(2,1)} %param.12) | copy-start | bytes 1572868
  0.7 5.7 %collective-permute-start.1 = (bf16[64,4096]{1,0:T(8,128)(2,1)}, bf16[64,4096]{1,0:T(8,128)(2,1)S(1)}, u32[]{:S(2)}, u32[]{:S(2)}) collective-permute-start(bf16[64,4096]{1,0:T(8,128)(2,1)} %bitcast.33), channel_id=1, source_target_pairs={{0,1},{1,0},{2,3},{3,2},{4,5},{5,4},{6,7},{7,6},{8,9},{9,8},{10,11... | collective-permute-start | bytes 1572872 | tf_op jit(solution)/shard_map/ppermute | solution.py:27
  1.2 5.2 %collective-permute-start.2 = (bf16[64,4096]{1,0:T(8,128)(2,1)}, bf16[64,4096]{1,0:T(8,128)(2,1)S(1)}, u32[]{:S(2)}, u32[]{:S(2)}) collective-permute-start(bf16[64,4096]{1,0:T(8,128)(2,1)} %bitcast.31), channel_id=1, source_target_pairs={{0,1},{1,0},{2,3},{3,2},{4,5},{5,4},{6,7},{7,6},{8,9},{9,8},{10,11... | collective-permute-start | bytes 1572872 | tf_op jit(solution)/shard_map/ppermute | solution.py:27
  1.2 5.2 %collective-permute-start.3 = (bf16[64,4096]{1,0:T(8,128)(2,1)}, bf16[64,4096]{1,0:T(8,128)(2,1)S(1)}, u32[]{:S(2)}, u32[]{:S(2)}) collective-permute-start(bf16[64,4096]{1,0:T(8,128)(2,1)} %bitcast.29), channel_id=1, source_target_pairs={{0,1},{1,0},{2,3},{3,2},{4,5},{5,4},{6,7},{7,6},{8,9},{9,8},{10,11... | collective-permute-start | bytes 1572872 | tf_op jit(solution)/shard_map/ppermute | solution.py:27
  1.7 4.4 %collective-permute-start = (s32[8,128]{1,0:T(8,128)}, s32[8,128]{1,0:T(8,128)S(1)}, u32[]{:S(2)}, u32[]{:S(2)}) collective-permute-start(s32[8,128]{1,0:T(8,128)} %bitcast.35), channel_id=1, source_target_pairs={{0,16},{16,0},{1,17},{17,1},{2,18},{18,2},{3,19},{19,3},{4,20},{20... | collective-permute-start | bytes 12296 | tf_op jit(solution)/shard_map/ppermute | solution.py:32
  6.4 19.1 %copy-start.3 = (f32[1,128,8]{1,2,0:T(8,128)S(1)}, f32[1,128,8]{1,2,0:T(8,128)}, u32[]{:S(2)}) copy-start(f32[1,128,8]{1,2,0:T(8,128)} %param.10) | copy-start | bytes 12292
  6.4 21.6 %copy-start = (bf16[1,64,4096]{2,1,0:T(8,128)(2,1)S(1)}, bf16[1,64,4096]{2,1,0:T(8,128)(2,1)}, u32[]{:S(2)}) copy-start(bf16[1,64,4096]{2,1,0:T(8,128)(2,1)} %param.13) | copy-start | bytes 1572868
  6.5 6.7 %collective-permute-start.7 = (bf16[8,5120]{1,0:T(8,128)(2,1)S(1)}, bf16[8,5120]{1,0:T(8,128)(2,1)S(1)}, u32[]{:S(2)}, u32[]{:S(2)}) collective-permute-start(bf16[8,5120]{1,0:T(8,128)(2,1)S(1)} %pick_grads.1), channel_id=1, source_target_pairs={{0,16},{1,17},{2,18},{3,19},{4,20},{5,21},{6,22},{7,23},{8,24},{9,... | collective-permute-start | bytes 245768 | tf_op jit(solution)/shard_map/ppermute | solution.py:431
  8.5 8.6 %collective-permute-start.8 = (bf16[8,5120]{1,0:T(8,128)(2,1)S(1)}, bf16[8,5120]{1,0:T(8,128)(2,1)S(1)}, u32[]{:S(2)}, u32[]{:S(2)}) collective-permute-start(bf16[8,5120]{1,0:T(8,128)(2,1)S(1)} %pick_grads.1), channel_id=1, source_target_pairs={{0,24},{1,25},{2,26},{3,27},{4,28},{5,29},{6,30},{7,31},{8,16},{9,... | collective-permute-start | bytes 245768 | tf_op jit(solution)/shard_map/ppermute | solution.py:431
  11.1 7.8 %collective-permute-start.4 = (bf16[8,5120]{1,0:T(8,128)(2,1)S(1)}, bf16[8,5120]{1,0:T(8,128)(2,1)S(1)}, u32[]{:S(2)}, u32[]{:S(2)}) collective-permute-start(bf16[8,5120]{1,0:T(8,128)(2,1)S(1)} %get-tuple-element.33.own), channel_id=1, source_target_pairs={{0,8},{1,9},{2,10},{3,11},{4,12},{5,13},{6,14},{7,15},{8,0},{9,1},... | collective-permute-start | bytes 245768 | tf_op jit(solution)/shard_map/ppermute | solution.py:425
  11.1 8.8 %collective-permute-start.13 = (bf16[8,5120]{1,0:T(8,128)(2,1)S(1)}, bf16[8,5120]{1,0:T(8,128)(2,1)S(1)}, u32[]{:S(2)}, u32[]{:S(2)}) collective-permute-start(bf16[8,5120]{1,0:T(8,128)(2,1)S(1)} %get-tuple-element.33.own), channel_id=1, source_target_pairs={{0,2},{1,3},{2,0},{3,1},{4,6},{5,7},{6,4},{7,5},{8,10},{9,11},{10,... | collective-permute-start | bytes 245768 | tf_op jit(solution)/shard_map/ppermute | solution.py:425
  17.2 8.4 %collective-permute-start.9 = (bf16[2,8,5120]{2,1,0:T(8,128)(2,1)S(1)}, bf16[2,8,5120]{2,1,0:T(8,128)(2,1)S(1)}, u32[]{:S(2)}, u32[]{:S(2)}) collective-permute-start(bf16[2,8,5120]{2,1,0:T(8,128)(2,1)S(1)} %pad_maximum_fusion.3), channel_id=1, source_target_pairs={{0,4},{1,5},{2,6},{3,7},{4,0},{5,1},{6,2},{7,3},{8,12},{9,13},{10,... | collective-permute-start | bytes 491528 | tf_op jit(solution)/shard_map/ppermute | solution.py:425
  17.4 13.8 %collective-permute-start.11 = (bf16[2,8,5120]{2,1,0:T(8,128)(2,1)S(1)}, bf16[2,8,5120]{2,1,0:T(8,128)(2,1)S(1)}, u32[]{:S(2)}, u32[]{:S(2)}) collective-permute-start(bf16[2,8,5120]{2,1,0:T(8,128)(2,1)S(1)} %pad_maximum_fusion.3), channel_id=1, source_target_pairs={{0,2},{1,3},{2,0},{3,1},{4,6},{5,7},{6,4},{7,5},{8,10},{9,11},{10,... | collective-permute-start | bytes 491528 | tf_op jit(solution)/shard_map/ppermute | solution.py:425
  18.9 6.0 %collective-permute-start.5 = (bf16[8,5120]{1,0:T(8,128)(2,1)S(1)}, bf16[8,5120]{1,0:T(8,128)(2,1)S(1)}, u32[]{:S(2)}, u32[]{:S(2)}) collective-permute-start(bf16[8,5120]{1,0:T(8,128)(2,1)S(1)} %collective-permute-done.4.z2), channel_id=1, source_target_pairs={{0,2},{1,3},{2,0},{3,1},{4,6},{5,7},{6,4},{7,5},{8,10},{9,11},{10,... | collective-permute-start | bytes 245768 | tf_op jit(solution)/shard_map/ppermute | solution.py:425
  20.0 10.3 %collective-permute-start.14 = (bf16[2,8,5120]{2,1,0:T(8,128)(2,1)S(1)}, bf16[2,8,5120]{2,1,0:T(8,128)(2,1)S(1)}, u32[]{:S(2)}, u32[]{:S(2)}) collective-permute-start(bf16[2,8,5120]{2,1,0:T(8,128)(2,1)S(1)} %pad_maximum_fusion.4), channel_id=1, source_target_pairs={{0,4},{1,5},{2,6},{3,7},{4,0},{5,1},{6,2},{7,3},{8,12},{9,13},{10,... | collective-permute-start | bytes 491528 | tf_op jit(solution)/shard_map/ppermute | solution.py:425
  24.9 5.4 %collective-permute-start.6 = (bf16[2,8,5120]{2,1,0:T(8,128)(2,1)S(1)}, bf16[2,8,5120]{2,1,0:T(8,128)(2,1)S(1)}, u32[]{:S(2)}, u32[]{:S(2)}) collective-permute-start(bf16[2,8,5120]{2,1,0:T(8,128)(2,1)S(1)} %pad_maximum_fusion.2), channel_id=1, source_target_pairs={{0,4},{1,5},{2,6},{3,7},{4,0},{5,1},{6,2},{7,3},{8,12},{9,13},{10,... | collective-permute-start | bytes 491528 | tf_op jit(solution)/shard_map/ppermute | solution.py:425
  25.6 3.6 %collective-permute-start.10 = (f32[8,128]{1,0:T(8,128)S(1)}, f32[8,128]{1,0:T(8,128)S(1)}, u32[]{:S(2)}, u32[]{:S(2)}) collective-permute-start(f32[8,128]{1,0:T(8,128)S(1)} %bitcast.39), channel_id=1, source_target_pairs={{0,16},{16,0},{1,17},{17,1},{2,18},{18,2},{3,19},{19,3},{4,20},{20... | collective-permute-start | bytes 12296 | tf_op jit(solution)/shard_map/ppermute | solution.py:32
  26.5 5.3 %collective-permute-start.12 = (bf16[2,8,5120]{2,1,0:T(8,128)(2,1)S(1)}, bf16[2,8,5120]{2,1,0:T(8,128)(2,1)S(1)}, u32[]{:S(2)}, u32[]{:S(2)}) collective-permute-start(bf16[2,8,5120]{2,1,0:T(8,128)(2,1)S(1)} %collective-permute-done.9.refs_2_), channel_id=1, source_target_pairs={{0,2},{1,3},{2,0},{3,1},{4,6},{5,7},{6,4},{7,5},{8,10},{9,11},{10,... | collective-permute-start | bytes 491528 | tf_op jit(solution)/shard_map/ppermute | solution.py:425
  33.1 5.5 %collective-permute-start.15 = (bf16[4,8,2688]{2,1,0:T(8,128)(2,1)S(1)}, bf16[4,8,2688]{2,1,0:T(8,128)(2,1)S(1)}, u32[]{:S(2)}, u32[]{:S(2)}) collective-permute-start(bf16[4,8,2688]{2,1,0:T(8,128)(2,1)S(1)} %get-tuple-element.46), channel_id=1, source_target_pairs={{0,2},{1,3},{2,0},{3,1},{4,6},{5,7},{6,4},{7,5},{8,10},{9,11},{10,... | collective-permute-start | bytes 516104 | tf_op jit(solution)/shard_map/ppermute | solution.py:425
  34.7 5.8 %collective-permute-start.17 = (bf16[4,8,2560]{2,1,0:T(8,128)(2,1)S(1)}, bf16[4,8,2560]{2,1,0:T(8,128)(2,1)S(1)}, u32[]{:S(2)}, u32[]{:S(2)}) collective-permute-start(bf16[4,8,2560]{2,1,0:T(8,128)(2,1)S(1)} %get-tuple-element.50), channel_id=1, source_target_pairs={{0,4},{1,5},{2,6},{3,7},{4,0},{5,1},{6,2},{7,3},{8,12},{9,13},{10,... | collective-permute-start | bytes 491528 | tf_op jit(solution)/shard_map/ppermute | solution.py:425
  38.7 6.7 %collective-permute-start.16 = (bf16[2,8,2816]{2,1,0:T(8,128)(2,1)S(1)}, bf16[2,8,2816]{2,1,0:T(8,128)(2,1)S(1)}, u32[]{:S(2)}, u32[]{:S(2)}) collective-permute-start(bf16[2,8,2816]{2,1,0:T(8,128)(2,1)S(1)} %get-tuple-element.48), channel_id=1, source_target_pairs={{0,4},{1,5},{2,6},{3,7},{4,0},{5,1},{6,2},{7,3},{8,12},{9,13},{10,... | collective-permute-start | bytes 270344 | tf_op jit(solution)/shard_map/ppermute | solution.py:425
  40.6 4.8 %collective-permute-start.18 = (bf16[2,8,2560]{2,1,0:T(8,128)(2,1)S(1)}, bf16[2,8,2560]{2,1,0:T(8,128)(2,1)S(1)}, u32[]{:S(2)}, u32[]{:S(2)}) collective-permute-start(bf16[2,8,2560]{2,1,0:T(8,128)(2,1)S(1)} %get-tuple-element.52), channel_id=1, source_target_pairs={{0,2},{1,3},{2,0},{3,1},{4,6},{5,7},{6,4},{7,5},{8,10},{9,11},{10,... | collective-permute-start | bytes 245768 | tf_op jit(solution)/shard_map/ppermute | solution.py:425
  45.4 5.0 %collective-permute-start.19 = (bf16[8,5120]{1,0:T(8,128)(2,1)S(1)}, bf16[8,5120]{1,0:T(8,128)(2,1)S(1)}, u32[]{:S(2)}, u32[]{:S(2)}) collective-permute-start(bf16[8,5120]{1,0:T(8,128)(2,1)S(1)} %get-tuple-element.53), channel_id=1, source_target_pairs={{0,16},{1,17},{2,18},{3,19},{4,20},{5,21},{6,22},{7,23},{8,24},{9,... | collective-permute-start | bytes 245768 | tf_op jit(solution)/shard_map/ppermute | solution.py:431
  46.3 6.5 %collective-permute-start.20 = (bf16[8,5120]{1,0:T(8,128)(2,1)S(1)}, bf16[8,5120]{1,0:T(8,128)(2,1)S(1)}, u32[]{:S(2)}, u32[]{:S(2)}) collective-permute-start(bf16[8,5120]{1,0:T(8,128)(2,1)S(1)} %get-tuple-element.54), channel_id=1, source_target_pairs={{0,24},{1,25},{2,26},{3,27},{4,28},{5,29},{6,30},{7,31},{8,16},{9,... | collective-permute-start | bytes 245768 | tf_op jit(solution)/shard_map/ppermute | solution.py:431
  50.3 4.5 %collective-permute-start.21 = (f32[8,128]{1,0:T(8,128)S(1)}, f32[8,128]{1,0:T(8,128)S(1)}, u32[]{:S(2)}, u32[]{:S(2)}) collective-permute-start(f32[8,128]{1,0:T(8,128)S(1)} %get-tuple-element.58), channel_id=1, source_target_pairs={{0,8},{1,9},{2,10},{3,11},{4,12},{5,13},{6,14},{7,15},{8,0},{9,1},... | collective-permute-start | bytes 12296 | tf_op jit(solution)/shard_map/ppermute | solution.py:425

commit v5 on v4

--- a/solution.py
+++ b/solution.py
@@ -187,6 +187,14 @@
     return jnp.concatenate(picks, axis=0).astype(BF16)
 
 
+def three_parts(value):
+    high = value.astype(BF16)
+    rest = value - high.astype(F32)
+    mid = rest.astype(BF16)
+    low = (rest - mid.astype(F32)).astype(BF16)
+    return [part.astype(F32) for part in (high, mid, low)]
+
+
 def pick_into(slot, rows_ref, out_ref, before=lambda fold: None):
     width = rows_ref.shape[1]
     part = width // FOLDS
@@ -200,10 +208,14 @@
     out_ref[:, width:] = tail.astype(BF16)
 
 
-def pick_inputs_kernel(routes_in, rows_in, base_in, out_ref, routes_ref, base_ref, rows_ref, sems):
+def pick_inputs_kernel(
+    routes_in, weight_in, rows_in, base_in, out_ref, slot_ref, weight_ref, base_ref, routes_ref, rows_ref, sems
+):
     part = rows_ref.shape[1] // FOLDS
-    routes_copy = pltpu.make_async_copy(routes_in, routes_ref, sems.at[FOLDS])
+    routes_copy = pltpu.make_async_copy(routes_in, routes_ref, sems.at[2 * FOLDS])
     routes_copy.start()
+    weight_copy = pltpu.make_async_copy(weight_in, weight_ref, sems.at[2 * FOLDS + 1])
+    weight_copy.start()
     copies = []
     for fold in range(FOLDS):
         span = slice(fold * part, (fold + 1) * part)
@@ -216,27 +228,33 @@
         span = slice(fold * part, (fold + 1) * part)
         base_copies.append(
             pltpu.make_async_copy(
-                base_in.at[:, span], base_ref.at[:, span], sems.at[FOLDS + 1 + fold]
+                base_in.at[:, span], base_ref.at[:, span], sems.at[FOLDS + fold]
             )
         )
         base_copies[-1].start()
     routes_copy.wait()
-    _, slot = slot_of_token(routes_ref[...])
+    hit, slot = slot_of_token(routes_ref[...])
+    slot_ref[...] = jnp.where(hit, slot, -1.0)
     pick_into(slot, rows_ref, out_ref, lambda fold: copies[fold].wait())
+    weight_copy.wait()
     for copy in base_copies:
         copy.wait()
 
 
-def pick_grads_kernel(routes_ref, rows_ref, out_ref):
+def pick_grads_kernel(routes_ref, rows_ref, weight_ref, out_ref, with_ref):
+    full = out_ref.shape[1]
     _, slot = slot_of_token(routes_ref[...])
     pick_into(slot, rows_ref, out_ref)
+    with_ref[:, :full] = out_ref[...]
+    for k, piece in enumerate(three_parts(weight_ref[...])):
+        with_ref[:, full + 128 * k : full + 128 * (k + 1)] = piece.astype(BF16)
 
 
 TN = (((0,), (0,)), ((), ()))
 NT = (((1,), (1,)), ((), ()))
 
 
-def back_kernel(routes_ref, weight_ref, back_ref, scale_ref):
+def back_kernel(routes_ref, with_ref, back_ref, scale_ref):
     hit, slot = slot_of_token(routes_ref[...])
     size = 2 * MAIN
     eye = as_bf16(
@@ -247,7 +265,11 @@
         back_ref[fold] = lax.dot_general(
             both_picks(slot, fold), eye, TN, preferred_element_type=F32
         ).astype(BF16)
-    weight_row = jnp.sum(jnp.where(hit, weight_ref[...], 0.0), axis=0, keepdims=True)
+    weight = jnp.zeros(hit.shape, F32)
+    for k in range(3, 0, -1):
+        start = with_ref.shape[1] - 128 * k
+        weight = weight + with_ref[:, start : start + 128].astype(F32)
+    weight_row = jnp.sum(jnp.where(hit, weight, 0.0), axis=0, keepdims=True)
     main = jnp.sum(jnp.where(main_pick(slot), weight_row, 0.0), axis=1, keepdims=True)
     tail = jnp.zeros_like(main)
     for fold in range(FOLDS):
@@ -264,7 +286,7 @@
     count = MAIN * len(blocks)
     for k, block in enumerate(blocks):
         rows_ref[MAIN * k : MAIN * (k + 1), :] = block[:, :width]
-        rows_ref[count + MAIN * k : count + MAIN * (k + 1), :part] = block[:, width:]
+        rows_ref[count + MAIN * k : count + MAIN * (k + 1), :part] = block[:, width : width + part]
     tails = rows_ref[count:, :part]
     quarter = lax.broadcasted_iota(jnp.int32, (count, weights_ref.shape[0]), 0) % MAIN // TAIL
     main = tail = None
@@ -286,14 +308,6 @@
 def forward_kernel(own, z2, y0, y2, low, high, gu_ref, h_ref, rows_ref):
     blocks = [own, low.at[0], z2, high.at[0], y0, low.at[1], y2, high.at[1]]
     h_ref[...] = against(blocks, gu_ref, rows_ref)
-
-
-def three_parts(value):
-    high = value.astype(BF16)
-    rest = value - high.astype(F32)
-    mid = rest.astype(BF16)
-    low = (rest - mid.astype(F32)).astype(BF16)
-    return [part.astype(F32) for part in (high, mid, low)]
 
 
 def backward_kernel(*refs):
@@ -372,19 +386,20 @@
         tile_ref[...] = tile
 
 
-def weight_kernel(routes_ref, own_tile, got_tile, after_ref, out_ref):
-    hit, slot = slot_of_token(routes_ref[...])
+def weight_kernel(slot_ref, own_tile, got_tile, after_ref, out_ref):
     tile = own_tile[...] + got_tile[...] + after_ref[...]
     lane = lax.broadcasted_iota(jnp.int32, tile.shape, 1)
     main = jnp.sum(jnp.where(lane < 3, tile, 0.0), axis=1, keepdims=True)
     tail = jnp.sum(jnp.where((lane >= 3) & (lane < 6), tile, 0.0), axis=1, keepdims=True)
+    table = slot_ref[...]
+    slot = jnp.broadcast_to(jnp.max(table, axis=0, keepdims=True), table.shape)
     row = lax.broadcasted_iota(jnp.int32, slot.shape, 0).astype(F32)
     value = jnp.sum(
         jnp.where(slot == row, main, 0.0) + jnp.where((slot == row + MAIN) & (row < TAIL), tail, 0.0),
         axis=0,
         keepdims=True,
     )
-    out_ref[...] = jnp.where(hit, value, 0.0)
+    out_ref[...] = jnp.where(table >= 0.0, value, 0.0)
 
 
 def final_kernel(back_ref, scale_ref, one_ref, two_ref, base_ref, out_ref, end_ref, done_ref, sems):
@@ -446,37 +461,46 @@
     hbm = pl.BlockSpec(memory_space=pltpu.HBM)
     tile = pltpu.VMEM((MAIN, 128), F32)
 
-    input_block, near_routes, base = near_call(
+    input_block, slot_table, near_weight, base = near_call(
         pick_inputs_kernel,
         [
             pltpu.VMEM((MAIN, full), BF16),
+            pltpu.VMEM(routes_t.shape, F32),
+            pltpu.VMEM(weight_t.shape, F32),
+            pltpu.VMEM((count, width), BF16),
+        ],
+        *(
+            pltpu.with_memory_space_constraint(v, pltpu.HBM)
+            for v in (routes_t, weight_t, saved[0], upstream[0])
+        ),
+        in_specs=[hbm] * 4,
+        scratch_shapes=[
             pltpu.VMEM(routes_t.shape, jnp.int32),
             pltpu.VMEM((count, width), BF16),
-        ],
-        *(pltpu.with_memory_space_constraint(v, pltpu.HBM) for v in (routes_t, saved[0], upstream[0])),
-        in_specs=[hbm] * 3,
-        scratch_shapes=[
-            pltpu.VMEM((count, width), BF16),
-            pltpu.SemaphoreType.DMA((2 * FOLDS + 1,)),
+            pltpu.SemaphoreType.DMA((2 * FOLDS + 2,)),
         ],
         name="pick_inputs",
     )
-    grad_block = near_call(
-        pick_grads_kernel, pltpu.VMEM((MAIN, full), BF16), next_routes, base, name="pick_grads"
-    )
-
-    own = (w_gate[0], w_up[0], w_down[0])
-    other = from_partner(own, "ep", 0)
-    input_block, grad_block, other = lax.optimization_barrier((input_block, grad_block, other))
+    grad_block, grad_with = near_call(
+        pick_grads_kernel,
+        [pltpu.VMEM((MAIN, full), BF16), pltpu.VMEM((MAIN, full + 384), BF16)],
+        next_routes,
+        base,
+        near_weight,
+        name="pick_grads",
+    )
 
     grad_z2 = sections_across(grad_block, Z2)
-    grad_z0 = sections_across(grad_block, 0)
+    grad_z0 = sections_across(grad_with, 0)
     input_z2 = across(input_block, Z2)
     input_y0 = across(input_block, Y1)
+    own = jnp.stack([w_gate[0], w_up[0], w_down[0]])
+    own, _ = lax.optimization_barrier((own, input_z2))
+    other = across(own, 1)
     gate_up = jnp.concatenate([own[0], other[0], own[1], other[1]], axis=0)
     down = jnp.concatenate([own[2], other[2]], axis=0)
 
-    grad_z = jnp.stack([grad_z0, grad_z2])
+    grad_z = jnp.stack([grad_z0[:, :full], grad_z2])
     grad_z1 = across(grad_z, Z1)
     grad_y = across(grad_z, Y1)
     input_y2 = across(input_z2, Y1)
@@ -484,12 +508,12 @@
     input_high = across(jnp.stack([input_z2, input_y2]), Z1)
     grad_yz1 = across(grad_z1, Y1)
 
-    late_routes, weight_t, _ = lax.optimization_barrier((next_routes, weight_t, grad_z1))
+    late_routes, late_with, _ = lax.optimization_barrier((next_routes, grad_z0, grad_z1))
     back, scale = near_call(
         back_kernel,
         [pltpu.VMEM((FOLDS, count, 4 * MAIN), BF16), pltpu.VMEM((MAIN, 256), F32)],
         late_routes,
-        passed_along(weight_t, "pp", 1),
+        late_with,
         name="back_rows",
     )
     input_high, back, scale = lax.optimization_barrier((input_high, back, scale))
@@ -556,7 +580,7 @@
     weight_out = near_call(
         weight_kernel,
         jax.ShapeDtypeStruct((TOP, count), F32),
-        near_routes,
+        slot_table,
         tile_0,
         across(tile_2, Z2),
         end,

time: 55.7 us -> 54.1 us (0.971)
  starting transfers between devices: 29.8 us -> 24.8 us
  waiting for transfers between devices: 18 us -> 21.1 us
    ppermute x13 -> x14, waiting for transfers between devices: 10.3 us -> 13.8 us  [across(): return lax.ppermute(value, 'ep', [(i, i ^ bits) for i in range(count)])]
    ppermute x4, starting transfers between devices: 9.62 us -> 6.39 us  [sections_across(): return lax.ppermute(value, ('pp', 'ep'), pairs)]
    ppermute x2 -> x1, waiting for transfers between devices: 1.21 us -> 0.01 us  [passed_along(): lax.ppermute(value, axis, [(i, (i + by) % size) for i in range(size)])]
    ppermute x3 -> x0, starting transfers between devices: 1.03 us -> none  [from_partner(): return lax.ppermute(block, axis, route)]
    ppermute x4, waiting for transfers between devices: 6.46 us -> 7.24 us  [sections_across(): return lax.ppermute(value, ('pp', 'ep'), pairs)]
    ppermute x2 -> x1, starting transfers between devices: 3.49 us -> 3 us  [passed_along(): lax.ppermute(value, axis, [(i, (i + by) % size) for i in range(size)])]
    ppermute x13 -> x14, starting transfers between devices: 15.7 us -> 15.4 us  [across(): return lax.ppermute(value, 'ep', [(i, i ^ bits) for i in range(count)])]
  transfers between devices with their start and end apart: 22 -> 19, of which waited for: 10 -> 10; matrix products, arithmetic and copies ran while one was open for 0% -> 1% of each run, Pallas kernels for 8% -> 9%
where the time goes in v5:
time: 54.1 us; the launch traced here: 54 us
  starting transfers between devices  24.8 us (46%)
  waiting for transfers between devices  21.1 us (39%)
  Pallas kernels  6.66 us (12%)
  between operations  0.81 us (1%)
    ppermute x14, starting transfers between devices, across(): return lax.ppermute(value, 'ep', [(i, i ^ bits) for i in range(count)])  15.4 us
    ppermute x14, waiting for transfers between devices, across(): return lax.ppermute(value, 'ep', [(i, i ^ bits) for i in range(count)])  13.8 us
    ppermute x4, waiting for transfers between devices, sections_across(): return lax.ppermute(value, ('pp', 'ep'), pairs)  7.24 us
    pallas_call x10, Pallas kernels, near_call(): pl.pallas_call(kernel, out_shape=out_shape, compiler_params=params, **kwa...  6.66 us
    ppermute x4, starting transfers between devices, sections_across(): return lax.ppermute(value, ('pp', 'ep'), pairs)  6.39 us
    ppermute x1, starting transfers between devices, passed_along(): lax.ppermute(value, axis, [(i, (i + by) % size) for i in range(size)])  3 us
  transfers between devices with their start and end apart: 19, of which 10 were waited for; matrix products, arithmetic and copies ran while one was open for 1% of the time, Pallas kernels for 9%

profile of v5, /device:TPU:0, one launch (start us, length us, event | category | flops | bytes accessed | tf_op | source)
XLA Modules:
  0.0 54.0 jit_solution(5961522978342127413)
XLA Ops:
  0.7 3.0 %collective-permute-start.3 = (s32[8,128]{1,0:T(8,128)}, s32[8,128]{1,0:T(8,128)S(1)}, u32[]{:S(2)}, u32[]{:S(2)}) collective-permute-start(s32[8,128]{1,0:T(8,128)} %bitcast.39), channel_id=1, source_target_pairs={{0,16},{16,0},{1,17},{17,1},{2,18},{18,2},{3,19},{19,3},{4,20},{20... | collective-permute-start | bytes 12296 | tf_op jit(solution)/shard_map/ppermute | solution.py:32
  3.7 1.7 %pick_inputs.1 = (bf16[8,5120]{1,0:T(8,128)(2,1)S(1)}, f32[8,128]{1,0:T(8,128)S(1)}, f32[8,128]{1,0:T(8,128)S(1)}, bf16[128,4096]{1,0:T(8,128)(2,1)S(1)}) custom-call(s32[8,128]{1,0:T(8,128)} %bitcast.40, f32[8,128]{1,0:T(8,128)} %bitcast.38, bf16[128,4096]{1,0:T(8,128)(2,1)} %bitcast.36, bf16[128,4096]{1,0:T(8,128)(2,1)} %bitcast.37), custom_call_target="tpu_custom_call" | custom-call | tf_op jit(solution)/shard_map/pick_inputs/pallas_call | solution.py:153
  5.4 2.7 %collective-permute-start = (bf16[8,5120]{1,0:T(8,128)(2,1)S(1)}, bf16[8,5120]{1,0:T(8,128)(2,1)S(1)}, u32[]{:S(2)}, u32[]{:S(2)}) collective-permute-start(bf16[8,5120]{1,0:T(8,128)(2,1)S(1)} %get-tuple-element.30.own), channel_id=1, source_target_pairs={{0,8},{1,9},{2,10},{3,11},{4,12},{5,13},{6,14},{7,15},{8,0},{9,1},... | collective-permute-start | bytes 245768 | tf_op jit(solution)/shard_map/ppermute | solution.py:440
  8.0 1.5 %collective-permute-start.10 = (bf16[8,5120]{1,0:T(8,128)(2,1)S(1)}, bf16[8,5120]{1,0:T(8,128)(2,1)S(1)}, u32[]{:S(2)}, u32[]{:S(2)}) collective-permute-start(bf16[8,5120]{1,0:T(8,128)(2,1)S(1)} %get-tuple-element.30.own), channel_id=1, source_target_pairs={{0,2},{1,3},{2,0},{3,1},{4,6},{5,7},{6,4},{7,5},{8,10},{9,11},{10,... | collective-permute-start | bytes 245768 | tf_op jit(solution)/shard_map/ppermute | solution.py:440
  9.7 0.4 pick_grads.1
  10.1 0.6 %collective-permute-start.4 = (bf16[8,5504]{1,0:T(8,128)(2,1)S(1)}, bf16[8,5504]{1,0:T(8,128)(2,1)S(1)}, u32[]{:S(2)}, u32[]{:S(2)}) collective-permute-start(bf16[8,5504]{1,0:T(8,128)(2,1)S(1)} %get-tuple-element.33), channel_id=1, source_target_pairs={{0,16},{1,17},{2,18},{3,19},{4,20},{5,21},{6,22},{7,23},{8,24},{9,... | collective-permute-start | bytes 264200 | tf_op jit(solution)/shard_map/ppermute | solution.py:446
  10.7 1.3 %collective-permute-start.5 = (bf16[8,5120]{1,0:T(8,128)(2,1)S(1)}, bf16[8,5120]{1,0:T(8,128)(2,1)S(1)}, u32[]{:S(2)}, u32[]{:S(2)}) collective-permute-start(bf16[8,5120]{1,0:T(8,128)(2,1)S(1)} %get-tuple-element.34), channel_id=1, source_target_pairs={{0,24},{1,25},{2,26},{3,27},{4,28},{5,29},{6,30},{7,31},{8,16},{9,... | collective-permute-start | bytes 245768 | tf_op jit(solution)/shard_map/ppermute | solution.py:446
  12.2 1.6 %collective-permute-start.1 = (bf16[8,5120]{1,0:T(8,128)(2,1)S(1)}, bf16[8,5120]{1,0:T(8,128)(2,1)S(1)}, u32[]{:S(2)}, u32[]{:S(2)}) collective-permute-start(bf16[8,5120]{1,0:T(8,128)(2,1)S(1)} %collective-permute-done.z2), channel_id=1, source_target_pairs={{0,2},{1,3},{2,0},{3,1},{4,6},{5,7},{6,4},{7,5},{8,10},{9,11},{10,... | collective-permute-start | bytes 245768 | tf_op jit(solution)/shard_map/ppermute | solution.py:440
  13.8 1.7 %collective-permute-done.4.with_ref.refs_0_ = bf16[8,5504]{1,0:T(8,128)(2,1)S(1)} collective-permute-done((bf16[8,5504]{1,0:T(8,128)(2,1)S(1)}, bf16[8,5504]{1,0:T(8,128)(2,1)S(1)}, u32[]{:S(2)}, u32[]{:S(2)}) %collective-permute-start.4) | collective-permute-done | bytes 88096 | tf_op jit(solution)/shard_map/ppermute | solution.py:446
  15.5 1.4 %collective-permute-done.5.refs_1_ = bf16[8,5120]{1,0:T(8,128)(2,1)S(1)} collective-permute-done((bf16[8,5120]{1,0:T(8,128)(2,1)S(1)}, bf16[8,5120]{1,0:T(8,128)(2,1)S(1)}, u32[]{:S(2)}, u32[]{:S(2)}) %collective-permute-start.5) | collective-permute-done | bytes 81952 | tf_op jit(solution)/shard_map/ppermute | solution.py:446
  16.9 1.6 %collective-permute-start.6 = (bf16[2,8,5120]{2,1,0:T(8,128)(2,1)S(1)}, bf16[2,8,5120]{2,1,0:T(8,128)(2,1)S(1)}, u32[]{:S(2)}, u32[]{:S(2)}) collective-permute-start(bf16[2,8,5120]{2,1,0:T(8,128)(2,1)S(1)} %pad_maximum_fusion.4), channel_id=1, source_target_pairs={{0,4},{1,5},{2,6},{3,7},{4,0},{5,1},{6,2},{7,3},{8,12},{9,13},{10,... | collective-permute-start | bytes 491528 | tf_op jit(solution)/shard_map/ppermute | solution.py:440
  18.6 1.2 %collective-permute-start.2 = (bf16[2,8,5120]{2,1,0:T(8,128)(2,1)S(1)}, bf16[2,8,5120]{2,1,0:T(8,128)(2,1)S(1)}, u32[]{:S(2)}, u32[]{:S(2)}) collective-permute-start(bf16[2,8,5120]{2,1,0:T(8,128)(2,1)S(1)} %pad_maximum_fusion.3), channel_id=1, source_target_pairs={{0,4},{1,5},{2,6},{3,7},{4,0},{5,1},{6,2},{7,3},{8,12},{9,13},{10,... | collective-permute-start | bytes 491528 | tf_op jit(solution)/shard_map/ppermute | solution.py:440
  19.9 0.9 %collective-permute-start.11 = (bf16[2,8,5120]{2,1,0:T(8,128)(2,1)S(1)}, bf16[2,8,5120]{2,1,0:T(8,128)(2,1)S(1)}, u32[]{:S(2)}, u32[]{:S(2)}) collective-permute-start(bf16[2,8,5120]{2,1,0:T(8,128)(2,1)S(1)} %pad_maximum_fusion.5), channel_id=1, source_target_pairs={{0,4},{1,5},{2,6},{3,7},{4,0},{5,1},{6,2},{7,3},{8,12},{9,13},{10,... | collective-permute-start | bytes 491528 | tf_op jit(solution)/shard_map/ppermute | solution.py:440
  20.8 1.0 %collective-permute-start.7 = (bf16[2,8,5120]{2,1,0:T(8,128)(2,1)S(1)}, bf16[2,8,5120]{2,1,0:T(8,128)(2,1)S(1)}, u32[]{:S(2)}, u32[]{:S(2)}) collective-permute-start(bf16[2,8,5120]{2,1,0:T(8,128)(2,1)S(1)} %pad_maximum_fusion.4), channel_id=1, source_target_pairs={{0,2},{1,3},{2,0},{3,1},{4,6},{5,7},{6,4},{7,5},{8,10},{9,11},{10,... | collective-permute-start | bytes 491528 | tf_op jit(solution)/shard_map/ppermute | solution.py:440
  21.8 2.3 %collective-permute-done.6.refs_2_ = bf16[2,8,5120]{2,1,0:T(8,128)(2,1)S(1)} collective-permute-done((bf16[2,8,5120]{2,1,0:T(8,128)(2,1)S(1)}, bf16[2,8,5120]{2,1,0:T(8,128)(2,1)S(1)}, u32[]{:S(2)}, u32[]{:S(2)}) %collective-permute-start.6) | collective-permute-done | bytes 163872 | tf_op jit(solution)/shard_map/ppermute | solution.py:440
  24.0 0.4 back_rows.1
  24.5 3.1 %collective-permute-done.2.high = bf16[2,8,5120]{2,1,0:T(8,128)(2,1)S(1)} collective-permute-done((bf16[2,8,5120]{2,1,0:T(8,128)(2,1)S(1)}, bf16[2,8,5120]{2,1,0:T(8,128)(2,1)S(1)}, u32[]{:S(2)}, u32[]{:S(2)}) %collective-permute-start.2) | collective-permute-done | bytes 163872 | tf_op jit(solution)/shard_map/ppermute | solution.py:440
  27.9 1.5 %collective-permute-done.11.low = bf16[2,8,5120]{2,1,0:T(8,128)(2,1)S(1)} collective-permute-done((bf16[2,8,5120]{2,1,0:T(8,128)(2,1)S(1)}, bf16[2,8,5120]{2,1,0:T(8,128)(2,1)S(1)}, u32[]{:S(2)}, u32[]{:S(2)}) %collective-permute-start.11) | collective-permute-done | bytes 163872 | tf_op jit(solution)/shard_map/ppermute | solution.py:440
  29.4 0.8 %expert_forward.1.refs_7_ = f32[128,256]{1,0:T(8,128)S(1)} custom-call(bf16[8,5120]{1,0:T(8,128)(2,1)S(1)} %get-tuple-element.30.own, bf16[8,5120]{1,0:T(8,128)(2,1)S(1)} %collective-permute-done.z2, bf16[8,5120]{1,0:T(8,128)(2,1)S(1)} %collective-permute-done.10.y0, bf16[8,5120]{1,0:T(8,128)(2,1)S(1)} %collective-permute-done.1.y2, ...), custom_call_target="tpu_custom_call" | custom-call | tf_op jit(solution)/shard_map/expert_forward/pallas_call | solution.py:153
  30.2 1.3 %expert_backward.1 = (bf16[4,8,2688]{2,1,0:T(8,128)(2,1)S(1)}, bf16[4,8,2688]{2,1,0:T(8,128)(2,1)S(1)}, bf16[4,8,2560]{2,1,0:T(8,128)(2,1)S(1)}, bf16[4,8,2560]{2,1,0:T(8,128)(2,1)S(1)}) custom-call(bf16[8,5504]{1,0:T(8,128)(2,1)S(1)} %collective-permute-done.4.with_ref.refs_0_, bf16[8,5120]{1,0:T(8,128)(2,1)S(1)} %collective-permute-done.5.refs_1_, ...), custom_call_target="tpu_custom_call" | custom-call | tf_op jit(solution)/shard_map/expert_backward/pallas_call | solution.py:153
  31.6 0.7 %collective-permute-start.12 = (bf16[4,8,2688]{2,1,0:T(8,128)(2,1)S(1)}, bf16[4,8,2688]{2,1,0:T(8,128)(2,1)S(1)}, u32[]{:S(2)}, u32[]{:S(2)}) collective-permute-start(bf16[4,8,2688]{2,1,0:T(8,128)(2,1)S(1)} %get-tuple-element.44), channel_id=1, source_target_pairs={{0,2},{1,3},{2,0},{3,1},{4,6},{5,7},{6,4},{7,5},{8,10},{9,11},{10,... | collective-permute-start | bytes 516104 | tf_op jit(solution)/shard_map/ppermute | solution.py:440
  32.2 1.7 %collective-permute-start.14 = (bf16[4,8,2560]{2,1,0:T(8,128)(2,1)S(1)}, bf16[4,8,2560]{2,1,0:T(8,128)(2,1)S(1)}, u32[]{:S(2)}, u32[]{:S(2)}) collective-permute-start(bf16[4,8,2560]{2,1,0:T(8,128)(2,1)S(1)} %get-tuple-element.48), channel_id=1, source_target_pairs={{0,4},{1,5},{2,6},{3,7},{4,0},{5,1},{6,2},{7,3},{8,12},{9,13},{10,... | collective-permute-start | bytes 491528 | tf_op jit(solution)/shard_map/ppermute | solution.py:440
  33.9 3.1 %collective-permute-done.12.got_ref = bf16[4,8,2688]{2,1,0:T(8,128)(2,1)S(1)} collective-permute-done((bf16[4,8,2688]{2,1,0:T(8,128)(2,1)S(1)}, bf16[4,8,2688]{2,1,0:T(8,128)(2,1)S(1)}, u32[]{:S(2)}, u32[]{:S(2)}) %collective-permute-start.12) | collective-permute-done | bytes 172064 | tf_op jit(solution)/shard_map/ppermute | solution.py:440
  37.1 1.6 %collective-permute-start.13 = (bf16[2,8,2816]{2,1,0:T(8,128)(2,1)S(1)}, bf16[2,8,2816]{2,1,0:T(8,128)(2,1)S(1)}, u32[]{:S(2)}, u32[]{:S(2)}) collective-permute-start(bf16[2,8,2816]{2,1,0:T(8,128)(2,1)S(1)} %get-tuple-element.46), channel_id=1, source_target_pairs={{0,4},{1,5},{2,6},{3,7},{4,0},{5,1},{6,2},{7,3},{8,12},{9,13},{10,... | collective-permute-start | bytes 270344 | tf_op jit(solution)/shard_map/ppermute | solution.py:440
  38.8 0.8 %collective-permute-start.15 = (bf16[2,8,2560]{2,1,0:T(8,128)(2,1)S(1)}, bf16[2,8,2560]{2,1,0:T(8,128)(2,1)S(1)}, u32[]{:S(2)}, u32[]{:S(2)}) collective-permute-start(bf16[2,8,2560]{2,1,0:T(8,128)(2,1)S(1)} %get-tuple-element.50), channel_id=1, source_target_pairs={{0,2},{1,3},{2,0},{3,1},{4,6},{5,7},{6,4},{7,5},{8,10},{9,11},{10,... | collective-permute-start | bytes 245768 | tf_op jit(solution)/shard_map/ppermute | solution.py:440
  39.5 3.7 %collective-permute-done.15.got_b = bf16[2,8,2560]{2,1,0:T(8,128)(2,1)S(1)} collective-permute-done((bf16[2,8,2560]{2,1,0:T(8,128)(2,1)S(1)}, bf16[2,8,2560]{2,1,0:T(8,128)(2,1)S(1)}, u32[]{:S(2)}, u32[]{:S(2)}) %collective-permute-start.15) | collective-permute-done | bytes 81952 | tf_op jit(solution)/shard_map/ppermute | solution.py:440
  43.3 1.7 %collective-permute-start.16 = (bf16[8,5120]{1,0:T(8,128)(2,1)S(1)}, bf16[8,5120]{1,0:T(8,128)(2,1)S(1)}, u32[]{:S(2)}, u32[]{:S(2)}) collective-permute-start(bf16[8,5120]{1,0:T(8,128)(2,1)S(1)} %get-tuple-element.51), channel_id=1, source_target_pairs={{0,16},{1,17},{2,18},{3,19},{4,20},{5,21},{6,22},{7,23},{8,24},{9,... | collective-permute-start | bytes 245768 | tf_op jit(solution)/shard_map/ppermute | solution.py:446
  45.0 2.8 %collective-permute-start.17 = (bf16[8,5120]{1,0:T(8,128)(2,1)S(1)}, bf16[8,5120]{1,0:T(8,128)(2,1)S(1)}, u32[]{:S(2)}, u32[]{:S(2)}) collective-permute-start(bf16[8,5120]{1,0:T(8,128)(2,1)S(1)} %get-tuple-element.52), channel_id=1, source_target_pairs={{0,24},{1,25},{2,26},{3,27},{4,28},{5,29},{6,30},{7,31},{8,16},{9,... | collective-permute-start | bytes 245768 | tf_op jit(solution)/shard_map/ppermute | solution.py:446
  47.9 0.3 collective-permute-done.16.one_ref
  48.1 3.9 %collective-permute-done.17.two_ref = bf16[8,5120]{1,0:T(8,128)(2,1)S(1)} collective-permute-done((bf16[8,5120]{1,0:T(8,128)(2,1)S(1)}, bf16[8,5120]{1,0:T(8,128)(2,1)S(1)}, u32[]{:S(2)}, u32[]{:S(2)}) %collective-permute-start.17) | collective-permute-done | bytes 81952 | tf_op jit(solution)/shard_map/ppermute | solution.py:446
  52.0 1.3 %final_rows.1 = (bf16[128,4096]{1,0:T(8,128)(2,1)}, f32[8,128]{1,0:T(8,128)S(1)}) custom-call(bf16[4,128,32]{2,1,0:T(8,128)(2,1)S(1)} %get-tuple-element.39.back_ref, f32[8,256]{1,0:T(8,128)S(1)} %get-tuple-element.40.scale_ref, bf16[8,5120]{1,0:T(8,128)(2,1)S(1)} %collective-permute-done.16.one_ref, bf16[8,5120]{1,0:T(8,128)(2,1)S(1)} %collective-permute-done.17.two_ref, ...), custom_call_target="tpu_custom_call" | custom-call | tf_op jit(solution)/shard_map/final_rows/pallas_call | solution.py:153
  53.3 0.7 %weight_out.1 = f32[8,128]{1,0:T(8,128)} custom-call(f32[8,128]{1,0:T(8,128)S(1)} %get-tuple-element.54.slot_ref, f32[8,128]{1,0:T(8,128)S(1)} %get-tuple-element.55.own_tile, f32[8,128]{1,0:T(8,128)S(1)} %collective-permute-done.18.got_tile, f32[8,128]{1,0:T(8,128)S(1)} %get-tuple-element.57.after_ref), custom_call_target="tpu_custom_call" | custom-call | tf_op jit(solution)/shard_map/weight_out/pallas_call | solution.py:153
  (31 shorter events, 1.1 us)
Async XLA Ops:
  0.6 8.9 %copy-start.2 = (bf16[1,64,4096]{2,1,0:T(8,128)(2,1)S(1)}, bf16[1,64,4096]{2,1,0:T(8,128)(2,1)}, u32[]{:S(2)}) copy-start(bf16[1,64,4096]{2,1,0:T(8,128)(2,1)} %param.11) | copy-start | bytes 1572868
  0.6 8.9 %copy-start.1 = (bf16[1,64,4096]{2,1,0:T(8,128)(2,1)S(1)}, bf16[1,64,4096]{2,1,0:T(8,128)(2,1)}, u32[]{:S(2)}) copy-start(bf16[1,64,4096]{2,1,0:T(8,128)(2,1)} %param.12) | copy-start | bytes 1572868
  0.7 8.9 %copy-start = (bf16[1,64,4096]{2,1,0:T(8,128)(2,1)S(1)}, bf16[1,64,4096]{2,1,0:T(8,128)(2,1)}, u32[]{:S(2)}) copy-start(bf16[1,64,4096]{2,1,0:T(8,128)(2,1)} %param.13) | copy-start | bytes 1572868
  0.7 9.1 %collective-permute-start.3 = (s32[8,128]{1,0:T(8,128)}, s32[8,128]{1,0:T(8,128)S(1)}, u32[]{:S(2)}, u32[]{:S(2)}) collective-permute-start(s32[8,128]{1,0:T(8,128)} %bitcast.39), channel_id=1, source_target_pairs={{0,16},{16,0},{1,17},{17,1},{2,18},{18,2},{3,19},{19,3},{4,20},{20... | collective-permute-start | bytes 12296 | tf_op jit(solution)/shard_map/ppermute | solution.py:32
  5.4 6.8 %collective-permute-start = (bf16[8,5120]{1,0:T(8,128)(2,1)S(1)}, bf16[8,5120]{1,0:T(8,128)(2,1)S(1)}, u32[]{:S(2)}, u32[]{:S(2)}) collective-permute-start(bf16[8,5120]{1,0:T(8,128)(2,1)S(1)} %get-tuple-element.30.own), channel_id=1, source_target_pairs={{0,8},{1,9},{2,10},{3,11},{4,12},{5,13},{6,14},{7,15},{8,0},{9,1},... | collective-permute-start | bytes 245768 | tf_op jit(solution)/shard_map/ppermute | solution.py:440
  8.0 11.8 %collective-permute-start.10 = (bf16[8,5120]{1,0:T(8,128)(2,1)S(1)}, bf16[8,5120]{1,0:T(8,128)(2,1)S(1)}, u32[]{:S(2)}, u32[]{:S(2)}) collective-permute-start(bf16[8,5120]{1,0:T(8,128)(2,1)S(1)} %get-tuple-element.30.own), channel_id=1, source_target_pairs={{0,2},{1,3},{2,0},{3,1},{4,6},{5,7},{6,4},{7,5},{8,10},{9,11},{10,... | collective-permute-start | bytes 245768 | tf_op jit(solution)/shard_map/ppermute | solution.py:440
  10.1 5.4 %collective-permute-start.4 = (bf16[8,5504]{1,0:T(8,128)(2,1)S(1)}, bf16[8,5504]{1,0:T(8,128)(2,1)S(1)}, u32[]{:S(2)}, u32[]{:S(2)}) collective-permute-start(bf16[8,5504]{1,0:T(8,128)(2,1)S(1)} %get-tuple-element.33), channel_id=1, source_target_pairs={{0,16},{1,17},{2,18},{3,19},{4,20},{5,21},{6,22},{7,23},{8,24},{9,... | collective-permute-start | bytes 264200 | tf_op jit(solution)/shard_map/ppermute | solution.py:446
  10.7 6.2 %collective-permute-start.5 = (bf16[8,5120]{1,0:T(8,128)(2,1)S(1)}, bf16[8,5120]{1,0:T(8,128)(2,1)S(1)}, u32[]{:S(2)}, u32[]{:S(2)}) collective-permute-start(bf16[8,5120]{1,0:T(8,128)(2,1)S(1)} %get-tuple-element.34), channel_id=1, source_target_pairs={{0,24},{1,25},{2,26},{3,27},{4,28},{5,29},{6,30},{7,31},{8,16},{9,... | collective-permute-start | bytes 245768 | tf_op jit(solution)/shard_map/ppermute | solution.py:446
  12.1 15.4 %collective-permute-start.9 = (bf16[3,64,4096]{2,1,0:T(8,128)(2,1)S(1)}, bf16[3,64,4096]{2,1,0:T(8,128)(2,1)S(1)}, u32[]{:S(2)}, u32[]{:S(2)}) collective-permute-start(bf16[3,64,4096]{2,1,0:T(8,128)(2,1)S(1)} %pad_maximum_fusion.1), channel_id=1, source_target_pairs={{0,1},{1,0},{2,3},{3,2},{4,5},{5,4},{6,7},{7,6},{8,9},{9,8},{10,11... | collective-permute-start | bytes 4718600 | tf_op jit(solution)/shard_map/ppermute | solution.py:440
  12.2 6.4 %collective-permute-start.1 = (bf16[8,5120]{1,0:T(8,128)(2,1)S(1)}, bf16[8,5120]{1,0:T(8,128)(2,1)S(1)}, u32[]{:S(2)}, u32[]{:S(2)}) collective-permute-start(bf16[8,5120]{1,0:T(8,128)(2,1)S(1)} %collective-permute-done.z2), channel_id=1, source_target_pairs={{0,2},{1,3},{2,0},{3,1},{4,6},{5,7},{6,4},{7,5},{8,10},{9,11},{10,... | collective-permute-start | bytes 245768 | tf_op jit(solution)/shard_map/ppermute | solution.py:440
  16.9 7.1 %collective-permute-start.6 = (bf16[2,8,5120]{2,1,0:T(8,128)(2,1)S(1)}, bf16[2,8,5120]{2,1,0:T(8,128)(2,1)S(1)}, u32[]{:S(2)}, u32[]{:S(2)}) collective-permute-start(bf16[2,8,5120]{2,1,0:T(8,128)(2,1)S(1)} %pad_maximum_fusion.4), channel_id=1, source_target_pairs={{0,4},{1,5},{2,6},{3,7},{4,0},{5,1},{6,2},{7,3},{8,12},{9,13},{10,... | collective-permute-start | bytes 491528 | tf_op jit(solution)/shard_map/ppermute | solution.py:440
  18.6 8.9 %collective-permute-start.2 = (bf16[2,8,5120]{2,1,0:T(8,128)(2,1)S(1)}, bf16[2,8,5120]{2,1,0:T(8,128)(2,1)S(1)}, u32[]{:S(2)}, u32[]{:S(2)}) collective-permute-start(bf16[2,8,5120]{2,1,0:T(8,128)(2,1)S(1)} %pad_maximum_fusion.3), channel_id=1, source_target_pairs={{0,4},{1,5},{2,6},{3,7},{4,0},{5,1},{6,2},{7,3},{8,12},{9,13},{10,... | collective-permute-start | bytes 491528 | tf_op jit(solution)/shard_map/ppermute | solution.py:440
  19.9 9.5 %collective-permute-start.11 = (bf16[2,8,5120]{2,1,0:T(8,128)(2,1)S(1)}, bf16[2,8,5120]{2,1,0:T(8,128)(2,1)S(1)}, u32[]{:S(2)}, u32[]{:S(2)}) collective-permute-start(bf16[2,8,5120]{2,1,0:T(8,128)(2,1)S(1)} %pad_maximum_fusion.5), channel_id=1, source_target_pairs={{0,4},{1,5},{2,6},{3,7},{4,0},{5,1},{6,2},{7,3},{8,12},{9,13},{10,... | collective-permute-start | bytes 491528 | tf_op jit(solution)/shard_map/ppermute | solution.py:440
  20.8 9.4 %collective-permute-start.7 = (bf16[2,8,5120]{2,1,0:T(8,128)(2,1)S(1)}, bf16[2,8,5120]{2,1,0:T(8,128)(2,1)S(1)}, u32[]{:S(2)}, u32[]{:S(2)}) collective-permute-start(bf16[2,8,5120]{2,1,0:T(8,128)(2,1)S(1)} %pad_maximum_fusion.4), channel_id=1, source_target_pairs={{0,2},{1,3},{2,0},{3,1},{4,6},{5,7},{6,4},{7,5},{8,10},{9,11},{10,... | collective-permute-start | bytes 491528 | tf_op jit(solution)/shard_map/ppermute | solution.py:440
  24.4 5.8 %collective-permute-start.8 = (bf16[2,8,5120]{2,1,0:T(8,128)(2,1)S(1)}, bf16[2,8,5120]{2,1,0:T(8,128)(2,1)S(1)}, u32[]{:S(2)}, u32[]{:S(2)}) collective-permute-start(bf16[2,8,5120]{2,1,0:T(8,128)(2,1)S(1)} %collective-permute-done.6.refs_2_), channel_id=1, source_target_pairs={{0,2},{1,3},{2,0},{3,1},{4,6},{5,7},{6,4},{7,5},{8,10},{9,11},{10,... | collective-permute-start | bytes 491528 | tf_op jit(solution)/shard_map/ppermute | solution.py:440
  31.6 5.5 %collective-permute-start.12 = (bf16[4,8,2688]{2,1,0:T(8,128)(2,1)S(1)}, bf16[4,8,2688]{2,1,0:T(8,128)(2,1)S(1)}, u32[]{:S(2)}, u32[]{:S(2)}) collective-permute-start(bf16[4,8,2688]{2,1,0:T(8,128)(2,1)S(1)} %get-tuple-element.44), channel_id=1, source_target_pairs={{0,2},{1,3},{2,0},{3,1},{4,6},{5,7},{6,4},{7,5},{8,10},{9,11},{10,... | collective-permute-start | bytes 516104 | tf_op jit(solution)/shard_map/ppermute | solution.py:440
  32.2 6.5 %collective-permute-start.14 = (bf16[4,8,2560]{2,1,0:T(8,128)(2,1)S(1)}, bf16[4,8,2560]{2,1,0:T(8,128)(2,1)S(1)}, u32[]{:S(2)}, u32[]{:S(2)}) collective-permute-start(bf16[4,8,2560]{2,1,0:T(8,128)(2,1)S(1)} %get-tuple-element.48), channel_id=1, source_target_pairs={{0,4},{1,5},{2,6},{3,7},{4,0},{5,1},{6,2},{7,3},{8,12},{9,13},{10,... | collective-permute-start | bytes 491528 | tf_op jit(solution)/shard_map/ppermute | solution.py:440
  37.1 6.2 %collective-permute-start.13 = (bf16[2,8,2816]{2,1,0:T(8,128)(2,1)S(1)}, bf16[2,8,2816]{2,1,0:T(8,128)(2,1)S(1)}, u32[]{:S(2)}, u32[]{:S(2)}) collective-permute-start(bf16[2,8,2816]{2,1,0:T(8,128)(2,1)S(1)} %get-tuple-element.46), channel_id=1, source_target_pairs={{0,4},{1,5},{2,6},{3,7},{4,0},{5,1},{6,2},{7,3},{8,12},{9,13},{10,... | collective-permute-start | bytes 270344 | tf_op jit(solution)/shard_map/ppermute | solution.py:440
  38.8 4.5 %collective-permute-start.15 = (bf16[2,8,2560]{2,1,0:T(8,128)(2,1)S(1)}, bf16[2,8,2560]{2,1,0:T(8,128)(2,1)S(1)}, u32[]{:S(2)}, u32[]{:S(2)}) collective-permute-start(bf16[2,8,2560]{2,1,0:T(8,128)(2,1)S(1)} %get-tuple-element.50), channel_id=1, source_target_pairs={{0,2},{1,3},{2,0},{3,1},{4,6},{5,7},{6,4},{7,5},{8,10},{9,11},{10,... | collective-permute-start | bytes 245768 | tf_op jit(solution)/shard_map/ppermute | solution.py:440
  43.3 4.8 %collective-permute-start.16 = (bf16[8,5120]{1,0:T(8,128)(2,1)S(1)}, bf16[8,5120]{1,0:T(8,128)(2,1)S(1)}, u32[]{:S(2)}, u32[]{:S(2)}) collective-permute-start(bf16[8,5120]{1,0:T(8,128)(2,1)S(1)} %get-tuple-element.51), channel_id=1, source_target_pairs={{0,16},{1,17},{2,18},{3,19},{4,20},{5,21},{6,22},{7,23},{8,24},{9,... | collective-permute-start | bytes 245768 | tf_op jit(solution)/shard_map/ppermute | solution.py:446
  45.0 7.0 %collective-permute-start.17 = (bf16[8,5120]{1,0:T(8,128)(2,1)S(1)}, bf16[8,5120]{1,0:T(8,128)(2,1)S(1)}, u32[]{:S(2)}, u32[]{:S(2)}) collective-permute-start(bf16[8,5120]{1,0:T(8,128)(2,1)S(1)} %get-tuple-element.52), channel_id=1, source_target_pairs={{0,24},{1,25},{2,26},{3,27},{4,28},{5,29},{6,30},{7,31},{8,16},{9,... | collective-permute-start | bytes 245768 | tf_op jit(solution)/shard_map/ppermute | solution.py:446
  47.8 5.4 %collective-permute-start.18 = (f32[8,128]{1,0:T(8,128)S(1)}, f32[8,128]{1,0:T(8,128)S(1)}, u32[]{:S(2)}, u32[]{:S(2)}) collective-permute-start(f32[8,128]{1,0:T(8,128)S(1)} %get-tuple-element.56), channel_id=1, source_target_pairs={{0,8},{1,9},{2,10},{3,11},{4,12},{5,13},{6,14},{7,15},{8,0},{9,1},... | collective-permute-start | bytes 12296 | tf_op jit(solution)/shard_map/ppermute | solution.py:440

commit v6 on v5

--- a/solution.py
+++ b/solution.py
@@ -305,8 +305,8 @@
     return jnp.concatenate([main, tail.reshape(count, -1)], axis=0)
 
 
-def forward_kernel(own, z2, y0, y2, low, high, gu_ref, h_ref, rows_ref):
-    blocks = [own, low.at[0], z2, high.at[0], y0, low.at[1], y2, high.at[1]]
+def forward_kernel(own, z2, y_refs, low, high, gu_ref, h_ref, rows_ref):
+    blocks = [own, low.at[0], z2, low.at[1], y_refs.at[0], high.at[0], y_refs.at[1], high.at[1]]
     h_ref[...] = against(blocks, gu_ref, rows_ref)
 
 
@@ -493,7 +493,6 @@
     grad_z2 = sections_across(grad_block, Z2)
     grad_z0 = sections_across(grad_with, 0)
     input_z2 = across(input_block, Z2)
-    input_y0 = across(input_block, Y1)
     own = jnp.stack([w_gate[0], w_up[0], w_down[0]])
     own, _ = lax.optimization_barrier((own, input_z2))
     other = across(own, 1)
@@ -503,9 +502,10 @@
     grad_z = jnp.stack([grad_z0[:, :full], grad_z2])
     grad_z1 = across(grad_z, Z1)
     grad_y = across(grad_z, Y1)
-    input_y2 = across(input_z2, Y1)
-    input_low = across(jnp.stack([input_block, input_y0]), Z1)
-    input_high = across(jnp.stack([input_z2, input_y2]), Z1)
+    input_z = jnp.stack([input_block, input_z2])
+    input_y = across(input_z, Y1)
+    input_low = across(input_z, Z1)
+    input_high = across(input_y, Z1)
     grad_yz1 = across(grad_z1, Y1)
 
     late_routes, late_with, _ = lax.optimization_barrier((next_routes, grad_z0, grad_z1))
@@ -522,8 +522,7 @@
         pltpu.VMEM((slots, 2 * units), F32),
         input_block,
         input_z2,
-        input_y0,
-        input_y2,
+        input_y,
         input_low,
         input_high,
         gate_up,

time: 54.1 us -> 53.5 us (0.989)
  waiting for transfers between devices: 21.1 us -> 18.6 us
  starting transfers between devices: 24.8 us -> 26.6 us
    ppermute x4, waiting for transfers between devices: 7.24 us -> 5 us  [sections_across(): return lax.ppermute(value, ('pp', 'ep'), pairs)]
    ppermute x14 -> x13, starting transfers between devices: 15.4 us -> 16.8 us  [across(): return lax.ppermute(value, 'ep', [(i, i ^ bits) for i in range(count)])]
    ppermute x14 -> x13, waiting for transfers between devices: 13.8 us -> 13.6 us  [across(): return lax.ppermute(value, 'ep', [(i, i ^ bits) for i in range(count)])]
  transfers between devices with their start and end apart: 19 -> 18, of which waited for: 10 -> 10; matrix products, arithmetic and copies ran while one was open for 1% -> 1% of each run, Pallas kernels for 9% -> 9%
where the time goes in v6:
time: 53.5 us; the launch traced here: 53.3 us
  starting transfers between devices  26.6 us (50%)
  waiting for transfers between devices  18.6 us (35%)
  Pallas kernels  6.66 us (12%)
  between operations  0.8 us (1%)
    ppermute x13, starting transfers between devices, across(): return lax.ppermute(value, 'ep', [(i, i ^ bits) for i in range(count)])  16.8 us
    ppermute x13, waiting for transfers between devices, across(): return lax.ppermute(value, 'ep', [(i, i ^ bits) for i in range(count)])  13.6 us
    ppermute x4, starting transfers between devices, sections_across(): return lax.ppermute(value, ('pp', 'ep'), pairs)  6.77 us
    pallas_call x10, Pallas kernels, near_call(): pl.pallas_call(kernel, out_shape=out_shape, compiler_params=params, **kwa...  6.66 us
    ppermute x4, waiting for transfers between devices, sections_across(): return lax.ppermute(value, ('pp', 'ep'), pairs)  5 us
    ppermute x1, starting transfers between devices, passed_along(): lax.ppermute(value, axis, [(i, (i + by) % size) for i in range(size)])  3 us
  transfers between devices with their start and end apart: 18, of which 10 were waited for; matrix products, arithmetic and copies ran while one was open for 1% of the time, Pallas kernels for 9%

profile of v6, /device:TPU:0, one launch (start us, length us, event | category | flops | bytes accessed | tf_op | source)
XLA Modules:
  0.0 53.3 jit_solution(2619939263512900393)
XLA Ops:
  0.7 3.0 %collective-permute-start.3 = (s32[8,128]{1,0:T(8,128)}, s32[8,128]{1,0:T(8,128)S(1)}, u32[]{:S(2)}, u32[]{:S(2)}) collective-permute-start(s32[8,128]{1,0:T(8,128)} %bitcast.35), channel_id=1, source_target_pairs={{0,16},{16,0},{1,17},{17,1},{2,18},{18,2},{3,19},{19,3},{4,20},{20... | collective-permute-start | bytes 12296 | tf_op jit(solution)/shard_map/ppermute | solution.py:32
  3.7 1.7 %pick_inputs.1 = (bf16[8,5120]{1,0:T(8,128)(2,1)S(1)}, f32[8,128]{1,0:T(8,128)S(1)}, f32[8,128]{1,0:T(8,128)S(1)}, bf16[128,4096]{1,0:T(8,128)(2,1)S(1)}) custom-call(s32[8,128]{1,0:T(8,128)} %bitcast.36, f32[8,128]{1,0:T(8,128)} %bitcast.34, bf16[128,4096]{1,0:T(8,128)(2,1)} %bitcast.32, bf16[128,4096]{1,0:T(8,128)(2,1)} %bitcast.33), custom_call_target="tpu_custom_call" | custom-call | tf_op jit(solution)/shard_map/pick_inputs/pallas_call | solution.py:153
  5.4 2.7 %collective-permute-start = (bf16[8,5120]{1,0:T(8,128)(2,1)S(1)}, bf16[8,5120]{1,0:T(8,128)(2,1)S(1)}, u32[]{:S(2)}, u32[]{:S(2)}) collective-permute-start(bf16[8,5120]{1,0:T(8,128)(2,1)S(1)} %get-tuple-element.30.own), channel_id=1, source_target_pairs={{0,8},{1,9},{2,10},{3,11},{4,12},{5,13},{6,14},{7,15},{8,0},{9,1},... | collective-permute-start | bytes 245768 | tf_op jit(solution)/shard_map/ppermute | solution.py:440
  8.2 0.4 pick_grads.1
  8.6 0.6 %collective-permute-start.4 = (bf16[8,5504]{1,0:T(8,128)(2,1)S(1)}, bf16[8,5504]{1,0:T(8,128)(2,1)S(1)}, u32[]{:S(2)}, u32[]{:S(2)}) collective-permute-start(bf16[8,5504]{1,0:T(8,128)(2,1)S(1)} %get-tuple-element.33), channel_id=1, source_target_pairs={{0,16},{1,17},{2,18},{3,19},{4,20},{5,21},{6,22},{7,23},{8,24},{9,... | collective-permute-start | bytes 264200 | tf_op jit(solution)/shard_map/ppermute | solution.py:446
  9.2 1.3 %collective-permute-start.5 = (bf16[8,5120]{1,0:T(8,128)(2,1)S(1)}, bf16[8,5120]{1,0:T(8,128)(2,1)S(1)}, u32[]{:S(2)}, u32[]{:S(2)}) collective-permute-start(bf16[8,5120]{1,0:T(8,128)(2,1)S(1)} %get-tuple-element.34), channel_id=1, source_target_pairs={{0,24},{1,25},{2,26},{3,27},{4,28},{5,29},{6,30},{7,31},{8,16},{9,... | collective-permute-start | bytes 245768 | tf_op jit(solution)/shard_map/ppermute | solution.py:446
  10.5 1.7 %collective-permute-done.z2 = bf16[8,5120]{1,0:T(8,128)(2,1)S(1)} collective-permute-done((bf16[8,5120]{1,0:T(8,128)(2,1)S(1)}, bf16[8,5120]{1,0:T(8,128)(2,1)S(1)}, u32[]{:S(2)}, u32[]{:S(2)}) %collective-permute-start) | collective-permute-done | bytes 81952 | tf_op jit(solution)/shard_map/ppermute | solution.py:440
  12.1 1.6 %collective-permute-start.1 = (bf16[2,8,5120]{2,1,0:T(8,128)(2,1)S(1)}, bf16[2,8,5120]{2,1,0:T(8,128)(2,1)S(1)}, u32[]{:S(2)}, u32[]{:S(2)}) collective-permute-start(bf16[2,8,5120]{2,1,0:T(8,128)(2,1)S(1)} %pad_maximum_fusion.3), channel_id=1, source_target_pairs={{0,2},{1,3},{2,0},{3,1},{4,6},{5,7},{6,4},{7,5},{8,10},{9,11},{10,... | collective-permute-start | bytes 491528 | tf_op jit(solution)/shard_map/ppermute | solution.py:440
  13.7 0.3 collective-permute-done.4.with_ref.refs_0_
  14.0 1.4 %collective-permute-done.5.refs_1_ = bf16[8,5120]{1,0:T(8,128)(2,1)S(1)} collective-permute-done((bf16[8,5120]{1,0:T(8,128)(2,1)S(1)}, bf16[8,5120]{1,0:T(8,128)(2,1)S(1)}, u32[]{:S(2)}, u32[]{:S(2)}) %collective-permute-start.5) | collective-permute-done | bytes 81952 | tf_op jit(solution)/shard_map/ppermute | solution.py:446
  15.5 1.6 %collective-permute-start.6 = (bf16[2,8,5120]{2,1,0:T(8,128)(2,1)S(1)}, bf16[2,8,5120]{2,1,0:T(8,128)(2,1)S(1)}, u32[]{:S(2)}, u32[]{:S(2)}) collective-permute-start(bf16[2,8,5120]{2,1,0:T(8,128)(2,1)S(1)} %pad_maximum_fusion.4), channel_id=1, source_target_pairs={{0,4},{1,5},{2,6},{3,7},{4,0},{5,1},{6,2},{7,3},{8,12},{9,13},{10,... | collective-permute-start | bytes 491528 | tf_op jit(solution)/shard_map/ppermute | solution.py:440
  17.1 0.5 collective-permute-done.1.y_refs
  17.5 3.0 %collective-permute-start.2 = (bf16[2,8,5120]{2,1,0:T(8,128)(2,1)S(1)}, bf16[2,8,5120]{2,1,0:T(8,128)(2,1)S(1)}, u32[]{:S(2)}, u32[]{:S(2)}) collective-permute-start(bf16[2,8,5120]{2,1,0:T(8,128)(2,1)S(1)} %collective-permute-done.1.y_refs), channel_id=1, source_target_pairs={{0,4},{1,5},{2,6},{3,7},{4,0},{5,1},{6,2},{7,3},{8,12},{9,13},{10,... | collective-permute-start | bytes 491528 | tf_op jit(solution)/shard_map/ppermute | solution.py:440
  20.7 1.6 %collective-permute-start.7 = (bf16[2,8,5120]{2,1,0:T(8,128)(2,1)S(1)}, bf16[2,8,5120]{2,1,0:T(8,128)(2,1)S(1)}, u32[]{:S(2)}, u32[]{:S(2)}) collective-permute-start(bf16[2,8,5120]{2,1,0:T(8,128)(2,1)S(1)} %pad_maximum_fusion.4), channel_id=1, source_target_pairs={{0,2},{1,3},{2,0},{3,1},{4,6},{5,7},{6,4},{7,5},{8,10},{9,11},{10,... | collective-permute-start | bytes 491528 | tf_op jit(solution)/shard_map/ppermute | solution.py:440
  22.3 0.3 collective-permute-done.6.refs_2_
  22.6 0.4 back_rows.1
  23.0 1.7 %collective-permute-start.8 = (bf16[2,8,5120]{2,1,0:T(8,128)(2,1)S(1)}, bf16[2,8,5120]{2,1,0:T(8,128)(2,1)S(1)}, u32[]{:S(2)}, u32[]{:S(2)}) collective-permute-start(bf16[2,8,5120]{2,1,0:T(8,128)(2,1)S(1)} %collective-permute-done.6.refs_2_), channel_id=1, source_target_pairs={{0,2},{1,3},{2,0},{3,1},{4,6},{5,7},{6,4},{7,5},{8,10},{9,11},{10,... | collective-permute-start | bytes 491528 | tf_op jit(solution)/shard_map/ppermute | solution.py:440
  24.6 1.5 %collective-permute-done.2.high = bf16[2,8,5120]{2,1,0:T(8,128)(2,1)S(1)} collective-permute-done((bf16[2,8,5120]{2,1,0:T(8,128)(2,1)S(1)}, bf16[2,8,5120]{2,1,0:T(8,128)(2,1)S(1)}, u32[]{:S(2)}, u32[]{:S(2)}) %collective-permute-start.2) | collective-permute-done | bytes 163872 | tf_op jit(solution)/shard_map/ppermute | solution.py:440
  26.4 2.3 %collective-permute-done.10.low = bf16[2,8,5120]{2,1,0:T(8,128)(2,1)S(1)} collective-permute-done((bf16[2,8,5120]{2,1,0:T(8,128)(2,1)S(1)}, bf16[2,8,5120]{2,1,0:T(8,128)(2,1)S(1)}, u32[]{:S(2)}, u32[]{:S(2)}) %collective-permute-start.10) | collective-permute-done | bytes 163872 | tf_op jit(solution)/shard_map/ppermute | solution.py:440
  28.7 0.8 %expert_forward.1.refs_7_ = f32[128,256]{1,0:T(8,128)S(1)} custom-call(bf16[8,5120]{1,0:T(8,128)(2,1)S(1)} %get-tuple-element.30.own, bf16[8,5120]{1,0:T(8,128)(2,1)S(1)} %collective-permute-done.z2, bf16[2,8,5120]{2,1,0:T(8,128)(2,1)S(1)} %collective-permute-done.1.y_refs, bf16[2,8,5120]{2,1,0:T(8,128)(2,1)S(1)} %collective-permute-done.10.low, ...), custom_call_target="tpu_custom_call" | custom-call | tf_op jit(solution)/shard_map/expert_forward/pallas_call | solution.py:153
  29.6 1.3 %expert_backward.1 = (bf16[4,8,2688]{2,1,0:T(8,128)(2,1)S(1)}, bf16[4,8,2688]{2,1,0:T(8,128)(2,1)S(1)}, bf16[4,8,2560]{2,1,0:T(8,128)(2,1)S(1)}, bf16[4,8,2560]{2,1,0:T(8,128)(2,1)S(1)}) custom-call(bf16[8,5504]{1,0:T(8,128)(2,1)S(1)} %collective-permute-done.4.with_ref.refs_0_, bf16[8,5120]{1,0:T(8,128)(2,1)S(1)} %collective-permute-done.5.refs_1_, ...), custom_call_target="tpu_custom_call" | custom-call | tf_op jit(solution)/shard_map/expert_backward/pallas_call | solution.py:153
  30.9 0.6 %collective-permute-start.11 = (bf16[4,8,2688]{2,1,0:T(8,128)(2,1)S(1)}, bf16[4,8,2688]{2,1,0:T(8,128)(2,1)S(1)}, u32[]{:S(2)}, u32[]{:S(2)}) collective-permute-start(bf16[4,8,2688]{2,1,0:T(8,128)(2,1)S(1)} %get-tuple-element.44), channel_id=1, source_target_pairs={{0,2},{1,3},{2,0},{3,1},{4,6},{5,7},{6,4},{7,5},{8,10},{9,11},{10,... | collective-permute-start | bytes 516104 | tf_op jit(solution)/shard_map/ppermute | solution.py:440
  31.5 1.7 %collective-permute-start.13 = (bf16[4,8,2560]{2,1,0:T(8,128)(2,1)S(1)}, bf16[4,8,2560]{2,1,0:T(8,128)(2,1)S(1)}, u32[]{:S(2)}, u32[]{:S(2)}) collective-permute-start(bf16[4,8,2560]{2,1,0:T(8,128)(2,1)S(1)} %get-tuple-element.48), channel_id=1, source_target_pairs={{0,4},{1,5},{2,6},{3,7},{4,0},{5,1},{6,2},{7,3},{8,12},{9,13},{10,... | collective-permute-start | bytes 491528 | tf_op jit(solution)/shard_map/ppermute | solution.py:440
  33.2 3.2 %collective-permute-done.11.got_ref = bf16[4,8,2688]{2,1,0:T(8,128)(2,1)S(1)} collective-permute-done((bf16[4,8,2688]{2,1,0:T(8,128)(2,1)S(1)}, bf16[4,8,2688]{2,1,0:T(8,128)(2,1)S(1)}, u32[]{:S(2)}, u32[]{:S(2)}) %collective-permute-start.11) | collective-permute-done | bytes 172064 | tf_op jit(solution)/shard_map/ppermute | solution.py:440
  36.5 2.0 %collective-permute-start.12 = (bf16[2,8,2816]{2,1,0:T(8,128)(2,1)S(1)}, bf16[2,8,2816]{2,1,0:T(8,128)(2,1)S(1)}, u32[]{:S(2)}, u32[]{:S(2)}) collective-permute-start(bf16[2,8,2816]{2,1,0:T(8,128)(2,1)S(1)} %get-tuple-element.46), channel_id=1, source_target_pairs={{0,4},{1,5},{2,6},{3,7},{4,0},{5,1},{6,2},{7,3},{8,12},{9,13},{10,... | collective-permute-start | bytes 270344 | tf_op jit(solution)/shard_map/ppermute | solution.py:440
  38.6 0.4 collective-permute-start.14
  39.0 4.2 %collective-permute-done.14.got_b = bf16[2,8,2560]{2,1,0:T(8,128)(2,1)S(1)} collective-permute-done((bf16[2,8,2560]{2,1,0:T(8,128)(2,1)S(1)}, bf16[2,8,2560]{2,1,0:T(8,128)(2,1)S(1)}, u32[]{:S(2)}, u32[]{:S(2)}) %collective-permute-start.14) | collective-permute-done | bytes 81952 | tf_op jit(solution)/shard_map/ppermute | solution.py:440
  43.2 0.8 %collective-permute-start.15 = (bf16[8,5120]{1,0:T(8,128)(2,1)S(1)}, bf16[8,5120]{1,0:T(8,128)(2,1)S(1)}, u32[]{:S(2)}, u32[]{:S(2)}) collective-permute-start(bf16[8,5120]{1,0:T(8,128)(2,1)S(1)} %get-tuple-element.51), channel_id=1, source_target_pairs={{0,16},{1,17},{2,18},{3,19},{4,20},{5,21},{6,22},{7,23},{8,24},{9,... | collective-permute-start | bytes 245768 | tf_op jit(solution)/shard_map/ppermute | solution.py:446
  43.9 4.1 %collective-permute-start.16 = (bf16[8,5120]{1,0:T(8,128)(2,1)S(1)}, bf16[8,5120]{1,0:T(8,128)(2,1)S(1)}, u32[]{:S(2)}, u32[]{:S(2)}) collective-permute-start(bf16[8,5120]{1,0:T(8,128)(2,1)S(1)} %get-tuple-element.52), channel_id=1, source_target_pairs={{0,24},{1,25},{2,26},{3,27},{4,28},{5,29},{6,30},{7,31},{8,16},{9,... | collective-permute-start | bytes 245768 | tf_op jit(solution)/shard_map/ppermute | solution.py:446
  48.0 3.3 %collective-permute-done.16.two_ref = bf16[8,5120]{1,0:T(8,128)(2,1)S(1)} collective-permute-done((bf16[8,5120]{1,0:T(8,128)(2,1)S(1)}, bf16[8,5120]{1,0:T(8,128)(2,1)S(1)}, u32[]{:S(2)}, u32[]{:S(2)}) %collective-permute-start.16) | collective-permute-done | bytes 81952 | tf_op jit(solution)/shard_map/ppermute | solution.py:446
  51.3 1.3 %final_rows.1 = (bf16[128,4096]{1,0:T(8,128)(2,1)}, f32[8,128]{1,0:T(8,128)S(1)}) custom-call(bf16[4,128,32]{2,1,0:T(8,128)(2,1)S(1)} %get-tuple-element.39.back_ref, f32[8,256]{1,0:T(8,128)S(1)} %get-tuple-element.40.scale_ref, bf16[8,5120]{1,0:T(8,128)(2,1)S(1)} %collective-permute-done.15.one_ref, bf16[8,5120]{1,0:T(8,128)(2,1)S(1)} %collective-permute-done.16.two_ref, ...), custom_call_target="tpu_custom_call" | custom-call | tf_op jit(solution)/shard_map/final_rows/pallas_call | solution.py:153
  52.6 0.7 %weight_out.1 = f32[8,128]{1,0:T(8,128)} custom-call(f32[8,128]{1,0:T(8,128)S(1)} %get-tuple-element.54.slot_ref, f32[8,128]{1,0:T(8,128)S(1)} %get-tuple-element.55.own_tile, f32[8,128]{1,0:T(8,128)S(1)} %collective-permute-done.17.got_tile, f32[8,128]{1,0:T(8,128)S(1)} %get-tuple-element.57.after_ref), custom_call_target="tpu_custom_call" | custom-call | tf_op jit(solution)/shard_map/weight_out/pallas_call | solution.py:153
  (28 shorter events, 0.9 us)
Async XLA Ops:
  0.6 7.4 %copy-start.2 = (bf16[1,64,4096]{2,1,0:T(8,128)(2,1)S(1)}, bf16[1,64,4096]{2,1,0:T(8,128)(2,1)}, u32[]{:S(2)}) copy-start(bf16[1,64,4096]{2,1,0:T(8,128)(2,1)} %param.11) | copy-start | bytes 1572868
  0.6 7.4 %copy-start.1 = (bf16[1,64,4096]{2,1,0:T(8,128)(2,1)S(1)}, bf16[1,64,4096]{2,1,0:T(8,128)(2,1)}, u32[]{:S(2)}) copy-start(bf16[1,64,4096]{2,1,0:T(8,128)(2,1)} %param.12) | copy-start | bytes 1572868
  0.7 7.4 %copy-start = (bf16[1,64,4096]{2,1,0:T(8,128)(2,1)S(1)}, bf16[1,64,4096]{2,1,0:T(8,128)(2,1)}, u32[]{:S(2)}) copy-start(bf16[1,64,4096]{2,1,0:T(8,128)(2,1)} %param.13) | copy-start | bytes 1572868
  0.7 7.5 %collective-permute-start.3 = (s32[8,128]{1,0:T(8,128)}, s32[8,128]{1,0:T(8,128)S(1)}, u32[]{:S(2)}, u32[]{:S(2)}) collective-permute-start(s32[8,128]{1,0:T(8,128)} %bitcast.35), channel_id=1, source_target_pairs={{0,16},{16,0},{1,17},{17,1},{2,18},{18,2},{3,19},{19,3},{4,20},{20... | collective-permute-start | bytes 12296 | tf_op jit(solution)/shard_map/ppermute | solution.py:32
  5.4 6.8 %collective-permute-start = (bf16[8,5120]{1,0:T(8,128)(2,1)S(1)}, bf16[8,5120]{1,0:T(8,128)(2,1)S(1)}, u32[]{:S(2)}, u32[]{:S(2)}) collective-permute-start(bf16[8,5120]{1,0:T(8,128)(2,1)S(1)} %get-tuple-element.30.own), channel_id=1, source_target_pairs={{0,8},{1,9},{2,10},{3,11},{4,12},{5,13},{6,14},{7,15},{8,0},{9,1},... | collective-permute-start | bytes 245768 | tf_op jit(solution)/shard_map/ppermute | solution.py:440
  8.6 5.4 %collective-permute-start.4 = (bf16[8,5504]{1,0:T(8,128)(2,1)S(1)}, bf16[8,5504]{1,0:T(8,128)(2,1)S(1)}, u32[]{:S(2)}, u32[]{:S(2)}) collective-permute-start(bf16[8,5504]{1,0:T(8,128)(2,1)S(1)} %get-tuple-element.33), channel_id=1, source_target_pairs={{0,16},{1,17},{2,18},{3,19},{4,20},{5,21},{6,22},{7,23},{8,24},{9,... | collective-permute-start | bytes 264200 | tf_op jit(solution)/shard_map/ppermute | solution.py:446
  9.2 6.3 %collective-permute-start.5 = (bf16[8,5120]{1,0:T(8,128)(2,1)S(1)}, bf16[8,5120]{1,0:T(8,128)(2,1)S(1)}, u32[]{:S(2)}, u32[]{:S(2)}) collective-permute-start(bf16[8,5120]{1,0:T(8,128)(2,1)S(1)} %get-tuple-element.34), channel_id=1, source_target_pairs={{0,24},{1,25},{2,26},{3,27},{4,28},{5,29},{6,30},{7,31},{8,16},{9,... | collective-permute-start | bytes 245768 | tf_op jit(solution)/shard_map/ppermute | solution.py:446
  12.1 5.4 %collective-permute-start.1 = (bf16[2,8,5120]{2,1,0:T(8,128)(2,1)S(1)}, bf16[2,8,5120]{2,1,0:T(8,128)(2,1)S(1)}, u32[]{:S(2)}, u32[]{:S(2)}) collective-permute-start(bf16[2,8,5120]{2,1,0:T(8,128)(2,1)S(1)} %pad_maximum_fusion.3), channel_id=1, source_target_pairs={{0,2},{1,3},{2,0},{3,1},{4,6},{5,7},{6,4},{7,5},{8,10},{9,11},{10,... | collective-permute-start | bytes 491528 | tf_op jit(solution)/shard_map/ppermute | solution.py:440
  13.7 12.4 %collective-permute-start.9 = (bf16[3,64,4096]{2,1,0:T(8,128)(2,1)S(1)}, bf16[3,64,4096]{2,1,0:T(8,128)(2,1)S(1)}, u32[]{:S(2)}, u32[]{:S(2)}) collective-permute-start(bf16[3,64,4096]{2,1,0:T(8,128)(2,1)S(1)} %pad_maximum_fusion.1), channel_id=1, source_target_pairs={{0,1},{1,0},{2,3},{3,2},{4,5},{5,4},{6,7},{7,6},{8,9},{9,8},{10,11... | collective-permute-start | bytes 4718600 | tf_op jit(solution)/shard_map/ppermute | solution.py:440
  15.5 7.1 %collective-permute-start.6 = (bf16[2,8,5120]{2,1,0:T(8,128)(2,1)S(1)}, bf16[2,8,5120]{2,1,0:T(8,128)(2,1)S(1)}, u32[]{:S(2)}, u32[]{:S(2)}) collective-permute-start(bf16[2,8,5120]{2,1,0:T(8,128)(2,1)S(1)} %pad_maximum_fusion.4), channel_id=1, source_target_pairs={{0,4},{1,5},{2,6},{3,7},{4,0},{5,1},{6,2},{7,3},{8,12},{9,13},{10,... | collective-permute-start | bytes 491528 | tf_op jit(solution)/shard_map/ppermute | solution.py:440
  17.5 8.6 %collective-permute-start.2 = (bf16[2,8,5120]{2,1,0:T(8,128)(2,1)S(1)}, bf16[2,8,5120]{2,1,0:T(8,128)(2,1)S(1)}, u32[]{:S(2)}, u32[]{:S(2)}) collective-permute-start(bf16[2,8,5120]{2,1,0:T(8,128)(2,1)S(1)} %collective-permute-done.1.y_refs), channel_id=1, source_target_pairs={{0,4},{1,5},{2,6},{3,7},{4,0},{5,1},{6,2},{7,3},{8,12},{9,13},{10,... | collective-permute-start | bytes 491528 | tf_op jit(solution)/shard_map/ppermute | solution.py:440
  20.6 8.1 %collective-permute-start.10 = (bf16[2,8,5120]{2,1,0:T(8,128)(2,1)S(1)}, bf16[2,8,5120]{2,1,0:T(8,128)(2,1)S(1)}, u32[]{:S(2)}, u32[]{:S(2)}) collective-permute-start(bf16[2,8,5120]{2,1,0:T(8,128)(2,1)S(1)} %pad_maximum_fusion.3), channel_id=1, source_target_pairs={{0,4},{1,5},{2,6},{3,7},{4,0},{5,1},{6,2},{7,3},{8,12},{9,13},{10,... | collective-permute-start | bytes 491528 | tf_op jit(solution)/shard_map/ppermute | solution.py:440
  20.7 8.9 %collective-permute-start.7 = (bf16[2,8,5120]{2,1,0:T(8,128)(2,1)S(1)}, bf16[2,8,5120]{2,1,0:T(8,128)(2,1)S(1)}, u32[]{:S(2)}, u32[]{:S(2)}) collective-permute-start(bf16[2,8,5120]{2,1,0:T(8,128)(2,1)S(1)} %pad_maximum_fusion.4), channel_id=1, source_target_pairs={{0,2},{1,3},{2,0},{3,1},{4,6},{5,7},{6,4},{7,5},{8,10},{9,11},{10,... | collective-permute-start | bytes 491528 | tf_op jit(solution)/shard_map/ppermute | solution.py:440
  23.0 6.6 %collective-permute-start.8 = (bf16[2,8,5120]{2,1,0:T(8,128)(2,1)S(1)}, bf16[2,8,5120]{2,1,0:T(8,128)(2,1)S(1)}, u32[]{:S(2)}, u32[]{:S(2)}) collective-permute-start(bf16[2,8,5120]{2,1,0:T(8,128)(2,1)S(1)} %collective-permute-done.6.refs_2_), channel_id=1, source_target_pairs={{0,2},{1,3},{2,0},{3,1},{4,6},{5,7},{6,4},{7,5},{8,10},{9,11},{10,... | collective-permute-start | bytes 491528 | tf_op jit(solution)/shard_map/ppermute | solution.py:440
  30.9 5.6 %collective-permute-start.11 = (bf16[4,8,2688]{2,1,0:T(8,128)(2,1)S(1)}, bf16[4,8,2688]{2,1,0:T(8,128)(2,1)S(1)}, u32[]{:S(2)}, u32[]{:S(2)}) collective-permute-start(bf16[4,8,2688]{2,1,0:T(8,128)(2,1)S(1)} %get-tuple-element.44), channel_id=1, source_target_pairs={{0,2},{1,3},{2,0},{3,1},{4,6},{5,7},{6,4},{7,5},{8,10},{9,11},{10,... | collective-permute-start | bytes 516104 | tf_op jit(solution)/shard_map/ppermute | solution.py:440
  31.5 7.1 %collective-permute-start.13 = (bf16[4,8,2560]{2,1,0:T(8,128)(2,1)S(1)}, bf16[4,8,2560]{2,1,0:T(8,128)(2,1)S(1)}, u32[]{:S(2)}, u32[]{:S(2)}) collective-permute-start(bf16[4,8,2560]{2,1,0:T(8,128)(2,1)S(1)} %get-tuple-element.48), channel_id=1, source_target_pairs={{0,4},{1,5},{2,6},{3,7},{4,0},{5,1},{6,2},{7,3},{8,12},{9,13},{10,... | collective-permute-start | bytes 491528 | tf_op jit(solution)/shard_map/ppermute | solution.py:440
  36.5 6.6 %collective-permute-start.12 = (bf16[2,8,2816]{2,1,0:T(8,128)(2,1)S(1)}, bf16[2,8,2816]{2,1,0:T(8,128)(2,1)S(1)}, u32[]{:S(2)}, u32[]{:S(2)}) collective-permute-start(bf16[2,8,2816]{2,1,0:T(8,128)(2,1)S(1)} %get-tuple-element.46), channel_id=1, source_target_pairs={{0,4},{1,5},{2,6},{3,7},{4,0},{5,1},{6,2},{7,3},{8,12},{9,13},{10,... | collective-permute-start | bytes 270344 | tf_op jit(solution)/shard_map/ppermute | solution.py:440
  38.6 4.5 %collective-permute-start.14 = (bf16[2,8,2560]{2,1,0:T(8,128)(2,1)S(1)}, bf16[2,8,2560]{2,1,0:T(8,128)(2,1)S(1)}, u32[]{:S(2)}, u32[]{:S(2)}) collective-permute-start(bf16[2,8,2560]{2,1,0:T(8,128)(2,1)S(1)} %get-tuple-element.50), channel_id=1, source_target_pairs={{0,2},{1,3},{2,0},{3,1},{4,6},{5,7},{6,4},{7,5},{8,10},{9,11},{10,... | collective-permute-start | bytes 245768 | tf_op jit(solution)/shard_map/ppermute | solution.py:440
  43.2 4.9 %collective-permute-start.15 = (bf16[8,5120]{1,0:T(8,128)(2,1)S(1)}, bf16[8,5120]{1,0:T(8,128)(2,1)S(1)}, u32[]{:S(2)}, u32[]{:S(2)}) collective-permute-start(bf16[8,5120]{1,0:T(8,128)(2,1)S(1)} %get-tuple-element.51), channel_id=1, source_target_pairs={{0,16},{1,17},{2,18},{3,19},{4,20},{5,21},{6,22},{7,23},{8,24},{9,... | collective-permute-start | bytes 245768 | tf_op jit(solution)/shard_map/ppermute | solution.py:446
  43.9 7.4 %collective-permute-start.16 = (bf16[8,5120]{1,0:T(8,128)(2,1)S(1)}, bf16[8,5120]{1,0:T(8,128)(2,1)S(1)}, u32[]{:S(2)}, u32[]{:S(2)}) collective-permute-start(bf16[8,5120]{1,0:T(8,128)(2,1)S(1)} %get-tuple-element.52), channel_id=1, source_target_pairs={{0,24},{1,25},{2,26},{3,27},{4,28},{5,29},{6,30},{7,31},{8,16},{9,... | collective-permute-start | bytes 245768 | tf_op jit(solution)/shard_map/ppermute | solution.py:446
  48.0 4.6 %collective-permute-start.17 = (f32[8,128]{1,0:T(8,128)S(1)}, f32[8,128]{1,0:T(8,128)S(1)}, u32[]{:S(2)}, u32[]{:S(2)}) collective-permute-start(f32[8,128]{1,0:T(8,128)S(1)} %get-tuple-element.56), channel_id=1, source_target_pairs={{0,8},{1,9},{2,10},{3,11},{4,12},{5,13},{6,14},{7,15},{8,0},{9,1},... | collective-permute-start | bytes 12296 | tf_op jit(solution)/shard_map/ppermute | solution.py:440

commit v7 on v6

--- a/solution.py
+++ b/solution.py
@@ -310,11 +310,27 @@
     h_ref[...] = against(blocks, gu_ref, rows_ref)
 
 
-def backward_kernel(*refs):
-    g0, g2, z_refs, y_refs, yz_refs, down_ref, gu_ref, h_ref, *outs, rows_ref = refs
-    near_a, far_a, near_b, far_b = outs
+def spread(both, gu_ref, start, places):
     half = gu_ref.shape[1] // 2
     part = half // FOLDS
+    count = MAIN * len(places)
+    quarter = lax.broadcasted_iota(jnp.int32, (count, part), 0) % MAIN // TAIL
+    tails = None
+    for fold in range(FOLDS):
+        span = slice(start + fold * part, start + (fold + 1) * part)
+        value = jnp.dot(both, gu_ref[:, span], preferred_element_type=F32)
+        here = jnp.where(quarter == fold, value[count:], 0.0)
+        tails = here if fold == 0 else tails + here
+        value = value[:count].astype(BF16)
+        for k, (ref, j) in enumerate(places):
+            ref[j, :, fold * part : (fold + 1) * part] = value[MAIN * k : MAIN * (k + 1), :]
+    tails = tails.astype(BF16)
+    for k, (ref, j) in enumerate(places):
+        ref[j, :, half : half + part] = tails[MAIN * k : MAIN * (k + 1), :]
+
+
+def backward_a_kernel(*refs):
+    g0, g2, z_refs, y_refs, yz_refs, down_ref, gu_ref, h_ref, near, far, both_ref, rows_ref = refs
     units = down_ref.shape[0]
     blocks = [g0, z_refs.at[0], g2, z_refs.at[1]]
     blocks += [y_refs.at[0], yz_refs.at[0], y_refs.at[1], yz_refs.at[1]]
@@ -327,22 +343,9 @@
     grad_up = (grad_hidden * swish).astype(BF16)
     grad_gate = (grad_hidden * up * sigmoid * (1.0 + gate * (1.0 - sigmoid))).astype(BF16)
     both = jnp.concatenate([grad_gate, grad_up], axis=1)
-    place_a = [(ref, k) for ref in (near_a, far_a) for k in range(4)]
-    place_b = [((near_b, far_b)[k % 2], k // 2) for k in range(8)]
-    quarter = lax.broadcasted_iota(jnp.int32, (count, part), 0) % MAIN // TAIL
-    for side, places in enumerate((place_a, place_b)):
-        tails = None
-        for fold in range(FOLDS):
-            start = side * half + fold * part
-            value = jnp.dot(both, gu_ref[:, start : start + part], preferred_element_type=F32)
-            here = jnp.where(quarter == fold, value[count:], 0.0)
-            tails = here if fold == 0 else tails + here
-            value = value[:count].astype(BF16)
-            for k, (ref, j) in enumerate(places):
-                ref[j, :, fold * part : (fold + 1) * part] = value[MAIN * k : MAIN * (k + 1), :]
-        tails = tails.astype(BF16)
-        for k, (ref, j) in enumerate(places):
-            ref[j, :, half : half + part] = tails[MAIN * k : MAIN * (k + 1), :]
+    both_ref[...] = both
+    places = [(ref, k) for ref in (near, far) for k in range(4)]
+    spread(both, gu_ref, 0, places)
     weight = jnp.sum(grad_hidden * (swish * up), axis=1, keepdims=True)
     lane = lax.broadcasted_iota(jnp.int32, (count, 128), 1)
     first = lax.broadcasted_iota(jnp.int32, (count, 128), 0) % MAIN < TAIL
@@ -351,8 +354,14 @@
         tile = jnp.where(lane == k, piece[:count], tile)
         tile = jnp.where((lane == k + 3) & first, piece[count:], tile)
     tile = tile.astype(BF16)
-    for k, (ref, j) in enumerate(place_a):
-        ref[j, :, half + part :] = tile[MAIN * k : MAIN * (k + 1), :]
+    full = near.shape[2] - 128
+    for k, (ref, j) in enumerate(places):
+        ref[j, :, full:] = tile[MAIN * k : MAIN * (k + 1), :]
+
+
+def backward_b_kernel(both_ref, gu_ref, near, far):
+    places = [((near, far)[k % 2], k // 2) for k in range(8)]
+    spread(both_ref[...], gu_ref, gu_ref.shape[1] // 2, places)
 
 
 def added(one, two):
@@ -506,6 +515,7 @@
     input_y = across(input_z, Y1)
     input_low = across(input_z, Z1)
     input_high = across(input_y, Z1)
+    grad_z1, grad_y = lax.optimization_barrier((grad_z1, grad_y))
     grad_yz1 = across(grad_z1, Y1)
 
     late_routes, late_with, _ = lax.optimization_barrier((next_routes, grad_z0, grad_z1))
@@ -531,9 +541,9 @@
     )
     side_a = pltpu.VMEM((4, MAIN, half + 128), BF16)
     side_b = pltpu.VMEM((4, MAIN, half), BF16)
-    near_a, far_a, near_b, far_b = near_call(
-        backward_kernel,
-        [side_a, side_a, side_b, side_b],
+    near_a, far_a, both = near_call(
+        backward_a_kernel,
+        [side_a, side_a, pltpu.VMEM((slots, 2 * units), BF16)],
         grad_z0,
         grad_z2,
         grad_z1,
@@ -543,9 +553,12 @@
         gate_up,
         hidden,
         scratch_shapes=[pltpu.VMEM((slots, width), BF16)],
-        name="expert_backward",
+        name="backward_a",
     )
     got_a = across(far_a, Y1)
+    near_b, far_b = near_call(
+        backward_b_kernel, [side_b, side_b], both, gate_up, name="backward_b"
+    )
     got_b = across(far_b, Z1)
     send_a, keep_a = near_call(
         fold_a_kernel, [pltpu.VMEM((2, MAIN, half + 256), BF16)] * 2, near_a, got_a, name="fold_a"
@@ -569,8 +582,8 @@
         [jax.ShapeDtypeStruct((count, width), BF16), tile],
         back,
         scale,
+        got_2,
         got_0,
-        got_2,
         base,
         out_specs=[hbm, pl.BlockSpec(memory_space=pltpu.VMEM)],
         scratch_shapes=[pltpu.VMEM((count, width), BF16), pltpu.SemaphoreType.DMA((FOLDS,))],

time: 53.5 us -> 52.7 us (0.985)
    pallas_call x10 -> x11, Pallas kernels: 6.66 us -> 6.58 us  [near_call(): pl.pallas_call(kernel, out_shape=out_shape, compiler_params=params, **kwa...]
  transfers between devices with their start and end apart: 18 -> 18, of which waited for: 10 -> 12; matrix products, arithmetic and copies ran while one was open for 1% -> 1% of each run, Pallas kernels for 9% -> 9%
where the time goes in v7:
time: 52.7 us; the launch traced here: 52.5 us
  starting transfers between devices  26.1 us (50%)
  waiting for transfers between devices  18.4 us (35%)
  Pallas kernels  6.58 us (12%)
  between operations  0.8 us (2%)
    ppermute x13, starting transfers between devices, across(): return lax.ppermute(value, 'ep', [(i, i ^ bits) for i in range(count)])  16.3 us
    ppermute x13, waiting for transfers between devices, across(): return lax.ppermute(value, 'ep', [(i, i ^ bits) for i in range(count)])  13.7 us
    ppermute x4, starting transfers between devices, sections_across(): return lax.ppermute(value, ('pp', 'ep'), pairs)  6.8 us
    pallas_call x11, Pallas kernels, near_call(): pl.pallas_call(kernel, out_shape=out_shape, compiler_params=params, **kwa...  6.58 us
    ppermute x4, waiting for transfers between devices, sections_across(): return lax.ppermute(value, ('pp', 'ep'), pairs)  4.67 us
    ppermute x1, starting transfers between devices, passed_along(): lax.ppermute(value, axis, [(i, (i + by) % size) for i in range(size)])  3 us
  transfers between devices with their start and end apart: 18, of which 12 were waited for; matrix products, arithmetic and copies ran while one was open for 1% of the time, Pallas kernels for 9%

profile of v7, /device:TPU:0, one launch (start us, length us, event | category | flops | bytes accessed | tf_op | source)
XLA Modules:
  0.0 52.5 jit_solution(15552308761006238748)
XLA Ops:
  0.7 3.0 %collective-permute-start.3 = (s32[8,128]{1,0:T(8,128)}, s32[8,128]{1,0:T(8,128)S(1)}, u32[]{:S(2)}, u32[]{:S(2)}) collective-permute-start(s32[8,128]{1,0:T(8,128)} %bitcast.35), channel_id=1, source_target_pairs={{0,16},{16,0},{1,17},{17,1},{2,18},{18,2},{3,19},{19,3},{4,20},{20... | collective-permute-start | bytes 12296 | tf_op jit(solution)/shard_map/ppermute | solution.py:32
  3.7 1.7 %pick_inputs.1 = (bf16[8,5120]{1,0:T(8,128)(2,1)S(1)}, f32[8,128]{1,0:T(8,128)S(1)}, f32[8,128]{1,0:T(8,128)S(1)}, bf16[128,4096]{1,0:T(8,128)(2,1)S(1)}) custom-call(s32[8,128]{1,0:T(8,128)} %bitcast.36, f32[8,128]{1,0:T(8,128)} %bitcast.34, bf16[128,4096]{1,0:T(8,128)(2,1)} %bitcast.32, bf16[128,4096]{1,0:T(8,128)(2,1)} %bitcast.33), custom_call_target="tpu_custom_call" | custom-call | tf_op jit(solution)/shard_map/pick_inputs/pallas_call | solution.py:153
  5.4 2.7 %collective-permute-start = (bf16[8,5120]{1,0:T(8,128)(2,1)S(1)}, bf16[8,5120]{1,0:T(8,128)(2,1)S(1)}, u32[]{:S(2)}, u32[]{:S(2)}) collective-permute-start(bf16[8,5120]{1,0:T(8,128)(2,1)S(1)} %get-tuple-element.33.own), channel_id=1, source_target_pairs={{0,8},{1,9},{2,10},{3,11},{4,12},{5,13},{6,14},{7,15},{8,0},{9,1},... | collective-permute-start | bytes 245768 | tf_op jit(solution)/shard_map/ppermute | solution.py:449
  8.2 0.4 pick_grads.1
  8.6 0.6 %collective-permute-start.4 = (bf16[8,5504]{1,0:T(8,128)(2,1)S(1)}, bf16[8,5504]{1,0:T(8,128)(2,1)S(1)}, u32[]{:S(2)}, u32[]{:S(2)}) collective-permute-start(bf16[8,5504]{1,0:T(8,128)(2,1)S(1)} %get-tuple-element.36), channel_id=1, source_target_pairs={{0,16},{1,17},{2,18},{3,19},{4,20},{5,21},{6,22},{7,23},{8,24},{9,... | collective-permute-start | bytes 264200 | tf_op jit(solution)/shard_map/ppermute | solution.py:455
  9.2 1.3 %collective-permute-start.5 = (bf16[8,5120]{1,0:T(8,128)(2,1)S(1)}, bf16[8,5120]{1,0:T(8,128)(2,1)S(1)}, u32[]{:S(2)}, u32[]{:S(2)}) collective-permute-start(bf16[8,5120]{1,0:T(8,128)(2,1)S(1)} %get-tuple-element.37), channel_id=1, source_target_pairs={{0,24},{1,25},{2,26},{3,27},{4,28},{5,29},{6,30},{7,31},{8,16},{9,... | collective-permute-start | bytes 245768 | tf_op jit(solution)/shard_map/ppermute | solution.py:455
  10.5 1.7 %collective-permute-done.z2 = bf16[8,5120]{1,0:T(8,128)(2,1)S(1)} collective-permute-done((bf16[8,5120]{1,0:T(8,128)(2,1)S(1)}, bf16[8,5120]{1,0:T(8,128)(2,1)S(1)}, u32[]{:S(2)}, u32[]{:S(2)}) %collective-permute-start) | collective-permute-done | bytes 81952 | tf_op jit(solution)/shard_map/ppermute | solution.py:449
  12.1 1.6 %collective-permute-start.1 = (bf16[2,8,5120]{2,1,0:T(8,128)(2,1)S(1)}, bf16[2,8,5120]{2,1,0:T(8,128)(2,1)S(1)}, u32[]{:S(2)}, u32[]{:S(2)}) collective-permute-start(bf16[2,8,5120]{2,1,0:T(8,128)(2,1)S(1)} %pad_maximum_fusion.3), channel_id=1, source_target_pairs={{0,2},{1,3},{2,0},{3,1},{4,6},{5,7},{6,4},{7,5},{8,10},{9,11},{10,... | collective-permute-start | bytes 491528 | tf_op jit(solution)/shard_map/ppermute | solution.py:449
  14.0 1.4 %collective-permute-done.5.refs_1_ = bf16[8,5120]{1,0:T(8,128)(2,1)S(1)} collective-permute-done((bf16[8,5120]{1,0:T(8,128)(2,1)S(1)}, bf16[8,5120]{1,0:T(8,128)(2,1)S(1)}, u32[]{:S(2)}, u32[]{:S(2)}) %collective-permute-start.5) | collective-permute-done | bytes 81952 | tf_op jit(solution)/shard_map/ppermute | solution.py:455
  15.5 1.6 %collective-permute-start.6 = (bf16[2,8,5120]{2,1,0:T(8,128)(2,1)S(1)}, bf16[2,8,5120]{2,1,0:T(8,128)(2,1)S(1)}, u32[]{:S(2)}, u32[]{:S(2)}) collective-permute-start(bf16[2,8,5120]{2,1,0:T(8,128)(2,1)S(1)} %pad_maximum_fusion.4), channel_id=1, source_target_pairs={{0,4},{1,5},{2,6},{3,7},{4,0},{5,1},{6,2},{7,3},{8,12},{9,13},{10,... | collective-permute-start | bytes 491528 | tf_op jit(solution)/shard_map/ppermute | solution.py:449
  17.1 1.5 %collective-permute-start.7 = (bf16[2,8,5120]{2,1,0:T(8,128)(2,1)S(1)}, bf16[2,8,5120]{2,1,0:T(8,128)(2,1)S(1)}, u32[]{:S(2)}, u32[]{:S(2)}) collective-permute-start(bf16[2,8,5120]{2,1,0:T(8,128)(2,1)S(1)} %pad_maximum_fusion.4), channel_id=1, source_target_pairs={{0,2},{1,3},{2,0},{3,1},{4,6},{5,7},{6,4},{7,5},{8,10},{9,11},{10,... | collective-permute-start | bytes 491528 | tf_op jit(solution)/shard_map/ppermute | solution.py:449
  18.6 2.5 %collective-permute-start.2 = (bf16[2,8,5120]{2,1,0:T(8,128)(2,1)S(1)}, bf16[2,8,5120]{2,1,0:T(8,128)(2,1)S(1)}, u32[]{:S(2)}, u32[]{:S(2)}) collective-permute-start(bf16[2,8,5120]{2,1,0:T(8,128)(2,1)S(1)} %collective-permute-done.1.y_refs), channel_id=1, source_target_pairs={{0,4},{1,5},{2,6},{3,7},{4,0},{5,1},{6,2},{7,3},{8,12},{9,13},{10,... | collective-permute-start | bytes 491528 | tf_op jit(solution)/shard_map/ppermute | solution.py:449
  21.3 1.3 %collective-permute-done.6.refs_2_ = bf16[2,8,5120]{2,1,0:T(8,128)(2,1)S(1)} collective-permute-done((bf16[2,8,5120]{2,1,0:T(8,128)(2,1)S(1)}, bf16[2,8,5120]{2,1,0:T(8,128)(2,1)S(1)}, u32[]{:S(2)}, u32[]{:S(2)}) %collective-permute-start.6) | collective-permute-done | bytes 163872 | tf_op jit(solution)/shard_map/ppermute | solution.py:449
  22.6 0.6 %collective-permute-done.7.refs_3_ = bf16[2,8,5120]{2,1,0:T(8,128)(2,1)S(1)} collective-permute-done((bf16[2,8,5120]{2,1,0:T(8,128)(2,1)S(1)}, bf16[2,8,5120]{2,1,0:T(8,128)(2,1)S(1)}, u32[]{:S(2)}, u32[]{:S(2)}) %collective-permute-start.7) | collective-permute-done | bytes 163872 | tf_op jit(solution)/shard_map/ppermute | solution.py:449
  23.2 0.8 %collective-permute-start.8 = (bf16[2,8,5120]{2,1,0:T(8,128)(2,1)S(1)}, bf16[2,8,5120]{2,1,0:T(8,128)(2,1)S(1)}, u32[]{:S(2)}, u32[]{:S(2)}) collective-permute-start(bf16[2,8,5120]{2,1,0:T(8,128)(2,1)S(1)} %collective-permute-done.6.refs_2_), channel_id=1, source_target_pairs={{0,2},{1,3},{2,0},{3,1},{4,6},{5,7},{6,4},{7,5},{8,10},{9,11},{10,... | collective-permute-start | bytes 491528 | tf_op jit(solution)/shard_map/ppermute | solution.py:449
  23.9 0.4 back_rows.1
  24.3 1.9 %collective-permute-done.2.high = bf16[2,8,5120]{2,1,0:T(8,128)(2,1)S(1)} collective-permute-done((bf16[2,8,5120]{2,1,0:T(8,128)(2,1)S(1)}, bf16[2,8,5120]{2,1,0:T(8,128)(2,1)S(1)}, u32[]{:S(2)}, u32[]{:S(2)}) %collective-permute-start.2) | collective-permute-done | bytes 163872 | tf_op jit(solution)/shard_map/ppermute | solution.py:449
  26.5 2.2 %collective-permute-done.10.low = bf16[2,8,5120]{2,1,0:T(8,128)(2,1)S(1)} collective-permute-done((bf16[2,8,5120]{2,1,0:T(8,128)(2,1)S(1)}, bf16[2,8,5120]{2,1,0:T(8,128)(2,1)S(1)}, u32[]{:S(2)}, u32[]{:S(2)}) %collective-permute-start.10) | collective-permute-done | bytes 163872 | tf_op jit(solution)/shard_map/ppermute | solution.py:449
  28.7 0.8 %expert_forward.1.refs_7_ = f32[128,256]{1,0:T(8,128)S(1)} custom-call(bf16[8,5120]{1,0:T(8,128)(2,1)S(1)} %get-tuple-element.33.own, bf16[8,5120]{1,0:T(8,128)(2,1)S(1)} %collective-permute-done.z2, bf16[2,8,5120]{2,1,0:T(8,128)(2,1)S(1)} %collective-permute-done.1.y_refs, bf16[2,8,5120]{2,1,0:T(8,128)(2,1)S(1)} %collective-permute-done.10.low, ...), custom_call_target="tpu_custom_call" | custom-call | tf_op jit(solution)/shard_map/expert_forward/pallas_call | solution.py:153
  29.6 0.9 %backward_a.1 = (bf16[4,8,2688]{2,1,0:T(8,128)(2,1)S(1)}, bf16[4,8,2688]{2,1,0:T(8,128)(2,1)S(1)}, bf16[128,256]{1,0:T(8,128)(2,1)S(1)}) custom-call(bf16[8,5504]{1,0:T(8,128)(2,1)S(1)} %collective-permute-done.4.with_ref.refs_0_, bf16[8,5120]{1,0:T(8,128)(2,1)S(1)} %collective-permute-done.5.refs_1_, ...), custom_call_target="tpu_custom_call" | custom-call | tf_op jit(solution)/shard_map/backward_a/pallas_call | solution.py:153
  30.5 0.7 %collective-permute-start.11 = (bf16[4,8,2688]{2,1,0:T(8,128)(2,1)S(1)}, bf16[4,8,2688]{2,1,0:T(8,128)(2,1)S(1)}, u32[]{:S(2)}, u32[]{:S(2)}) collective-permute-start(bf16[4,8,2688]{2,1,0:T(8,128)(2,1)S(1)} %get-tuple-element.49), channel_id=1, source_target_pairs={{0,2},{1,3},{2,0},{3,1},{4,6},{5,7},{6,4},{7,5},{8,10},{9,11},{10,... | collective-permute-start | bytes 516104 | tf_op jit(solution)/shard_map/ppermute | solution.py:449
  31.6 1.6 %collective-permute-start.13 = (bf16[4,8,2560]{2,1,0:T(8,128)(2,1)S(1)}, bf16[4,8,2560]{2,1,0:T(8,128)(2,1)S(1)}, u32[]{:S(2)}, u32[]{:S(2)}) collective-permute-start(bf16[4,8,2560]{2,1,0:T(8,128)(2,1)S(1)} %get-tuple-element.54), channel_id=1, source_target_pairs={{0,4},{1,5},{2,6},{3,7},{4,0},{5,1},{6,2},{7,3},{8,12},{9,13},{10,... | collective-permute-start | bytes 491528 | tf_op jit(solution)/shard_map/ppermute | solution.py:449
  33.2 2.8 %collective-permute-done.11.got_ref = bf16[4,8,2688]{2,1,0:T(8,128)(2,1)S(1)} collective-permute-done((bf16[4,8,2688]{2,1,0:T(8,128)(2,1)S(1)}, bf16[4,8,2688]{2,1,0:T(8,128)(2,1)S(1)}, u32[]{:S(2)}, u32[]{:S(2)}) %collective-permute-start.11) | collective-permute-done | bytes 172064 | tf_op jit(solution)/shard_map/ppermute | solution.py:449
  36.1 1.8 %collective-permute-start.12 = (bf16[2,8,2816]{2,1,0:T(8,128)(2,1)S(1)}, bf16[2,8,2816]{2,1,0:T(8,128)(2,1)S(1)}, u32[]{:S(2)}, u32[]{:S(2)}) collective-permute-start(bf16[2,8,2816]{2,1,0:T(8,128)(2,1)S(1)} %get-tuple-element.51), channel_id=1, source_target_pairs={{0,4},{1,5},{2,6},{3,7},{4,0},{5,1},{6,2},{7,3},{8,12},{9,13},{10,... | collective-permute-start | bytes 270344 | tf_op jit(solution)/shard_map/ppermute | solution.py:449
  37.9 1.5 %collective-permute-start.14 = (bf16[2,8,2560]{2,1,0:T(8,128)(2,1)S(1)}, bf16[2,8,2560]{2,1,0:T(8,128)(2,1)S(1)}, u32[]{:S(2)}, u32[]{:S(2)}) collective-permute-start(bf16[2,8,2560]{2,1,0:T(8,128)(2,1)S(1)} %get-tuple-element.56), channel_id=1, source_target_pairs={{0,2},{1,3},{2,0},{3,1},{4,6},{5,7},{6,4},{7,5},{8,10},{9,11},{10,... | collective-permute-start | bytes 245768 | tf_op jit(solution)/shard_map/ppermute | solution.py:449
  39.4 3.0 %collective-permute-done.14.got_b = bf16[2,8,2560]{2,1,0:T(8,128)(2,1)S(1)} collective-permute-done((bf16[2,8,2560]{2,1,0:T(8,128)(2,1)S(1)}, bf16[2,8,2560]{2,1,0:T(8,128)(2,1)S(1)}, u32[]{:S(2)}, u32[]{:S(2)}) %collective-permute-start.14) | collective-permute-done | bytes 81952 | tf_op jit(solution)/shard_map/ppermute | solution.py:449
  42.4 3.3 %collective-permute-start.15 = (bf16[8,5120]{1,0:T(8,128)(2,1)S(1)}, bf16[8,5120]{1,0:T(8,128)(2,1)S(1)}, u32[]{:S(2)}, u32[]{:S(2)}) collective-permute-start(bf16[8,5120]{1,0:T(8,128)(2,1)S(1)} %get-tuple-element.57), channel_id=1, source_target_pairs={{0,24},{1,25},{2,26},{3,27},{4,28},{5,29},{6,30},{7,31},{8,16},{9,... | collective-permute-start | bytes 245768 | tf_op jit(solution)/shard_map/ppermute | solution.py:455
  45.7 1.6 %collective-permute-start.16 = (bf16[8,5120]{1,0:T(8,128)(2,1)S(1)}, bf16[8,5120]{1,0:T(8,128)(2,1)S(1)}, u32[]{:S(2)}, u32[]{:S(2)}) collective-permute-start(bf16[8,5120]{1,0:T(8,128)(2,1)S(1)} %get-tuple-element.58), channel_id=1, source_target_pairs={{0,16},{1,17},{2,18},{3,19},{4,20},{5,21},{6,22},{7,23},{8,24},{9,... | collective-permute-start | bytes 245768 | tf_op jit(solution)/shard_map/ppermute | solution.py:455
  47.4 2.4 %collective-permute-done.15.one_ref = bf16[8,5120]{1,0:T(8,128)(2,1)S(1)} collective-permute-done((bf16[8,5120]{1,0:T(8,128)(2,1)S(1)}, bf16[8,5120]{1,0:T(8,128)(2,1)S(1)}, u32[]{:S(2)}, u32[]{:S(2)}) %collective-permute-start.15) | collective-permute-done | bytes 81952 | tf_op jit(solution)/shard_map/ppermute | solution.py:455
  49.7 0.6 %collective-permute-done.16.two_ref = bf16[8,5120]{1,0:T(8,128)(2,1)S(1)} collective-permute-done((bf16[8,5120]{1,0:T(8,128)(2,1)S(1)}, bf16[8,5120]{1,0:T(8,128)(2,1)S(1)}, u32[]{:S(2)}, u32[]{:S(2)}) %collective-permute-start.16) | collective-permute-done | bytes 81952 | tf_op jit(solution)/shard_map/ppermute | solution.py:455
  50.3 1.3 %final_rows.1 = (bf16[128,4096]{1,0:T(8,128)(2,1)}, f32[8,128]{1,0:T(8,128)S(1)}) custom-call(bf16[4,128,32]{2,1,0:T(8,128)(2,1)S(1)} %get-tuple-element.43.back_ref, f32[8,256]{1,0:T(8,128)S(1)} %get-tuple-element.44.scale_ref, bf16[8,5120]{1,0:T(8,128)(2,1)S(1)} %collective-permute-done.15.one_ref, bf16[8,5120]{1,0:T(8,128)(2,1)S(1)} %collective-permute-done.16.two_ref, ...), custom_call_target="tpu_custom_call" | custom-call | tf_op jit(solution)/shard_map/final_rows/pallas_call | solution.py:153
  51.9 0.7 %weight_out.1 = f32[8,128]{1,0:T(8,128)} custom-call(f32[8,128]{1,0:T(8,128)S(1)} %get-tuple-element.60.slot_ref, f32[8,128]{1,0:T(8,128)S(1)} %get-tuple-element.61.own_tile, f32[8,128]{1,0:T(8,128)S(1)} %collective-permute-done.17.got_tile, f32[8,128]{1,0:T(8,128)S(1)} %get-tuple-element.63.after_ref), custom_call_target="tpu_custom_call" | custom-call | tf_op jit(solution)/shard_map/weight_out/pallas_call | solution.py:153
  (29 shorter events, 1.8 us)
Async XLA Ops:
  0.6 7.4 %copy-start.2 = (bf16[1,64,4096]{2,1,0:T(8,128)(2,1)S(1)}, bf16[1,64,4096]{2,1,0:T(8,128)(2,1)}, u32[]{:S(2)}) copy-start(bf16[1,64,4096]{2,1,0:T(8,128)(2,1)} %param.11) | copy-start | bytes 1572868
  0.6 7.4 %copy-start.1 = (bf16[1,64,4096]{2,1,0:T(8,128)(2,1)S(1)}, bf16[1,64,4096]{2,1,0:T(8,128)(2,1)}, u32[]{:S(2)}) copy-start(bf16[1,64,4096]{2,1,0:T(8,128)(2,1)} %param.12) | copy-start | bytes 1572868
  0.7 7.4 %copy-start = (bf16[1,64,4096]{2,1,0:T(8,128)(2,1)S(1)}, bf16[1,64,4096]{2,1,0:T(8,128)(2,1)}, u32[]{:S(2)}) copy-start(bf16[1,64,4096]{2,1,0:T(8,128)(2,1)} %param.13) | copy-start | bytes 1572868
  0.7 7.5 %collective-permute-start.3 = (s32[8,128]{1,0:T(8,128)}, s32[8,128]{1,0:T(8,128)S(1)}, u32[]{:S(2)}, u32[]{:S(2)}) collective-permute-start(s32[8,128]{1,0:T(8,128)} %bitcast.35), channel_id=1, source_target_pairs={{0,16},{16,0},{1,17},{17,1},{2,18},{18,2},{3,19},{19,3},{4,20},{20... | collective-permute-start | bytes 12296 | tf_op jit(solution)/shard_map/ppermute | solution.py:32
  5.4 6.8 %collective-permute-start = (bf16[8,5120]{1,0:T(8,128)(2,1)S(1)}, bf16[8,5120]{1,0:T(8,128)(2,1)S(1)}, u32[]{:S(2)}, u32[]{:S(2)}) collective-permute-start(bf16[8,5120]{1,0:T(8,128)(2,1)S(1)} %get-tuple-element.33.own), channel_id=1, source_target_pairs={{0,8},{1,9},{2,10},{3,11},{4,12},{5,13},{6,14},{7,15},{8,0},{9,1},... | collective-permute-start | bytes 245768 | tf_op jit(solution)/shard_map/ppermute | solution.py:449
  8.6 5.4 %collective-permute-start.4 = (bf16[8,5504]{1,0:T(8,128)(2,1)S(1)}, bf16[8,5504]{1,0:T(8,128)(2,1)S(1)}, u32[]{:S(2)}, u32[]{:S(2)}) collective-permute-start(bf16[8,5504]{1,0:T(8,128)(2,1)S(1)} %get-tuple-element.36), channel_id=1, source_target_pairs={{0,16},{1,17},{2,18},{3,19},{4,20},{5,21},{6,22},{7,23},{8,24},{9,... | collective-permute-start | bytes 264200 | tf_op jit(solution)/shard_map/ppermute | solution.py:455
  9.2 6.3 %collective-permute-start.5 = (bf16[8,5120]{1,0:T(8,128)(2,1)S(1)}, bf16[8,5120]{1,0:T(8,128)(2,1)S(1)}, u32[]{:S(2)}, u32[]{:S(2)}) collective-permute-start(bf16[8,5120]{1,0:T(8,128)(2,1)S(1)} %get-tuple-element.37), channel_id=1, source_target_pairs={{0,24},{1,25},{2,26},{3,27},{4,28},{5,29},{6,30},{7,31},{8,16},{9,... | collective-permute-start | bytes 245768 | tf_op jit(solution)/shard_map/ppermute | solution.py:455
  12.1 6.5 %collective-permute-start.1 = (bf16[2,8,5120]{2,1,0:T(8,128)(2,1)S(1)}, bf16[2,8,5120]{2,1,0:T(8,128)(2,1)S(1)}, u32[]{:S(2)}, u32[]{:S(2)}) collective-permute-start(bf16[2,8,5120]{2,1,0:T(8,128)(2,1)S(1)} %pad_maximum_fusion.3), channel_id=1, source_target_pairs={{0,2},{1,3},{2,0},{3,1},{4,6},{5,7},{6,4},{7,5},{8,10},{9,11},{10,... | collective-permute-start | bytes 491528 | tf_op jit(solution)/shard_map/ppermute | solution.py:449
  13.7 12.4 %collective-permute-start.9 = (bf16[3,64,4096]{2,1,0:T(8,128)(2,1)S(1)}, bf16[3,64,4096]{2,1,0:T(8,128)(2,1)S(1)}, u32[]{:S(2)}, u32[]{:S(2)}) collective-permute-start(bf16[3,64,4096]{2,1,0:T(8,128)(2,1)S(1)} %pad_maximum_fusion.1), channel_id=1, source_target_pairs={{0,1},{1,0},{2,3},{3,2},{4,5},{5,4},{6,7},{7,6},{8,9},{9,8},{10,11... | collective-permute-start | bytes 4718600 | tf_op jit(solution)/shard_map/ppermute | solution.py:449
  15.5 7.1 %collective-permute-start.6 = (bf16[2,8,5120]{2,1,0:T(8,128)(2,1)S(1)}, bf16[2,8,5120]{2,1,0:T(8,128)(2,1)S(1)}, u32[]{:S(2)}, u32[]{:S(2)}) collective-permute-start(bf16[2,8,5120]{2,1,0:T(8,128)(2,1)S(1)} %pad_maximum_fusion.4), channel_id=1, source_target_pairs={{0,4},{1,5},{2,6},{3,7},{4,0},{5,1},{6,2},{7,3},{8,12},{9,13},{10,... | collective-permute-start | bytes 491528 | tf_op jit(solution)/shard_map/ppermute | solution.py:449
  17.1 6.1 %collective-permute-start.7 = (bf16[2,8,5120]{2,1,0:T(8,128)(2,1)S(1)}, bf16[2,8,5120]{2,1,0:T(8,128)(2,1)S(1)}, u32[]{:S(2)}, u32[]{:S(2)}) collective-permute-start(bf16[2,8,5120]{2,1,0:T(8,128)(2,1)S(1)} %pad_maximum_fusion.4), channel_id=1, source_target_pairs={{0,2},{1,3},{2,0},{3,1},{4,6},{5,7},{6,4},{7,5},{8,10},{9,11},{10,... | collective-permute-start | bytes 491528 | tf_op jit(solution)/shard_map/ppermute | solution.py:449
  18.6 7.6 %collective-permute-start.2 = (bf16[2,8,5120]{2,1,0:T(8,128)(2,1)S(1)}, bf16[2,8,5120]{2,1,0:T(8,128)(2,1)S(1)}, u32[]{:S(2)}, u32[]{:S(2)}) collective-permute-start(bf16[2,8,5120]{2,1,0:T(8,128)(2,1)S(1)} %collective-permute-done.1.y_refs), channel_id=1, source_target_pairs={{0,4},{1,5},{2,6},{3,7},{4,0},{5,1},{6,2},{7,3},{8,12},{9,13},{10,... | collective-permute-start | bytes 491528 | tf_op jit(solution)/shard_map/ppermute | solution.py:449
  21.2 7.5 %collective-permute-start.10 = (bf16[2,8,5120]{2,1,0:T(8,128)(2,1)S(1)}, bf16[2,8,5120]{2,1,0:T(8,128)(2,1)S(1)}, u32[]{:S(2)}, u32[]{:S(2)}) collective-permute-start(bf16[2,8,5120]{2,1,0:T(8,128)(2,1)S(1)} %pad_maximum_fusion.3), channel_id=1, source_target_pairs={{0,4},{1,5},{2,6},{3,7},{4,0},{5,1},{6,2},{7,3},{8,12},{9,13},{10,... | collective-permute-start | bytes 491528 | tf_op jit(solution)/shard_map/ppermute | solution.py:449
  23.2 6.4 %collective-permute-start.8 = (bf16[2,8,5120]{2,1,0:T(8,128)(2,1)S(1)}, bf16[2,8,5120]{2,1,0:T(8,128)(2,1)S(1)}, u32[]{:S(2)}, u32[]{:S(2)}) collective-permute-start(bf16[2,8,5120]{2,1,0:T(8,128)(2,1)S(1)} %collective-permute-done.6.refs_2_), channel_id=1, source_target_pairs={{0,2},{1,3},{2,0},{3,1},{4,6},{5,7},{6,4},{7,5},{8,10},{9,11},{10,... | collective-permute-start | bytes 491528 | tf_op jit(solution)/shard_map/ppermute | solution.py:449
  30.5 5.5 %collective-permute-start.11 = (bf16[4,8,2688]{2,1,0:T(8,128)(2,1)S(1)}, bf16[4,8,2688]{2,1,0:T(8,128)(2,1)S(1)}, u32[]{:S(2)}, u32[]{:S(2)}) collective-permute-start(bf16[4,8,2688]{2,1,0:T(8,128)(2,1)S(1)} %get-tuple-element.49), channel_id=1, source_target_pairs={{0,2},{1,3},{2,0},{3,1},{4,6},{5,7},{6,4},{7,5},{8,10},{9,11},{10,... | collective-permute-start | bytes 516104 | tf_op jit(solution)/shard_map/ppermute | solution.py:449
  31.6 6.3 %collective-permute-start.13 = (bf16[4,8,2560]{2,1,0:T(8,128)(2,1)S(1)}, bf16[4,8,2560]{2,1,0:T(8,128)(2,1)S(1)}, u32[]{:S(2)}, u32[]{:S(2)}) collective-permute-start(bf16[4,8,2560]{2,1,0:T(8,128)(2,1)S(1)} %get-tuple-element.54), channel_id=1, source_target_pairs={{0,4},{1,5},{2,6},{3,7},{4,0},{5,1},{6,2},{7,3},{8,12},{9,13},{10,... | collective-permute-start | bytes 491528 | tf_op jit(solution)/shard_map/ppermute | solution.py:449
  36.1 6.3 %collective-permute-start.12 = (bf16[2,8,2816]{2,1,0:T(8,128)(2,1)S(1)}, bf16[2,8,2816]{2,1,0:T(8,128)(2,1)S(1)}, u32[]{:S(2)}, u32[]{:S(2)}) collective-permute-start(bf16[2,8,2816]{2,1,0:T(8,128)(2,1)S(1)} %get-tuple-element.51), channel_id=1, source_target_pairs={{0,4},{1,5},{2,6},{3,7},{4,0},{5,1},{6,2},{7,3},{8,12},{9,13},{10,... | collective-permute-start | bytes 270344 | tf_op jit(solution)/shard_map/ppermute | solution.py:449
  37.9 4.5 %collective-permute-start.14 = (bf16[2,8,2560]{2,1,0:T(8,128)(2,1)S(1)}, bf16[2,8,2560]{2,1,0:T(8,128)(2,1)S(1)}, u32[]{:S(2)}, u32[]{:S(2)}) collective-permute-start(bf16[2,8,2560]{2,1,0:T(8,128)(2,1)S(1)} %get-tuple-element.56), channel_id=1, source_target_pairs={{0,2},{1,3},{2,0},{3,1},{4,6},{5,7},{6,4},{7,5},{8,10},{9,11},{10,... | collective-permute-start | bytes 245768 | tf_op jit(solution)/shard_map/ppermute | solution.py:449
  42.4 7.3 %collective-permute-start.15 = (bf16[8,5120]{1,0:T(8,128)(2,1)S(1)}, bf16[8,5120]{1,0:T(8,128)(2,1)S(1)}, u32[]{:S(2)}, u32[]{:S(2)}) collective-permute-start(bf16[8,5120]{1,0:T(8,128)(2,1)S(1)} %get-tuple-element.57), channel_id=1, source_target_pairs={{0,24},{1,25},{2,26},{3,27},{4,28},{5,29},{6,30},{7,31},{8,16},{9,... | collective-permute-start | bytes 245768 | tf_op jit(solution)/shard_map/ppermute | solution.py:455
  45.7 4.6 %collective-permute-start.16 = (bf16[8,5120]{1,0:T(8,128)(2,1)S(1)}, bf16[8,5120]{1,0:T(8,128)(2,1)S(1)}, u32[]{:S(2)}, u32[]{:S(2)}) collective-permute-start(bf16[8,5120]{1,0:T(8,128)(2,1)S(1)} %get-tuple-element.58), channel_id=1, source_target_pairs={{0,16},{1,17},{2,18},{3,19},{4,20},{5,21},{6,22},{7,23},{8,24},{9,... | collective-permute-start | bytes 245768 | tf_op jit(solution)/shard_map/ppermute | solution.py:455
  47.4 4.5 %collective-permute-start.17 = (f32[8,128]{1,0:T(8,128)S(1)}, f32[8,128]{1,0:T(8,128)S(1)}, u32[]{:S(2)}, u32[]{:S(2)}) collective-permute-start(f32[8,128]{1,0:T(8,128)S(1)} %get-tuple-element.62), channel_id=1, source_target_pairs={{0,8},{1,9},{2,10},{3,11},{4,12},{5,13},{6,14},{7,15},{8,0},{9,1},... | collective-permute-start | bytes 12296 | tf_op jit(solution)/shard_map/ppermute | solution.py:449

commit v8 on v7

--- a/solution.py
+++ b/solution.py
@@ -305,9 +305,15 @@
     return jnp.concatenate([main, tail.reshape(count, -1)], axis=0)
 
 
-def forward_kernel(own, z2, y_refs, low, high, gu_ref, h_ref, rows_ref):
-    blocks = [own, low.at[0], z2, low.at[1], y_refs.at[0], high.at[0], y_refs.at[1], high.at[1]]
-    h_ref[...] = against(blocks, gu_ref, rows_ref)
+def early_kernel(own, z2, y_refs, gu_ref, h_ref, rows_ref):
+    h_ref[...] = against([own, z2, y_refs.at[0], y_refs.at[1]], gu_ref, rows_ref)
+
+
+def late_kernel(early_ref, low, high, gu_ref, h_ref, rows_ref):
+    late = against([low.at[0], low.at[1], high.at[0], high.at[1]], gu_ref, rows_ref)
+    for k in range(2 * FOLDS * 2):
+        source = early_ref if k % 2 == 0 else late
+        h_ref[MAIN * k : MAIN * (k + 1), :] = source[MAIN * (k // 2) : MAIN * (k // 2 + 1), :]
 
 
 def spread(both, gu_ref, start, places):
@@ -329,13 +335,17 @@
         ref[j, :, half : half + part] = tails[MAIN * k : MAIN * (k + 1), :]
 
 
-def backward_a_kernel(*refs):
-    g0, g2, z_refs, y_refs, yz_refs, down_ref, gu_ref, h_ref, near, far, both_ref, rows_ref = refs
-    units = down_ref.shape[0]
+def grad_hidden_kernel(g0, g2, z_refs, y_refs, yz_refs, down_ref, grad_ref, rows_ref):
     blocks = [g0, z_refs.at[0], g2, z_refs.at[1]]
     blocks += [y_refs.at[0], yz_refs.at[0], y_refs.at[1], yz_refs.at[1]]
-    count = MAIN * len(blocks)
-    grad_hidden = against(blocks, down_ref, rows_ref)
+    grad_ref[...] = against(blocks, down_ref, rows_ref)
+
+
+def backward_a_kernel(*refs):
+    grad_ref, gu_ref, h_ref, near, far, both_ref = refs
+    count = grad_ref.shape[0] // 2
+    units = grad_ref.shape[1]
+    grad_hidden = grad_ref[...]
     gate = h_ref[:, :units]
     up = h_ref[:, units:]
     sigmoid = 1.0 / (1.0 + jnp.exp(-gate))
@@ -527,32 +537,46 @@
         name="back_rows",
     )
     input_high, back, scale = lax.optimization_barrier((input_high, back, scale))
-    hidden = near_call(
-        forward_kernel,
-        pltpu.VMEM((slots, 2 * units), F32),
-        input_block,
-        input_z2,
-        input_y,
-        input_low,
-        input_high,
-        gate_up,
-        scratch_shapes=[pltpu.VMEM((slots, width), BF16)],
-        name="expert_forward",
-    )
-    side_a = pltpu.VMEM((4, MAIN, half + 128), BF16)
-    side_b = pltpu.VMEM((4, MAIN, half), BF16)
-    near_a, far_a, both = near_call(
-        backward_a_kernel,
-        [side_a, side_a, pltpu.VMEM((slots, 2 * units), BF16)],
+    grad_hidden = near_call(
+        grad_hidden_kernel,
+        pltpu.VMEM((slots, units), F32),
         grad_z0,
         grad_z2,
         grad_z1,
         grad_y,
         grad_yz1,
         down,
+        scratch_shapes=[pltpu.VMEM((slots, width), BF16)],
+        name="grad_hidden",
+    )
+    early = near_call(
+        early_kernel,
+        pltpu.VMEM((slots // 2, 2 * units), F32),
+        input_block,
+        input_z2,
+        input_y,
+        gate_up,
+        scratch_shapes=[pltpu.VMEM((slots // 2, width), BF16)],
+        name="forward_early",
+    )
+    hidden = near_call(
+        late_kernel,
+        pltpu.VMEM((slots, 2 * units), F32),
+        early,
+        input_low,
+        input_high,
+        gate_up,
+        scratch_shapes=[pltpu.VMEM((slots // 2, width), BF16)],
+        name="forward_late",
+    )
+    side_a = pltpu.VMEM((4, MAIN, half + 128), BF16)
+    side_b = pltpu.VMEM((4, MAIN, half), BF16)
+    near_a, far_a, both = near_call(
+        backward_a_kernel,
+        [side_a, side_a, pltpu.VMEM((slots, 2 * units), BF16)],
+        grad_hidden,
         gate_up,
         hidden,
-        scratch_shapes=[pltpu.VMEM((slots, width), BF16)],
         name="backward_a",
     )
     got_a = across(far_a, Y1)

time: 52.7 us -> 52 us (0.987)
  waiting for transfers between devices: 18.4 us -> 16.8 us
    ppermute x13, waiting for transfers between devices: 13.7 us -> 11.8 us  [across(): return lax.ppermute(value, 'ep', [(i, i ^ bits) for i in range(count)])]
    pallas_call x11 -> x13, Pallas kernels: 6.58 us -> 7.1 us  [near_call(): pl.pallas_call(kernel, out_shape=out_shape, compiler_params=params, **kwa...]
  transfers between devices with their start and end apart: 18 -> 18, of which waited for: 12 -> 11; matrix products, arithmetic and copies ran while one was open for 1% -> 1% of each run, Pallas kernels for 9% -> 10%
where the time goes in v8:
time: 52 us; the launch traced here: 51.9 us
  starting transfers between devices  26.5 us (51%)
  waiting for transfers between devices  16.8 us (32%)
  Pallas kernels  7.1 us (14%)
  between operations  0.82 us (2%)
    ppermute x13, starting transfers between devices, across(): return lax.ppermute(value, 'ep', [(i, i ^ bits) for i in range(count)])  16.7 us
    ppermute x13, waiting for transfers between devices, across(): return lax.ppermute(value, 'ep', [(i, i ^ bits) for i in range(count)])  11.8 us
    pallas_call x13, Pallas kernels, near_call(): pl.pallas_call(kernel, out_shape=out_shape, compiler_params=params, **kwa...  7.1 us
    ppermute x4, starting transfers between devices, sections_across(): return lax.ppermute(value, ('pp', 'ep'), pairs)  6.8 us
    ppermute x4, waiting for transfers between devices, sections_across(): return lax.ppermute(value, ('pp', 'ep'), pairs)  4.94 us
    ppermute x1, starting transfers between devices, passed_along(): lax.ppermute(value, axis, [(i, (i + by) % size) for i in range(size)])  3 us
  transfers between devices with their start and end apart: 18, of which 11 were waited for; matrix products, arithmetic and copies ran while one was open for 1% of the time, Pallas kernels for 10%

profile of v8, /device:TPU:0, one launch (start us, length us, event | category | flops | bytes accessed | tf_op | source)
XLA Modules:
  0.0 51.9 jit_solution(13251338901435506885)
XLA Ops:
  0.7 3.0 %collective-permute-start.3 = (s32[8,128]{1,0:T(8,128)}, s32[8,128]{1,0:T(8,128)S(1)}, u32[]{:S(2)}, u32[]{:S(2)}) collective-permute-start(s32[8,128]{1,0:T(8,128)} %bitcast.35), channel_id=1, source_target_pairs={{0,16},{16,0},{1,17},{17,1},{2,18},{18,2},{3,19},{19,3},{4,20},{20... | collective-permute-start | bytes 12296 | tf_op jit(solution)/shard_map/ppermute | solution.py:32
  3.7 1.7 %pick_inputs.1 = (bf16[8,5120]{1,0:T(8,128)(2,1)S(1)}, f32[8,128]{1,0:T(8,128)S(1)}, f32[8,128]{1,0:T(8,128)S(1)}, bf16[128,4096]{1,0:T(8,128)(2,1)S(1)}) custom-call(s32[8,128]{1,0:T(8,128)} %bitcast.36, f32[8,128]{1,0:T(8,128)} %bitcast.34, bf16[128,4096]{1,0:T(8,128)(2,1)} %bitcast.32, bf16[128,4096]{1,0:T(8,128)(2,1)} %bitcast.33), custom_call_target="tpu_custom_call" | custom-call | tf_op jit(solution)/shard_map/pick_inputs/pallas_call | solution.py:153
  5.4 2.7 %collective-permute-start = (bf16[8,5120]{1,0:T(8,128)(2,1)S(1)}, bf16[8,5120]{1,0:T(8,128)(2,1)S(1)}, u32[]{:S(2)}, u32[]{:S(2)}) collective-permute-start(bf16[8,5120]{1,0:T(8,128)(2,1)S(1)} %get-tuple-element.33.own), channel_id=1, source_target_pairs={{0,8},{1,9},{2,10},{3,11},{4,12},{5,13},{6,14},{7,15},{8,0},{9,1},... | collective-permute-start | bytes 245768 | tf_op jit(solution)/shard_map/ppermute | solution.py:459
  8.6 0.6 %collective-permute-start.4 = (bf16[8,5504]{1,0:T(8,128)(2,1)S(1)}, bf16[8,5504]{1,0:T(8,128)(2,1)S(1)}, u32[]{:S(2)}, u32[]{:S(2)}) collective-permute-start(bf16[8,5504]{1,0:T(8,128)(2,1)S(1)} %get-tuple-element.36), channel_id=1, source_target_pairs={{0,16},{1,17},{2,18},{3,19},{4,20},{5,21},{6,22},{7,23},{8,24},{9,... | collective-permute-start | bytes 264200 | tf_op jit(solution)/shard_map/ppermute | solution.py:465
  9.2 1.3 %collective-permute-start.5 = (bf16[8,5120]{1,0:T(8,128)(2,1)S(1)}, bf16[8,5120]{1,0:T(8,128)(2,1)S(1)}, u32[]{:S(2)}, u32[]{:S(2)}) collective-permute-start(bf16[8,5120]{1,0:T(8,128)(2,1)S(1)} %get-tuple-element.37), channel_id=1, source_target_pairs={{0,24},{1,25},{2,26},{3,27},{4,28},{5,29},{6,30},{7,31},{8,16},{9,... | collective-permute-start | bytes 245768 | tf_op jit(solution)/shard_map/ppermute | solution.py:465
  10.5 1.7 %collective-permute-done.z2 = bf16[8,5120]{1,0:T(8,128)(2,1)S(1)} collective-permute-done((bf16[8,5120]{1,0:T(8,128)(2,1)S(1)}, bf16[8,5120]{1,0:T(8,128)(2,1)S(1)}, u32[]{:S(2)}, u32[]{:S(2)}) %collective-permute-start) | collective-permute-done | bytes 81952 | tf_op jit(solution)/shard_map/ppermute | solution.py:459
  12.1 1.6 %collective-permute-start.1 = (bf16[2,8,5120]{2,1,0:T(8,128)(2,1)S(1)}, bf16[2,8,5120]{2,1,0:T(8,128)(2,1)S(1)}, u32[]{:S(2)}, u32[]{:S(2)}) collective-permute-start(bf16[2,8,5120]{2,1,0:T(8,128)(2,1)S(1)} %pad_maximum_fusion.3), channel_id=1, source_target_pairs={{0,2},{1,3},{2,0},{3,1},{4,6},{5,7},{6,4},{7,5},{8,10},{9,11},{10,... | collective-permute-start | bytes 491528 | tf_op jit(solution)/shard_map/ppermute | solution.py:459
  14.0 1.4 %collective-permute-done.5.g2 = bf16[8,5120]{1,0:T(8,128)(2,1)S(1)} collective-permute-done((bf16[8,5120]{1,0:T(8,128)(2,1)S(1)}, bf16[8,5120]{1,0:T(8,128)(2,1)S(1)}, u32[]{:S(2)}, u32[]{:S(2)}) %collective-permute-start.5) | collective-permute-done | bytes 81952 | tf_op jit(solution)/shard_map/ppermute | solution.py:465
  15.5 1.6 %collective-permute-start.6 = (bf16[2,8,5120]{2,1,0:T(8,128)(2,1)S(1)}, bf16[2,8,5120]{2,1,0:T(8,128)(2,1)S(1)}, u32[]{:S(2)}, u32[]{:S(2)}) collective-permute-start(bf16[2,8,5120]{2,1,0:T(8,128)(2,1)S(1)} %pad_maximum_fusion.4), channel_id=1, source_target_pairs={{0,4},{1,5},{2,6},{3,7},{4,0},{5,1},{6,2},{7,3},{8,12},{9,13},{10,... | collective-permute-start | bytes 491528 | tf_op jit(solution)/shard_map/ppermute | solution.py:459
  17.1 1.5 %collective-permute-start.7 = (bf16[2,8,5120]{2,1,0:T(8,128)(2,1)S(1)}, bf16[2,8,5120]{2,1,0:T(8,128)(2,1)S(1)}, u32[]{:S(2)}, u32[]{:S(2)}) collective-permute-start(bf16[2,8,5120]{2,1,0:T(8,128)(2,1)S(1)} %pad_maximum_fusion.4), channel_id=1, source_target_pairs={{0,2},{1,3},{2,0},{3,1},{4,6},{5,7},{6,4},{7,5},{8,10},{9,11},{10,... | collective-permute-start | bytes 491528 | tf_op jit(solution)/shard_map/ppermute | solution.py:459
  18.6 2.5 %collective-permute-start.2 = (bf16[2,8,5120]{2,1,0:T(8,128)(2,1)S(1)}, bf16[2,8,5120]{2,1,0:T(8,128)(2,1)S(1)}, u32[]{:S(2)}, u32[]{:S(2)}) collective-permute-start(bf16[2,8,5120]{2,1,0:T(8,128)(2,1)S(1)} %collective-permute-done.1.y_refs), channel_id=1, source_target_pairs={{0,4},{1,5},{2,6},{3,7},{4,0},{5,1},{6,2},{7,3},{8,12},{9,13},{10,... | collective-permute-start | bytes 491528 | tf_op jit(solution)/shard_map/ppermute | solution.py:459
  21.3 1.3 %collective-permute-done.6.z_refs = bf16[2,8,5120]{2,1,0:T(8,128)(2,1)S(1)} collective-permute-done((bf16[2,8,5120]{2,1,0:T(8,128)(2,1)S(1)}, bf16[2,8,5120]{2,1,0:T(8,128)(2,1)S(1)}, u32[]{:S(2)}, u32[]{:S(2)}) %collective-permute-start.6) | collective-permute-done | bytes 163872 | tf_op jit(solution)/shard_map/ppermute | solution.py:459
  22.6 0.6 %collective-permute-done.7.y_refs = bf16[2,8,5120]{2,1,0:T(8,128)(2,1)S(1)} collective-permute-done((bf16[2,8,5120]{2,1,0:T(8,128)(2,1)S(1)}, bf16[2,8,5120]{2,1,0:T(8,128)(2,1)S(1)}, u32[]{:S(2)}, u32[]{:S(2)}) %collective-permute-start.7) | collective-permute-done | bytes 163872 | tf_op jit(solution)/shard_map/ppermute | solution.py:459
  23.2 0.8 %collective-permute-start.8 = (bf16[2,8,5120]{2,1,0:T(8,128)(2,1)S(1)}, bf16[2,8,5120]{2,1,0:T(8,128)(2,1)S(1)}, u32[]{:S(2)}, u32[]{:S(2)}) collective-permute-start(bf16[2,8,5120]{2,1,0:T(8,128)(2,1)S(1)} %collective-permute-done.6.z_refs), channel_id=1, source_target_pairs={{0,2},{1,3},{2,0},{3,1},{4,6},{5,7},{6,4},{7,5},{8,10},{9,11},{10,... | collective-permute-start | bytes 491528 | tf_op jit(solution)/shard_map/ppermute | solution.py:459
  23.9 0.4 back_rows.1
  24.3 1.9 %collective-permute-done.2.high = bf16[2,8,5120]{2,1,0:T(8,128)(2,1)S(1)} collective-permute-done((bf16[2,8,5120]{2,1,0:T(8,128)(2,1)S(1)}, bf16[2,8,5120]{2,1,0:T(8,128)(2,1)S(1)}, u32[]{:S(2)}, u32[]{:S(2)}) %collective-permute-start.2) | collective-permute-done | bytes 163872 | tf_op jit(solution)/shard_map/ppermute | solution.py:459
  26.5 0.8 %forward_early.1.early_ref = f32[64,256]{1,0:T(8,128)S(1)} custom-call(bf16[8,5120]{1,0:T(8,128)(2,1)S(1)} %get-tuple-element.33.own, bf16[8,5120]{1,0:T(8,128)(2,1)S(1)} %collective-permute-done.z2, bf16[2,8,5120]{2,1,0:T(8,128)(2,1)S(1)} %collective-permute-done.1.y_refs, bf16[256,4096]{1,0:T(8,128)(2,1)S(1)} %pad_maximum_fusion.gu_ref.refs_1_), custom_call_target="tpu_custom_call" | custom-call | tf_op jit(solution)/shard_map/forward_early/pallas_call | solution.py:153
  27.3 1.2 %collective-permute-done.8.yz_refs = bf16[2,8,5120]{2,1,0:T(8,128)(2,1)S(1)} collective-permute-done((bf16[2,8,5120]{2,1,0:T(8,128)(2,1)S(1)}, bf16[2,8,5120]{2,1,0:T(8,128)(2,1)S(1)}, u32[]{:S(2)}, u32[]{:S(2)}) %collective-permute-start.8) | collective-permute-done | bytes 163872 | tf_op jit(solution)/shard_map/ppermute | solution.py:459
  28.5 0.4 grad_hidden.1.refs_0_
  28.9 0.8 %forward_late.1.refs_2_ = f32[128,256]{1,0:T(8,128)S(1)} custom-call(f32[64,256]{1,0:T(8,128)S(1)} %forward_early.1.early_ref, bf16[2,8,5120]{2,1,0:T(8,128)(2,1)S(1)} %collective-permute-done.10.low, bf16[2,8,5120]{2,1,0:T(8,128)(2,1)S(1)} %collective-permute-done.2.high, bf16[256,4096]{1,0:T(8,128)(2,1)S(1)} %pad_maximum_fusion.gu_ref.refs_1_), custom_call_target="tpu_custom_call" | custom-call | tf_op jit(solution)/shard_map/forward_late/pallas_call | solution.py:153
  30.0 0.8 %collective-permute-start.11 = (bf16[4,8,2688]{2,1,0:T(8,128)(2,1)S(1)}, bf16[4,8,2688]{2,1,0:T(8,128)(2,1)S(1)}, u32[]{:S(2)}, u32[]{:S(2)}) collective-permute-start(bf16[4,8,2688]{2,1,0:T(8,128)(2,1)S(1)} %get-tuple-element.49), channel_id=1, source_target_pairs={{0,2},{1,3},{2,0},{3,1},{4,6},{5,7},{6,4},{7,5},{8,10},{9,11},{10,... | collective-permute-start | bytes 516104 | tf_op jit(solution)/shard_map/ppermute | solution.py:459
  31.2 1.9 %collective-permute-start.13 = (bf16[4,8,2560]{2,1,0:T(8,128)(2,1)S(1)}, bf16[4,8,2560]{2,1,0:T(8,128)(2,1)S(1)}, u32[]{:S(2)}, u32[]{:S(2)}) collective-permute-start(bf16[4,8,2560]{2,1,0:T(8,128)(2,1)S(1)} %get-tuple-element.54), channel_id=1, source_target_pairs={{0,4},{1,5},{2,6},{3,7},{4,0},{5,1},{6,2},{7,3},{8,12},{9,13},{10,... | collective-permute-start | bytes 491528 | tf_op jit(solution)/shard_map/ppermute | solution.py:459
  33.1 2.4 %collective-permute-done.11.got_ref = bf16[4,8,2688]{2,1,0:T(8,128)(2,1)S(1)} collective-permute-done((bf16[4,8,2688]{2,1,0:T(8,128)(2,1)S(1)}, bf16[4,8,2688]{2,1,0:T(8,128)(2,1)S(1)}, u32[]{:S(2)}, u32[]{:S(2)}) %collective-permute-start.11) | collective-permute-done | bytes 172064 | tf_op jit(solution)/shard_map/ppermute | solution.py:459
  35.5 1.6 %collective-permute-start.12 = (bf16[2,8,2816]{2,1,0:T(8,128)(2,1)S(1)}, bf16[2,8,2816]{2,1,0:T(8,128)(2,1)S(1)}, u32[]{:S(2)}, u32[]{:S(2)}) collective-permute-start(bf16[2,8,2816]{2,1,0:T(8,128)(2,1)S(1)} %get-tuple-element.51), channel_id=1, source_target_pairs={{0,4},{1,5},{2,6},{3,7},{4,0},{5,1},{6,2},{7,3},{8,12},{9,13},{10,... | collective-permute-start | bytes 270344 | tf_op jit(solution)/shard_map/ppermute | solution.py:459
  37.2 1.7 %collective-permute-start.14 = (bf16[2,8,2560]{2,1,0:T(8,128)(2,1)S(1)}, bf16[2,8,2560]{2,1,0:T(8,128)(2,1)S(1)}, u32[]{:S(2)}, u32[]{:S(2)}) collective-permute-start(bf16[2,8,2560]{2,1,0:T(8,128)(2,1)S(1)} %get-tuple-element.56), channel_id=1, source_target_pairs={{0,2},{1,3},{2,0},{3,1},{4,6},{5,7},{6,4},{7,5},{8,10},{9,11},{10,... | collective-permute-start | bytes 245768 | tf_op jit(solution)/shard_map/ppermute | solution.py:459
  38.9 2.8 %collective-permute-done.14.got_b = bf16[2,8,2560]{2,1,0:T(8,128)(2,1)S(1)} collective-permute-done((bf16[2,8,2560]{2,1,0:T(8,128)(2,1)S(1)}, bf16[2,8,2560]{2,1,0:T(8,128)(2,1)S(1)}, u32[]{:S(2)}, u32[]{:S(2)}) %collective-permute-start.14) | collective-permute-done | bytes 81952 | tf_op jit(solution)/shard_map/ppermute | solution.py:459
  41.7 3.7 %collective-permute-start.15 = (bf16[8,5120]{1,0:T(8,128)(2,1)S(1)}, bf16[8,5120]{1,0:T(8,128)(2,1)S(1)}, u32[]{:S(2)}, u32[]{:S(2)}) collective-permute-start(bf16[8,5120]{1,0:T(8,128)(2,1)S(1)} %get-tuple-element.57), channel_id=1, source_target_pairs={{0,24},{1,25},{2,26},{3,27},{4,28},{5,29},{6,30},{7,31},{8,16},{9,... | collective-permute-start | bytes 245768 | tf_op jit(solution)/shard_map/ppermute | solution.py:465
  45.4 1.2 %collective-permute-start.16 = (bf16[8,5120]{1,0:T(8,128)(2,1)S(1)}, bf16[8,5120]{1,0:T(8,128)(2,1)S(1)}, u32[]{:S(2)}, u32[]{:S(2)}) collective-permute-start(bf16[8,5120]{1,0:T(8,128)(2,1)S(1)} %get-tuple-element.58), channel_id=1, source_target_pairs={{0,16},{1,17},{2,18},{3,19},{4,20},{5,21},{6,22},{7,23},{8,24},{9,... | collective-permute-start | bytes 245768 | tf_op jit(solution)/shard_map/ppermute | solution.py:465
  46.7 1.4 %collective-permute-done.15.one_ref = bf16[8,5120]{1,0:T(8,128)(2,1)S(1)} collective-permute-done((bf16[8,5120]{1,0:T(8,128)(2,1)S(1)}, bf16[8,5120]{1,0:T(8,128)(2,1)S(1)}, u32[]{:S(2)}, u32[]{:S(2)}) %collective-permute-start.15) | collective-permute-done | bytes 81952 | tf_op jit(solution)/shard_map/ppermute | solution.py:465
  48.1 1.8 %collective-permute-done.16.two_ref = bf16[8,5120]{1,0:T(8,128)(2,1)S(1)} collective-permute-done((bf16[8,5120]{1,0:T(8,128)(2,1)S(1)}, bf16[8,5120]{1,0:T(8,128)(2,1)S(1)}, u32[]{:S(2)}, u32[]{:S(2)}) %collective-permute-start.16) | collective-permute-done | bytes 81952 | tf_op jit(solution)/shard_map/ppermute | solution.py:465
  49.9 1.3 %final_rows.1 = (bf16[128,4096]{1,0:T(8,128)(2,1)}, f32[8,128]{1,0:T(8,128)S(1)}) custom-call(bf16[4,128,32]{2,1,0:T(8,128)(2,1)S(1)} %get-tuple-element.43.back_ref, f32[8,256]{1,0:T(8,128)S(1)} %get-tuple-element.44.scale_ref, bf16[8,5120]{1,0:T(8,128)(2,1)S(1)} %collective-permute-done.15.one_ref, bf16[8,5120]{1,0:T(8,128)(2,1)S(1)} %collective-permute-done.16.two_ref, ...), custom_call_target="tpu_custom_call" | custom-call | tf_op jit(solution)/shard_map/final_rows/pallas_call | solution.py:153
  51.2 0.7 %weight_out.1 = f32[8,128]{1,0:T(8,128)} custom-call(f32[8,128]{1,0:T(8,128)S(1)} %get-tuple-element.60.slot_ref, f32[8,128]{1,0:T(8,128)S(1)} %get-tuple-element.61.own_tile, f32[8,128]{1,0:T(8,128)S(1)} %collective-permute-done.17.got_tile, f32[8,128]{1,0:T(8,128)S(1)} %get-tuple-element.63.after_ref), custom_call_target="tpu_custom_call" | custom-call | tf_op jit(solution)/shard_map/weight_out/pallas_call | solution.py:153
  (31 shorter events, 2.2 us)
Async XLA Ops:
  0.6 7.4 %copy-start = (bf16[1,64,4096]{2,1,0:T(8,128)(2,1)S(1)}, bf16[1,64,4096]{2,1,0:T(8,128)(2,1)}, u32[]{:S(2)}) copy-start(bf16[1,64,4096]{2,1,0:T(8,128)(2,1)} %param.13) | copy-start | bytes 1572868
  0.6 7.4 %copy-start.1 = (bf16[1,64,4096]{2,1,0:T(8,128)(2,1)S(1)}, bf16[1,64,4096]{2,1,0:T(8,128)(2,1)}, u32[]{:S(2)}) copy-start(bf16[1,64,4096]{2,1,0:T(8,128)(2,1)} %param.12) | copy-start | bytes 1572868
  0.7 7.4 %copy-start.2 = (bf16[1,64,4096]{2,1,0:T(8,128)(2,1)S(1)}, bf16[1,64,4096]{2,1,0:T(8,128)(2,1)}, u32[]{:S(2)}) copy-start(bf16[1,64,4096]{2,1,0:T(8,128)(2,1)} %param.11) | copy-start | bytes 1572868
  0.7 7.5 %collective-permute-start.3 = (s32[8,128]{1,0:T(8,128)}, s32[8,128]{1,0:T(8,128)S(1)}, u32[]{:S(2)}, u32[]{:S(2)}) collective-permute-start(s32[8,128]{1,0:T(8,128)} %bitcast.35), channel_id=1, source_target_pairs={{0,16},{16,0},{1,17},{17,1},{2,18},{18,2},{3,19},{19,3},{4,20},{20... | collective-permute-start | bytes 12296 | tf_op jit(solution)/shard_map/ppermute | solution.py:32
  5.4 6.8 %collective-permute-start = (bf16[8,5120]{1,0:T(8,128)(2,1)S(1)}, bf16[8,5120]{1,0:T(8,128)(2,1)S(1)}, u32[]{:S(2)}, u32[]{:S(2)}) collective-permute-start(bf16[8,5120]{1,0:T(8,128)(2,1)S(1)} %get-tuple-element.33.own), channel_id=1, source_target_pairs={{0,8},{1,9},{2,10},{3,11},{4,12},{5,13},{6,14},{7,15},{8,0},{9,1},... | collective-permute-start | bytes 245768 | tf_op jit(solution)/shard_map/ppermute | solution.py:459
  8.6 5.4 %collective-permute-start.4 = (bf16[8,5504]{1,0:T(8,128)(2,1)S(1)}, bf16[8,5504]{1,0:T(8,128)(2,1)S(1)}, u32[]{:S(2)}, u32[]{:S(2)}) collective-permute-start(bf16[8,5504]{1,0:T(8,128)(2,1)S(1)} %get-tuple-element.36), channel_id=1, source_target_pairs={{0,16},{1,17},{2,18},{3,19},{4,20},{5,21},{6,22},{7,23},{8,24},{9,... | collective-permute-start | bytes 264200 | tf_op jit(solution)/shard_map/ppermute | solution.py:465
  9.2 6.3 %collective-permute-start.5 = (bf16[8,5120]{1,0:T(8,128)(2,1)S(1)}, bf16[8,5120]{1,0:T(8,128)(2,1)S(1)}, u32[]{:S(2)}, u32[]{:S(2)}) collective-permute-start(bf16[8,5120]{1,0:T(8,128)(2,1)S(1)} %get-tuple-element.37), channel_id=1, source_target_pairs={{0,24},{1,25},{2,26},{3,27},{4,28},{5,29},{6,30},{7,31},{8,16},{9,... | collective-permute-start | bytes 245768 | tf_op jit(solution)/shard_map/ppermute | solution.py:465
  12.1 6.5 %collective-permute-start.1 = (bf16[2,8,5120]{2,1,0:T(8,128)(2,1)S(1)}, bf16[2,8,5120]{2,1,0:T(8,128)(2,1)S(1)}, u32[]{:S(2)}, u32[]{:S(2)}) collective-permute-start(bf16[2,8,5120]{2,1,0:T(8,128)(2,1)S(1)} %pad_maximum_fusion.3), channel_id=1, source_target_pairs={{0,2},{1,3},{2,0},{3,1},{4,6},{5,7},{6,4},{7,5},{8,10},{9,11},{10,... | collective-permute-start | bytes 491528 | tf_op jit(solution)/shard_map/ppermute | solution.py:459
  13.7 12.4 %collective-permute-start.9 = (bf16[3,64,4096]{2,1,0:T(8,128)(2,1)S(1)}, bf16[3,64,4096]{2,1,0:T(8,128)(2,1)S(1)}, u32[]{:S(2)}, u32[]{:S(2)}) collective-permute-start(bf16[3,64,4096]{2,1,0:T(8,128)(2,1)S(1)} %pad_maximum_fusion.1), channel_id=1, source_target_pairs={{0,1},{1,0},{2,3},{3,2},{4,5},{5,4},{6,7},{7,6},{8,9},{9,8},{10,11... | collective-permute-start | bytes 4718600 | tf_op jit(solution)/shard_map/ppermute | solution.py:459
  15.5 7.1 %collective-permute-start.6 = (bf16[2,8,5120]{2,1,0:T(8,128)(2,1)S(1)}, bf16[2,8,5120]{2,1,0:T(8,128)(2,1)S(1)}, u32[]{:S(2)}, u32[]{:S(2)}) collective-permute-start(bf16[2,8,5120]{2,1,0:T(8,128)(2,1)S(1)} %pad_maximum_fusion.4), channel_id=1, source_target_pairs={{0,4},{1,5},{2,6},{3,7},{4,0},{5,1},{6,2},{7,3},{8,12},{9,13},{10,... | collective-permute-start | bytes 491528 | tf_op jit(solution)/shard_map/ppermute | solution.py:459
  17.1 6.1 %collective-permute-start.7 = (bf16[2,8,5120]{2,1,0:T(8,128)(2,1)S(1)}, bf16[2,8,5120]{2,1,0:T(8,128)(2,1)S(1)}, u32[]{:S(2)}, u32[]{:S(2)}) collective-permute-start(bf16[2,8,5120]{2,1,0:T(8,128)(2,1)S(1)} %pad_maximum_fusion.4), channel_id=1, source_target_pairs={{0,2},{1,3},{2,0},{3,1},{4,6},{5,7},{6,4},{7,5},{8,10},{9,11},{10,... | collective-permute-start | bytes 491528 | tf_op jit(solution)/shard_map/ppermute | solution.py:459
  18.6 7.6 %collective-permute-start.2 = (bf16[2,8,5120]{2,1,0:T(8,128)(2,1)S(1)}, bf16[2,8,5120]{2,1,0:T(8,128)(2,1)S(1)}, u32[]{:S(2)}, u32[]{:S(2)}) collective-permute-start(bf16[2,8,5120]{2,1,0:T(8,128)(2,1)S(1)} %collective-permute-done.1.y_refs), channel_id=1, source_target_pairs={{0,4},{1,5},{2,6},{3,7},{4,0},{5,1},{6,2},{7,3},{8,12},{9,13},{10,... | collective-permute-start | bytes 491528 | tf_op jit(solution)/shard_map/ppermute | solution.py:459
  21.2 7.7 %collective-permute-start.10 = (bf16[2,8,5120]{2,1,0:T(8,128)(2,1)S(1)}, bf16[2,8,5120]{2,1,0:T(8,128)(2,1)S(1)}, u32[]{:S(2)}, u32[]{:S(2)}) collective-permute-start(bf16[2,8,5120]{2,1,0:T(8,128)(2,1)S(1)} %pad_maximum_fusion.3), channel_id=1, source_target_pairs={{0,4},{1,5},{2,6},{3,7},{4,0},{5,1},{6,2},{7,3},{8,12},{9,13},{10,... | collective-permute-start | bytes 491528 | tf_op jit(solution)/shard_map/ppermute | solution.py:459
  23.2 5.3 %collective-permute-start.8 = (bf16[2,8,5120]{2,1,0:T(8,128)(2,1)S(1)}, bf16[2,8,5120]{2,1,0:T(8,128)(2,1)S(1)}, u32[]{:S(2)}, u32[]{:S(2)}) collective-permute-start(bf16[2,8,5120]{2,1,0:T(8,128)(2,1)S(1)} %collective-permute-done.6.z_refs), channel_id=1, source_target_pairs={{0,2},{1,3},{2,0},{3,1},{4,6},{5,7},{6,4},{7,5},{8,10},{9,11},{10,... | collective-permute-start | bytes 491528 | tf_op jit(solution)/shard_map/ppermute | solution.py:459
  30.0 5.5 %collective-permute-start.11 = (bf16[4,8,2688]{2,1,0:T(8,128)(2,1)S(1)}, bf16[4,8,2688]{2,1,0:T(8,128)(2,1)S(1)}, u32[]{:S(2)}, u32[]{:S(2)}) collective-permute-start(bf16[4,8,2688]{2,1,0:T(8,128)(2,1)S(1)} %get-tuple-element.49), channel_id=1, source_target_pairs={{0,2},{1,3},{2,0},{3,1},{4,6},{5,7},{6,4},{7,5},{8,10},{9,11},{10,... | collective-permute-start | bytes 516104 | tf_op jit(solution)/shard_map/ppermute | solution.py:459
  31.2 6.0 %collective-permute-start.13 = (bf16[4,8,2560]{2,1,0:T(8,128)(2,1)S(1)}, bf16[4,8,2560]{2,1,0:T(8,128)(2,1)S(1)}, u32[]{:S(2)}, u32[]{:S(2)}) collective-permute-start(bf16[4,8,2560]{2,1,0:T(8,128)(2,1)S(1)} %get-tuple-element.54), channel_id=1, source_target_pairs={{0,4},{1,5},{2,6},{3,7},{4,0},{5,1},{6,2},{7,3},{8,12},{9,13},{10,... | collective-permute-start | bytes 491528 | tf_op jit(solution)/shard_map/ppermute | solution.py:459
  35.5 6.1 %collective-permute-start.12 = (bf16[2,8,2816]{2,1,0:T(8,128)(2,1)S(1)}, bf16[2,8,2816]{2,1,0:T(8,128)(2,1)S(1)}, u32[]{:S(2)}, u32[]{:S(2)}) collective-permute-start(bf16[2,8,2816]{2,1,0:T(8,128)(2,1)S(1)} %get-tuple-element.51), channel_id=1, source_target_pairs={{0,4},{1,5},{2,6},{3,7},{4,0},{5,1},{6,2},{7,3},{8,12},{9,13},{10,... | collective-permute-start | bytes 270344 | tf_op jit(solution)/shard_map/ppermute | solution.py:459
  37.2 4.5 %collective-permute-start.14 = (bf16[2,8,2560]{2,1,0:T(8,128)(2,1)S(1)}, bf16[2,8,2560]{2,1,0:T(8,128)(2,1)S(1)}, u32[]{:S(2)}, u32[]{:S(2)}) collective-permute-start(bf16[2,8,2560]{2,1,0:T(8,128)(2,1)S(1)} %get-tuple-element.56), channel_id=1, source_target_pairs={{0,2},{1,3},{2,0},{3,1},{4,6},{5,7},{6,4},{7,5},{8,10},{9,11},{10,... | collective-permute-start | bytes 245768 | tf_op jit(solution)/shard_map/ppermute | solution.py:459
  41.7 6.3 %collective-permute-start.15 = (bf16[8,5120]{1,0:T(8,128)(2,1)S(1)}, bf16[8,5120]{1,0:T(8,128)(2,1)S(1)}, u32[]{:S(2)}, u32[]{:S(2)}) collective-permute-start(bf16[8,5120]{1,0:T(8,128)(2,1)S(1)} %get-tuple-element.57), channel_id=1, source_target_pairs={{0,24},{1,25},{2,26},{3,27},{4,28},{5,29},{6,30},{7,31},{8,16},{9,... | collective-permute-start | bytes 245768 | tf_op jit(solution)/shard_map/ppermute | solution.py:465
  45.4 4.4 %collective-permute-start.16 = (bf16[8,5120]{1,0:T(8,128)(2,1)S(1)}, bf16[8,5120]{1,0:T(8,128)(2,1)S(1)}, u32[]{:S(2)}, u32[]{:S(2)}) collective-permute-start(bf16[8,5120]{1,0:T(8,128)(2,1)S(1)} %get-tuple-element.58), channel_id=1, source_target_pairs={{0,16},{1,17},{2,18},{3,19},{4,20},{5,21},{6,22},{7,23},{8,24},{9,... | collective-permute-start | bytes 245768 | tf_op jit(solution)/shard_map/ppermute | solution.py:465
  46.6 4.5 %collective-permute-start.17 = (f32[8,128]{1,0:T(8,128)S(1)}, f32[8,128]{1,0:T(8,128)S(1)}, u32[]{:S(2)}, u32[]{:S(2)}) collective-permute-start(f32[8,128]{1,0:T(8,128)S(1)} %get-tuple-element.62), channel_id=1, source_target_pairs={{0,8},{1,9},{2,10},{3,11},{4,12},{5,13},{6,14},{7,15},{8,0},{9,1},... | collective-permute-start | bytes 12296 | tf_op jit(solution)/shard_map/ppermute | solution.py:459

commit v9 on v8

--- a/solution.py
+++ b/solution.py
@@ -327,17 +327,16 @@
         value = jnp.dot(both, gu_ref[:, span], preferred_element_type=F32)
         here = jnp.where(quarter == fold, value[count:], 0.0)
         tails = here if fold == 0 else tails + here
-        value = value[:count].astype(BF16)
         for k, (ref, j) in enumerate(places):
-            ref[j, :, fold * part : (fold + 1) * part] = value[MAIN * k : MAIN * (k + 1), :]
-    tails = tails.astype(BF16)
+            rows = value[MAIN * k : MAIN * (k + 1), :].astype(ref.dtype)
+            ref[j, :, fold * part : (fold + 1) * part] = rows
     for k, (ref, j) in enumerate(places):
-        ref[j, :, half : half + part] = tails[MAIN * k : MAIN * (k + 1), :]
+        ref[j, :, half : half + part] = tails[MAIN * k : MAIN * (k + 1), :].astype(ref.dtype)
 
 
 def grad_hidden_kernel(g0, g2, z_refs, y_refs, yz_refs, down_ref, grad_ref, rows_ref):
-    blocks = [g0, z_refs.at[0], g2, z_refs.at[1]]
-    blocks += [y_refs.at[0], yz_refs.at[0], y_refs.at[1], yz_refs.at[1]]
+    blocks = [g0, z_refs.at[1], g2, z_refs.at[0]]
+    blocks += [y_refs.at[1], yz_refs.at[1], y_refs.at[0], yz_refs.at[0]]
     grad_ref[...] = against(blocks, down_ref, rows_ref)
 
 
@@ -363,10 +362,9 @@
     for k, piece in enumerate(three_parts(weight)):
         tile = jnp.where(lane == k, piece[:count], tile)
         tile = jnp.where((lane == k + 3) & first, piece[count:], tile)
-    tile = tile.astype(BF16)
     full = near.shape[2] - 128
     for k, (ref, j) in enumerate(places):
-        ref[j, :, full:] = tile[MAIN * k : MAIN * (k + 1), :]
+        ref[j, :, full:] = tile[MAIN * k : MAIN * (k + 1), :].astype(ref.dtype)
 
 
 def backward_b_kernel(both_ref, gu_ref, near, far):
@@ -374,30 +372,30 @@
     spread(both_ref[...], gu_ref, gu_ref.shape[1] // 2, places)
 
 
-def added(one, two):
-    return (one.astype(F32) + two.astype(F32)).astype(BF16)
+def added(one, two, dtype):
+    return (one.astype(F32) + two.astype(F32)).astype(dtype)
 
 
 def fold_a_kernel(near_ref, got_ref, send_ref, keep_ref):
     full = near_ref.shape[2] - 128
     for k in range(near_ref.shape[0]):
         ref = (keep_ref, send_ref)[k % 2]
-        ref[k // 2, :, :full] = added(near_ref[k, :, :full], got_ref[k, :, :full])
-        ref[k // 2, :, full : full + 128] = near_ref[k, :, full:]
-        ref[k // 2, :, full + 128 :] = got_ref[k, :, full:]
+        ref[k // 2, :, :full] = added(near_ref[k, :, :full], got_ref[k, :, :full], ref.dtype)
+        ref[k // 2, :, full : full + 128] = near_ref[k, :, full:].astype(ref.dtype)
+        ref[k // 2, :, full + 128 :] = got_ref[k, :, full:].astype(ref.dtype)
 
 
 def fold_b_kernel(near_ref, got_ref, send_ref, keep_ref):
     for k in range(near_ref.shape[0]):
         ref = (keep_ref, send_ref)[k // 2]
-        ref[k % 2] = added(near_ref[k], got_ref[k])
+        ref[k % 2] = added(near_ref[k], got_ref[k], ref.dtype)
 
 
 def fold_both_kernel(keep_a, got_a, keep_b, got_b, own_ref, send_ref, own_tile, send_tile):
     full = keep_b.shape[2]
     for k, (ref, tile_ref) in enumerate(((own_ref, own_tile), (send_ref, send_tile))):
-        ref[:, :full] = added(keep_a[k, :, :full], got_a[k, :, :full])
-        ref[:, full:] = added(keep_b[k], got_b[k])
+        ref[:, :full] = added(keep_a[k, :, :full], got_a[k, :, :full], BF16)
+        ref[:, full:] = added(keep_b[k], got_b[k], BF16)
         tile = jnp.zeros((MAIN, 128), F32)
         for source in (keep_a, got_a):
             for start in (full, full + 128):
@@ -518,7 +516,7 @@
     gate_up = jnp.concatenate([own[0], other[0], own[1], other[1]], axis=0)
     down = jnp.concatenate([own[2], other[2]], axis=0)
 
-    grad_z = jnp.stack([grad_z0[:, :full], grad_z2])
+    grad_z = jnp.stack([grad_z2, grad_z0[:, :full]])
     grad_z1 = across(grad_z, Z1)
     grad_y = across(grad_z, Y1)
     input_z = jnp.stack([input_block, input_z2])
@@ -569,11 +567,11 @@
         scratch_shapes=[pltpu.VMEM((slots // 2, width), BF16)],
         name="forward_late",
     )
-    side_a = pltpu.VMEM((4, MAIN, half + 128), BF16)
-    side_b = pltpu.VMEM((4, MAIN, half), BF16)
+    side_a = (4, MAIN, half + 128)
+    side_b = (4, MAIN, half)
     near_a, far_a, both = near_call(
         backward_a_kernel,
-        [side_a, side_a, pltpu.VMEM((slots, 2 * units), BF16)],
+        [pltpu.VMEM(side_a, F32), pltpu.VMEM(side_a, BF16), pltpu.VMEM((slots, 2 * units), BF16)],
         grad_hidden,
         gate_up,
         hidden,
@@ -581,14 +579,14 @@
     )
     got_a = across(far_a, Y1)
     near_b, far_b = near_call(
-        backward_b_kernel, [side_b, side_b], both, gate_up, name="backward_b"
+        backward_b_kernel, [pltpu.VMEM(side_b, F32), pltpu.VMEM(side_b, BF16)], both, gate_up, name="backward_b"
     )
     got_b = across(far_b, Z1)
     send_a, keep_a = near_call(
-        fold_a_kernel, [pltpu.VMEM((2, MAIN, half + 256), BF16)] * 2, near_a, got_a, name="fold_a"
+        fold_a_kernel, [pltpu.VMEM((2, MAIN, half + 256), t) for t in (BF16, F32)], near_a, got_a, name="fold_a"
     )
     send_b, keep_b = near_call(
-        fold_b_kernel, [pltpu.VMEM((2, MAIN, half), BF16)] * 2, near_b, got_b, name="fold_b"
+        fold_b_kernel, [pltpu.VMEM((2, MAIN, half), t) for t in (BF16, F32)], near_b, got_b, name="fold_b"
     )
     rows_0, rows_2, tile_0, tile_2 = near_call(
         fold_both_kernel,

time: 52 us -> 52 us (level)
  no operation moved by 1% of the time
where the time goes in v9:
time: 52 us; the launch traced here: 51.9 us
  starting transfers between devices  26.5 us (51%)
  waiting for transfers between devices  16.8 us (32%)
  Pallas kernels  7.08 us (14%)
  between operations  0.82 us (2%)
    ppermute x13, starting transfers between devices, across(): return lax.ppermute(value, 'ep', [(i, i ^ bits) for i in range(count)])  16.7 us
    ppermute x13, waiting for transfers between devices, across(): return lax.ppermute(value, 'ep', [(i, i ^ bits) for i in range(count)])  11.8 us
    pallas_call x13, Pallas kernels, near_call(): pl.pallas_call(kernel, out_shape=out_shape, compiler_params=params, **kwa...  7.08 us
    ppermute x4, starting transfers between devices, sections_across(): return lax.ppermute(value, ('pp', 'ep'), pairs)  6.79 us
    ppermute x4, waiting for transfers between devices, sections_across(): return lax.ppermute(value, ('pp', 'ep'), pairs)  4.97 us
    ppermute x1, starting transfers between devices, passed_along(): lax.ppermute(value, axis, [(i, (i + by) % size) for i in range(size)])  3 us
  transfers between devices with their start and end apart: 18, of which 11 were waited for; matrix products, arithmetic and copies ran while one was open for 1% of the time, Pallas kernels for 10%

profile of v9, /device:TPU:0, one launch (start us, length us, event | category | flops | bytes accessed | tf_op | source)
XLA Modules:
  0.0 51.9 jit_solution(13875911203240163762)
XLA Ops:
  0.7 3.0 %collective-permute-start.3 = (s32[8,128]{1,0:T(8,128)}, s32[8,128]{1,0:T(8,128)S(1)}, u32[]{:S(2)}, u32[]{:S(2)}) collective-permute-start(s32[8,128]{1,0:T(8,128)} %bitcast.35), channel_id=1, source_target_pairs={{0,16},{16,0},{1,17},{17,1},{2,18},{18,2},{3,19},{19,3},{4,20},{20... | collective-permute-start | bytes 12296 | tf_op jit(solution)/shard_map/ppermute | solution.py:32
  3.7 1.7 %pick_inputs.1 = (bf16[8,5120]{1,0:T(8,128)(2,1)S(1)}, f32[8,128]{1,0:T(8,128)S(1)}, f32[8,128]{1,0:T(8,128)S(1)}, bf16[128,4096]{1,0:T(8,128)(2,1)S(1)}) custom-call(s32[8,128]{1,0:T(8,128)} %bitcast.36, f32[8,128]{1,0:T(8,128)} %bitcast.34, bf16[128,4096]{1,0:T(8,128)(2,1)} %bitcast.32, bf16[128,4096]{1,0:T(8,128)(2,1)} %bitcast.33), custom_call_target="tpu_custom_call" | custom-call | tf_op jit(solution)/shard_map/pick_inputs/pallas_call | solution.py:153
  5.4 2.7 %collective-permute-start = (bf16[8,5120]{1,0:T(8,128)(2,1)S(1)}, bf16[8,5120]{1,0:T(8,128)(2,1)S(1)}, u32[]{:S(2)}, u32[]{:S(2)}) collective-permute-start(bf16[8,5120]{1,0:T(8,128)(2,1)S(1)} %get-tuple-element.33.own), channel_id=1, source_target_pairs={{0,8},{1,9},{2,10},{3,11},{4,12},{5,13},{6,14},{7,15},{8,0},{9,1},... | collective-permute-start | bytes 245768 | tf_op jit(solution)/shard_map/ppermute | solution.py:457
  8.6 0.6 %collective-permute-start.4 = (bf16[8,5504]{1,0:T(8,128)(2,1)S(1)}, bf16[8,5504]{1,0:T(8,128)(2,1)S(1)}, u32[]{:S(2)}, u32[]{:S(2)}) collective-permute-start(bf16[8,5504]{1,0:T(8,128)(2,1)S(1)} %get-tuple-element.36), channel_id=1, source_target_pairs={{0,16},{1,17},{2,18},{3,19},{4,20},{5,21},{6,22},{7,23},{8,24},{9,... | collective-permute-start | bytes 264200 | tf_op jit(solution)/shard_map/ppermute | solution.py:463
  9.2 1.3 %collective-permute-start.5 = (bf16[8,5120]{1,0:T(8,128)(2,1)S(1)}, bf16[8,5120]{1,0:T(8,128)(2,1)S(1)}, u32[]{:S(2)}, u32[]{:S(2)}) collective-permute-start(bf16[8,5120]{1,0:T(8,128)(2,1)S(1)} %get-tuple-element.37), channel_id=1, source_target_pairs={{0,24},{1,25},{2,26},{3,27},{4,28},{5,29},{6,30},{7,31},{8,16},{9,... | collective-permute-start | bytes 245768 | tf_op jit(solution)/shard_map/ppermute | solution.py:463
  10.5 1.7 %collective-permute-done.z2 = bf16[8,5120]{1,0:T(8,128)(2,1)S(1)} collective-permute-done((bf16[8,5120]{1,0:T(8,128)(2,1)S(1)}, bf16[8,5120]{1,0:T(8,128)(2,1)S(1)}, u32[]{:S(2)}, u32[]{:S(2)}) %collective-permute-start) | collective-permute-done | bytes 81952 | tf_op jit(solution)/shard_map/ppermute | solution.py:457
  12.1 1.6 %collective-permute-start.1 = (bf16[2,8,5120]{2,1,0:T(8,128)(2,1)S(1)}, bf16[2,8,5120]{2,1,0:T(8,128)(2,1)S(1)}, u32[]{:S(2)}, u32[]{:S(2)}) collective-permute-start(bf16[2,8,5120]{2,1,0:T(8,128)(2,1)S(1)} %pad_maximum_fusion.3), channel_id=1, source_target_pairs={{0,2},{1,3},{2,0},{3,1},{4,6},{5,7},{6,4},{7,5},{8,10},{9,11},{10,... | collective-permute-start | bytes 491528 | tf_op jit(solution)/shard_map/ppermute | solution.py:457
  14.0 1.4 %collective-permute-done.5.g2 = bf16[8,5120]{1,0:T(8,128)(2,1)S(1)} collective-permute-done((bf16[8,5120]{1,0:T(8,128)(2,1)S(1)}, bf16[8,5120]{1,0:T(8,128)(2,1)S(1)}, u32[]{:S(2)}, u32[]{:S(2)}) %collective-permute-start.5) | collective-permute-done | bytes 81952 | tf_op jit(solution)/shard_map/ppermute | solution.py:463
  15.5 1.6 %collective-permute-start.6 = (bf16[2,8,5120]{2,1,0:T(8,128)(2,1)S(1)}, bf16[2,8,5120]{2,1,0:T(8,128)(2,1)S(1)}, u32[]{:S(2)}, u32[]{:S(2)}) collective-permute-start(bf16[2,8,5120]{2,1,0:T(8,128)(2,1)S(1)} %pad_maximum_fusion.4), channel_id=1, source_target_pairs={{0,4},{1,5},{2,6},{3,7},{4,0},{5,1},{6,2},{7,3},{8,12},{9,13},{10,... | collective-permute-start | bytes 491528 | tf_op jit(solution)/shard_map/ppermute | solution.py:457
  17.1 1.5 %collective-permute-start.7 = (bf16[2,8,5120]{2,1,0:T(8,128)(2,1)S(1)}, bf16[2,8,5120]{2,1,0:T(8,128)(2,1)S(1)}, u32[]{:S(2)}, u32[]{:S(2)}) collective-permute-start(bf16[2,8,5120]{2,1,0:T(8,128)(2,1)S(1)} %pad_maximum_fusion.4), channel_id=1, source_target_pairs={{0,2},{1,3},{2,0},{3,1},{4,6},{5,7},{6,4},{7,5},{8,10},{9,11},{10,... | collective-permute-start | bytes 491528 | tf_op jit(solution)/shard_map/ppermute | solution.py:457
  18.6 2.5 %collective-permute-start.2 = (bf16[2,8,5120]{2,1,0:T(8,128)(2,1)S(1)}, bf16[2,8,5120]{2,1,0:T(8,128)(2,1)S(1)}, u32[]{:S(2)}, u32[]{:S(2)}) collective-permute-start(bf16[2,8,5120]{2,1,0:T(8,128)(2,1)S(1)} %collective-permute-done.1.y_refs), channel_id=1, source_target_pairs={{0,4},{1,5},{2,6},{3,7},{4,0},{5,1},{6,2},{7,3},{8,12},{9,13},{10,... | collective-permute-start | bytes 491528 | tf_op jit(solution)/shard_map/ppermute | solution.py:457
  21.3 1.3 %collective-permute-done.6.z_refs = bf16[2,8,5120]{2,1,0:T(8,128)(2,1)S(1)} collective-permute-done((bf16[2,8,5120]{2,1,0:T(8,128)(2,1)S(1)}, bf16[2,8,5120]{2,1,0:T(8,128)(2,1)S(1)}, u32[]{:S(2)}, u32[]{:S(2)}) %collective-permute-start.6) | collective-permute-done | bytes 163872 | tf_op jit(solution)/shard_map/ppermute | solution.py:457
  22.6 0.6 %collective-permute-done.7.y_refs = bf16[2,8,5120]{2,1,0:T(8,128)(2,1)S(1)} collective-permute-done((bf16[2,8,5120]{2,1,0:T(8,128)(2,1)S(1)}, bf16[2,8,5120]{2,1,0:T(8,128)(2,1)S(1)}, u32[]{:S(2)}, u32[]{:S(2)}) %collective-permute-start.7) | collective-permute-done | bytes 163872 | tf_op jit(solution)/shard_map/ppermute | solution.py:457
  23.2 0.8 %collective-permute-start.8 = (bf16[2,8,5120]{2,1,0:T(8,128)(2,1)S(1)}, bf16[2,8,5120]{2,1,0:T(8,128)(2,1)S(1)}, u32[]{:S(2)}, u32[]{:S(2)}) collective-permute-start(bf16[2,8,5120]{2,1,0:T(8,128)(2,1)S(1)} %collective-permute-done.6.z_refs), channel_id=1, source_target_pairs={{0,2},{1,3},{2,0},{3,1},{4,6},{5,7},{6,4},{7,5},{8,10},{9,11},{10,... | collective-permute-start | bytes 491528 | tf_op jit(solution)/shard_map/ppermute | solution.py:457
  23.9 0.4 back_rows.1
  24.3 1.9 %collective-permute-done.2.high = bf16[2,8,5120]{2,1,0:T(8,128)(2,1)S(1)} collective-permute-done((bf16[2,8,5120]{2,1,0:T(8,128)(2,1)S(1)}, bf16[2,8,5120]{2,1,0:T(8,128)(2,1)S(1)}, u32[]{:S(2)}, u32[]{:S(2)}) %collective-permute-start.2) | collective-permute-done | bytes 163872 | tf_op jit(solution)/shard_map/ppermute | solution.py:457
  26.5 0.8 %forward_early.1.early_ref = f32[64,256]{1,0:T(8,128)S(1)} custom-call(bf16[8,5120]{1,0:T(8,128)(2,1)S(1)} %get-tuple-element.33.own, bf16[8,5120]{1,0:T(8,128)(2,1)S(1)} %collective-permute-done.z2, bf16[2,8,5120]{2,1,0:T(8,128)(2,1)S(1)} %collective-permute-done.1.y_refs, bf16[256,4096]{1,0:T(8,128)(2,1)S(1)} %pad_maximum_fusion.gu_ref.refs_1_), custom_call_target="tpu_custom_call" | custom-call | tf_op jit(solution)/shard_map/forward_early/pallas_call | solution.py:153
  27.3 1.2 %collective-permute-done.8.yz_refs = bf16[2,8,5120]{2,1,0:T(8,128)(2,1)S(1)} collective-permute-done((bf16[2,8,5120]{2,1,0:T(8,128)(2,1)S(1)}, bf16[2,8,5120]{2,1,0:T(8,128)(2,1)S(1)}, u32[]{:S(2)}, u32[]{:S(2)}) %collective-permute-start.8) | collective-permute-done | bytes 163872 | tf_op jit(solution)/shard_map/ppermute | solution.py:457
  28.5 0.4 grad_hidden.1.refs_0_
  28.9 0.8 %forward_late.1.refs_2_ = f32[128,256]{1,0:T(8,128)S(1)} custom-call(f32[64,256]{1,0:T(8,128)S(1)} %forward_early.1.early_ref, bf16[2,8,5120]{2,1,0:T(8,128)(2,1)S(1)} %collective-permute-done.10.low, bf16[2,8,5120]{2,1,0:T(8,128)(2,1)S(1)} %collective-permute-done.2.high, bf16[256,4096]{1,0:T(8,128)(2,1)S(1)} %pad_maximum_fusion.gu_ref.refs_1_), custom_call_target="tpu_custom_call" | custom-call | tf_op jit(solution)/shard_map/forward_late/pallas_call | solution.py:153
  30.0 0.8 %collective-permute-start.11 = (bf16[4,8,2688]{2,1,0:T(8,128)(2,1)S(1)}, bf16[4,8,2688]{2,1,0:T(8,128)(2,1)S(1)}, u32[]{:S(2)}, u32[]{:S(2)}) collective-permute-start(bf16[4,8,2688]{2,1,0:T(8,128)(2,1)S(1)} %get-tuple-element.49), channel_id=1, source_target_pairs={{0,2},{1,3},{2,0},{3,1},{4,6},{5,7},{6,4},{7,5},{8,10},{9,11},{10,... | collective-permute-start | bytes 516104 | tf_op jit(solution)/shard_map/ppermute | solution.py:457
  31.2 2.0 %collective-permute-start.13 = (bf16[4,8,2560]{2,1,0:T(8,128)(2,1)S(1)}, bf16[4,8,2560]{2,1,0:T(8,128)(2,1)S(1)}, u32[]{:S(2)}, u32[]{:S(2)}) collective-permute-start(bf16[4,8,2560]{2,1,0:T(8,128)(2,1)S(1)} %get-tuple-element.54), channel_id=1, source_target_pairs={{0,4},{1,5},{2,6},{3,7},{4,0},{5,1},{6,2},{7,3},{8,12},{9,13},{10,... | collective-permute-start | bytes 491528 | tf_op jit(solution)/shard_map/ppermute | solution.py:457
  33.1 2.4 %collective-permute-done.11.got_ref = bf16[4,8,2688]{2,1,0:T(8,128)(2,1)S(1)} collective-permute-done((bf16[4,8,2688]{2,1,0:T(8,128)(2,1)S(1)}, bf16[4,8,2688]{2,1,0:T(8,128)(2,1)S(1)}, u32[]{:S(2)}, u32[]{:S(2)}) %collective-permute-start.11) | collective-permute-done | bytes 172064 | tf_op jit(solution)/shard_map/ppermute | solution.py:457
  35.5 1.6 %collective-permute-start.12 = (bf16[2,8,2816]{2,1,0:T(8,128)(2,1)S(1)}, bf16[2,8,2816]{2,1,0:T(8,128)(2,1)S(1)}, u32[]{:S(2)}, u32[]{:S(2)}) collective-permute-start(bf16[2,8,2816]{2,1,0:T(8,128)(2,1)S(1)} %get-tuple-element.51), channel_id=1, source_target_pairs={{0,4},{1,5},{2,6},{3,7},{4,0},{5,1},{6,2},{7,3},{8,12},{9,13},{10,... | collective-permute-start | bytes 270344 | tf_op jit(solution)/shard_map/ppermute | solution.py:457
  37.2 1.7 %collective-permute-start.14 = (bf16[2,8,2560]{2,1,0:T(8,128)(2,1)S(1)}, bf16[2,8,2560]{2,1,0:T(8,128)(2,1)S(1)}, u32[]{:S(2)}, u32[]{:S(2)}) collective-permute-start(bf16[2,8,2560]{2,1,0:T(8,128)(2,1)S(1)} %get-tuple-element.56), channel_id=1, source_target_pairs={{0,2},{1,3},{2,0},{3,1},{4,6},{5,7},{6,4},{7,5},{8,10},{9,11},{10,... | collective-permute-start | bytes 245768 | tf_op jit(solution)/shard_map/ppermute | solution.py:457
  38.9 2.8 %collective-permute-done.14.got_b = bf16[2,8,2560]{2,1,0:T(8,128)(2,1)S(1)} collective-permute-done((bf16[2,8,2560]{2,1,0:T(8,128)(2,1)S(1)}, bf16[2,8,2560]{2,1,0:T(8,128)(2,1)S(1)}, u32[]{:S(2)}, u32[]{:S(2)}) %collective-permute-start.14) | collective-permute-done | bytes 81952 | tf_op jit(solution)/shard_map/ppermute | solution.py:457
  41.7 3.7 %collective-permute-start.15 = (bf16[8,5120]{1,0:T(8,128)(2,1)S(1)}, bf16[8,5120]{1,0:T(8,128)(2,1)S(1)}, u32[]{:S(2)}, u32[]{:S(2)}) collective-permute-start(bf16[8,5120]{1,0:T(8,128)(2,1)S(1)} %get-tuple-element.57), channel_id=1, source_target_pairs={{0,24},{1,25},{2,26},{3,27},{4,28},{5,29},{6,30},{7,31},{8,16},{9,... | collective-permute-start | bytes 245768 | tf_op jit(solution)/shard_map/ppermute | solution.py:463
  45.4 1.2 %collective-permute-start.16 = (bf16[8,5120]{1,0:T(8,128)(2,1)S(1)}, bf16[8,5120]{1,0:T(8,128)(2,1)S(1)}, u32[]{:S(2)}, u32[]{:S(2)}) collective-permute-start(bf16[8,5120]{1,0:T(8,128)(2,1)S(1)} %get-tuple-element.58), channel_id=1, source_target_pairs={{0,16},{1,17},{2,18},{3,19},{4,20},{5,21},{6,22},{7,23},{8,24},{9,... | collective-permute-start | bytes 245768 | tf_op jit(solution)/shard_map/ppermute | solution.py:463
  46.6 1.4 %collective-permute-done.15.one_ref = bf16[8,5120]{1,0:T(8,128)(2,1)S(1)} collective-permute-done((bf16[8,5120]{1,0:T(8,128)(2,1)S(1)}, bf16[8,5120]{1,0:T(8,128)(2,1)S(1)}, u32[]{:S(2)}, u32[]{:S(2)}) %collective-permute-start.15) | collective-permute-done | bytes 81952 | tf_op jit(solution)/shard_map/ppermute | solution.py:463
  48.0 1.9 %collective-permute-done.16.two_ref = bf16[8,5120]{1,0:T(8,128)(2,1)S(1)} collective-permute-done((bf16[8,5120]{1,0:T(8,128)(2,1)S(1)}, bf16[8,5120]{1,0:T(8,128)(2,1)S(1)}, u32[]{:S(2)}, u32[]{:S(2)}) %collective-permute-start.16) | collective-permute-done | bytes 81952 | tf_op jit(solution)/shard_map/ppermute | solution.py:463
  49.9 1.3 %final_rows.1 = (bf16[128,4096]{1,0:T(8,128)(2,1)}, f32[8,128]{1,0:T(8,128)S(1)}) custom-call(bf16[4,128,32]{2,1,0:T(8,128)(2,1)S(1)} %get-tuple-element.43.back_ref, f32[8,256]{1,0:T(8,128)S(1)} %get-tuple-element.44.scale_ref, bf16[8,5120]{1,0:T(8,128)(2,1)S(1)} %collective-permute-done.15.one_ref, bf16[8,5120]{1,0:T(8,128)(2,1)S(1)} %collective-permute-done.16.two_ref, ...), custom_call_target="tpu_custom_call" | custom-call | tf_op jit(solution)/shard_map/final_rows/pallas_call | solution.py:153
  51.2 0.7 %weight_out.1 = f32[8,128]{1,0:T(8,128)} custom-call(f32[8,128]{1,0:T(8,128)S(1)} %get-tuple-element.60.slot_ref, f32[8,128]{1,0:T(8,128)S(1)} %get-tuple-element.61.own_tile, f32[8,128]{1,0:T(8,128)S(1)} %collective-permute-done.17.got_tile, f32[8,128]{1,0:T(8,128)S(1)} %get-tuple-element.63.after_ref), custom_call_target="tpu_custom_call" | custom-call | tf_op jit(solution)/shard_map/weight_out/pallas_call | solution.py:153
  (31 shorter events, 2.1 us)
Async XLA Ops:
  0.6 7.4 %copy-start = (bf16[1,64,4096]{2,1,0:T(8,128)(2,1)S(1)}, bf16[1,64,4096]{2,1,0:T(8,128)(2,1)}, u32[]{:S(2)}) copy-start(bf16[1,64,4096]{2,1,0:T(8,128)(2,1)} %param.13) | copy-start | bytes 1572868
  0.6 7.4 %copy-start.1 = (bf16[1,64,4096]{2,1,0:T(8,128)(2,1)S(1)}, bf16[1,64,4096]{2,1,0:T(8,128)(2,1)}, u32[]{:S(2)}) copy-start(bf16[1,64,4096]{2,1,0:T(8,128)(2,1)} %param.12) | copy-start | bytes 1572868
  0.7 7.4 %copy-start.2 = (bf16[1,64,4096]{2,1,0:T(8,128)(2,1)S(1)}, bf16[1,64,4096]{2,1,0:T(8,128)(2,1)}, u32[]{:S(2)}) copy-start(bf16[1,64,4096]{2,1,0:T(8,128)(2,1)} %param.11) | copy-start | bytes 1572868
  0.7 7.5 %collective-permute-start.3 = (s32[8,128]{1,0:T(8,128)}, s32[8,128]{1,0:T(8,128)S(1)}, u32[]{:S(2)}, u32[]{:S(2)}) collective-permute-start(s32[8,128]{1,0:T(8,128)} %bitcast.35), channel_id=1, source_target_pairs={{0,16},{16,0},{1,17},{17,1},{2,18},{18,2},{3,19},{19,3},{4,20},{20... | collective-permute-start | bytes 12296 | tf_op jit(solution)/shard_map/ppermute | solution.py:32
  5.4 6.8 %collective-permute-start = (bf16[8,5120]{1,0:T(8,128)(2,1)S(1)}, bf16[8,5120]{1,0:T(8,128)(2,1)S(1)}, u32[]{:S(2)}, u32[]{:S(2)}) collective-permute-start(bf16[8,5120]{1,0:T(8,128)(2,1)S(1)} %get-tuple-element.33.own), channel_id=1, source_target_pairs={{0,8},{1,9},{2,10},{3,11},{4,12},{5,13},{6,14},{7,15},{8,0},{9,1},... | collective-permute-start | bytes 245768 | tf_op jit(solution)/shard_map/ppermute | solution.py:457
  8.6 5.4 %collective-permute-start.4 = (bf16[8,5504]{1,0:T(8,128)(2,1)S(1)}, bf16[8,5504]{1,0:T(8,128)(2,1)S(1)}, u32[]{:S(2)}, u32[]{:S(2)}) collective-permute-start(bf16[8,5504]{1,0:T(8,128)(2,1)S(1)} %get-tuple-element.36), channel_id=1, source_target_pairs={{0,16},{1,17},{2,18},{3,19},{4,20},{5,21},{6,22},{7,23},{8,24},{9,... | collective-permute-start | bytes 264200 | tf_op jit(solution)/shard_map/ppermute | solution.py:463
  9.2 6.3 %collective-permute-start.5 = (bf16[8,5120]{1,0:T(8,128)(2,1)S(1)}, bf16[8,5120]{1,0:T(8,128)(2,1)S(1)}, u32[]{:S(2)}, u32[]{:S(2)}) collective-permute-start(bf16[8,5120]{1,0:T(8,128)(2,1)S(1)} %get-tuple-element.37), channel_id=1, source_target_pairs={{0,24},{1,25},{2,26},{3,27},{4,28},{5,29},{6,30},{7,31},{8,16},{9,... | collective-permute-start | bytes 245768 | tf_op jit(solution)/shard_map/ppermute | solution.py:463
  12.1 6.5 %collective-permute-start.1 = (bf16[2,8,5120]{2,1,0:T(8,128)(2,1)S(1)}, bf16[2,8,5120]{2,1,0:T(8,128)(2,1)S(1)}, u32[]{:S(2)}, u32[]{:S(2)}) collective-permute-start(bf16[2,8,5120]{2,1,0:T(8,128)(2,1)S(1)} %pad_maximum_fusion.3), channel_id=1, source_target_pairs={{0,2},{1,3},{2,0},{3,1},{4,6},{5,7},{6,4},{7,5},{8,10},{9,11},{10,... | collective-permute-start | bytes 491528 | tf_op jit(solution)/shard_map/ppermute | solution.py:457
  13.7 12.4 %collective-permute-start.9 = (bf16[3,64,4096]{2,1,0:T(8,128)(2,1)S(1)}, bf16[3,64,4096]{2,1,0:T(8,128)(2,1)S(1)}, u32[]{:S(2)}, u32[]{:S(2)}) collective-permute-start(bf16[3,64,4096]{2,1,0:T(8,128)(2,1)S(1)} %pad_maximum_fusion.1), channel_id=1, source_target_pairs={{0,1},{1,0},{2,3},{3,2},{4,5},{5,4},{6,7},{7,6},{8,9},{9,8},{10,11... | collective-permute-start | bytes 4718600 | tf_op jit(solution)/shard_map/ppermute | solution.py:457
  15.5 7.1 %collective-permute-start.6 = (bf16[2,8,5120]{2,1,0:T(8,128)(2,1)S(1)}, bf16[2,8,5120]{2,1,0:T(8,128)(2,1)S(1)}, u32[]{:S(2)}, u32[]{:S(2)}) collective-permute-start(bf16[2,8,5120]{2,1,0:T(8,128)(2,1)S(1)} %pad_maximum_fusion.4), channel_id=1, source_target_pairs={{0,4},{1,5},{2,6},{3,7},{4,0},{5,1},{6,2},{7,3},{8,12},{9,13},{10,... | collective-permute-start | bytes 491528 | tf_op jit(solution)/shard_map/ppermute | solution.py:457
  17.1 6.1 %collective-permute-start.7 = (bf16[2,8,5120]{2,1,0:T(8,128)(2,1)S(1)}, bf16[2,8,5120]{2,1,0:T(8,128)(2,1)S(1)}, u32[]{:S(2)}, u32[]{:S(2)}) collective-permute-start(bf16[2,8,5120]{2,1,0:T(8,128)(2,1)S(1)} %pad_maximum_fusion.4), channel_id=1, source_target_pairs={{0,2},{1,3},{2,0},{3,1},{4,6},{5,7},{6,4},{7,5},{8,10},{9,11},{10,... | collective-permute-start | bytes 491528 | tf_op jit(solution)/shard_map/ppermute | solution.py:457
  18.6 7.6 %collective-permute-start.2 = (bf16[2,8,5120]{2,1,0:T(8,128)(2,1)S(1)}, bf16[2,8,5120]{2,1,0:T(8,128)(2,1)S(1)}, u32[]{:S(2)}, u32[]{:S(2)}) collective-permute-start(bf16[2,8,5120]{2,1,0:T(8,128)(2,1)S(1)} %collective-permute-done.1.y_refs), channel_id=1, source_target_pairs={{0,4},{1,5},{2,6},{3,7},{4,0},{5,1},{6,2},{7,3},{8,12},{9,13},{10,... | collective-permute-start | bytes 491528 | tf_op jit(solution)/shard_map/ppermute | solution.py:457
  21.2 7.7 %collective-permute-start.10 = (bf16[2,8,5120]{2,1,0:T(8,128)(2,1)S(1)}, bf16[2,8,5120]{2,1,0:T(8,128)(2,1)S(1)}, u32[]{:S(2)}, u32[]{:S(2)}) collective-permute-start(bf16[2,8,5120]{2,1,0:T(8,128)(2,1)S(1)} %pad_maximum_fusion.3), channel_id=1, source_target_pairs={{0,4},{1,5},{2,6},{3,7},{4,0},{5,1},{6,2},{7,3},{8,12},{9,13},{10,... | collective-permute-start | bytes 491528 | tf_op jit(solution)/shard_map/ppermute | solution.py:457
  23.2 5.3 %collective-permute-start.8 = (bf16[2,8,5120]{2,1,0:T(8,128)(2,1)S(1)}, bf16[2,8,5120]{2,1,0:T(8,128)(2,1)S(1)}, u32[]{:S(2)}, u32[]{:S(2)}) collective-permute-start(bf16[2,8,5120]{2,1,0:T(8,128)(2,1)S(1)} %collective-permute-done.6.z_refs), channel_id=1, source_target_pairs={{0,2},{1,3},{2,0},{3,1},{4,6},{5,7},{6,4},{7,5},{8,10},{9,11},{10,... | collective-permute-start | bytes 491528 | tf_op jit(solution)/shard_map/ppermute | solution.py:457
  30.0 5.5 %collective-permute-start.11 = (bf16[4,8,2688]{2,1,0:T(8,128)(2,1)S(1)}, bf16[4,8,2688]{2,1,0:T(8,128)(2,1)S(1)}, u32[]{:S(2)}, u32[]{:S(2)}) collective-permute-start(bf16[4,8,2688]{2,1,0:T(8,128)(2,1)S(1)} %get-tuple-element.49), channel_id=1, source_target_pairs={{0,2},{1,3},{2,0},{3,1},{4,6},{5,7},{6,4},{7,5},{8,10},{9,11},{10,... | collective-permute-start | bytes 516104 | tf_op jit(solution)/shard_map/ppermute | solution.py:457
  31.2 6.0 %collective-permute-start.13 = (bf16[4,8,2560]{2,1,0:T(8,128)(2,1)S(1)}, bf16[4,8,2560]{2,1,0:T(8,128)(2,1)S(1)}, u32[]{:S(2)}, u32[]{:S(2)}) collective-permute-start(bf16[4,8,2560]{2,1,0:T(8,128)(2,1)S(1)} %get-tuple-element.54), channel_id=1, source_target_pairs={{0,4},{1,5},{2,6},{3,7},{4,0},{5,1},{6,2},{7,3},{8,12},{9,13},{10,... | collective-permute-start | bytes 491528 | tf_op jit(solution)/shard_map/ppermute | solution.py:457
  35.5 6.1 %collective-permute-start.12 = (bf16[2,8,2816]{2,1,0:T(8,128)(2,1)S(1)}, bf16[2,8,2816]{2,1,0:T(8,128)(2,1)S(1)}, u32[]{:S(2)}, u32[]{:S(2)}) collective-permute-start(bf16[2,8,2816]{2,1,0:T(8,128)(2,1)S(1)} %get-tuple-element.51), channel_id=1, source_target_pairs={{0,4},{1,5},{2,6},{3,7},{4,0},{5,1},{6,2},{7,3},{8,12},{9,13},{10,... | collective-permute-start | bytes 270344 | tf_op jit(solution)/shard_map/ppermute | solution.py:457
  37.2 4.5 %collective-permute-start.14 = (bf16[2,8,2560]{2,1,0:T(8,128)(2,1)S(1)}, bf16[2,8,2560]{2,1,0:T(8,128)(2,1)S(1)}, u32[]{:S(2)}, u32[]{:S(2)}) collective-permute-start(bf16[2,8,2560]{2,1,0:T(8,128)(2,1)S(1)} %get-tuple-element.56), channel_id=1, source_target_pairs={{0,2},{1,3},{2,0},{3,1},{4,6},{5,7},{6,4},{7,5},{8,10},{9,11},{10,... | collective-permute-start | bytes 245768 | tf_op jit(solution)/shard_map/ppermute | solution.py:457
  41.7 6.3 %collective-permute-start.15 = (bf16[8,5120]{1,0:T(8,128)(2,1)S(1)}, bf16[8,5120]{1,0:T(8,128)(2,1)S(1)}, u32[]{:S(2)}, u32[]{:S(2)}) collective-permute-start(bf16[8,5120]{1,0:T(8,128)(2,1)S(1)} %get-tuple-element.57), channel_id=1, source_target_pairs={{0,24},{1,25},{2,26},{3,27},{4,28},{5,29},{6,30},{7,31},{8,16},{9,... | collective-permute-start | bytes 245768 | tf_op jit(solution)/shard_map/ppermute | solution.py:463
  45.4 4.4 %collective-permute-start.16 = (bf16[8,5120]{1,0:T(8,128)(2,1)S(1)}, bf16[8,5120]{1,0:T(8,128)(2,1)S(1)}, u32[]{:S(2)}, u32[]{:S(2)}) collective-permute-start(bf16[8,5120]{1,0:T(8,128)(2,1)S(1)} %get-tuple-element.58), channel_id=1, source_target_pairs={{0,16},{1,17},{2,18},{3,19},{4,20},{5,21},{6,22},{7,23},{8,24},{9,... | collective-permute-start | bytes 245768 | tf_op jit(solution)/shard_map/ppermute | solution.py:463
  46.6 4.6 %collective-permute-start.17 = (f32[8,128]{1,0:T(8,128)S(1)}, f32[8,128]{1,0:T(8,128)S(1)}, u32[]{:S(2)}, u32[]{:S(2)}) collective-permute-start(f32[8,128]{1,0:T(8,128)S(1)} %get-tuple-element.62), channel_id=1, source_target_pairs={{0,8},{1,9},{2,10},{3,11},{4,12},{5,13},{6,14},{7,15},{8,0},{9,1},... | collective-permute-start | bytes 12296 | tf_op jit(solution)/shard_map/ppermute | solution.py:457
